TPU v7x, 256 devices: a whole 4x4x8 slice. The times are simulated.
256 devices in a mesh: wide: 32 (over y, z), narrow: 8 (over x, core).
Axes of the slice: x: 4, y: 4, z: 8, core: 2. Of those that a mesh axis runs over, the one named last changes fastest.
Arguments:
- activations: bfloat16 [1024, 28672], P('wide', 'narrow'), may hold values from -6 to 6
- out_grads: bfloat16 [1024, 8192], P('wide'), may hold values from -6 to 6
- basis_in: bfloat16 [28672, 28672], P('narrow', 'wide'), may hold values from -0.03125 to 0.03125
- basis_out: bfloat16 [8192, 8192], P('wide', 'narrow'), may hold values from -0.0625 to 0.0625
- eigenvalues: bfloat16 [8192, 28672], P('narrow', 'wide'), may hold values from 0.29882812 to 10
- queries: bfloat16 [2, 8192, 28672], P(None, 'narrow', 'wide'), may hold values from -0.00036621094 to 0.00036621094
- doc_ids: int32 [1024], replicated, may hold values from 0 to 63, never falling along the last dimension, each value on 1 to 32 neighbouring positions
Outputs:
- scores: float32 [64, 2], replicated
Inputs may be any that keep to these rules, and one draw needn't show every extreme that they name: `doc_ids`: document numbers never fall along the tokens; each document has 1 to 32 tokens.
All inputs are finite; a program needn't handle non-finite values.
Results may differ from a plain program's by a relative error of at most 0.0051.
Values may be sent and summed in bfloat16 or wider, within the bound.
No kernel may reach another device: no remote copies, remote signals or barrier semaphores. Data moves between devices by JAX's collectives and lax.ppermute only.
A program may use at most 128 MiB of HBM per device.

v0:
```python
import functools

import jax
import jax.numpy as jnp
from jax import lax
from jax.experimental import pallas as pl
from jax.experimental.pallas import tpu as pltpu
from jax.sharding import Mesh
from jax.sharding import PartitionSpec as P

WIDE = ("y", "z")
NARROW = ("x", "c")
ALL = ("y", "z", "x", "c")
SIZE = {"y": 4, "z": 8, "x": 4, "c": 2}
DOCS = 64
DAMPING = 0.1
F32 = jnp.float32
BF16 = jnp.bfloat16
STEP = 512


def shift(value, axis, hops):
    size = SIZE[axis]
    return lax.ppermute(value, axis, [(i, (i + hops) % size) for i in range(size)])


def ring(chunk, axis):
    size = SIZE[axis]
    half = size // 2
    got = [(0, 0, chunk)]
    ahead = back = chunk
    for step in range(1, half):
        ahead, back = shift(ahead, axis, 1), shift(back, axis, -1)
        got += [(step, 0, ahead), (size - step, 0, back)]
    cut = chunk.shape[1] // 2
    got += [(half, 0, shift(ahead[:, :cut], axis, 1)), (half, cut, shift(back[:, cut:], axis, -1))]
    return got


def spread(value, axes, size):
    return lax.all_to_all(jnp.broadcast_to(value[None], (size,) + value.shape), axes, 0, 0)


def rotate_kernel(places, size, rows, here, *refs):
    chunks, (basis, out, lhs, rhs, total, chunk_sems, basis_sems) = refs[: len(places)], refs[len(places) :]
    steps = basis.shape[0] // STEP
    loads = []
    for n, ((back, first, width), chunk) in enumerate(zip(places, chunks)):
        slot = lax.rem(here[0] + size - back, size) * rows
        into = lhs.at[pl.ds(pl.multiple_of(slot, rows), rows), pl.ds(first, width)]
        loads.append(pltpu.make_async_copy(chunk, into, chunk_sems.at[n]))

    def basis_load(k):
        span = pl.ds(pl.multiple_of(k * STEP, STEP), STEP)
        return pltpu.make_async_copy(basis.at[span], rhs.at[k], basis_sems.at[k])

    for load in loads:
        load.start()
    for k in range(steps):
        basis_load(k).start()
    for load in loads:
        load.wait()
    basis_load(0).wait()
    total[...] = jnp.dot(lhs[:, :STEP], rhs[0], preferred_element_type=F32)

    @pl.loop(1, steps)
    def _(k):
        basis_load(k).wait()
        part = lhs[:, pl.ds(pl.multiple_of(k * STEP, STEP), STEP)]
        total[...] += jnp.dot(part, rhs[k], preferred_element_type=F32)

    out[...] = total[...].astype(BF16)


def rotate(chunks, axis, basis, here):
    size = SIZE[axis]
    rows = chunks[0][2].shape[0]
    depth, cols = basis.shape
    places = [(back, first, chunk.shape[1]) for back, first, chunk in chunks]
    count = size * rows
    steps = depth // STEP
    return pl.pallas_call(
        functools.partial(rotate_kernel, places, size, rows),
        out_shape=jax.ShapeDtypeStruct((count, cols), BF16),
        in_specs=[pl.BlockSpec(memory_space=pltpu.SMEM)]
        + [pl.BlockSpec(memory_space=pl.ANY)] * (len(places) + 1),
        out_specs=pl.BlockSpec(memory_space=pltpu.VMEM),
        scratch_shapes=[
            pltpu.VMEM((count, depth), BF16),
            pltpu.VMEM((steps, STEP, cols), BF16),
            pltpu.VMEM((count, cols), F32),
            pltpu.SemaphoreType.DMA((len(places),)),
            pltpu.SemaphoreType.DMA((steps,)),
        ],
        cost_estimate=pl.CostEstimate(
            flops=2 * count * depth * cols,
            bytes_accessed=2 * (count * depth + depth * cols + count * cols),
            transcendentals=0,
        ),
        compiler_params=pltpu.CompilerParams(vmem_limit_bytes=24 << 20),
        name="rotate_" + axis,
    )(here.reshape(1), *[chunk for _, _, chunk in chunks], basis)


def score_kernel(grads, precond, acts, ids, out):
    mixed = jnp.dot(grads[...], precond[0], preferred_element_type=F32)
    token = jnp.sum(mixed * acts[...].astype(F32), axis=1, keepdims=True)
    docs = lax.broadcasted_iota(jnp.int32, (token.shape[0], 128), 1)
    out[0] = jnp.sum(jnp.where(ids[...] == docs, token, 0.0), axis=0, keepdims=True)


def score(grads, precond, acts, ids):
    tokens, rows = grads.shape
    count, _, cols = precond.shape
    return pl.pallas_call(
        score_kernel,
        grid=(count,),
        out_shape=jax.ShapeDtypeStruct((count, 1, 128), F32),
        in_specs=[
            pl.BlockSpec((tokens, rows), lambda q: (0, 0)),
            pl.BlockSpec((1, rows, cols), lambda q: (q, 0, 0)),
            pl.BlockSpec((tokens, cols), lambda q: (0, 0)),
            pl.BlockSpec((tokens, 1), lambda q: (0, 0)),
        ],
        out_specs=pl.BlockSpec((1, 1, 128), lambda q: (q, 0, 0)),
        cost_estimate=pl.CostEstimate(
            flops=2 * count * tokens * rows * cols,
            bytes_accessed=2 * (tokens * rows + count * rows * cols + tokens * cols),
            transcendentals=0,
        ),
        compiler_params=pltpu.CompilerParams(vmem_limit_bytes=24 << 20),
        name="score",
    )(grads, precond, acts, ids.reshape(tokens, 1))


def over_narrow(partial):
    rows, cols = partial.shape
    parts = lax.all_to_all(partial.reshape(8, rows // 8, cols), NARROW, 0, 0)
    share = jnp.sum(parts.astype(F32), axis=0).astype(BF16)
    return spread(share, NARROW, 8).reshape(rows, cols)


def rotated_grads(out_grads, basis_out):
    cols = basis_out.shape[1]
    basis = spread(basis_out, "y", 4).reshape(1024, cols)
    rows = out_grads.reshape(32, 4, 8, 256).transpose(2, 0, 1, 3)
    rows = lax.all_to_all(rows, "z", 0, 0).reshape(256, 1024)
    partial = jnp.dot(rows, basis, preferred_element_type=F32).astype(BF16)
    parts = lax.all_to_all(partial.reshape(8, 32, cols), "z", 0, 0)
    return jnp.sum(parts.astype(F32), axis=0).astype(BF16)


def shards(activations, out_grads, basis_in, basis_out, eigenvalues, queries, doc_ids):
    y, z = lax.axis_index("y"), lax.axis_index("z")
    low = spread(activations[16:], "y", 4).reshape(64, -1)
    high = spread(activations[:16], "z", 8).reshape(128, -1)
    low = over_narrow(rotate(ring(low, "z"), "z", basis_in, z))
    high = over_narrow(rotate(ring(high, "y"), "y", basis_in, y))
    grads = rotated_grads(out_grads, basis_out)
    low_grads = spread(spread(grads[16:], "y", 4).reshape(64, -1), "z", 8).reshape(512, -1)
    high_grads = spread(spread(grads[:16], "z", 8).reshape(128, -1), "y", 4).reshape(512, -1)
    precond = (queries.astype(F32) / (eigenvalues.astype(F32)[None] + DAMPING)).astype(BF16)
    ids = doc_ids.reshape(4, 8, 2, 16)
    docs = score(low_grads, precond, low, ids[:, :, 1].transpose(1, 0, 2))
    docs += score(high_grads, precond, high, ids[:, :, 0])
    total = jnp.sum(spread(docs[:, 0, :DOCS].reshape(1, 2 * DOCS), ALL, 256), axis=0)
    return total.reshape(2, DOCS).T


def solution(mesh):
    finer = Mesh(mesh.devices.reshape(4, 8, 4, 2), ALL)
    in_specs = (
        P(WIDE, NARROW),
        P(WIDE, None),
        P(NARROW, WIDE),
        P(WIDE, NARROW),
        P(NARROW, WIDE),
        P(None, NARROW, WIDE),
        P(),
    )
    return jax.shard_map(
        shards, mesh=finer, in_specs=in_specs, out_specs=P(), check_vma=False
    )
```

profile of v0, /device:TPU:1, one launch (start us, length us, event | category | flops | bytes accessed | tf_op | source)
XLA Modules:
  0.0 363.0 jit_solution(3416792587879276005)
XLA Ops:
  1.4 24.9 %all_to_all.70 = bf16[8,32,4,256]{3,2,1,0:T(4,128)(2,1)S(1)} all-to-all(bf16[8,32,4,256]{3,2,1,0:T(4,128)(2,1)S(1)} %bitcast.43), channel_id=1, replica_groups=mesh['y'=4,'z'=8,'x'=4,'c'=2] {'z'}, dimensions={0} | all-to-all | bytes 1048576 | tf_op jit(solution)/shard_map/all_to_all | solution.py:147
  26.3 2.7 broadcast_in_dim.26
  29.0 4.2 %all-to-all-start.1 = ((bf16[4,256,1024]{2,1,0:T(8,128)(2,1)}), bf16[4,256,1024]{2,1,0:T(8,128)(2,1)S(1)}, u32[]{:S(2)}, u32[]{:S(2)}) async-start(bf16[4,256,1024]{2,1,0:T(8,128)(2,1)} %broadcast_in_dim.26), calls=%async_computation.1 | async-start | bytes 4194304 | tf_op jit(solution)/shard_map/all_to_all | solution.py:41
  33.2 23.6 %all-to-all-done.1 = bf16[4,256,1024]{2,1,0:T(8,128)(2,1)S(1)} async-done(((bf16[4,256,1024]{2,1,0:T(8,128)(2,1)}), bf16[4,256,1024]{2,1,0:T(8,128)(2,1)S(1)}, u32[]{:S(2)}, u32[]{:S(2)}) %all-to-all-start.1) | async-done | bytes 2097184 | tf_op jit(solution)/shard_map/all_to_all | solution.py:41
  58.3 3.5 all-to-all-start.5
  61.9 3.1 convolution_convert_fusion
  65.0 3.3 all-to-all-done.5
  68.3 4.0 %all-to-all-start.2 = ((bf16[8,32,1024]{2,1,0:T(8,128)(2,1)}), bf16[8,32,1024]{2,1,0:T(8,128)(2,1)S(1)}, u32[]{:S(2)}, u32[]{:S(2)}) async-start(bf16[8,32,1024]{2,1,0:T(8,128)(2,1)} %bitcast.2), calls=%async_computation.2 | async-start | bytes 1048576 | tf_op jit(solution)/shard_map/all_to_all | solution.py:149
  72.3 1.5 collective-permute-start
  73.7 10.3 %all-to-all-done.2 = bf16[8,32,1024]{2,1,0:T(8,128)(2,1)S(1)} async-done(((bf16[8,32,1024]{2,1,0:T(8,128)(2,1)}), bf16[8,32,1024]{2,1,0:T(8,128)(2,1)S(1)}, u32[]{:S(2)}, u32[]{:S(2)}) %all-to-all-start.2) | async-done | bytes 524320 | tf_op jit(solution)/shard_map/all_to_all | solution.py:149
  85.2 3.8 %all-to-all-start.10 = ((bf16[8,16,3584]{2,1,0:T(8,128)(2,1)}), bf16[8,16,3584]{2,1,0:T(8,128)(2,1)S(1)}, u32[]{:S(2)}, u32[]{:S(2)}) async-start(bf16[8,16,3584]{2,1,0:T(8,128)(2,1)} %broadcast_in_dim.35), calls=%async_computation.10 | async-start | bytes 1835008 | tf_op jit(solution)/shard_map/all_to_all | solution.py:41
  89.0 2.7 collective-permute-start.1
  91.7 3.1 collective-permute-done.refs_1_
  94.8 21.1 %collective-permute-done.1.refs_2_ = bf16[64,3584]{1,0:T(8,128)(2,1)S(1)} collective-permute-done((bf16[64,3584]{1,0:T(8,128)(2,1)S(1)}, bf16[64,3584]{1,0:T(8,128)(2,1)S(1)}, u32[]{:S(2)}, u32[]{:S(2)}) %collective-permute-start.1) | collective-permute-done | bytes 458784 | tf_op jit(solution)/shard_map/ppermute | solution.py:24
  115.9 8.3 %collective-permute-done.2.refs_3_ = bf16[64,3584]{1,0:T(8,128)(2,1)S(1)} collective-permute-done((bf16[64,3584]{1,0:T(8,128)(2,1)S(1)}, bf16[64,3584]{1,0:T(8,128)(2,1)S(1)}, u32[]{:S(2)}, u32[]{:S(2)}) %collective-permute-start.2) | collective-permute-done | bytes 458784 | tf_op jit(solution)/shard_map/ppermute | solution.py:24
  126.3 1.4 collective-permute-start.5
  128.5 5.9 %collective-permute-done.4.refs_5_ = bf16[64,3584]{1,0:T(8,128)(2,1)S(1)} collective-permute-done((bf16[64,3584]{1,0:T(8,128)(2,1)S(1)}, bf16[64,3584]{1,0:T(8,128)(2,1)S(1)}, u32[]{:S(2)}, u32[]{:S(2)}) %collective-permute-start.4) | collective-permute-done | bytes 458784 | tf_op jit(solution)/shard_map/ppermute | solution.py:24
  135.1 2.9 collective-permute-done.5.refs_6_
  141.8 3.3 all-to-all-start.3
  145.1 1.8 collective-permute-done.7.refs_8_
  146.9 2.8 copy-done.3
  153.8 8.9 %rotate_z.1 = bf16[512,896]{1,0:T(8,128)(2,1)S(1)} custom-call(s32[1]{0:T(128)} %bitcast.5.here, bf16[64,3584]{1,0:T(8,128)(2,1)S(1)} %bitcast.40, bf16[64,3584]{1,0:T(8,128)(2,1)S(1)} %copy-done.6, bf16[64,3584]{1,0:T(8,128)(2,1)S(1)} %copy-done.8, bf16[64,3584]{1,0:T(8,128)(2,1)S(1)} %copy-done.10, bf16[64,3584]{1,0:T(8,128)(2,1)S(1)} %copy-done.12, ...), custom_call_target="tpu_custom_call" | custom-call | flops 3288334336 | bytes 11010048 | tf_op jit(solution)/shard_map/rotate_z/pallas_call | solution.py:82
  162.7 27.4 %all_to_all.71 = bf16[8,64,896]{2,1,0:T(8,128)(2,1)S(1)} all-to-all(bf16[8,64,896]{2,1,0:T(8,128)(2,1)S(1)} %bitcast.36), channel_id=1, replica_groups=mesh['y'=4,'z'=8,'x'=4,'c'=2] {'x','c'}, dimensions={0} | all-to-all | bytes 1835008 | tf_op jit(solution)/shard_map/all_to_all | solution.py:138
  190.9 3.4 all-to-all-start.8
  194.3 1.6 collective-permute-start.8
  197.4 7.0 %all-to-all-done.8 = bf16[8,16,1024]{2,1,0:T(8,128)(2,1)S(1)} async-done(((bf16[8,16,1024]{2,1,0:T(8,128)(2,1)}), bf16[8,16,1024]{2,1,0:T(8,128)(2,1)S(1)}, u32[]{:S(2)}, u32[]{:S(2)}) %all-to-all-start.8) | async-done | bytes 262176 | tf_op jit(solution)/shard_map/all_to_all | solution.py:41
  204.5 19.0 %all_to_all.72 = bf16[8,64,896]{2,1,0:T(8,128)(2,1)S(1)} all-to-all(bf16[8,64,896]{2,1,0:T(8,128)(2,1)S(1)} %broadcast_in_dim.31), channel_id=1, replica_groups=mesh['y'=4,'z'=8,'x'=4,'c'=2] {'x','c'}, dimensions={0} | all-to-all | bytes 1835008 | tf_op jit(solution)/shard_map/all_to_all | solution.py:41
  224.7 4.4 %all-to-all-start.9 = ((bf16[4,128,1024]{2,1,0:T(8,128)(2,1)}), bf16[4,128,1024]{2,1,0:T(8,128)(2,1)S(1)}, u32[]{:S(2)}, u32[]{:S(2)}) async-start(bf16[4,128,1024]{2,1,0:T(8,128)(2,1)} %broadcast_in_dim.34), calls=%async_computation.9 | async-start | bytes 2097152 | tf_op jit(solution)/shard_map/all_to_all | solution.py:41
  229.1 1.8 slice.49
  230.9 1.5 collective-permute-start.10
  232.4 1.8 slice.50
  235.4 17.2 %collective-permute-done.10.refs_3_ = bf16[128,1792]{1,0:T(8,128)(2,1)S(1)} collective-permute-done((bf16[128,1792]{1,0:T(8,128)(2,1)}, bf16[128,1792]{1,0:T(8,128)(2,1)S(1)}, u32[]{:S(2)}, u32[]{:S(2)}) %collective-permute-start.10) | collective-permute-done | bytes 458784 | tf_op jit(solution)/shard_map/ppermute | solution.py:24
  252.6 2.8 copy-done.4
  255.4 7.0 %rotate_y.1 = bf16[512,896]{1,0:T(8,128)(2,1)S(1)} custom-call(s32[1]{0:T(128)} %bitcast.13.here, bf16[128,3584]{1,0:T(8,128)(2,1)S(1)} %bitcast.34, bf16[128,3584]{1,0:T(8,128)(2,1)} %collective-permute-done.8.refs_1_, bf16[128,3584]{1,0:T(8,128)(2,1)} %collective-permute-done.9.refs_2_, bf16[128,1792]{1,0:T(8,128)(2,1)S(1)} %collective-permute-done.10.refs_3_, ...), custom_call_target="tpu_custom_call" | custom-call | flops 3288334336 | bytes 11010048 | tf_op jit(solution)/shard_map/rotate_y/pallas_call | solution.py:82
  263.4 20.2 %all_to_all.73 = bf16[8,64,896]{2,1,0:T(8,128)(2,1)} all-to-all(bf16[8,64,896]{2,1,0:T(8,128)(2,1)} %bitcast.37), channel_id=1, replica_groups=mesh['y'=4,'z'=8,'x'=4,'c'=2] {'x','c'}, dimensions={0} | all-to-all | bytes 1835008 | tf_op jit(solution)/shard_map/all_to_all | solution.py:138
  284.7 3.6 all-to-all-start.4
  288.8 3.6 convert_add_fusion
  292.4 2.0 reduce_sum.47
  294.3 20.9 %all-to-all-done.4 = bf16[8,64,1024]{2,1,0:T(8,128)(2,1)S(1)} async-done(((bf16[8,64,1024]{2,1,0:T(8,128)(2,1)}), bf16[8,64,1024]{2,1,0:T(8,128)(2,1)S(1)}, u32[]{:S(2)}, u32[]{:S(2)}) %all-to-all-start.4) | async-done | bytes 1048608 | tf_op jit(solution)/shard_map/all_to_all | solution.py:41
  315.2 2.0 broadcast_in_dim.36
  317.2 6.7 %all-to-all-start.12 = ((bf16[8,64,896]{2,1,0:T(8,128)(2,1)}), bf16[8,64,896]{2,1,0:T(8,128)(2,1)}, u32[]{:S(2)}, u32[]{:S(2)}) async-start(bf16[8,64,896]{2,1,0:T(8,128)(2,1)} %broadcast_in_dim.36), calls=%async_computation.12 | async-start | bytes 1835008 | tf_op jit(solution)/shard_map/all_to_all | solution.py:41
  323.9 4.1 %divide_convert_fusion.precond = bf16[2,1024,896]{2,1,0:T(8,128)(2,1)S(1)} fusion(bf16[2,1024,896]{2,1,0:T(8,128)(2,1)} %param.12, f32[1024,896]{1,0:T(8,128)} %convert_add_fusion), kind=kLoop, calls=%fused_computation | loop fusion | flops 5505024 | bytes 11010048 | tf_op jit(solution)/shard_map/convert_element_type | solution.py:162
  328.0 2.7 score.2
  330.7 1.8 copy-done
  332.5 5.2 %all-to-all-done.12 = bf16[8,64,896]{2,1,0:T(8,128)(2,1)} async-done(((bf16[8,64,896]{2,1,0:T(8,128)(2,1)}), bf16[8,64,896]{2,1,0:T(8,128)(2,1)}, u32[]{:S(2)}, u32[]{:S(2)}) %all-to-all-start.12) | async-done | bytes 917536 | tf_op jit(solution)/shard_map/all_to_all | solution.py:41
  337.7 2.0 copy-done.1
  339.7 3.9 %score.3 = f32[2,1,128]{2,1,0:T(1,128)S(1)} custom-call(bf16[512,1024]{1,0:T(8,128)(2,1)S(1)} %bitcast.30, bf16[2,1024,896]{2,1,0:T(8,128)(2,1)S(1)} %copy-done.1, bf16[512,896]{1,0:T(8,128)(2,1)} %bitcast.16.acts, s32[512,1]{1,0:T(8,128)S(1)} %reshape_squeeze.4.ids), custom_call_target="tpu_custom_call" | custom-call | flops 1879048192 | bytes 5636096 | tf_op jit(solution)/shard_map/score/pallas_call | solution.py:115
  343.8 18.5 %all_to_all.74 = f32[256,1,128]{2,1,0:T(1,128)S(1)} all-to-all(f32[256,1,128]{2,1,0:T(1,128)S(1)} %broadcast_in_dim.76), channel_id=1, replica_groups=mesh['y'=4,'z'=8,'x'=4,'c'=2] {'y','z','x','c'}, dimensions={0} | all-to-all | bytes 262144 | tf_op jit(solution)/shard_map/all_to_all | solution.py:41
  (75 shorter events, 23.4 us)
Async XLA Ops:
  1.4 31.8 %copy-start.17 = (bf16[32,3584]{1,0:T(8,128)(2,1)S(1)}, bf16[32,3584]{1,0:T(8,128)(2,1)}, u32[]{:S(2)}) copy-start(bf16[32,3584]{1,0:T(8,128)(2,1)} %param.7) | copy-start | bytes 688132
  29.0 27.8 %all-to-all-start.1 = ((bf16[4,256,1024]{2,1,0:T(8,128)(2,1)}), bf16[4,256,1024]{2,1,0:T(8,128)(2,1)S(1)}, u32[]{:S(2)}, u32[]{:S(2)}) async-start(bf16[4,256,1024]{2,1,0:T(8,128)(2,1)} %broadcast_in_dim.26), calls=%async_computation.1 | async-start | bytes 4194304 | tf_op jit(solution)/shard_map/all_to_all | solution.py:41
  56.8 1.5 copy-start.13
  58.3 10.0 %all-to-all-start.5 = ((bf16[4,16,3584]{2,1,0:T(8,128)(2,1)}), bf16[4,16,3584]{2,1,0:T(8,128)(2,1)S(1)}, u32[]{:S(2)}, u32[]{:S(2)}) async-start(bf16[4,16,3584]{2,1,0:T(8,128)(2,1)} %broadcast_in_dim.30), calls=%async_computation.5 | async-start | bytes 917504 | tf_op jit(solution)/shard_map/all_to_all | solution.py:41
  68.3 15.7 %all-to-all-start.2 = ((bf16[8,32,1024]{2,1,0:T(8,128)(2,1)}), bf16[8,32,1024]{2,1,0:T(8,128)(2,1)S(1)}, u32[]{:S(2)}, u32[]{:S(2)}) async-start(bf16[8,32,1024]{2,1,0:T(8,128)(2,1)} %bitcast.2), calls=%async_computation.2 | async-start | bytes 1048576 | tf_op jit(solution)/shard_map/all_to_all | solution.py:149
  72.3 22.5 %collective-permute-start = (bf16[64,3584]{1,0:T(8,128)(2,1)S(1)}, bf16[64,3584]{1,0:T(8,128)(2,1)S(1)}, u32[]{:S(2)}, u32[]{:S(2)}) collective-permute-start(bf16[64,3584]{1,0:T(8,128)(2,1)S(1)} %bitcast.38), channel_id=1, source_target_pairs={{0,8},{8,16},{16,24},{24,32},{32,40},{40,48},{48,56},{56,0},{1,9},... | collective-permute-start | bytes 1376264 | tf_op jit(solution)/shard_map/ppermute | solution.py:24
  84.0 1.1 copy-start.14
  85.2 55.9 %all-to-all-start.10 = ((bf16[8,16,3584]{2,1,0:T(8,128)(2,1)}), bf16[8,16,3584]{2,1,0:T(8,128)(2,1)S(1)}, u32[]{:S(2)}, u32[]{:S(2)}) async-start(bf16[8,16,3584]{2,1,0:T(8,128)(2,1)} %broadcast_in_dim.35), calls=%async_computation.10 | async-start | bytes 1835008 | tf_op jit(solution)/shard_map/all_to_all | solution.py:41
  89.0 26.9 %collective-permute-start.1 = (bf16[64,3584]{1,0:T(8,128)(2,1)S(1)}, bf16[64,3584]{1,0:T(8,128)(2,1)S(1)}, u32[]{:S(2)}, u32[]{:S(2)}) collective-permute-start(bf16[64,3584]{1,0:T(8,128)(2,1)S(1)} %bitcast.39), channel_id=1, source_target_pairs={{0,56},{8,0},{16,8},{24,16},{32,24},{40,32},{48,40},{56,48},{1,57}... | collective-permute-start | bytes 1376264 | tf_op jit(solution)/shard_map/ppermute | solution.py:24
  94.8 52.1 %copy-start.5 = (bf16[64,3584]{1,0:T(8,128)(2,1)}, bf16[64,3584]{1,0:T(8,128)(2,1)S(1)}, u32[]{:S(2)}) copy-start(bf16[64,3584]{1,0:T(8,128)(2,1)S(1)} %collective-permute-done.refs_1_) | copy-start | bytes 1376260
  94.8 29.5 %collective-permute-start.2 = (bf16[64,3584]{1,0:T(8,128)(2,1)S(1)}, bf16[64,3584]{1,0:T(8,128)(2,1)S(1)}, u32[]{:S(2)}, u32[]{:S(2)}) collective-permute-start(bf16[64,3584]{1,0:T(8,128)(2,1)S(1)} %collective-permute-done.refs_1_), channel_id=1, source_target_pairs={{0,8},{8,16},{16,24},{24,32},{32,40},{40,48},{48,56},{56,0},{1,9},... | collective-permute-start | bytes 1376264 | tf_op jit(solution)/shard_map/ppermute | solution.py:24
  115.9 31.0 %copy-start.7 = (bf16[64,3584]{1,0:T(8,128)(2,1)}, bf16[64,3584]{1,0:T(8,128)(2,1)S(1)}, u32[]{:S(2)}) copy-start(bf16[64,3584]{1,0:T(8,128)(2,1)S(1)} %collective-permute-done.1.refs_2_) | copy-start | bytes 1376260
  115.9 10.4 %collective-permute-start.3 = (bf16[64,3584]{1,0:T(8,128)(2,1)S(1)}, bf16[64,3584]{1,0:T(8,128)(2,1)S(1)}, u32[]{:S(2)}, u32[]{:S(2)}) collective-permute-start(bf16[64,3584]{1,0:T(8,128)(2,1)S(1)} %collective-permute-done.1.refs_2_), channel_id=1, source_target_pairs={{0,56},{8,0},{16,8},{24,16},{32,24},{40,32},{48,40},{56,48},{1,57}... | collective-permute-start | bytes 1376264 | tf_op jit(solution)/shard_map/ppermute | solution.py:24
  124.3 10.1 %collective-permute-start.4 = (bf16[64,3584]{1,0:T(8,128)(2,1)S(1)}, bf16[64,3584]{1,0:T(8,128)(2,1)S(1)}, u32[]{:S(2)}, u32[]{:S(2)}) collective-permute-start(bf16[64,3584]{1,0:T(8,128)(2,1)S(1)} %collective-permute-done.2.refs_3_), channel_id=1, source_target_pairs={{0,8},{8,16},{16,24},{24,32},{32,40},{40,48},{48,56},{56,0},{1,9},... | collective-permute-start | bytes 1376264 | tf_op jit(solution)/shard_map/ppermute | solution.py:24
  124.3 0.8 copy-start.9
  126.3 11.7 %collective-permute-start.5 = (bf16[64,3584]{1,0:T(8,128)(2,1)S(1)}, bf16[64,3584]{1,0:T(8,128)(2,1)S(1)}, u32[]{:S(2)}, u32[]{:S(2)}) collective-permute-start(bf16[64,3584]{1,0:T(8,128)(2,1)S(1)} %collective-permute-done.3.refs_4_), channel_id=1, source_target_pairs={{0,56},{8,0},{16,8},{24,16},{32,24},{40,32},{48,40},{56,48},{1,57}... | collective-permute-start | bytes 1376264 | tf_op jit(solution)/shard_map/ppermute | solution.py:24
  127.7 0.8 copy-start.11
  135.1 10.0 %collective-permute-start.6 = (bf16[64,1792]{1,0:T(8,128)(2,1)}, bf16[64,1792]{1,0:T(8,128)(2,1)}, u32[]{:S(2)}, u32[]{:S(2)}) collective-permute-start(bf16[64,1792]{1,0:T(8,128)(2,1)} %slice.45), channel_id=1, source_target_pairs={{0,8},{8,16},{16,24},{24,32},{32,40},{40,48},{48,56},{56,0},{1,9},... | collective-permute-start | bytes 688136 | tf_op jit(solution)/shard_map/ppermute | solution.py:24
  138.7 8.2 %collective-permute-start.7 = (bf16[64,1792]{1,0:T(8,128)(2,1)}, bf16[64,1792]{1,0:T(8,128)(2,1)}, u32[]{:S(2)}, u32[]{:S(2)}) collective-permute-start(bf16[64,1792]{1,0:T(8,128)(2,1)} %slice.46), channel_id=1, source_target_pairs={{0,56},{8,0},{16,8},{24,16},{32,24},{40,32},{48,40},{56,48},{1,57}... | collective-permute-start | bytes 688136 | tf_op jit(solution)/shard_map/ppermute | solution.py:24
  141.8 21.0 %all-to-all-start.3 = ((bf16[4,16,1024]{2,1,0:T(8,128)(2,1)}), bf16[4,16,1024]{2,1,0:T(8,128)(2,1)S(1)}, u32[]{:S(2)}, u32[]{:S(2)}) async-start(bf16[4,16,1024]{2,1,0:T(8,128)(2,1)} %broadcast_in_dim.27), calls=%async_computation.3 | async-start | bytes 262144 | tf_op jit(solution)/shard_map/all_to_all | solution.py:41
  146.9 2.8 copy-start.3
  149.7 1.0 copy-start.6
  150.7 1.0 copy-start.8
  151.7 1.0 copy-start.10
  152.8 1.0 copy-start.12
  162.7 61.9 %copy-start.15 = (bf16[4,16,1024]{2,1,0:T(8,128)(2,1)}, bf16[4,16,1024]{2,1,0:T(8,128)(2,1)S(1)}, u32[]{:S(2)}) copy-start(bf16[4,16,1024]{2,1,0:T(8,128)(2,1)S(1)} %all-to-all-done.3) | copy-start | bytes 393220
  190.9 13.5 %all-to-all-start.8 = ((bf16[8,16,1024]{2,1,0:T(8,128)(2,1)}), bf16[8,16,1024]{2,1,0:T(8,128)(2,1)S(1)}, u32[]{:S(2)}, u32[]{:S(2)}) async-start(bf16[8,16,1024]{2,1,0:T(8,128)(2,1)} %broadcast_in_dim.32), calls=%async_computation.8 | async-start | bytes 524288 | tf_op jit(solution)/shard_map/all_to_all | solution.py:41
  194.3 34.8 %collective-permute-start.8 = (bf16[128,3584]{1,0:T(8,128)(2,1)S(1)}, bf16[128,3584]{1,0:T(8,128)(2,1)}, u32[]{:S(2)}, u32[]{:S(2)}) collective-permute-start(bf16[128,3584]{1,0:T(8,128)(2,1)S(1)} %bitcast.32), channel_id=1, source_target_pairs={{0,64},{64,128},{128,192},{192,0},{1,65},{65,129},{129,193},{193,1... | collective-permute-start | bytes 2752520 | tf_op jit(solution)/shard_map/ppermute | solution.py:24
  195.9 36.5 %collective-permute-start.9 = (bf16[128,3584]{1,0:T(8,128)(2,1)S(1)}, bf16[128,3584]{1,0:T(8,128)(2,1)}, u32[]{:S(2)}, u32[]{:S(2)}) collective-permute-start(bf16[128,3584]{1,0:T(8,128)(2,1)S(1)} %bitcast.33), channel_id=1, source_target_pairs={{0,192},{64,0},{128,64},{192,128},{1,193},{65,1},{129,65},{193,129... | collective-permute-start | bytes 2752520 | tf_op jit(solution)/shard_map/ppermute | solution.py:24
  224.7 38.7 %all-to-all-start.9 = ((bf16[4,128,1024]{2,1,0:T(8,128)(2,1)}), bf16[4,128,1024]{2,1,0:T(8,128)(2,1)S(1)}, u32[]{:S(2)}, u32[]{:S(2)}) async-start(bf16[4,128,1024]{2,1,0:T(8,128)(2,1)} %broadcast_in_dim.34), calls=%async_computation.9 | async-start | bytes 2097152 | tf_op jit(solution)/shard_map/all_to_all | solution.py:41
  230.9 21.7 %collective-permute-start.10 = (bf16[128,1792]{1,0:T(8,128)(2,1)}, bf16[128,1792]{1,0:T(8,128)(2,1)S(1)}, u32[]{:S(2)}, u32[]{:S(2)}) collective-permute-start(bf16[128,1792]{1,0:T(8,128)(2,1)} %slice.49), channel_id=1, source_target_pairs={{0,64},{64,128},{128,192},{192,0},{1,65},{65,129},{129,193},{193,1... | collective-permute-start | bytes 1376264 | tf_op jit(solution)/shard_map/ppermute | solution.py:24
  234.2 18.4 %collective-permute-start.11 = (bf16[128,1792]{1,0:T(8,128)(2,1)}, bf16[128,1792]{1,0:T(8,128)(2,1)}, u32[]{:S(2)}, u32[]{:S(2)}) collective-permute-start(bf16[128,1792]{1,0:T(8,128)(2,1)} %slice.50), channel_id=1, source_target_pairs={{0,192},{64,0},{128,64},{192,128},{1,193},{65,1},{129,65},{193,129... | collective-permute-start | bytes 1376264 | tf_op jit(solution)/shard_map/ppermute | solution.py:24
  252.6 2.8 copy-start.4
  255.4 28.1 %copy-start.16 = (bf16[4,16,1024]{2,1,0:T(8,128)(2,1)S(1)}, bf16[4,16,1024]{2,1,0:T(8,128)(2,1)}, u32[]{:S(2)}) copy-start(bf16[4,16,1024]{2,1,0:T(8,128)(2,1)} %copy-done.15) | copy-start | bytes 393220
  262.4 0.9 copy-start.2
  263.4 24.9 %copy-start.18 = (s32[1024]{0:T(1024)S(1)}, s32[1024]{0:T(1024)}, u32[]{:S(2)}) copy-start(s32[1024]{0:T(1024)} %param.13) | copy-start | bytes 12292
  284.7 30.6 %all-to-all-start.4 = ((bf16[8,64,1024]{2,1,0:T(8,128)(2,1)}), bf16[8,64,1024]{2,1,0:T(8,128)(2,1)S(1)}, u32[]{:S(2)}, u32[]{:S(2)}) async-start(bf16[8,64,1024]{2,1,0:T(8,128)(2,1)} %broadcast_in_dim.29), calls=%async_computation.4 | async-start | bytes 2097152 | tf_op jit(solution)/shard_map/all_to_all | solution.py:41
  317.2 20.5 %all-to-all-start.12 = ((bf16[8,64,896]{2,1,0:T(8,128)(2,1)}), bf16[8,64,896]{2,1,0:T(8,128)(2,1)}, u32[]{:S(2)}, u32[]{:S(2)}) async-start(bf16[8,64,896]{2,1,0:T(8,128)(2,1)} %broadcast_in_dim.36), calls=%async_computation.12 | async-start | bytes 1835008 | tf_op jit(solution)/shard_map/all_to_all | solution.py:41
  330.7 1.8 copy-start
  337.7 2.0 copy-start.1
where the time goes:
time: 365 us; the launch traced here: 363 us
  waiting for transfers between devices  132 us (36%)
  blocking collectives  110 us (30%)
  starting transfers between devices  49.2 us (13%)
  local copies, waits for them, and re-layouts  34.8 us (10%)
  Pallas kernels  22.5 us (6%)
  other arithmetic  11 us (3%)
    ppermute x12, waiting for transfers between devices, shift(): lax.ppermute(value, axis, [(i, (i + hops) % size) for i in range(size)])  61.6 us
    all_to_all x8, waiting for transfers between devices, spread(): lax.all_to_all(jnp.broadcast_to(value[None], (size,) + value.shape), axes...  60.1 us
    all_to_all x2, blocking collectives, over_narrow(): parts = lax.all_to_all(partial.reshape(8, rows // 8, cols), NARROW, 0, 0)  47.6 us
    all_to_all x2, blocking collectives, spread(): lax.all_to_all(jnp.broadcast_to(value[None], (size,) + value.shape), axes...  37.6 us
    all_to_all x8, starting transfers between devices, spread(): lax.all_to_all(jnp.broadcast_to(value[None], (size,) + value.shape), axes...  32.9 us
    all_to_all x1, blocking collectives, rotated_grads(): rows = lax.all_to_all(rows, 'z', 0, 0).reshape(256, 1024)  24.9 us
    unnamed x40, local copies, waits for them, and re-layouts  18 us
    pallas_call x2, Pallas kernels, rotate(): pl.pallas_call(functools.partial(rotate_kernel, places, size, rows), out_...  15.9 us
  transfers between devices with their start and end apart: 21, of which 14 were waited for; matrix products, arithmetic and copies ran while one was open for 6% of the time, Pallas kernels for 5%

commit v1 on v0

v1 whole, which is shorter than its diff:
```python
import functools

import jax
import jax.numpy as jnp
from jax import lax
from jax.experimental import pallas as pl
from jax.experimental.pallas import tpu as pltpu
from jax.sharding import Mesh
from jax.sharding import PartitionSpec as P

WIDE = ("y", "z")
NARROW = ("x", "c")
ALL = ("y", "z", "x", "c")
SIZE = {"y": 4, "z": 8, "x": 4, "c": 2}
DOCS = 64
DAMPING = 0.1
F32 = jnp.float32
BF16 = jnp.bfloat16
STEP = 512
SPLIT = 3072


def shift(value, axis, hops):
    size = SIZE[axis]
    return lax.ppermute(value, axis, [(i, (i + hops) % size) for i in range(size)])


def ring(chunk, axis):
    size = SIZE[axis]
    half = size // 2
    got = [(0, 0, chunk)]
    ahead = back = chunk
    for step in range(1, half):
        ahead, back = shift(ahead, axis, 1), shift(back, axis, -1)
        got += [(step, 0, ahead), (size - step, 0, back)]
    cut = chunk.shape[1] // 2
    got += [(half, 0, shift(ahead[:, :cut], axis, 1)), (half, cut, shift(back[:, cut:], axis, -1))]
    return got


def spread(value, axes, size):
    return lax.all_to_all(jnp.broadcast_to(value[None], (size,) + value.shape), axes, 0, 0)


def join_kernel(places, rows, here, *refs):
    chunks, out = refs[: len(places)], refs[-1]
    for back, chunk in zip(places, chunks):
        row = pl.multiple_of(lax.rem(here[0] + len(places) - back, len(places)) * rows, rows)
        out[pl.ds(row, rows), :] = chunk[...]


def join(value, axis, here):
    rows, cols = value.shape
    size = SIZE[axis]
    places = [0, 1, size - 1] + list(range(2, size - 1))
    chunks = [value] + [shift(value, axis, back) for back in places[1:]]
    return pl.pallas_call(
        functools.partial(join_kernel, places, rows),
        out_shape=jax.ShapeDtypeStruct((size * rows, cols), BF16),
        in_specs=[pl.BlockSpec(memory_space=pltpu.SMEM)] + [pl.BlockSpec(memory_space=pltpu.VMEM)] * size,
        out_specs=pl.BlockSpec(memory_space=pltpu.VMEM),
        cost_estimate=pl.CostEstimate(flops=0, bytes_accessed=4 * size * rows * cols, transcendentals=0),
        name="join",
    )(here, *chunks)


def rotate_kernel(y_places, z_places, here, *refs):
    count = len(y_places) + len(z_places)
    chunks, (own, other, out, lhs, rhs, total, chunk_sems, basis_sems) = refs[:count], refs[count:]
    half = own.shape[0]
    steps = half // STEP
    loads = []

    def load(chunk, row, rows, first, width):
        into = lhs.at[pl.ds(pl.multiple_of(row, rows), rows), pl.ds(first, width)]
        loads.append(pltpu.make_async_copy(chunk, into, chunk_sems.at[len(loads)]))

    for (back, first, width), chunk in zip(y_places, chunks):
        load(chunk, lax.rem(here[0] + 4 - back, 4) * 128, 128, first, width)
    for (back, first, width), chunk in zip(z_places, chunks[len(y_places) :]):
        for y in range(4):
            row = y * 128 + lax.rem(here[1] + 8 - back, 8) * 16
            load(chunk.at[pl.ds(y * 16, 16)], row, 16, SPLIT + first, width)

    def basis_load(basis, k, at):
        span = pl.ds(pl.multiple_of(k * STEP, STEP), STEP)
        return pltpu.make_async_copy(basis.at[span], rhs.at[at], basis_sems.at[at])

    for n in loads:
        n.start()
    for basis, base in ((own, 0), (other, steps)):
        for k in range(steps):
            basis_load(basis, k, base + k).start()
    for n in loads:
        n.wait()
    total[...] = jnp.zeros_like(total)

    @pl.loop(0, steps)
    def _(k):
        basis_load(own, 0, 2 * k).wait()
        basis_load(own, 0, 2 * k + 1).wait()
        part = lhs[:, pl.ds(pl.multiple_of(k * 2 * STEP, 2 * STEP), 2 * STEP)]
        both = rhs[pl.ds(2 * k, 2)].reshape(2 * STEP, rhs.shape[2])
        total[...] += jnp.dot(part, both, preferred_element_type=F32)

    out[...] = total[...].astype(BF16)


def rotate(y_chunks, z_chunks, own, other, here):
    depth, cols = own.shape
    y_places, z_places = (
        [(back, first, chunk.shape[1]) for back, first, chunk in chunks] for chunks in (y_chunks, z_chunks)
    )
    count = 512
    steps = 2 * depth // STEP
    return pl.pallas_call(
        functools.partial(rotate_kernel, y_places, z_places),
        out_shape=jax.ShapeDtypeStruct((count, cols), BF16),
        in_specs=[pl.BlockSpec(memory_space=pltpu.SMEM)]
        + [pl.BlockSpec(memory_space=pl.ANY)] * (len(y_places) + len(z_places))
        + [pl.BlockSpec(memory_space=pltpu.HBM)] * 2,
        out_specs=pl.BlockSpec(memory_space=pltpu.VMEM),
        scratch_shapes=[
            pltpu.VMEM((count, 2 * depth), BF16),
            pltpu.VMEM((steps, STEP, cols), BF16),
            pltpu.VMEM((count, cols), F32),
            pltpu.SemaphoreType.DMA((len(y_places) + 4 * len(z_places),)),
            pltpu.SemaphoreType.DMA((steps,)),
        ],
        cost_estimate=pl.CostEstimate(
            flops=4 * count * depth * cols,
            bytes_accessed=2 * (2 * count * depth + 2 * depth * cols + count * cols),
            transcendentals=0,
        ),
        compiler_params=pltpu.CompilerParams(vmem_limit_bytes=32 << 20),
        name="rotate",
    )(here, *[chunk for _, _, chunk in y_chunks + z_chunks], own, other)


def score_kernel(grads, own, other, acts, ids, out):
    half = own.shape[1]
    mixed = jnp.dot(grads[:, :half], own[0], preferred_element_type=F32)
    mixed += jnp.dot(grads[:, half:], other[0], preferred_element_type=F32)
    token = jnp.sum(mixed * acts[...].astype(F32), axis=1, keepdims=True)
    docs = lax.broadcasted_iota(jnp.int32, (token.shape[0], 128), 1)
    out[0] = jnp.sum(jnp.where(ids[...] == docs, token, 0.0), axis=0, keepdims=True)


def score(grads, own, other, acts, ids):
    tokens, rows = grads.shape
    count, half, cols = own.shape
    return pl.pallas_call(
        score_kernel,
        grid=(count,),
        out_shape=jax.ShapeDtypeStruct((count, 1, 128), F32),
        in_specs=[
            pl.BlockSpec((tokens, rows), lambda q: (0, 0)),
            pl.BlockSpec((1, half, cols), lambda q: (q, 0, 0)),
            pl.BlockSpec((1, half, cols), lambda q: (q, 0, 0)),
            pl.BlockSpec((tokens, cols), lambda q: (0, 0)),
            pl.BlockSpec((tokens, 1), lambda q: (0, 0)),
        ],
        out_specs=pl.BlockSpec((1, 1, 128), lambda q: (q, 0, 0)),
        cost_estimate=pl.CostEstimate(
            flops=2 * count * tokens * rows * cols,
            bytes_accessed=2 * (tokens * rows + count * rows * cols + tokens * cols),
            transcendentals=0,
        ),
        compiler_params=pltpu.CompilerParams(vmem_limit_bytes=24 << 20),
        name="score",
    )(grads, own, other, acts, ids.reshape(tokens, 1))


def over_x(partial):
    rows, cols = partial.shape
    parts = lax.all_to_all(partial.reshape(4, rows // 4, cols), "x", 0, 0)
    share = jnp.sum(parts.astype(F32), axis=0).astype(BF16)
    return spread(share, "x", 4).reshape(rows, cols)


def swap(value):
    return shift(value, "c", 1)


def shards(activations, out_grads, basis_in, basis_out, eigenvalues, queries, doc_ids):
    y, z, c = (lax.axis_index(axis) for axis in "yzc")
    here = jnp.stack([y, z])
    other_in = swap(basis_in)
    mine = lax.dynamic_slice_in_dim(activations, c * 16, 16)
    theirs = swap(lax.dynamic_slice_in_dim(activations, (1 - c) * 16, 16))
    low = join(jnp.concatenate([mine[:, SPLIT:], theirs], axis=1), "y", here)
    rows = lax.dynamic_slice_in_dim(out_grads, c * 16, 16).reshape(16, 4, 8, 256)
    rows = rows.transpose(2, 0, 1, 3).reshape(8, 16, 1024)
    copies = jnp.broadcast_to(mine[None, :, :SPLIT], (8, 16, SPLIT))
    sent = lax.all_to_all(jnp.concatenate([copies, rows], axis=2), "z", 0, 0)
    high = sent[:, :, :SPLIT].reshape(128, SPLIT)
    rows = sent[:, :, SPLIT:].reshape(128, 1024)
    partial_acts = rotate(ring(high, "y"), ring(low, "z"), basis_in, other_in, here)
    rot_acts = over_x(partial_acts)

    basis = lax.all_gather(basis_out, "y", axis=0, tiled=True)
    partial = [jnp.dot(part, basis, preferred_element_type=F32).astype(BF16) for part in (rows, swap(rows))]
    partial = jnp.stack([part.reshape(8, 16, 1024) for part in partial], axis=1)
    parts = lax.all_to_all(partial, "z", 0, 0)
    grads = jnp.sum(parts.astype(F32), axis=0).astype(BF16)
    grads = jnp.concatenate([grads[0], swap(grads[1])], axis=1)
    grads = spread(grads, "z", 8).reshape(128, 2048)
    rot_grads = lax.all_gather(grads, "y", axis=0, tiled=True)
    precond = (queries.astype(F32) / (eigenvalues.astype(F32)[None] + DAMPING)).astype(BF16)
    ids = lax.dynamic_index_in_dim(doc_ids.reshape(32, 2, 16), c, 1, keepdims=False)
    docs = score(rot_grads, precond, swap(precond), rot_acts, ids)
    total = jnp.sum(spread(docs[:, 0, :DOCS].reshape(1, 2 * DOCS), ALL, 256), axis=0)
    return total.reshape(2, DOCS).T


def solution(mesh):
    finer = Mesh(mesh.devices.reshape(4, 8, 4, 2), ALL)
    in_specs = (
        P(WIDE, NARROW),
        P(WIDE, None),
        P(NARROW, WIDE),
        P(WIDE, NARROW),
        P(NARROW, WIDE),
        P(None, NARROW, WIDE),
        P(),
    )
    return jax.shard_map(
        shards, mesh=finer, in_specs=in_specs, out_specs=P(), check_vma=False
    )
```

time: 365 us -> 246 us (0.67)
  blocking collectives: 110 us -> 41.3 us
  waiting for transfers between devices: 132 us -> 90.6 us
  local copies, waits for them, and re-layouts: 34.8 us -> 13.6 us
  between operations: 0.27 us -> 13.7 us
    all_to_all x3 -> x1, blocking collectives: 72.6 us -> 12.6 us  [over_x(): parts = lax.all_to_all(partial.reshape(4, rows // 4, cols), 'x', 0, 0)]
    all_to_all x8 -> x2, waiting for transfers between devices: 60.1 us -> 10.3 us  [spread(): lax.all_to_all(jnp.broadcast_to(value[None], (size,) + value.shape), axes...]
    all_to_all x8 -> x2, starting transfers between devices: 32.9 us -> 9.86 us  [spread(): lax.all_to_all(jnp.broadcast_to(value[None], (size,) + value.shape), axes...]
    all_to_all x1 -> x2, waiting for transfers between devices: 10.3 us -> 28.2 us  [the longest x1 28.2 us: shards(): sent = lax.all_to_all(jnp.concatenate([copies, rows], axis=2), 'z', 0, 0)]
    ppermute x12 -> x20, waiting for transfers between devices: 61.6 us -> 51.3 us  [shift(): lax.ppermute(value, axis, [(i, (i + hops) % size) for i in range(size)])]
    ppermute x12 -> x20, starting transfers between devices: 12.4 us -> 22.6 us  [shift(): lax.ppermute(value, axis, [(i, (i + hops) % size) for i in range(size)])]
    unnamed x40 -> x35, local copies, waits for them, and re-layouts: 18 us -> 8.15 us
    all_to_all x1 -> x2, starting transfers between devices: 3.97 us -> 13.4 us  [the longest x1 9.01 us: shards(): sent = lax.all_to_all(jnp.concatenate([copies, rows], axis=2), 'z', 0, 0)]
  transfers between devices with their start and end apart: 21 -> 26, of which waited for: 14 -> 13; matrix products, arithmetic and copies ran while one was open for 6% -> 9% of each run, Pallas kernels for 5% -> 7%
where the time goes in v1:
time: 246 us; the launch traced here: 245 us
  waiting for transfers between devices  90.6 us (37%)
  starting transfers between devices  45.8 us (19%)
  blocking collectives  41.3 us (17%)
  Pallas kernels  23 us (9%)
  between operations  13.7 us (6%)
  local copies, waits for them, and re-layouts  13.6 us (6%)
  other arithmetic  12.6 us (5%)
  matrix products  4.07 us (2%)
    ppermute x20, waiting for transfers between devices, shift(): lax.ppermute(value, axis, [(i, (i + hops) % size) for i in range(size)])  51.3 us
    all_to_all x1, blocking collectives, spread(): lax.all_to_all(jnp.broadcast_to(value[None], (size,) + value.shape), axes...  28.6 us
    all_to_all x1, waiting for transfers between devices, shards(): sent = lax.all_to_all(jnp.concatenate([copies, rows], axis=2), 'z', 0, 0)  28.2 us
    ppermute x20, starting transfers between devices, shift(): lax.ppermute(value, axis, [(i, (i + hops) % size) for i in range(size)])  22.6 us
    pallas_call x1, Pallas kernels, rotate(): pl.pallas_call(functools.partial(rotate_kernel, y_places, z_places), out_...  14.1 us
    all_to_all x1, blocking collectives, over_x(): parts = lax.all_to_all(partial.reshape(4, rows // 4, cols), 'x', 0, 0)  12.6 us
    all_to_all x2, waiting for transfers between devices, spread(): lax.all_to_all(jnp.broadcast_to(value[None], (size,) + value.shape), axes...  10.3 us
    all_to_all x2, starting transfers between devices, spread(): lax.all_to_all(jnp.broadcast_to(value[None], (size,) + value.shape), axes...  9.86 us
  transfers between devices with their start and end apart: 26, of which 13 were waited for; matrix products, arithmetic and copies ran while one was open for 9% of the time, Pallas kernels for 7%

profile of v1, /device:TPU:1, one launch (start us, length us, event | category | flops | bytes accessed | tf_op | source)
XLA Modules:
  0.0 244.7 jit_solution(17943544683870956525)
XLA Ops:
  7.9 0.9 constant_dynamic-slice_fusion
  8.9 1.1 pad_maximum_fusion
  10.0 9.0 %all-to-all-start = ((bf16[8,16,4096]{2,1,0:T(8,128)(2,1)}), bf16[8,16,4096]{2,1,0:T(8,128)(2,1)S(1)}, u32[]{:S(2)}, u32[]{:S(2)}) async-start(bf16[8,16,4096]{2,1,0:T(8,128)(2,1)} %pad_maximum_fusion), calls=%async_computation | async-start | bytes 2097152 | tf_op jit(solution)/shard_map/all_to_all | solution.py:195
  19.0 1.0 collective-permute-start.19
  20.0 28.2 %all-to-all-done = bf16[8,16,4096]{2,1,0:T(8,128)(2,1)S(1)} async-done(((bf16[8,16,4096]{2,1,0:T(8,128)(2,1)}), bf16[8,16,4096]{2,1,0:T(8,128)(2,1)S(1)}, u32[]{:S(2)}, u32[]{:S(2)}) %all-to-all-start) | async-done | bytes 1048608 | tf_op jit(solution)/shard_map/all_to_all | solution.py:195
  48.8 2.0 convolution_convert_fusion.1
  50.9 2.0 convolution_convert_fusion
  53.8 4.3 %all-to-all-start.1 = ((bf16[8,2,16,1024]{3,2,1,0:T(8,128)(2,1)}), bf16[8,2,16,1024]{3,2,1,0:T(8,128)(2,1)S(1)}, u32[]{:S(2)}, u32[]{:S(2)}) async-start(bf16[8,2,16,1024]{3,2,1,0:T(8,128)(2,1)} %pad_maximum_fusion.1), calls=%async_computation.1 | async-start | bytes 1048576 | tf_op jit(solution)/shard_map/all_to_all | solution.py:204
  58.1 1.0 collective-permute-start.7
  59.2 1.0 collective-permute-done.7
  60.2 1.6 collective-permute-start.10
  62.2 2.3 collective-permute-start.9
  65.1 1.4 collective-permute-done.10.refs_3_
  66.5 3.5 %collective-permute-done.8.refs_1_ = bf16[16,4096]{1,0:T(8,128)(2,1)S(1)} collective-permute-done((bf16[16,4096]{1,0:T(8,128)(2,1)S(1)}, bf16[16,4096]{1,0:T(8,128)(2,1)S(1)}, u32[]{:S(2)}, u32[]{:S(2)}) %collective-permute-start.8) | collective-permute-done | bytes 131104 | tf_op jit(solution)/shard_map/ppermute | solution.py:25
  71.2 2.0 join.1.refs_5_
  73.2 1.7 collective-permute-start.11
  74.9 1.2 collective-permute-start.12
  76.2 0.9 collective-permute-start.1
  77.1 3.7 %convert_add_fusion = f32[1024,896]{1,0:T(8,128)} fusion(bf16[1024,896]{1,0:T(8,128)(2,1)} %param.11), kind=kLoop, calls=%fused_computation.1 | loop fusion | flops 1835008 | bytes 5505024 | tf_op jit(solution)/shard_map/add | solution.py:209
  80.9 7.3 %collective-permute-done.11.refs_6_ = bf16[64,4096]{1,0:T(8,128)(2,1)S(1)} collective-permute-done((bf16[64,4096]{1,0:T(8,128)(2,1)}, bf16[64,4096]{1,0:T(8,128)(2,1)S(1)}, u32[]{:S(2)}, u32[]{:S(2)}) %collective-permute-start.11) | collective-permute-done | bytes 524320 | tf_op jit(solution)/shard_map/ppermute | solution.py:25
  88.1 2.7 %collective-permute-start.14 = (bf16[64,4096]{1,0:T(8,128)(2,1)S(1)}, bf16[64,4096]{1,0:T(8,128)(2,1)}, u32[]{:S(2)}, u32[]{:S(2)}) collective-permute-start(bf16[64,4096]{1,0:T(8,128)(2,1)S(1)} %collective-permute-done.12.refs_7_), channel_id=1, source_target_pairs={{0,56},{8,0},{16,8},{24,16},{32,24},{40,32},{48,40},{56,48},{1,57}... | collective-permute-start | bytes 1572872 | tf_op jit(solution)/shard_map/ppermute | solution.py:25
  90.8 0.9 broadcast_in_dim.11
  91.7 6.4 %all-to-all-start.2 = ((bf16[8,16,2048]{2,1,0:T(8,128)(2,1)}), bf16[8,16,2048]{2,1,0:T(8,128)(2,1)}, u32[]{:S(2)}, u32[]{:S(2)}) async-start(bf16[8,16,2048]{2,1,0:T(8,128)(2,1)} %broadcast_in_dim.11), calls=%async_computation.2 | async-start | bytes 1048576 | tf_op jit(solution)/shard_map/all_to_all | solution.py:42
  98.1 6.0 %divide_convert_fusion.own = bf16[2,1024,896]{2,1,0:T(8,128)(2,1)} fusion(bf16[2,1024,896]{2,1,0:T(8,128)(2,1)} %param.12, f32[1024,896]{1,0:T(8,128)} %convert_add_fusion), kind=kLoop, calls=%fused_computation | loop fusion | flops 5505024 | bytes 11010048 | tf_op jit(solution)/shard_map/convert_element_type | solution.py:209
  104.2 2.3 collective-permute-start.2
  106.5 1.7 collective-permute-start.15
  108.3 2.7 %collective-permute-start.4 = (bf16[128,3072]{1,0:T(8,128)(2,1)S(1)}, bf16[128,3072]{1,0:T(8,128)(2,1)S(1)}, u32[]{:S(2)}, u32[]{:S(2)}) collective-permute-start(bf16[128,3072]{1,0:T(8,128)(2,1)S(1)} %bitcast.31), channel_id=1, source_target_pairs={{0,192},{64,0},{128,64},{192,128},{1,193},{65,1},{129,65},{193,129... | collective-permute-start | bytes 2359304 | tf_op jit(solution)/shard_map/ppermute | solution.py:25
  111.0 1.7 all-to-all-done.2
  112.7 12.2 %collective-permute-done.15.refs_10_ = bf16[64,4096]{1,0:T(8,128)(2,1)} collective-permute-done((bf16[64,4096]{1,0:T(8,128)(2,1)}, bf16[64,4096]{1,0:T(8,128)(2,1)}, u32[]{:S(2)}, u32[]{:S(2)}) %collective-permute-start.15) | collective-permute-done | bytes 524320 | tf_op jit(solution)/shard_map/ppermute | solution.py:25
  124.9 1.0 slice.50
  125.9 2.2 collective-permute-done.3.refs_1_
  128.0 1.2 collective-permute-start.17
  129.4 7.9 %collective-permute-done.16.refs_11_ = bf16[64,4096]{1,0:T(8,128)(2,1)S(1)} collective-permute-done((bf16[64,4096]{1,0:T(8,128)(2,1)}, bf16[64,4096]{1,0:T(8,128)(2,1)S(1)}, u32[]{:S(2)}, u32[]{:S(2)}) %collective-permute-start.16) | collective-permute-done | bytes 524320 | tf_op jit(solution)/shard_map/ppermute | solution.py:25
  137.3 1.2 collective-permute-start.18
  138.5 4.6 %collective-permute-done.18.refs_13_ = bf16[64,2048]{1,0:T(8,128)(2,1)S(1)} collective-permute-done((bf16[64,2048]{1,0:T(8,128)(2,1)S(1)}, bf16[64,2048]{1,0:T(8,128)(2,1)S(1)}, u32[]{:S(2)}, u32[]{:S(2)}) %collective-permute-start.18) | collective-permute-done | bytes 262176 | tf_op jit(solution)/shard_map/ppermute | solution.py:25
  143.2 5.8 %collective-permute-done.5.refs_3_ = bf16[128,1536]{1,0:T(8,128)(2,1)S(1)} collective-permute-done((bf16[128,1536]{1,0:T(8,128)(2,1)S(1)}, bf16[128,1536]{1,0:T(8,128)(2,1)S(1)}, u32[]{:S(2)}, u32[]{:S(2)}) %collective-permute-start.5) | collective-permute-done | bytes 393248 | tf_op jit(solution)/shard_map/ppermute | solution.py:25
  149.0 5.4 %collective-permute-done.6.refs_4_ = bf16[128,1536]{1,0:T(8,128)(2,1)S(1)} collective-permute-done((bf16[128,1536]{1,0:T(8,128)(2,1)S(1)}, bf16[128,1536]{1,0:T(8,128)(2,1)S(1)}, u32[]{:S(2)}, u32[]{:S(2)}) %collective-permute-start.6) | collective-permute-done | bytes 393248 | tf_op jit(solution)/shard_map/ppermute | solution.py:25
  154.5 2.8 %copy-done.3 = bf16[3584,896]{1,0:T(8,128)(2,1)S(1)} copy-done((bf16[3584,896]{1,0:T(8,128)(2,1)S(1)}, bf16[3584,896]{1,0:T(8,128)(2,1)}, u32[]{:S(2)}) %copy-start.3) | copy-done | bytes 6422552
  157.3 1.0 copy-done.6
  158.3 1.0 copy-done.8
  159.4 14.1 %rotate.1 = bf16[512,896]{1,0:T(8,128)(2,1)S(1)} custom-call(s32[2]{0:T(128)S(1)} %copy-done.2, bf16[128,3072]{1,0:T(8,128)(2,1)S(1)} %bitcast.32, bf16[128,3072]{1,0:T(8,128)(2,1)S(1)} %collective-permute-done.3.refs_1_, bf16[128,3072]{1,0:T(8,128)(2,1)S(1)} %collective-permute-done.4.refs_2_, bf16[128,1536]{1,0:T(8,128)(2,1)S(1)} %collective-permute-done.5.refs_3_, ...), custom_call_target="tpu_custom_call" | custom-call | flops 6576668672 | bytes 21102592 | tf_op jit(solution)/shard_map/rotate/pallas_call | solution.py:116
  173.5 12.6 %all_to_all.30 = bf16[4,128,896]{2,1,0:T(8,128)(2,1)S(1)} all-to-all(bf16[4,128,896]{2,1,0:T(8,128)(2,1)S(1)} %bitcast.29), channel_id=1, replica_groups=mesh['y'=4,'z'=8,'x'=4,'c'=2] {'x'}, dimensions={0} | all-to-all | bytes 1835008 | tf_op jit(solution)/shard_map/all_to_all | solution.py:176
  186.3 1.0 broadcast_in_dim.12
  187.3 3.5 %all-to-all-start.4 = ((bf16[4,128,896]{2,1,0:T(8,128)(2,1)}), bf16[4,128,896]{2,1,0:T(8,128)(2,1)S(1)}, u32[]{:S(2)}, u32[]{:S(2)}) async-start(bf16[4,128,896]{2,1,0:T(8,128)(2,1)} %broadcast_in_dim.12), calls=%async_computation.4 | async-start | bytes 1835008 | tf_op jit(solution)/shard_map/all_to_all | solution.py:42
  191.2 8.7 %all-to-all-done.4 = bf16[4,128,896]{2,1,0:T(8,128)(2,1)S(1)} async-done(((bf16[4,128,896]{2,1,0:T(8,128)(2,1)}), bf16[4,128,896]{2,1,0:T(8,128)(2,1)S(1)}, u32[]{:S(2)}, u32[]{:S(2)}) %all-to-all-start.4) | async-done | bytes 917536 | tf_op jit(solution)/shard_map/all_to_all | solution.py:42
  199.8 1.6 copy-done.4
  201.4 6.9 %score.1 = f32[2,1,128]{2,1,0:T(1,128)S(1)} custom-call(bf16[512,2048]{1,0:T(8,128)(2,1)S(1)} %copy-done.4, bf16[2,1024,896]{2,1,0:T(8,128)(2,1)} %divide_convert_fusion.own, bf16[2,1024,896]{2,1,0:T(8,128)(2,1)} %collective-permute-done.2.other, bf16[512,896]{1,0:T(8,128)(2,1)S(1)} %bitcast.28, s32[512,1]{1,0:T(8,128)S(1)} %reshape.51.ids), custom_call_target="tpu_custom_call" | custom-call | flops 3758096384 | bytes 10354688 | tf_op jit(solution)/shard_map/score/pallas_call | solution.py:152
  208.6 28.6 %all_to_all.31 = f32[256,1,128]{2,1,0:T(1,128)S(1)} all-to-all(f32[256,1,128]{2,1,0:T(1,128)S(1)} %broadcast_in_dim.14), channel_id=1, replica_groups=mesh['y'=4,'z'=8,'x'=4,'c'=2] {'y','z','x','c'}, dimensions={0} | all-to-all | bytes 262144 | tf_op jit(solution)/shard_map/all_to_all | solution.py:42
  (81 shorter events, 7.1 us)
Async XLA Ops:
  6.5 1.0 copy-start
  6.5 42.3 %all-gather.3.cloned.1.call-start = ((), (), s32[]{:S(2)}) async-start(), calls=%async_computation.6 | async-start | bytes 2621440 | tf_op jit(solution)/shard_map/all_gather | solution.py:201
  10.0 38.2 %all-to-all-start = ((bf16[8,16,4096]{2,1,0:T(8,128)(2,1)}), bf16[8,16,4096]{2,1,0:T(8,128)(2,1)S(1)}, u32[]{:S(2)}, u32[]{:S(2)}) async-start(bf16[8,16,4096]{2,1,0:T(8,128)(2,1)} %pad_maximum_fusion), calls=%async_computation | async-start | bytes 2097152 | tf_op jit(solution)/shard_map/all_to_all | solution.py:195
  19.0 135.4 %collective-permute-start.19 = (bf16[3584,896]{1,0:T(8,128)(2,1)}, bf16[3584,896]{1,0:T(8,128)(2,1)}, u32[]{:S(2)}, u32[]{:S(2)}) collective-permute-start(bf16[3584,896]{1,0:T(8,128)(2,1)} %refs_14_.1), channel_id=1, source_target_pairs={{0,1},{1,0},{2,3},{3,2},{4,5},{5,4},{6,7},{7,6},{8,9},{9,8},{10,11... | collective-permute-start | bytes 19267592 | tf_op jit(solution)/shard_map/ppermute | solution.py:25
  48.2 5.6 %copy-start.9 = (bf16[8,16,4096]{2,1,0:T(8,128)(2,1)}, bf16[8,16,4096]{2,1,0:T(8,128)(2,1)S(1)}, u32[]{:S(2)}) copy-start(bf16[8,16,4096]{2,1,0:T(8,128)(2,1)S(1)} %all-to-all-done) | copy-start | bytes 3145732
  48.2 9.9 %copy-start.12 = (bf16[32,3584]{1,0:T(8,128)(2,1)S(1)}, bf16[32,3584]{1,0:T(8,128)(2,1)}, u32[]{:S(2)}) copy-start(bf16[32,3584]{1,0:T(8,128)(2,1)} %param.7) | copy-start | bytes 688132
  48.2 2.6 %collective-permute-start = (bf16[128,1024]{1,0:T(8,128)(2,1)S(1)}, bf16[128,1024]{1,0:T(8,128)(2,1)S(1)}, u32[]{:S(2)}, u32[]{:S(2)}) collective-permute-start(bf16[128,1024]{1,0:T(8,128)(2,1)S(1)} %bitcast.33), channel_id=1, source_target_pairs={{0,1},{1,0},{2,3},{3,2},{4,5},{5,4},{6,7},{7,6},{8,9},{9,8},{10,11... | collective-permute-start | bytes 786440 | tf_op jit(solution)/shard_map/ppermute | solution.py:25
  53.8 22.4 %all-to-all-start.1 = ((bf16[8,2,16,1024]{3,2,1,0:T(8,128)(2,1)}), bf16[8,2,16,1024]{3,2,1,0:T(8,128)(2,1)S(1)}, u32[]{:S(2)}, u32[]{:S(2)}) async-start(bf16[8,2,16,1024]{3,2,1,0:T(8,128)(2,1)} %pad_maximum_fusion.1), calls=%async_computation.1 | async-start | bytes 1048576 | tf_op jit(solution)/shard_map/all_to_all | solution.py:204
  58.1 2.0 collective-permute-start.7
  60.2 9.8 %copy-start.11 = (bf16[16,4096]{1,0:T(8,128)(2,1)}, bf16[16,4096]{1,0:T(8,128)(2,1)S(1)}, u32[]{:S(2)}) copy-start(bf16[16,4096]{1,0:T(8,128)(2,1)S(1)} %pad_maximum_fusion.2.refs_0_) | copy-start | bytes 393220
  60.2 6.3 %collective-permute-start.10 = (bf16[16,4096]{1,0:T(8,128)(2,1)S(1)}, bf16[16,4096]{1,0:T(8,128)(2,1)S(1)}, u32[]{:S(2)}, u32[]{:S(2)}) collective-permute-start(bf16[16,4096]{1,0:T(8,128)(2,1)S(1)} %pad_maximum_fusion.2.refs_0_), channel_id=1, source_target_pairs={{0,128},{64,192},{128,0},{192,64},{1,129},{65,193},{129,1},{193,65... | collective-permute-start | bytes 393224 | tf_op jit(solution)/shard_map/ppermute | solution.py:25
  61.8 8.2 %collective-permute-start.8 = (bf16[16,4096]{1,0:T(8,128)(2,1)S(1)}, bf16[16,4096]{1,0:T(8,128)(2,1)S(1)}, u32[]{:S(2)}, u32[]{:S(2)}) collective-permute-start(bf16[16,4096]{1,0:T(8,128)(2,1)S(1)} %pad_maximum_fusion.2.refs_0_), channel_id=1, source_target_pairs={{0,64},{64,128},{128,192},{192,0},{1,65},{65,129},{129,193},{193,1... | collective-permute-start | bytes 393224 | tf_op jit(solution)/shard_map/ppermute | solution.py:25
  62.2 7.8 %collective-permute-start.9 = (bf16[16,4096]{1,0:T(8,128)(2,1)S(1)}, bf16[16,4096]{1,0:T(8,128)(2,1)S(1)}, u32[]{:S(2)}, u32[]{:S(2)}) collective-permute-start(bf16[16,4096]{1,0:T(8,128)(2,1)S(1)} %pad_maximum_fusion.2.refs_0_), channel_id=1, source_target_pairs={{0,192},{64,0},{128,64},{192,128},{1,193},{65,1},{129,65},{193,129... | collective-permute-start | bytes 393224 | tf_op jit(solution)/shard_map/ppermute | solution.py:25
  66.5 3.5 %copy-start.13 = (bf16[16,4096]{1,0:T(8,128)(2,1)}, bf16[16,4096]{1,0:T(8,128)(2,1)S(1)}, u32[]{:S(2)}) copy-start(bf16[16,4096]{1,0:T(8,128)(2,1)S(1)} %collective-permute-done.10.refs_3_) | copy-start | bytes 393220
  69.9 0.6 copy-start.14
  70.6 0.6 copy-start.15
  73.2 15.0 %collective-permute-start.11 = (bf16[64,4096]{1,0:T(8,128)(2,1)}, bf16[64,4096]{1,0:T(8,128)(2,1)S(1)}, u32[]{:S(2)}, u32[]{:S(2)}) collective-permute-start(bf16[64,4096]{1,0:T(8,128)(2,1)} %join.1.refs_5_), channel_id=1, source_target_pairs={{0,8},{8,16},{16,24},{24,32},{32,40},{40,48},{48,56},{56,0},{1,9},... | collective-permute-start | bytes 1572872 | tf_op jit(solution)/shard_map/ppermute | solution.py:25
  74.9 13.2 %collective-permute-start.12 = (bf16[64,4096]{1,0:T(8,128)(2,1)}, bf16[64,4096]{1,0:T(8,128)(2,1)S(1)}, u32[]{:S(2)}, u32[]{:S(2)}) collective-permute-start(bf16[64,4096]{1,0:T(8,128)(2,1)} %join.1.refs_5_), channel_id=1, source_target_pairs={{0,56},{8,0},{16,8},{24,16},{32,24},{40,32},{48,40},{56,48},{1,57}... | collective-permute-start | bytes 1572872 | tf_op jit(solution)/shard_map/ppermute | solution.py:25
  76.2 14.6 %collective-permute-start.1 = (bf16[16,1024]{1,0:T(8,128)(2,1)S(1)}, bf16[16,1024]{1,0:T(8,128)(2,1)S(1)}, u32[]{:S(2)}, u32[]{:S(2)}) collective-permute-start(bf16[16,1024]{1,0:T(8,128)(2,1)S(1)} %get-tuple-element.6), channel_id=1, source_target_pairs={{0,1},{1,0},{2,3},{3,2},{4,5},{5,4},{6,7},{7,6},{8,9},{9,8},{10,11... | collective-permute-start | bytes 98312 | tf_op jit(solution)/shard_map/ppermute | solution.py:25
  88.1 16.0 %copy-start.5 = (bf16[64,4096]{1,0:T(8,128)(2,1)}, bf16[64,4096]{1,0:T(8,128)(2,1)S(1)}, u32[]{:S(2)}) copy-start(bf16[64,4096]{1,0:T(8,128)(2,1)S(1)} %collective-permute-done.11.refs_6_) | copy-start | bytes 1572868
  88.1 18.3 %collective-permute-start.13 = (bf16[64,4096]{1,0:T(8,128)(2,1)S(1)}, bf16[64,4096]{1,0:T(8,128)(2,1)}, u32[]{:S(2)}, u32[]{:S(2)}) collective-permute-start(bf16[64,4096]{1,0:T(8,128)(2,1)S(1)} %collective-permute-done.11.refs_6_), channel_id=1, source_target_pairs={{0,8},{8,16},{16,24},{24,32},{32,40},{40,48},{48,56},{56,0},{1,9},... | collective-permute-start | bytes 1572872 | tf_op jit(solution)/shard_map/ppermute | solution.py:25
  88.1 16.0 %copy-start.7 = (bf16[64,4096]{1,0:T(8,128)(2,1)}, bf16[64,4096]{1,0:T(8,128)(2,1)S(1)}, u32[]{:S(2)}) copy-start(bf16[64,4096]{1,0:T(8,128)(2,1)S(1)} %collective-permute-done.12.refs_7_) | copy-start | bytes 1572868
  88.1 20.2 %collective-permute-start.14 = (bf16[64,4096]{1,0:T(8,128)(2,1)S(1)}, bf16[64,4096]{1,0:T(8,128)(2,1)}, u32[]{:S(2)}, u32[]{:S(2)}) collective-permute-start(bf16[64,4096]{1,0:T(8,128)(2,1)S(1)} %collective-permute-done.12.refs_7_), channel_id=1, source_target_pairs={{0,56},{8,0},{16,8},{24,16},{32,24},{40,32},{48,40},{56,48},{1,57}... | collective-permute-start | bytes 1572872 | tf_op jit(solution)/shard_map/ppermute | solution.py:25
  91.7 21.0 %all-to-all-start.2 = ((bf16[8,16,2048]{2,1,0:T(8,128)(2,1)}), bf16[8,16,2048]{2,1,0:T(8,128)(2,1)}, u32[]{:S(2)}, u32[]{:S(2)}) async-start(bf16[8,16,2048]{2,1,0:T(8,128)(2,1)} %broadcast_in_dim.11), calls=%async_computation.2 | async-start | bytes 1048576 | tf_op jit(solution)/shard_map/all_to_all | solution.py:42
  98.0 101.8 %all-gather.5.cloned.1.call-start = ((), (), s32[]{:S(2)}) async-start(), calls=%async_computation.7 | async-start | bytes 2621440 | tf_op jit(solution)/shard_map/all_gather | solution.py:208
  98.1 10.1 %copy-start.10 = (bf16[8,16,4096]{2,1,0:T(8,128)(2,1)S(1)}, bf16[8,16,4096]{2,1,0:T(8,128)(2,1)}, u32[]{:S(2)}) copy-start(bf16[8,16,4096]{2,1,0:T(8,128)(2,1)} %copy-done.9) | copy-start | bytes 3145732
  104.1 50.3 %copy-start.1 = (bf16[64,4096]{1,0:T(8,128)(2,1)S(1)}, bf16[64,4096]{1,0:T(8,128)(2,1)}, u32[]{:S(2)}) copy-start(bf16[64,4096]{1,0:T(8,128)(2,1)} %join.1.refs_5_) | copy-start | bytes 1572868
  104.1 50.3 %copy-start.2 = (s32[2]{0:T(128)S(1)}, s32[2]{0:T(128)}, u32[]{:S(2)}) copy-start(s32[2]{0:T(128)} %pad_add_fusion.here) | copy-start | bytes 28
  104.2 87.0 %collective-permute-start.2 = (bf16[2,1024,896]{2,1,0:T(8,128)(2,1)}, bf16[2,1024,896]{2,1,0:T(8,128)(2,1)}, u32[]{:S(2)}, u32[]{:S(2)}) collective-permute-start(bf16[2,1024,896]{2,1,0:T(8,128)(2,1)} %divide_convert_fusion.own), channel_id=1, source_target_pairs={{0,1},{1,0},{2,3},{3,2},{4,5},{5,4},{6,7},{7,6},{8,9},{9,8},{10,11... | collective-permute-start | bytes 11010056 | tf_op jit(solution)/shard_map/ppermute | solution.py:25
  106.5 18.5 %collective-permute-start.15 = (bf16[64,4096]{1,0:T(8,128)(2,1)}, bf16[64,4096]{1,0:T(8,128)(2,1)}, u32[]{:S(2)}, u32[]{:S(2)}) collective-permute-start(bf16[64,4096]{1,0:T(8,128)(2,1)} %collective-permute-done.13.refs_8_), channel_id=1, source_target_pairs={{0,8},{8,16},{16,24},{24,32},{32,40},{40,48},{48,56},{56,0},{1,9},... | collective-permute-start | bytes 1572872 | tf_op jit(solution)/shard_map/ppermute | solution.py:25
  108.2 19.8 %collective-permute-start.3 = (bf16[128,3072]{1,0:T(8,128)(2,1)S(1)}, bf16[128,3072]{1,0:T(8,128)(2,1)S(1)}, u32[]{:S(2)}, u32[]{:S(2)}) collective-permute-start(bf16[128,3072]{1,0:T(8,128)(2,1)S(1)} %bitcast.30), channel_id=1, source_target_pairs={{0,64},{64,128},{128,192},{192,0},{1,65},{65,129},{129,193},{193,1... | collective-permute-start | bytes 2359304 | tf_op jit(solution)/shard_map/ppermute | solution.py:25
  108.3 20.9 %collective-permute-start.4 = (bf16[128,3072]{1,0:T(8,128)(2,1)S(1)}, bf16[128,3072]{1,0:T(8,128)(2,1)S(1)}, u32[]{:S(2)}, u32[]{:S(2)}) collective-permute-start(bf16[128,3072]{1,0:T(8,128)(2,1)S(1)} %bitcast.31), channel_id=1, source_target_pairs={{0,192},{64,0},{128,64},{192,128},{1,193},{65,1},{129,65},{193,129... | collective-permute-start | bytes 2359304 | tf_op jit(solution)/shard_map/ppermute | solution.py:25
  124.9 12.4 %collective-permute-start.16 = (bf16[64,4096]{1,0:T(8,128)(2,1)}, bf16[64,4096]{1,0:T(8,128)(2,1)S(1)}, u32[]{:S(2)}, u32[]{:S(2)}) collective-permute-start(bf16[64,4096]{1,0:T(8,128)(2,1)} %collective-permute-done.14.refs_9_), channel_id=1, source_target_pairs={{0,56},{8,0},{16,8},{24,16},{32,24},{40,32},{48,40},{56,48},{1,57}... | collective-permute-start | bytes 1572872 | tf_op jit(solution)/shard_map/ppermute | solution.py:25
  128.0 9.3 %collective-permute-start.17 = (bf16[64,2048]{1,0:T(8,128)(2,1)S(1)}, bf16[64,2048]{1,0:T(8,128)(2,1)S(1)}, u32[]{:S(2)}, u32[]{:S(2)}) collective-permute-start(bf16[64,2048]{1,0:T(8,128)(2,1)S(1)} %slice.50), channel_id=1, source_target_pairs={{0,8},{8,16},{16,24},{24,32},{32,40},{40,48},{48,56},{56,0},{1,9},... | collective-permute-start | bytes 786440 | tf_op jit(solution)/shard_map/ppermute | solution.py:25
  129.3 19.7 %collective-permute-start.5 = (bf16[128,1536]{1,0:T(8,128)(2,1)S(1)}, bf16[128,1536]{1,0:T(8,128)(2,1)S(1)}, u32[]{:S(2)}, u32[]{:S(2)}) collective-permute-start(bf16[128,1536]{1,0:T(8,128)(2,1)S(1)} %slice.48), channel_id=1, source_target_pairs={{0,64},{64,128},{128,192},{192,0},{1,65},{65,129},{129,193},{193,1... | collective-permute-start | bytes 1179656 | tf_op jit(solution)/shard_map/ppermute | solution.py:25
  137.3 17.1 %collective-permute-start.6 = (bf16[128,1536]{1,0:T(8,128)(2,1)S(1)}, bf16[128,1536]{1,0:T(8,128)(2,1)S(1)}, u32[]{:S(2)}, u32[]{:S(2)}) collective-permute-start(bf16[128,1536]{1,0:T(8,128)(2,1)S(1)} %slice.49), channel_id=1, source_target_pairs={{0,192},{64,0},{128,64},{192,128},{1,193},{65,1},{129,65},{193,129... | collective-permute-start | bytes 1179656 | tf_op jit(solution)/shard_map/ppermute | solution.py:25
  137.3 5.8 %collective-permute-start.18 = (bf16[64,2048]{1,0:T(8,128)(2,1)S(1)}, bf16[64,2048]{1,0:T(8,128)(2,1)S(1)}, u32[]{:S(2)}, u32[]{:S(2)}) collective-permute-start(bf16[64,2048]{1,0:T(8,128)(2,1)S(1)} %slice.51), channel_id=1, source_target_pairs={{0,56},{8,0},{16,8},{24,16},{32,24},{40,32},{48,40},{56,48},{1,57}... | collective-permute-start | bytes 786440 | tf_op jit(solution)/shard_map/ppermute | solution.py:25
  154.5 2.8 %copy-start.3 = (bf16[3584,896]{1,0:T(8,128)(2,1)S(1)}, bf16[3584,896]{1,0:T(8,128)(2,1)}, u32[]{:S(2)}) copy-start(bf16[3584,896]{1,0:T(8,128)(2,1)} %refs_14_.1) | copy-start | bytes 19267588
  157.3 1.0 copy-start.6
  158.3 1.0 copy-start.8
  173.5 17.3 %copy-start.16 = (s32[1024]{0:T(1024)S(1)}, s32[1024]{0:T(1024)}, u32[]{:S(2)}) copy-start(s32[1024]{0:T(1024)} %param.13) | copy-start | bytes 12292
  187.3 12.5 %all-to-all-start.4 = ((bf16[4,128,896]{2,1,0:T(8,128)(2,1)}), bf16[4,128,896]{2,1,0:T(8,128)(2,1)S(1)}, u32[]{:S(2)}, u32[]{:S(2)}) async-start(bf16[4,128,896]{2,1,0:T(8,128)(2,1)} %broadcast_in_dim.12), calls=%async_computation.4 | async-start | bytes 1835008 | tf_op jit(solution)/shard_map/all_to_all | solution.py:42
  199.8 1.6 copy-start.4
Sparse Core Ops, SparseCore 0:
  9.2 37.2 all-gather.2
  112.8 45.0 all-gather.4

commit v2 on v1

--- a/solution.py
+++ b/solution.py
@@ -128,11 +128,11 @@
             pltpu.SemaphoreType.DMA((steps,)),
         ],
         cost_estimate=pl.CostEstimate(
-            flops=4 * count * depth * cols,
+            flops=4 * 4 * count * depth * cols,
             bytes_accessed=2 * (2 * count * depth + 2 * depth * cols + count * cols),
             transcendentals=0,
         ),
-        compiler_params=pltpu.CompilerParams(vmem_limit_bytes=32 << 20),
+        compiler_params=pltpu.CompilerParams(vmem_limit_bytes=56 << 20),
         name="rotate",
     )(here, *[chunk for _, _, chunk in y_chunks + z_chunks], own, other)
 

time: 246 us -> 232 us (0.943)
  waiting for transfers between devices: 90.6 us -> 68.8 us
  starting transfers between devices: 45.8 us -> 53.7 us
  blocking collectives: 41.3 us -> 37.2 us
  Pallas kernels: 23 us -> 26.3 us
    all_to_all x1, waiting for transfers between devices: 28.2 us -> 9.52 us  [shards(): sent = lax.all_to_all(jnp.concatenate([copies, rows], axis=2), 'z', 0, 0)]
    ppermute x20, waiting for transfers between devices: 51.3 us -> 37.2 us  [shift(): lax.ppermute(value, axis, [(i, (i + hops) % size) for i in range(size)])]
    all_to_all x2, waiting for transfers between devices: 10.3 us -> 22 us  [spread(): lax.all_to_all(jnp.broadcast_to(value[None], (size,) + value.shape), axes...]
    ppermute x20, starting transfers between devices: 22.6 us -> 32.4 us  [shift(): lax.ppermute(value, axis, [(i, (i + hops) % size) for i in range(size)])]
    all_to_all x1, blocking collectives: 28.6 us -> 19.7 us  [spread(): lax.all_to_all(jnp.broadcast_to(value[None], (size,) + value.shape), axes...]
    all_to_all x1, blocking collectives: 12.6 us -> 17.5 us  [over_x(): parts = lax.all_to_all(partial.reshape(4, rows // 4, cols), 'x', 0, 0)]
    pallas_call x1, Pallas kernels: 14.1 us -> 18 us  [rotate(): pl.pallas_call(functools.partial(rotate_kernel, y_places, z_places), out_...]
  transfers between devices with their start and end apart: 26 -> 26, of which waited for: 13 -> 8; matrix products, arithmetic and copies ran while one was open for 9% -> 10% of each run, Pallas kernels for 7% -> 9%
where the time goes in v2:
time: 232 us; the launch traced here: 231 us
  waiting for transfers between devices  68.8 us (30%)
  starting transfers between devices  53.7 us (23%)
  blocking collectives  37.2 us (16%)
  Pallas kernels  26.3 us (11%)
  local copies, waits for them, and re-layouts  14.7 us (6%)
  between operations  13.8 us (6%)
  other arithmetic  12.5 us (5%)
  matrix products  4.07 us (2%)
    ppermute x20, waiting for transfers between devices, shift(): lax.ppermute(value, axis, [(i, (i + hops) % size) for i in range(size)])  37.2 us
    ppermute x20, starting transfers between devices, shift(): lax.ppermute(value, axis, [(i, (i + hops) % size) for i in range(size)])  32.4 us
    all_to_all x2, waiting for transfers between devices, spread(): lax.all_to_all(jnp.broadcast_to(value[None], (size,) + value.shape), axes...  22 us
    all_to_all x1, blocking collectives, spread(): lax.all_to_all(jnp.broadcast_to(value[None], (size,) + value.shape), axes...  19.7 us
    pallas_call x1, Pallas kernels, rotate(): pl.pallas_call(functools.partial(rotate_kernel, y_places, z_places), out_...  18 us
    all_to_all x1, blocking collectives, over_x(): parts = lax.all_to_all(partial.reshape(4, rows // 4, cols), 'x', 0, 0)  17.5 us
    all_to_all x1, waiting for transfers between devices, shards(): sent = lax.all_to_all(jnp.concatenate([copies, rows], axis=2), 'z', 0, 0)  9.52 us
    all_to_all x2, starting transfers between devices, spread(): lax.all_to_all(jnp.broadcast_to(value[None], (size,) + value.shape), axes...  8.09 us
  transfers between devices with their start and end apart: 26, of which 8 were waited for; matrix products, arithmetic and copies ran while one was open for 10% of the time, Pallas kernels for 9%

profile of v2, /device:TPU:1, one launch (start us, length us, event | category | flops | bytes accessed | tf_op | source)
XLA Modules:
  0.0 231.0 jit_solution(6786874183218366939)
XLA Ops:
  6.5 3.2 %collective-permute-start.19 = (bf16[3584,896]{1,0:T(8,128)(2,1)}, bf16[3584,896]{1,0:T(8,128)(2,1)}, u32[]{:S(2)}, u32[]{:S(2)}) collective-permute-start(bf16[3584,896]{1,0:T(8,128)(2,1)} %refs_14_.1), channel_id=1, source_target_pairs={{0,1},{1,0},{2,3},{3,2},{4,5},{5,4},{6,7},{7,6},{8,9},{9,8},{10,11... | collective-permute-start | bytes 19267592 | tf_op jit(solution)/shard_map/ppermute | solution.py:25
  10.2 0.9 constant_dynamic-slice_fusion
  11.2 1.1 pad_maximum_fusion
  12.2 6.7 %all-to-all-start = ((bf16[8,16,4096]{2,1,0:T(8,128)(2,1)}), bf16[8,16,4096]{2,1,0:T(8,128)(2,1)S(1)}, u32[]{:S(2)}, u32[]{:S(2)}) async-start(bf16[8,16,4096]{2,1,0:T(8,128)(2,1)} %pad_maximum_fusion), calls=%async_computation | async-start | bytes 2097152 | tf_op jit(solution)/shard_map/all_to_all | solution.py:195
  19.0 1.0 collective-permute-start.7
  20.1 1.0 collective-permute-done.7
  21.1 3.0 %collective-permute-start.10 = (bf16[16,4096]{1,0:T(8,128)(2,1)S(1)}, bf16[16,4096]{1,0:T(8,128)(2,1)S(1)}, u32[]{:S(2)}, u32[]{:S(2)}) collective-permute-start(bf16[16,4096]{1,0:T(8,128)(2,1)S(1)} %pad_maximum_fusion.2.refs_0_), channel_id=1, source_target_pairs={{0,128},{64,192},{128,0},{192,64},{1,129},{65,193},{129,1},{193,65... | collective-permute-start | bytes 393224 | tf_op jit(solution)/shard_map/ppermute | solution.py:25
  24.5 2.3 collective-permute-start.9
  27.4 5.3 %collective-permute-done.8.refs_1_ = bf16[16,4096]{1,0:T(8,128)(2,1)S(1)} collective-permute-done((bf16[16,4096]{1,0:T(8,128)(2,1)S(1)}, bf16[16,4096]{1,0:T(8,128)(2,1)S(1)}, u32[]{:S(2)}, u32[]{:S(2)}) %collective-permute-start.8) | collective-permute-done | bytes 131104 | tf_op jit(solution)/shard_map/ppermute | solution.py:25
  34.0 1.9 join.1.refs_5_
  35.9 2.1 collective-permute-start.11
  38.7 9.5 %all-to-all-done = bf16[8,16,4096]{2,1,0:T(8,128)(2,1)S(1)} async-done(((bf16[8,16,4096]{2,1,0:T(8,128)(2,1)}), bf16[8,16,4096]{2,1,0:T(8,128)(2,1)S(1)}, u32[]{:S(2)}, u32[]{:S(2)}) %all-to-all-start) | async-done | bytes 1048608 | tf_op jit(solution)/shard_map/all_to_all | solution.py:195
  48.3 0.8 collective-permute-start
  49.0 2.0 convolution_convert_fusion.1
  51.1 2.0 convolution_convert_fusion
  53.1 0.8 pad_maximum_fusion.1
  54.0 6.4 %all-to-all-start.1 = ((bf16[8,2,16,1024]{3,2,1,0:T(8,128)(2,1)}), bf16[8,2,16,1024]{3,2,1,0:T(8,128)(2,1)S(1)}, u32[]{:S(2)}, u32[]{:S(2)}) async-start(bf16[8,2,16,1024]{3,2,1,0:T(8,128)(2,1)} %pad_maximum_fusion.1), calls=%async_computation.1 | async-start | bytes 1048576 | tf_op jit(solution)/shard_map/all_to_all | solution.py:204
  60.4 1.5 collective-permute-start.13
  61.9 1.3 collective-permute-start.14
  63.2 22.8 %collective-permute-done.13.refs_8_ = bf16[64,4096]{1,0:T(8,128)(2,1)} collective-permute-done((bf16[64,4096]{1,0:T(8,128)(2,1)S(1)}, bf16[64,4096]{1,0:T(8,128)(2,1)}, u32[]{:S(2)}, u32[]{:S(2)}) %collective-permute-start.13) | collective-permute-done | bytes 524320 | tf_op jit(solution)/shard_map/ppermute | solution.py:25
  86.1 1.2 collective-permute-start.3
  87.3 1.5 collective-permute-start.4
  88.9 2.7 %collective-permute-start.16 = (bf16[64,4096]{1,0:T(8,128)(2,1)}, bf16[64,4096]{1,0:T(8,128)(2,1)}, u32[]{:S(2)}, u32[]{:S(2)}) collective-permute-start(bf16[64,4096]{1,0:T(8,128)(2,1)} %collective-permute-done.14.refs_9_), channel_id=1, source_target_pairs={{0,56},{8,0},{16,8},{24,16},{32,24},{40,32},{48,40},{56,48},{1,57}... | collective-permute-start | bytes 1572872 | tf_op jit(solution)/shard_map/ppermute | solution.py:25
  91.6 7.8 %collective-permute-done.15.refs_10_ = bf16[64,4096]{1,0:T(8,128)(2,1)S(1)} collective-permute-done((bf16[64,4096]{1,0:T(8,128)(2,1)}, bf16[64,4096]{1,0:T(8,128)(2,1)S(1)}, u32[]{:S(2)}, u32[]{:S(2)}) %collective-permute-start.15) | collective-permute-done | bytes 524320 | tf_op jit(solution)/shard_map/ppermute | solution.py:25
  99.4 2.3 %collective-permute-start.1 = (bf16[16,1024]{1,0:T(8,128)(2,1)S(1)}, bf16[16,1024]{1,0:T(8,128)(2,1)S(1)}, u32[]{:S(2)}, u32[]{:S(2)}) collective-permute-start(bf16[16,1024]{1,0:T(8,128)(2,1)S(1)} %get-tuple-element.6), channel_id=1, source_target_pairs={{0,1},{1,0},{2,3},{3,2},{4,5},{5,4},{6,7},{7,6},{8,9},{9,8},{10,11... | collective-permute-start | bytes 98312 | tf_op jit(solution)/shard_map/ppermute | solution.py:25
  101.8 3.7 %convert_add_fusion = f32[1024,896]{1,0:T(8,128)} fusion(bf16[1024,896]{1,0:T(8,128)(2,1)} %param.11), kind=kLoop, calls=%fused_computation.1 | loop fusion | flops 1835008 | bytes 5505024 | tf_op jit(solution)/shard_map/add | solution.py:209
  105.6 1.0 slice.51
  106.6 0.9 copy-done.7
  107.5 2.7 %collective-permute-start.18 = (bf16[64,2048]{1,0:T(8,128)(2,1)S(1)}, bf16[64,2048]{1,0:T(8,128)(2,1)S(1)}, u32[]{:S(2)}, u32[]{:S(2)}) collective-permute-start(bf16[64,2048]{1,0:T(8,128)(2,1)S(1)} %slice.51), channel_id=1, source_target_pairs={{0,56},{8,0},{16,8},{24,16},{32,24},{40,32},{48,40},{56,48},{1,57}... | collective-permute-start | bytes 786440 | tf_op jit(solution)/shard_map/ppermute | solution.py:25
  110.2 1.0 slice.48
  111.2 1.2 collective-permute-start.5
  112.4 1.0 slice.49
  113.5 1.6 collective-permute-start.6
  115.1 0.8 broadcast_in_dim.11
  115.9 4.6 %all-to-all-start.2 = ((bf16[8,16,2048]{2,1,0:T(8,128)(2,1)}), bf16[8,16,2048]{2,1,0:T(8,128)(2,1)S(1)}, u32[]{:S(2)}, u32[]{:S(2)}) async-start(bf16[8,16,2048]{2,1,0:T(8,128)(2,1)} %broadcast_in_dim.11), calls=%async_computation.2 | async-start | bytes 1048576 | tf_op jit(solution)/shard_map/all_to_all | solution.py:42
  120.6 6.0 %divide_convert_fusion.own = bf16[2,1024,896]{2,1,0:T(8,128)(2,1)} fusion(bf16[2,1024,896]{2,1,0:T(8,128)(2,1)} %param.12, f32[1024,896]{1,0:T(8,128)} %convert_add_fusion), kind=kLoop, calls=%fused_computation | loop fusion | flops 5505024 | bytes 11010048 | tf_op jit(solution)/shard_map/convert_element_type | solution.py:209
  126.5 9.9 %all-to-all-done.2 = bf16[8,16,2048]{2,1,0:T(8,128)(2,1)S(1)} async-done(((bf16[8,16,2048]{2,1,0:T(8,128)(2,1)}), bf16[8,16,2048]{2,1,0:T(8,128)(2,1)S(1)}, u32[]{:S(2)}, u32[]{:S(2)}) %all-to-all-start.2) | async-done | bytes 524320 | tf_op jit(solution)/shard_map/all_to_all | solution.py:42
  136.4 0.8 copy-done.3
  137.2 2.7 %collective-permute-start.2 = (bf16[2,1024,896]{2,1,0:T(8,128)(2,1)}, bf16[2,1024,896]{2,1,0:T(8,128)(2,1)}, u32[]{:S(2)}, u32[]{:S(2)}) collective-permute-start(bf16[2,1024,896]{2,1,0:T(8,128)(2,1)} %divide_convert_fusion.own), channel_id=1, source_target_pairs={{0,1},{1,0},{2,3},{3,2},{4,5},{5,4},{6,7},{7,6},{8,9},{9,8},{10,11... | collective-permute-start | bytes 11010056 | tf_op jit(solution)/shard_map/ppermute | solution.py:25
  140.8 18.0 %rotate.1 = bf16[512,896]{1,0:T(8,128)(2,1)} custom-call(s32[2]{0:T(128)} %pad_add_fusion.here, bf16[128,3072]{1,0:T(8,128)(2,1)} %bitcast.39, bf16[128,3072]{1,0:T(8,128)(2,1)} %copy-done.7, bf16[128,3072]{1,0:T(8,128)(2,1)} %collective-permute-done.4.refs_2_, bf16[128,1536]{1,0:T(8,128)(2,1)} %copy-done.14, bf16[128,1536]{1,0:T(8,128)(2,1)} %copy-done.15, ...), custom_call_target="tpu_custom_call" | custom-call | flops 26306674688 | bytes 21102592 | tf_op jit(solution)/shard_map/rotate/pallas_call | solution.py:116
  158.9 17.5 %all_to_all.30 = bf16[4,128,896]{2,1,0:T(8,128)(2,1)S(1)} all-to-all(bf16[4,128,896]{2,1,0:T(8,128)(2,1)} %bitcast.36), channel_id=1, replica_groups=mesh['y'=4,'z'=8,'x'=4,'c'=2] {'x'}, dimensions={0} | all-to-all | bytes 1835008 | tf_op jit(solution)/shard_map/all_to_all | solution.py:176
  176.5 1.0 broadcast_in_dim.12
  177.5 3.5 %all-to-all-start.4 = ((bf16[4,128,896]{2,1,0:T(8,128)(2,1)}), bf16[4,128,896]{2,1,0:T(8,128)(2,1)S(1)}, u32[]{:S(2)}, u32[]{:S(2)}) async-start(bf16[4,128,896]{2,1,0:T(8,128)(2,1)} %broadcast_in_dim.12), calls=%async_computation.4 | async-start | bytes 1835008 | tf_op jit(solution)/shard_map/all_to_all | solution.py:42
  181.4 12.2 %all-to-all-done.4 = bf16[4,128,896]{2,1,0:T(8,128)(2,1)S(1)} async-done(((bf16[4,128,896]{2,1,0:T(8,128)(2,1)}), bf16[4,128,896]{2,1,0:T(8,128)(2,1)S(1)}, u32[]{:S(2)}, u32[]{:S(2)}) %all-to-all-start.4) | async-done | bytes 917536 | tf_op jit(solution)/shard_map/all_to_all | solution.py:42
  193.6 2.0 copy-done.1
  195.6 1.6 copy-done.2
  197.2 6.4 %score.1 = f32[2,1,128]{2,1,0:T(1,128)S(1)} custom-call(bf16[512,2048]{1,0:T(8,128)(2,1)S(1)} %copy-done.2, bf16[2,1024,896]{2,1,0:T(8,128)(2,1)S(1)} %copy-done.1, bf16[2,1024,896]{2,1,0:T(8,128)(2,1)} %collective-permute-done.2.other, bf16[512,896]{1,0:T(8,128)(2,1)S(1)} %bitcast.28, s32[512,1]{1,0:T(8,128)S(1)} %reshape.51.ids), custom_call_target="tpu_custom_call" | custom-call | flops 3758096384 | bytes 10354688 | tf_op jit(solution)/shard_map/score/pallas_call | solution.py:152
  203.8 19.7 %all_to_all.31 = f32[256,1,128]{2,1,0:T(1,128)S(1)} all-to-all(f32[256,1,128]{2,1,0:T(1,128)S(1)} %broadcast_in_dim.14), channel_id=1, replica_groups=mesh['y'=4,'z'=8,'x'=4,'c'=2] {'y','z','x','c'}, dimensions={0} | all-to-all | bytes 262144 | tf_op jit(solution)/shard_map/all_to_all | solution.py:42
  (81 shorter events, 6.1 us)
Async XLA Ops:
  6.5 3.3 %copy-start = (bf16[32,8192]{1,0:T(8,128)(2,1)S(1)}, bf16[32,8192]{1,0:T(8,128)(2,1)}, u32[]{:S(2)}) copy-start(bf16[32,8192]{1,0:T(8,128)(2,1)} %param.8) | copy-start | bytes 1572868
  6.5 42.5 %all-gather.3.cloned.1.call-start = ((), (), s32[]{:S(2)}) async-start(), calls=%async_computation.6 | async-start | bytes 2621440 | tf_op jit(solution)/shard_map/all_gather | solution.py:201
  6.5 133.4 %collective-permute-start.19 = (bf16[3584,896]{1,0:T(8,128)(2,1)}, bf16[3584,896]{1,0:T(8,128)(2,1)}, u32[]{:S(2)}, u32[]{:S(2)}) collective-permute-start(bf16[3584,896]{1,0:T(8,128)(2,1)} %refs_14_.1), channel_id=1, source_target_pairs={{0,1},{1,0},{2,3},{3,2},{4,5},{5,4},{6,7},{7,6},{8,9},{9,8},{10,11... | collective-permute-start | bytes 19267592 | tf_op jit(solution)/shard_map/ppermute | solution.py:25
  9.8 9.2 %copy-start.6 = (bf16[32,3584]{1,0:T(8,128)(2,1)S(1)}, bf16[32,3584]{1,0:T(8,128)(2,1)}, u32[]{:S(2)}) copy-start(bf16[32,3584]{1,0:T(8,128)(2,1)} %param.7) | copy-start | bytes 688132
  12.2 36.0 %all-to-all-start = ((bf16[8,16,4096]{2,1,0:T(8,128)(2,1)}), bf16[8,16,4096]{2,1,0:T(8,128)(2,1)S(1)}, u32[]{:S(2)}, u32[]{:S(2)}) async-start(bf16[8,16,4096]{2,1,0:T(8,128)(2,1)} %pad_maximum_fusion), calls=%async_computation | async-start | bytes 2097152 | tf_op jit(solution)/shard_map/all_to_all | solution.py:195
  19.0 2.0 collective-permute-start.7
  21.0 11.9 %copy-start.5 = (bf16[16,4096]{1,0:T(8,128)(2,1)}, bf16[16,4096]{1,0:T(8,128)(2,1)S(1)}, u32[]{:S(2)}) copy-start(bf16[16,4096]{1,0:T(8,128)(2,1)S(1)} %pad_maximum_fusion.2.refs_0_) | copy-start | bytes 393220
  21.1 6.3 %collective-permute-start.10 = (bf16[16,4096]{1,0:T(8,128)(2,1)S(1)}, bf16[16,4096]{1,0:T(8,128)(2,1)S(1)}, u32[]{:S(2)}, u32[]{:S(2)}) collective-permute-start(bf16[16,4096]{1,0:T(8,128)(2,1)S(1)} %pad_maximum_fusion.2.refs_0_), channel_id=1, source_target_pairs={{0,128},{64,192},{128,0},{192,64},{1,129},{65,193},{129,1},{193,65... | collective-permute-start | bytes 393224 | tf_op jit(solution)/shard_map/ppermute | solution.py:25
  24.1 8.6 %collective-permute-start.8 = (bf16[16,4096]{1,0:T(8,128)(2,1)S(1)}, bf16[16,4096]{1,0:T(8,128)(2,1)S(1)}, u32[]{:S(2)}, u32[]{:S(2)}) collective-permute-start(bf16[16,4096]{1,0:T(8,128)(2,1)S(1)} %pad_maximum_fusion.2.refs_0_), channel_id=1, source_target_pairs={{0,64},{64,128},{128,192},{192,0},{1,65},{65,129},{129,193},{193,1... | collective-permute-start | bytes 393224 | tf_op jit(solution)/shard_map/ppermute | solution.py:25
  24.5 8.5 %collective-permute-start.9 = (bf16[16,4096]{1,0:T(8,128)(2,1)S(1)}, bf16[16,4096]{1,0:T(8,128)(2,1)S(1)}, u32[]{:S(2)}, u32[]{:S(2)}) collective-permute-start(bf16[16,4096]{1,0:T(8,128)(2,1)S(1)} %pad_maximum_fusion.2.refs_0_), channel_id=1, source_target_pairs={{0,192},{64,0},{128,64},{192,128},{1,193},{65,1},{129,65},{193,129... | collective-permute-start | bytes 393224 | tf_op jit(solution)/shard_map/ppermute | solution.py:25
  27.4 5.6 %copy-start.9 = (bf16[16,4096]{1,0:T(8,128)(2,1)}, bf16[16,4096]{1,0:T(8,128)(2,1)S(1)}, u32[]{:S(2)}) copy-start(bf16[16,4096]{1,0:T(8,128)(2,1)S(1)} %collective-permute-done.10.refs_3_) | copy-start | bytes 393220
  32.7 0.7 copy-start.10
  33.3 0.6 copy-start.11
  35.9 24.4 %collective-permute-start.11 = (bf16[64,4096]{1,0:T(8,128)(2,1)}, bf16[64,4096]{1,0:T(8,128)(2,1)S(1)}, u32[]{:S(2)}, u32[]{:S(2)}) collective-permute-start(bf16[64,4096]{1,0:T(8,128)(2,1)} %join.1.refs_5_), channel_id=1, source_target_pairs={{0,8},{8,16},{16,24},{24,32},{32,40},{40,48},{48,56},{56,0},{1,9},... | collective-permute-start | bytes 1572872 | tf_op jit(solution)/shard_map/ppermute | solution.py:25
  38.0 23.9 %collective-permute-start.12 = (bf16[64,4096]{1,0:T(8,128)(2,1)}, bf16[64,4096]{1,0:T(8,128)(2,1)}, u32[]{:S(2)}, u32[]{:S(2)}) collective-permute-start(bf16[64,4096]{1,0:T(8,128)(2,1)} %join.1.refs_5_), channel_id=1, source_target_pairs={{0,56},{8,0},{16,8},{24,16},{32,24},{40,32},{48,40},{56,48},{1,57}... | collective-permute-start | bytes 1572872 | tf_op jit(solution)/shard_map/ppermute | solution.py:25
  48.3 2.8 %collective-permute-start = (bf16[128,1024]{1,0:T(8,128)(2,1)S(1)}, bf16[128,1024]{1,0:T(8,128)(2,1)S(1)}, u32[]{:S(2)}, u32[]{:S(2)}) collective-permute-start(bf16[128,1024]{1,0:T(8,128)(2,1)S(1)} %bitcast.30), channel_id=1, source_target_pairs={{0,1},{1,0},{2,3},{3,2},{4,5},{5,4},{6,7},{7,6},{8,9},{9,8},{10,11... | collective-permute-start | bytes 786440 | tf_op jit(solution)/shard_map/ppermute | solution.py:25
  54.0 37.6 %all-to-all-start.1 = ((bf16[8,2,16,1024]{3,2,1,0:T(8,128)(2,1)}), bf16[8,2,16,1024]{3,2,1,0:T(8,128)(2,1)S(1)}, u32[]{:S(2)}, u32[]{:S(2)}) async-start(bf16[8,2,16,1024]{3,2,1,0:T(8,128)(2,1)} %pad_maximum_fusion.1), calls=%async_computation.1 | async-start | bytes 1048576 | tf_op jit(solution)/shard_map/all_to_all | solution.py:204
  60.3 25.7 %copy-start.13 = (bf16[64,4096]{1,0:T(8,128)(2,1)}, bf16[64,4096]{1,0:T(8,128)(2,1)S(1)}, u32[]{:S(2)}) copy-start(bf16[64,4096]{1,0:T(8,128)(2,1)S(1)} %collective-permute-done.11.refs_6_) | copy-start | bytes 1572868
  60.4 25.7 %collective-permute-start.13 = (bf16[64,4096]{1,0:T(8,128)(2,1)S(1)}, bf16[64,4096]{1,0:T(8,128)(2,1)}, u32[]{:S(2)}, u32[]{:S(2)}) collective-permute-start(bf16[64,4096]{1,0:T(8,128)(2,1)S(1)} %collective-permute-done.11.refs_6_), channel_id=1, source_target_pairs={{0,8},{8,16},{16,24},{24,32},{32,40},{40,48},{48,56},{56,0},{1,9},... | collective-permute-start | bytes 1572872 | tf_op jit(solution)/shard_map/ppermute | solution.py:25
  61.9 27.0 %collective-permute-start.14 = (bf16[64,4096]{1,0:T(8,128)(2,1)}, bf16[64,4096]{1,0:T(8,128)(2,1)}, u32[]{:S(2)}, u32[]{:S(2)}) collective-permute-start(bf16[64,4096]{1,0:T(8,128)(2,1)} %collective-permute-done.12.refs_7_), channel_id=1, source_target_pairs={{0,56},{8,0},{16,8},{24,16},{32,24},{40,32},{48,40},{56,48},{1,57}... | collective-permute-start | bytes 1572872 | tf_op jit(solution)/shard_map/ppermute | solution.py:25
  86.0 13.4 %collective-permute-start.15 = (bf16[64,4096]{1,0:T(8,128)(2,1)}, bf16[64,4096]{1,0:T(8,128)(2,1)S(1)}, u32[]{:S(2)}, u32[]{:S(2)}) collective-permute-start(bf16[64,4096]{1,0:T(8,128)(2,1)} %collective-permute-done.13.refs_8_), channel_id=1, source_target_pairs={{0,8},{8,16},{16,24},{24,32},{32,40},{40,48},{48,56},{56,0},{1,9},... | collective-permute-start | bytes 1572872 | tf_op jit(solution)/shard_map/ppermute | solution.py:25
  86.1 25.1 %copy-start.4 = (bf16[8,16,3072]{2,1,0:T(8,128)(2,1)}, bf16[8,16,3072]{2,1,0:T(8,128)(2,1)S(1)}, u32[]{:S(2)}) copy-start(bf16[8,16,3072]{2,1,0:T(8,128)(2,1)S(1)} %slice.47) | copy-start | bytes 2359300
  86.1 20.5 %collective-permute-start.3 = (bf16[128,3072]{1,0:T(8,128)(2,1)S(1)}, bf16[128,3072]{1,0:T(8,128)(2,1)S(1)}, u32[]{:S(2)}, u32[]{:S(2)}) collective-permute-start(bf16[128,3072]{1,0:T(8,128)(2,1)S(1)} %bitcast.37), channel_id=1, source_target_pairs={{0,64},{64,128},{128,192},{192,0},{1,65},{65,129},{129,193},{193,1... | collective-permute-start | bytes 2359304 | tf_op jit(solution)/shard_map/ppermute | solution.py:25
  87.3 23.9 %collective-permute-start.4 = (bf16[128,3072]{1,0:T(8,128)(2,1)S(1)}, bf16[128,3072]{1,0:T(8,128)(2,1)}, u32[]{:S(2)}, u32[]{:S(2)}) collective-permute-start(bf16[128,3072]{1,0:T(8,128)(2,1)S(1)} %bitcast.38), channel_id=1, source_target_pairs={{0,192},{64,0},{128,64},{192,128},{1,193},{65,1},{129,65},{193,129... | collective-permute-start | bytes 2359304 | tf_op jit(solution)/shard_map/ppermute | solution.py:25
  88.9 16.7 %collective-permute-start.16 = (bf16[64,4096]{1,0:T(8,128)(2,1)}, bf16[64,4096]{1,0:T(8,128)(2,1)}, u32[]{:S(2)}, u32[]{:S(2)}) collective-permute-start(bf16[64,4096]{1,0:T(8,128)(2,1)} %collective-permute-done.14.refs_9_), channel_id=1, source_target_pairs={{0,56},{8,0},{16,8},{24,16},{32,24},{40,32},{48,40},{56,48},{1,57}... | collective-permute-start | bytes 1572872 | tf_op jit(solution)/shard_map/ppermute | solution.py:25
  99.4 6.1 %copy-start.8 = (bf16[64,4096]{1,0:T(8,128)(2,1)}, bf16[64,4096]{1,0:T(8,128)(2,1)S(1)}, u32[]{:S(2)}) copy-start(bf16[64,4096]{1,0:T(8,128)(2,1)S(1)} %collective-permute-done.15.refs_10_) | copy-start | bytes 1572868
  99.4 14.0 %collective-permute-start.1 = (bf16[16,1024]{1,0:T(8,128)(2,1)S(1)}, bf16[16,1024]{1,0:T(8,128)(2,1)S(1)}, u32[]{:S(2)}, u32[]{:S(2)}) collective-permute-start(bf16[16,1024]{1,0:T(8,128)(2,1)S(1)} %get-tuple-element.6), channel_id=1, source_target_pairs={{0,1},{1,0},{2,3},{3,2},{4,5},{5,4},{6,7},{7,6},{8,9},{9,8},{10,11... | collective-permute-start | bytes 98312 | tf_op jit(solution)/shard_map/ppermute | solution.py:25
  105.5 31.7 %collective-permute-start.17 = (bf16[64,2048]{1,0:T(8,128)(2,1)S(1)}, bf16[64,2048]{1,0:T(8,128)(2,1)}, u32[]{:S(2)}, u32[]{:S(2)}) collective-permute-start(bf16[64,2048]{1,0:T(8,128)(2,1)S(1)} %slice.50), channel_id=1, source_target_pairs={{0,8},{8,16},{16,24},{24,32},{32,40},{40,48},{48,56},{56,0},{1,9},... | collective-permute-start | bytes 786440 | tf_op jit(solution)/shard_map/ppermute | solution.py:25
  106.6 0.9 copy-start.7
  107.5 32.4 %collective-permute-start.18 = (bf16[64,2048]{1,0:T(8,128)(2,1)S(1)}, bf16[64,2048]{1,0:T(8,128)(2,1)S(1)}, u32[]{:S(2)}, u32[]{:S(2)}) collective-permute-start(bf16[64,2048]{1,0:T(8,128)(2,1)S(1)} %slice.51), channel_id=1, source_target_pairs={{0,56},{8,0},{16,8},{24,16},{32,24},{40,32},{48,40},{56,48},{1,57}... | collective-permute-start | bytes 786440 | tf_op jit(solution)/shard_map/ppermute | solution.py:25
  111.2 28.7 %collective-permute-start.5 = (bf16[128,1536]{1,0:T(8,128)(2,1)S(1)}, bf16[128,1536]{1,0:T(8,128)(2,1)S(1)}, u32[]{:S(2)}, u32[]{:S(2)}) collective-permute-start(bf16[128,1536]{1,0:T(8,128)(2,1)S(1)} %slice.48), channel_id=1, source_target_pairs={{0,64},{64,128},{128,192},{192,0},{1,65},{65,129},{129,193},{193,1... | collective-permute-start | bytes 1179656 | tf_op jit(solution)/shard_map/ppermute | solution.py:25
  113.5 26.4 %collective-permute-start.6 = (bf16[128,1536]{1,0:T(8,128)(2,1)S(1)}, bf16[128,1536]{1,0:T(8,128)(2,1)S(1)}, u32[]{:S(2)}, u32[]{:S(2)}) collective-permute-start(bf16[128,1536]{1,0:T(8,128)(2,1)S(1)} %slice.49), channel_id=1, source_target_pairs={{0,192},{64,0},{128,64},{192,128},{1,193},{65,1},{129,65},{193,129... | collective-permute-start | bytes 1179656 | tf_op jit(solution)/shard_map/ppermute | solution.py:25
  115.9 20.5 %all-to-all-start.2 = ((bf16[8,16,2048]{2,1,0:T(8,128)(2,1)}), bf16[8,16,2048]{2,1,0:T(8,128)(2,1)S(1)}, u32[]{:S(2)}, u32[]{:S(2)}) async-start(bf16[8,16,2048]{2,1,0:T(8,128)(2,1)} %broadcast_in_dim.11), calls=%async_computation.2 | async-start | bytes 1048576 | tf_op jit(solution)/shard_map/all_to_all | solution.py:42
  120.5 73.0 %all-gather.5.cloned.1.call-start = ((), (), s32[]{:S(2)}) async-start(), calls=%async_computation.7 | async-start | bytes 2621440 | tf_op jit(solution)/shard_map/all_gather | solution.py:208
  136.4 0.8 copy-start.3
  137.2 44.2 %collective-permute-start.2 = (bf16[2,1024,896]{2,1,0:T(8,128)(2,1)}, bf16[2,1024,896]{2,1,0:T(8,128)(2,1)}, u32[]{:S(2)}, u32[]{:S(2)}) collective-permute-start(bf16[2,1024,896]{2,1,0:T(8,128)(2,1)} %divide_convert_fusion.own), channel_id=1, source_target_pairs={{0,1},{1,0},{2,3},{3,2},{4,5},{5,4},{6,7},{7,6},{8,9},{9,8},{10,11... | collective-permute-start | bytes 11010056 | tf_op jit(solution)/shard_map/ppermute | solution.py:25
  139.9 0.8 copy-start.16
  139.9 0.8 copy-start.14
  139.9 0.9 copy-start.15
  158.9 22.2 %copy-start.12 = (s32[1024]{0:T(1024)S(1)}, s32[1024]{0:T(1024)}, u32[]{:S(2)}) copy-start(s32[1024]{0:T(1024)} %param.13) | copy-start | bytes 12292
  177.5 16.0 %all-to-all-start.4 = ((bf16[4,128,896]{2,1,0:T(8,128)(2,1)}), bf16[4,128,896]{2,1,0:T(8,128)(2,1)S(1)}, u32[]{:S(2)}, u32[]{:S(2)}) async-start(bf16[4,128,896]{2,1,0:T(8,128)(2,1)} %broadcast_in_dim.12), calls=%async_computation.4 | async-start | bytes 1835008 | tf_op jit(solution)/shard_map/all_to_all | solution.py:42
  193.6 2.0 copy-start.1
  195.6 1.6 copy-start.2
Sparse Core Ops, SparseCore 0:
  9.9 38.5 all-gather.2
  137.3 29.9 all-gather.4

commit v3 on v2

--- a/solution.py
+++ b/solution.py
@@ -17,7 +17,6 @@
 F32 = jnp.float32
 BF16 = jnp.bfloat16
 STEP = 512
-SPLIT = 3072
 
 
 def shift(value, axis, hops):
@@ -64,77 +63,75 @@
     )(here, *chunks)
 
 
-def rotate_kernel(y_places, z_places, here, *refs):
-    count = len(y_places) + len(z_places)
-    chunks, (own, other, out, lhs, rhs, total, chunk_sems, basis_sems) = refs[:count], refs[count:]
-    half = own.shape[0]
-    steps = half // STEP
+def rotate_kernel(places, axis, summed, here, *refs):
+    count = len(places)
+    chunks, basis, refs = refs[:count], refs[count], refs[count + 1 :]
+    before, (out, lhs, rhs, total, chunk_sems, basis_sems) = refs[:summed], refs[summed:]
+    steps = basis.shape[0] // STEP
     loads = []
 
     def load(chunk, row, rows, first, width):
         into = lhs.at[pl.ds(pl.multiple_of(row, rows), rows), pl.ds(first, width)]
         loads.append(pltpu.make_async_copy(chunk, into, chunk_sems.at[len(loads)]))
 
-    for (back, first, width), chunk in zip(y_places, chunks):
-        load(chunk, lax.rem(here[0] + 4 - back, 4) * 128, 128, first, width)
-    for (back, first, width), chunk in zip(z_places, chunks[len(y_places) :]):
-        for y in range(4):
-            row = y * 128 + lax.rem(here[1] + 8 - back, 8) * 16
-            load(chunk.at[pl.ds(y * 16, 16)], row, 16, SPLIT + first, width)
-
-    def basis_load(basis, k, at):
+    for (back, first, width), chunk in zip(places, chunks):
+        if axis == "y":
+            load(chunk, lax.rem(here[0] + 4 - back, 4) * 128, 128, first, width)
+        else:
+            for y in range(4):
+                row = y * 128 + lax.rem(here[1] + 8 - back, 8) * 16
+                load(chunk.at[pl.ds(y * 16, 16)], row, 16, first, width)
+
+    def basis_load(k):
         span = pl.ds(pl.multiple_of(k * STEP, STEP), STEP)
-        return pltpu.make_async_copy(basis.at[span], rhs.at[at], basis_sems.at[at])
+        return pltpu.make_async_copy(basis.at[span], rhs.at[k], basis_sems.at[k])
 
     for n in loads:
         n.start()
-    for basis, base in ((own, 0), (other, steps)):
-        for k in range(steps):
-            basis_load(basis, k, base + k).start()
+    for k in range(steps):
+        basis_load(k).start()
+    total[...] = before[0][...] if summed else jnp.zeros_like(total)
     for n in loads:
         n.wait()
-    total[...] = jnp.zeros_like(total)
 
     @pl.loop(0, steps)
     def _(k):
-        basis_load(own, 0, 2 * k).wait()
-        basis_load(own, 0, 2 * k + 1).wait()
-        part = lhs[:, pl.ds(pl.multiple_of(k * 2 * STEP, 2 * STEP), 2 * STEP)]
-        both = rhs[pl.ds(2 * k, 2)].reshape(2 * STEP, rhs.shape[2])
-        total[...] += jnp.dot(part, both, preferred_element_type=F32)
-
-    out[...] = total[...].astype(BF16)
-
-
-def rotate(y_chunks, z_chunks, own, other, here):
-    depth, cols = own.shape
-    y_places, z_places = (
-        [(back, first, chunk.shape[1]) for back, first, chunk in chunks] for chunks in (y_chunks, z_chunks)
-    )
+        basis_load(k).wait()
+        part = lhs[:, pl.ds(pl.multiple_of(k * STEP, STEP), STEP)]
+        total[...] += jnp.dot(part, rhs[k], preferred_element_type=F32)
+
+    out[...] = total[...].astype(out.dtype)
+
+
+def rotate(chunks, axis, basis, here, dtype, before=()):
+    depth, cols = basis.shape
+    places = [(back, first, chunk.shape[1]) for back, first, chunk in chunks]
     count = 512
-    steps = 2 * depth // STEP
+    steps = depth // STEP
+    copies = len(places) * (1 if axis == "y" else 4)
     return pl.pallas_call(
-        functools.partial(rotate_kernel, y_places, z_places),
-        out_shape=jax.ShapeDtypeStruct((count, cols), BF16),
+        functools.partial(rotate_kernel, places, axis, len(before)),
+        out_shape=jax.ShapeDtypeStruct((count, cols), dtype),
         in_specs=[pl.BlockSpec(memory_space=pltpu.SMEM)]
-        + [pl.BlockSpec(memory_space=pl.ANY)] * (len(y_places) + len(z_places))
-        + [pl.BlockSpec(memory_space=pltpu.HBM)] * 2,
+        + [pl.BlockSpec(memory_space=pl.ANY)] * len(places)
+        + [pl.BlockSpec(memory_space=pltpu.HBM)]
+        + [pl.BlockSpec(memory_space=pltpu.VMEM)] * len(before),
         out_specs=pl.BlockSpec(memory_space=pltpu.VMEM),
         scratch_shapes=[
-            pltpu.VMEM((count, 2 * depth), BF16),
+            pltpu.VMEM((count, depth), BF16),
             pltpu.VMEM((steps, STEP, cols), BF16),
             pltpu.VMEM((count, cols), F32),
-            pltpu.SemaphoreType.DMA((len(y_places) + 4 * len(z_places),)),
+            pltpu.SemaphoreType.DMA((copies,)),
             pltpu.SemaphoreType.DMA((steps,)),
         ],
         cost_estimate=pl.CostEstimate(
-            flops=4 * 4 * count * depth * cols,
-            bytes_accessed=2 * (2 * count * depth + 2 * depth * cols + count * cols),
+            flops=(4 if axis == "y" else 8) * 2 * count * depth * cols,
+            bytes_accessed=2 * (count * depth + depth * cols + count * cols),
             transcendentals=0,
         ),
-        compiler_params=pltpu.CompilerParams(vmem_limit_bytes=56 << 20),
-        name="rotate",
-    )(here, *[chunk for _, _, chunk in y_chunks + z_chunks], own, other)
+        compiler_params=pltpu.CompilerParams(vmem_limit_bytes=48 << 20),
+        name="rotate_" + axis,
+    )(here, *[chunk for _, _, chunk in chunks], basis, *before)
 
 
 def score_kernel(grads, own, other, acts, ids, out):
@@ -188,14 +185,15 @@
     other_in = swap(basis_in)
     mine = lax.dynamic_slice_in_dim(activations, c * 16, 16)
     theirs = swap(lax.dynamic_slice_in_dim(activations, (1 - c) * 16, 16))
-    low = join(jnp.concatenate([mine[:, SPLIT:], theirs], axis=1), "y", here)
+    low = join(theirs, "y", here)
     rows = lax.dynamic_slice_in_dim(out_grads, c * 16, 16).reshape(16, 4, 8, 256)
     rows = rows.transpose(2, 0, 1, 3).reshape(8, 16, 1024)
-    copies = jnp.broadcast_to(mine[None, :, :SPLIT], (8, 16, SPLIT))
+    copies = jnp.broadcast_to(mine[None], (8,) + mine.shape)
     sent = lax.all_to_all(jnp.concatenate([copies, rows], axis=2), "z", 0, 0)
-    high = sent[:, :, :SPLIT].reshape(128, SPLIT)
-    rows = sent[:, :, SPLIT:].reshape(128, 1024)
-    partial_acts = rotate(ring(high, "y"), ring(low, "z"), basis_in, other_in, here)
+    high = sent[:, :, : mine.shape[1]].reshape(128, -1)
+    rows = sent[:, :, mine.shape[1] :].reshape(128, 1024)
+    partial_acts = rotate(ring(high, "y"), "y", basis_in, here, F32)
+    partial_acts = rotate(ring(low, "z"), "z", other_in, here, BF16, (partial_acts,))
     rot_acts = over_x(partial_acts)
 
     basis = lax.all_gather(basis_out, "y", axis=0, tiled=True)

time: 232 us -> 221 us (0.953)
  waiting for transfers between devices: 68.8 us -> 56.5 us
  starting transfers between devices: 53.7 us -> 48.4 us
  Pallas kernels: 26.3 us -> 30.5 us
  blocking collectives: 37.2 us -> 40.2 us
    ppermute x20, waiting for transfers between devices: 37.2 us -> 27.1 us  [shift(): lax.ppermute(value, axis, [(i, (i + hops) % size) for i in range(size)])]
    all_to_all x2, waiting for transfers between devices: 22 us -> 15.1 us  [spread(): lax.all_to_all(jnp.broadcast_to(value[None], (size,) + value.shape), axes...]
    all_to_all x1, blocking collectives: 19.7 us -> 24.5 us  [spread(): lax.all_to_all(jnp.broadcast_to(value[None], (size,) + value.shape), axes...]
    all_to_all x1, waiting for transfers between devices: 9.52 us -> 14.2 us  [shards(): sent = lax.all_to_all(jnp.concatenate([copies, rows], axis=2), 'z', 0, 0)]
    pallas_call x1 -> x2, Pallas kernels: 18 us -> 21.7 us  [rotate(): pl.pallas_call(functools.partial(rotate_kernel, places, axis, len(before)...]
    ppermute x20, starting transfers between devices: 32.4 us -> 29.5 us  [shift(): lax.ppermute(value, axis, [(i, (i + hops) % size) for i in range(size)])]
  transfers between devices with their start and end apart: 26 -> 26, of which waited for: 8 -> 7; matrix products, arithmetic and copies ran while one was open for 10% -> 11% of each run, Pallas kernels for 9% -> 11%
where the time goes in v3:
time: 221 us
  waiting for transfers between devices  56.5 us (26%)
  starting transfers between devices  48.4 us (22%)
  blocking collectives  40.2 us (18%)
  Pallas kernels  30.5 us (14%)
  local copies, waits for them, and re-layouts  15.1 us (7%)
  between operations  13.7 us (6%)
  other arithmetic  13.5 us (6%)
  matrix products  2.63 us (1%)
    ppermute x20, starting transfers between devices, shift(): lax.ppermute(value, axis, [(i, (i + hops) % size) for i in range(size)])  29.5 us
    ppermute x20, waiting for transfers between devices, shift(): lax.ppermute(value, axis, [(i, (i + hops) % size) for i in range(size)])  27.1 us
    all_to_all x1, blocking collectives, spread(): lax.all_to_all(jnp.broadcast_to(value[None], (size,) + value.shape), axes...  24.5 us
    pallas_call x2, Pallas kernels, rotate(): pl.pallas_call(functools.partial(rotate_kernel, places, axis, len(before)...  21.7 us
    all_to_all x1, blocking collectives, over_x(): parts = lax.all_to_all(partial.reshape(4, rows // 4, cols), 'x', 0, 0)  15.7 us
    all_to_all x2, waiting for transfers between devices, spread(): lax.all_to_all(jnp.broadcast_to(value[None], (size,) + value.shape), axes...  15.1 us
    all_to_all x1, waiting for transfers between devices, shards(): sent = lax.all_to_all(jnp.concatenate([copies, rows], axis=2), 'z', 0, 0)  14.2 us
    all_to_all x2, starting transfers between devices, spread(): lax.all_to_all(jnp.broadcast_to(value[None], (size,) + value.shape), axes...  8.01 us
  transfers between devices with their start and end apart: 26, of which 7 were waited for; matrix products, arithmetic and copies ran while one was open for 11% of the time, Pallas kernels for 11%

profile of v3, /device:TPU:1, one launch (start us, length us, event | category | flops | bytes accessed | tf_op | source)
XLA Modules:
  0.0 220.6 jit_solution(12481908604390616158)
XLA Ops:
  6.5 3.2 %collective-permute-start.15 = (bf16[3584,896]{1,0:T(8,128)(2,1)}, bf16[3584,896]{1,0:T(8,128)(2,1)}, u32[]{:S(2)}, u32[]{:S(2)}) collective-permute-start(bf16[3584,896]{1,0:T(8,128)(2,1)} %refs_5_.1), channel_id=1, source_target_pairs={{0,1},{1,0},{2,3},{3,2},{4,5},{5,4},{6,7},{7,6},{8,9},{9,8},{10,11... | collective-permute-start | bytes 19267592 | tf_op jit(solution)/shard_map/ppermute | solution.py:24
  10.3 1.1 pad_maximum_fusion
  11.4 6.8 %all-to-all-start = ((bf16[8,16,4608]{2,1,0:T(8,128)(2,1)}), bf16[8,16,4608]{2,1,0:T(8,128)(2,1)S(1)}, u32[]{:S(2)}, u32[]{:S(2)}) async-start(bf16[8,16,4608]{2,1,0:T(8,128)(2,1)} %pad_maximum_fusion), calls=%async_computation | async-start | bytes 2359296 | tf_op jit(solution)/shard_map/all_to_all | solution.py:192
  18.2 1.0 collective-permute-start.3
  19.1 1.0 collective-permute-done.3.refs_0_
  20.1 1.3 collective-permute-start.4
  21.4 1.4 collective-permute-start.5
  22.8 1.6 collective-permute-start.6
  25.8 3.7 %collective-permute-done.6.refs_3_ = bf16[16,3584]{1,0:T(8,128)(2,1)S(1)} collective-permute-done((bf16[16,3584]{1,0:T(8,128)(2,1)S(1)}, bf16[16,3584]{1,0:T(8,128)(2,1)S(1)}, u32[]{:S(2)}, u32[]{:S(2)}) %collective-permute-start.6) | collective-permute-done | bytes 114720 | tf_op jit(solution)/shard_map/ppermute | solution.py:24
  30.1 1.9 join.1.refs_0_
  32.0 1.8 collective-permute-start.7
  33.8 2.2 collective-permute-start.8
  36.0 14.2 %all-to-all-done = bf16[8,16,4608]{2,1,0:T(8,128)(2,1)S(1)} async-done(((bf16[8,16,4608]{2,1,0:T(8,128)(2,1)}), bf16[8,16,4608]{2,1,0:T(8,128)(2,1)S(1)}, u32[]{:S(2)}, u32[]{:S(2)}) %all-to-all-start) | async-done | bytes 1179680 | tf_op jit(solution)/shard_map/all_to_all | solution.py:192
  50.3 0.9 copy-done.10
  51.2 1.3 collective-permute-start.16
  52.5 1.0 slice.36
  53.5 1.0 collective-permute-start
  54.5 2.2 convolution_convert_fusion.1
  56.7 1.5 collective-permute-start.17
  58.6 0.8 pad_maximum_fusion.1
  59.4 4.1 %all-to-all-start.1 = ((bf16[8,2,16,1024]{3,2,1,0:T(8,128)(2,1)}), bf16[8,2,16,1024]{3,2,1,0:T(8,128)(2,1)}, u32[]{:S(2)}, u32[]{:S(2)}) async-start(bf16[8,2,16,1024]{3,2,1,0:T(8,128)(2,1)} %pad_maximum_fusion.1), calls=%async_computation.1 | async-start | bytes 1048576 | tf_op jit(solution)/shard_map/all_to_all | solution.py:202
  63.6 1.6 collective-permute-start.9
  65.2 1.1 collective-permute-start.10
  66.4 21.6 %collective-permute-done.9.refs_3_ = bf16[64,3584]{1,0:T(8,128)(2,1)} collective-permute-done((bf16[64,3584]{1,0:T(8,128)(2,1)S(1)}, bf16[64,3584]{1,0:T(8,128)(2,1)}, u32[]{:S(2)}, u32[]{:S(2)}) %collective-permute-start.9) | collective-permute-done | bytes 458784 | tf_op jit(solution)/shard_map/ppermute | solution.py:24
  88.0 3.7 %convert_add_fusion = f32[1024,896]{1,0:T(8,128)} fusion(bf16[1024,896]{1,0:T(8,128)(2,1)} %param.11), kind=kLoop, calls=%fused_computation.1 | loop fusion | flops 1835008 | bytes 5505024 | tf_op jit(solution)/shard_map/add | solution.py:207
  91.7 2.7 %collective-permute-start.12 = (bf16[64,3584]{1,0:T(8,128)(2,1)}, bf16[64,3584]{1,0:T(8,128)(2,1)S(1)}, u32[]{:S(2)}, u32[]{:S(2)}) collective-permute-start(bf16[64,3584]{1,0:T(8,128)(2,1)} %collective-permute-done.10.refs_4_), channel_id=1, source_target_pairs={{0,56},{8,0},{16,8},{24,16},{32,24},{40,32},{48,40},{56,48},{1,57}... | collective-permute-start | bytes 1376264 | tf_op jit(solution)/shard_map/ppermute | solution.py:24
  94.4 0.8 slice.42
  95.3 1.8 slice.43
  97.2 2.6 %collective-permute-start.19 = (bf16[128,1792]{1,0:T(8,128)(2,1)}, bf16[128,1792]{1,0:T(8,128)(2,1)}, u32[]{:S(2)}, u32[]{:S(2)}) collective-permute-start(bf16[128,1792]{1,0:T(8,128)(2,1)} %slice.43), channel_id=1, source_target_pairs={{0,192},{64,0},{128,64},{192,128},{1,193},{65,1},{129,65},{193,129... | collective-permute-start | bytes 1376264 | tf_op jit(solution)/shard_map/ppermute | solution.py:24
  99.8 1.1 reduce_sum.33
  100.9 2.4 %collective-permute-start.1 = (bf16[16,1024]{1,0:T(8,128)(2,1)S(1)}, bf16[16,1024]{1,0:T(8,128)(2,1)S(1)}, u32[]{:S(2)}, u32[]{:S(2)}) collective-permute-start(bf16[16,1024]{1,0:T(8,128)(2,1)S(1)} %get-tuple-element.8), channel_id=1, source_target_pairs={{0,1},{1,0},{2,3},{3,2},{4,5},{5,4},{6,7},{7,6},{8,9},{9,8},{10,11... | collective-permute-start | bytes 98312 | tf_op jit(solution)/shard_map/ppermute | solution.py:24
  103.3 6.0 %divide_convert_fusion.own = bf16[2,1024,896]{2,1,0:T(8,128)(2,1)} fusion(bf16[2,1024,896]{2,1,0:T(8,128)(2,1)} %param.12, f32[1024,896]{1,0:T(8,128)} %convert_add_fusion), kind=kLoop, calls=%fused_computation | loop fusion | flops 5505024 | bytes 11010048 | tf_op jit(solution)/shard_map/convert_element_type | solution.py:207
  110.8 0.9 broadcast_in_dim.11
  111.6 4.5 %all-to-all-start.2 = ((bf16[8,16,2048]{2,1,0:T(8,128)(2,1)}), bf16[8,16,2048]{2,1,0:T(8,128)(2,1)}, u32[]{:S(2)}, u32[]{:S(2)}) async-start(bf16[8,16,2048]{2,1,0:T(8,128)(2,1)} %broadcast_in_dim.11), calls=%async_computation.2 | async-start | bytes 1048576 | tf_op jit(solution)/shard_map/all_to_all | solution.py:41
  116.2 2.7 %collective-permute-start.14 = (bf16[64,1792]{1,0:T(8,128)(2,1)}, bf16[64,1792]{1,0:T(8,128)(2,1)}, u32[]{:S(2)}, u32[]{:S(2)}) collective-permute-start(bf16[64,1792]{1,0:T(8,128)(2,1)} %slice.40), channel_id=1, source_target_pairs={{0,56},{8,0},{16,8},{24,16},{32,24},{40,32},{48,40},{56,48},{1,57}... | collective-permute-start | bytes 688136 | tf_op jit(solution)/shard_map/ppermute | solution.py:24
  118.9 9.3 %rotate_y.1.refs_10_ = f32[512,896]{1,0:T(8,128)S(1)} custom-call(s32[2]{0:T(128)S(1)} %copy-done.4, bf16[128,3584]{1,0:T(8,128)(2,1)S(1)} %bitcast.30, bf16[128,3584]{1,0:T(8,128)(2,1)S(1)} %collective-permute-done.16.refs_1_, bf16[128,3584]{1,0:T(8,128)(2,1)} %collective-permute-done.17.refs_2_, bf16[128,1792]{1,0:T(8,128)(2,1)} %collective-permute-done.18.refs_3_, ...), custom_call_target="tpu_custom_call" | custom-call | flops 13153337344 | bytes 11010048 | tf_op jit(solution)/shard_map/rotate_y/pallas_call | solution.py:112
  128.2 1.2 copy-done.8
  129.5 4.8 %all-to-all-done.2 = bf16[8,16,2048]{2,1,0:T(8,128)(2,1)} async-done(((bf16[8,16,2048]{2,1,0:T(8,128)(2,1)}), bf16[8,16,2048]{2,1,0:T(8,128)(2,1)}, u32[]{:S(2)}, u32[]{:S(2)}) %all-to-all-start.2) | async-done | bytes 524320 | tf_op jit(solution)/shard_map/all_to_all | solution.py:41
  134.3 1.0 copy-done.3
  135.3 1.0 copy-done.7
  136.3 12.4 %rotate_z.1 = bf16[512,896]{1,0:T(8,128)(2,1)S(1)} custom-call(s32[2]{0:T(128)S(1)} %copy-done.4, bf16[64,3584]{1,0:T(8,128)(2,1)S(1)} %copy-done.1, bf16[64,3584]{1,0:T(8,128)(2,1)S(1)} %copy-done.7, bf16[64,3584]{1,0:T(8,128)(2,1)} %collective-permute-done.8.refs_2_, bf16[64,3584]{1,0:T(8,128)(2,1)} %collective-permute-done.9.refs_3_, ...), custom_call_target="tpu_custom_call" | custom-call | flops 26306674688 | bytes 11010048 | tf_op jit(solution)/shard_map/rotate_z/pallas_call | solution.py:112
  148.7 15.7 %all_to_all.30 = bf16[4,128,896]{2,1,0:T(8,128)(2,1)S(1)} all-to-all(bf16[4,128,896]{2,1,0:T(8,128)(2,1)S(1)} %bitcast.32), channel_id=1, replica_groups=mesh['y'=4,'z'=8,'x'=4,'c'=2] {'x'}, dimensions={0} | all-to-all | bytes 1835008 | tf_op jit(solution)/shard_map/all_to_all | solution.py:173
  164.6 1.0 broadcast_in_dim.12
  165.6 3.5 %all-to-all-start.4 = ((bf16[4,128,896]{2,1,0:T(8,128)(2,1)}), bf16[4,128,896]{2,1,0:T(8,128)(2,1)S(1)}, u32[]{:S(2)}, u32[]{:S(2)}) async-start(bf16[4,128,896]{2,1,0:T(8,128)(2,1)} %broadcast_in_dim.12), calls=%async_computation.4 | async-start | bytes 1835008 | tf_op jit(solution)/shard_map/all_to_all | solution.py:41
  169.5 10.3 %all-to-all-done.4 = bf16[4,128,896]{2,1,0:T(8,128)(2,1)S(1)} async-done(((bf16[4,128,896]{2,1,0:T(8,128)(2,1)}), bf16[4,128,896]{2,1,0:T(8,128)(2,1)S(1)}, u32[]{:S(2)}, u32[]{:S(2)}) %all-to-all-start.4) | async-done | bytes 917536 | tf_op jit(solution)/shard_map/all_to_all | solution.py:41
  179.8 1.6 copy-done.5
  181.4 6.9 %score.1 = f32[2,1,128]{2,1,0:T(1,128)S(1)} custom-call(bf16[512,2048]{1,0:T(8,128)(2,1)S(1)} %copy-done.5, bf16[2,1024,896]{2,1,0:T(8,128)(2,1)} %divide_convert_fusion.own, bf16[2,1024,896]{2,1,0:T(8,128)(2,1)} %collective-permute-done.2.other, bf16[512,896]{1,0:T(8,128)(2,1)S(1)} %bitcast.31, s32[512,1]{1,0:T(8,128)S(1)} %reshape.51.ids), custom_call_target="tpu_custom_call" | custom-call | flops 3758096384 | bytes 10354688 | tf_op jit(solution)/shard_map/score/pallas_call | solution.py:149
  188.5 24.5 %all_to_all.31 = f32[256,1,128]{2,1,0:T(1,128)S(1)} all-to-all(f32[256,1,128]{2,1,0:T(1,128)S(1)} %broadcast_in_dim.14), channel_id=1, replica_groups=mesh['y'=4,'z'=8,'x'=4,'c'=2] {'y','z','x','c'}, dimensions={0} | all-to-all | bytes 262144 | tf_op jit(solution)/shard_map/all_to_all | solution.py:41
  (79 shorter events, 6.0 us)
Async XLA Ops:
  6.5 3.3 %copy-start = (bf16[32,8192]{1,0:T(8,128)(2,1)S(1)}, bf16[32,8192]{1,0:T(8,128)(2,1)}, u32[]{:S(2)}) copy-start(bf16[32,8192]{1,0:T(8,128)(2,1)} %param.8) | copy-start | bytes 1572868
  6.5 3.7 %copy-start.11 = (bf16[32,3584]{1,0:T(8,128)(2,1)S(1)}, bf16[32,3584]{1,0:T(8,128)(2,1)}, u32[]{:S(2)}) copy-start(bf16[32,3584]{1,0:T(8,128)(2,1)} %param.7) | copy-start | bytes 688132
  6.5 47.9 %all-gather.3.cloned.1.call-start = ((), (), s32[]{:S(2)}) async-start(), calls=%async_computation.6 | async-start | bytes 2621440 | tf_op jit(solution)/shard_map/all_gather | solution.py:199
  6.5 127.7 %collective-permute-start.15 = (bf16[3584,896]{1,0:T(8,128)(2,1)}, bf16[3584,896]{1,0:T(8,128)(2,1)}, u32[]{:S(2)}, u32[]{:S(2)}) collective-permute-start(bf16[3584,896]{1,0:T(8,128)(2,1)} %refs_5_.1), channel_id=1, source_target_pairs={{0,1},{1,0},{2,3},{3,2},{4,5},{5,4},{6,7},{7,6},{8,9},{9,8},{10,11... | collective-permute-start | bytes 19267592 | tf_op jit(solution)/shard_map/ppermute | solution.py:24
  11.4 38.8 %all-to-all-start = ((bf16[8,16,4608]{2,1,0:T(8,128)(2,1)}), bf16[8,16,4608]{2,1,0:T(8,128)(2,1)S(1)}, u32[]{:S(2)}, u32[]{:S(2)}) async-start(bf16[8,16,4608]{2,1,0:T(8,128)(2,1)} %pad_maximum_fusion), calls=%async_computation | async-start | bytes 2359296 | tf_op jit(solution)/shard_map/all_to_all | solution.py:192
  18.2 1.9 collective-permute-start.3
  20.1 9.4 %copy-start.12 = (bf16[16,3584]{1,0:T(8,128)(2,1)}, bf16[16,3584]{1,0:T(8,128)(2,1)S(1)}, u32[]{:S(2)}) copy-start(bf16[16,3584]{1,0:T(8,128)(2,1)S(1)} %collective-permute-done.3.refs_0_) | copy-start | bytes 344068
  20.1 5.7 %collective-permute-start.4 = (bf16[16,3584]{1,0:T(8,128)(2,1)S(1)}, bf16[16,3584]{1,0:T(8,128)(2,1)S(1)}, u32[]{:S(2)}, u32[]{:S(2)}) collective-permute-start(bf16[16,3584]{1,0:T(8,128)(2,1)S(1)} %collective-permute-done.3.refs_0_), channel_id=1, source_target_pairs={{0,64},{64,128},{128,192},{192,0},{1,65},{65,129},{129,193},{193,1... | collective-permute-start | bytes 344072 | tf_op jit(solution)/shard_map/ppermute | solution.py:24
  21.4 4.4 %collective-permute-start.5 = (bf16[16,3584]{1,0:T(8,128)(2,1)S(1)}, bf16[16,3584]{1,0:T(8,128)(2,1)S(1)}, u32[]{:S(2)}, u32[]{:S(2)}) collective-permute-start(bf16[16,3584]{1,0:T(8,128)(2,1)S(1)} %collective-permute-done.3.refs_0_), channel_id=1, source_target_pairs={{0,192},{64,0},{128,64},{192,128},{1,193},{65,1},{129,65},{193,129... | collective-permute-start | bytes 344072 | tf_op jit(solution)/shard_map/ppermute | solution.py:24
  22.8 6.7 %collective-permute-start.6 = (bf16[16,3584]{1,0:T(8,128)(2,1)S(1)}, bf16[16,3584]{1,0:T(8,128)(2,1)S(1)}, u32[]{:S(2)}, u32[]{:S(2)}) collective-permute-start(bf16[16,3584]{1,0:T(8,128)(2,1)S(1)} %collective-permute-done.3.refs_0_), channel_id=1, source_target_pairs={{0,128},{64,192},{128,0},{192,64},{1,129},{65,193},{129,1},{193,65... | collective-permute-start | bytes 344072 | tf_op jit(solution)/shard_map/ppermute | solution.py:24
  25.8 3.7 %copy-start.13 = (bf16[16,3584]{1,0:T(8,128)(2,1)}, bf16[16,3584]{1,0:T(8,128)(2,1)S(1)}, u32[]{:S(2)}) copy-start(bf16[16,3584]{1,0:T(8,128)(2,1)S(1)} %collective-permute-done.4.refs_1_) | copy-start | bytes 344068
  25.8 3.7 %copy-start.14 = (bf16[16,3584]{1,0:T(8,128)(2,1)}, bf16[16,3584]{1,0:T(8,128)(2,1)S(1)}, u32[]{:S(2)}) copy-start(bf16[16,3584]{1,0:T(8,128)(2,1)S(1)} %collective-permute-done.5.refs_2_) | copy-start | bytes 344068
  29.5 0.7 copy-start.15
  32.0 31.6 %collective-permute-start.7 = (bf16[64,3584]{1,0:T(8,128)(2,1)}, bf16[64,3584]{1,0:T(8,128)(2,1)S(1)}, u32[]{:S(2)}, u32[]{:S(2)}) collective-permute-start(bf16[64,3584]{1,0:T(8,128)(2,1)} %join.1.refs_0_), channel_id=1, source_target_pairs={{0,8},{8,16},{16,24},{24,32},{32,40},{40,48},{48,56},{56,0},{1,9},... | collective-permute-start | bytes 1376264 | tf_op jit(solution)/shard_map/ppermute | solution.py:24
  33.8 31.4 %collective-permute-start.8 = (bf16[64,3584]{1,0:T(8,128)(2,1)}, bf16[64,3584]{1,0:T(8,128)(2,1)}, u32[]{:S(2)}, u32[]{:S(2)}) collective-permute-start(bf16[64,3584]{1,0:T(8,128)(2,1)} %join.1.refs_0_), channel_id=1, source_target_pairs={{0,56},{8,0},{16,8},{24,16},{32,24},{40,32},{48,40},{56,48},{1,57}... | collective-permute-start | bytes 1376264 | tf_op jit(solution)/shard_map/ppermute | solution.py:24
  50.2 1.0 copy-start.10
  51.2 43.2 %collective-permute-start.16 = (bf16[128,3584]{1,0:T(8,128)(2,1)S(1)}, bf16[128,3584]{1,0:T(8,128)(2,1)S(1)}, u32[]{:S(2)}, u32[]{:S(2)}) collective-permute-start(bf16[128,3584]{1,0:T(8,128)(2,1)S(1)} %bitcast.28), channel_id=1, source_target_pairs={{0,64},{64,128},{128,192},{192,0},{1,65},{65,129},{129,193},{193,1... | collective-permute-start | bytes 2752520 | tf_op jit(solution)/shard_map/ppermute | solution.py:24
  53.5 3.2 %collective-permute-start = (bf16[128,1024]{1,0:T(8,128)(2,1)S(1)}, bf16[128,1024]{1,0:T(8,128)(2,1)S(1)}, u32[]{:S(2)}, u32[]{:S(2)}) collective-permute-start(bf16[128,1024]{1,0:T(8,128)(2,1)S(1)} %bitcast.33), channel_id=1, source_target_pairs={{0,1},{1,0},{2,3},{3,2},{4,5},{5,4},{6,7},{7,6},{8,9},{9,8},{10,11... | collective-permute-start | bytes 786440 | tf_op jit(solution)/shard_map/ppermute | solution.py:24
  54.5 3.7 %copy-start.9 = (bf16[1024,1024]{1,0:T(8,128)(2,1)S(1)}, bf16[1024,1024]{1,0:T(8,128)(2,1)}, u32[]{:S(2)}) copy-start(bf16[1024,1024]{1,0:T(8,128)(2,1)} %all-gather.3.cloned.1.call-done) | copy-start | bytes 6291460
  56.7 38.6 %collective-permute-start.17 = (bf16[128,3584]{1,0:T(8,128)(2,1)S(1)}, bf16[128,3584]{1,0:T(8,128)(2,1)}, u32[]{:S(2)}, u32[]{:S(2)}) collective-permute-start(bf16[128,3584]{1,0:T(8,128)(2,1)S(1)} %bitcast.29), channel_id=1, source_target_pairs={{0,192},{64,0},{128,64},{192,128},{1,193},{65,1},{129,65},{193,129... | collective-permute-start | bytes 2752520 | tf_op jit(solution)/shard_map/ppermute | solution.py:24
  59.4 40.3 %all-to-all-start.1 = ((bf16[8,2,16,1024]{3,2,1,0:T(8,128)(2,1)}), bf16[8,2,16,1024]{3,2,1,0:T(8,128)(2,1)}, u32[]{:S(2)}, u32[]{:S(2)}) async-start(bf16[8,2,16,1024]{3,2,1,0:T(8,128)(2,1)} %pad_maximum_fusion.1), calls=%async_computation.1 | async-start | bytes 1048576 | tf_op jit(solution)/shard_map/all_to_all | solution.py:202
  63.6 28.1 %copy-start.6 = (bf16[64,3584]{1,0:T(8,128)(2,1)}, bf16[64,3584]{1,0:T(8,128)(2,1)S(1)}, u32[]{:S(2)}) copy-start(bf16[64,3584]{1,0:T(8,128)(2,1)S(1)} %collective-permute-done.7.refs_1_) | copy-start | bytes 1376260
  63.6 24.4 %collective-permute-start.9 = (bf16[64,3584]{1,0:T(8,128)(2,1)S(1)}, bf16[64,3584]{1,0:T(8,128)(2,1)}, u32[]{:S(2)}, u32[]{:S(2)}) collective-permute-start(bf16[64,3584]{1,0:T(8,128)(2,1)S(1)} %collective-permute-done.7.refs_1_), channel_id=1, source_target_pairs={{0,8},{8,16},{16,24},{24,32},{32,40},{40,48},{48,56},{56,0},{1,9},... | collective-permute-start | bytes 1376264 | tf_op jit(solution)/shard_map/ppermute | solution.py:24
  65.2 26.5 %collective-permute-start.10 = (bf16[64,3584]{1,0:T(8,128)(2,1)}, bf16[64,3584]{1,0:T(8,128)(2,1)}, u32[]{:S(2)}, u32[]{:S(2)}) collective-permute-start(bf16[64,3584]{1,0:T(8,128)(2,1)} %collective-permute-done.8.refs_2_), channel_id=1, source_target_pairs={{0,56},{8,0},{16,8},{24,16},{32,24},{40,32},{48,40},{56,48},{1,57}... | collective-permute-start | bytes 1376264 | tf_op jit(solution)/shard_map/ppermute | solution.py:24
  88.0 12.9 %collective-permute-start.11 = (bf16[64,3584]{1,0:T(8,128)(2,1)}, bf16[64,3584]{1,0:T(8,128)(2,1)S(1)}, u32[]{:S(2)}, u32[]{:S(2)}) collective-permute-start(bf16[64,3584]{1,0:T(8,128)(2,1)} %collective-permute-done.9.refs_3_), channel_id=1, source_target_pairs={{0,8},{8,16},{16,24},{24,32},{32,40},{40,48},{48,56},{56,0},{1,9},... | collective-permute-start | bytes 1376264 | tf_op jit(solution)/shard_map/ppermute | solution.py:24
  91.7 18.2 %collective-permute-start.12 = (bf16[64,3584]{1,0:T(8,128)(2,1)}, bf16[64,3584]{1,0:T(8,128)(2,1)S(1)}, u32[]{:S(2)}, u32[]{:S(2)}) collective-permute-start(bf16[64,3584]{1,0:T(8,128)(2,1)} %collective-permute-done.10.refs_4_), channel_id=1, source_target_pairs={{0,56},{8,0},{16,8},{24,16},{32,24},{40,32},{48,40},{56,48},{1,57}... | collective-permute-start | bytes 1376264 | tf_op jit(solution)/shard_map/ppermute | solution.py:24
  95.2 21.0 %collective-permute-start.18 = (bf16[128,1792]{1,0:T(8,128)(2,1)}, bf16[128,1792]{1,0:T(8,128)(2,1)}, u32[]{:S(2)}, u32[]{:S(2)}) collective-permute-start(bf16[128,1792]{1,0:T(8,128)(2,1)} %slice.42), channel_id=1, source_target_pairs={{0,64},{64,128},{128,192},{192,0},{1,65},{65,129},{129,193},{193,1... | collective-permute-start | bytes 1376264 | tf_op jit(solution)/shard_map/ppermute | solution.py:24
  97.2 21.8 %collective-permute-start.19 = (bf16[128,1792]{1,0:T(8,128)(2,1)}, bf16[128,1792]{1,0:T(8,128)(2,1)}, u32[]{:S(2)}, u32[]{:S(2)}) collective-permute-start(bf16[128,1792]{1,0:T(8,128)(2,1)} %slice.43), channel_id=1, source_target_pairs={{0,192},{64,0},{128,64},{192,128},{1,193},{65,1},{129,65},{193,129... | collective-permute-start | bytes 1376264 | tf_op jit(solution)/shard_map/ppermute | solution.py:24
  100.9 9.9 %collective-permute-start.1 = (bf16[16,1024]{1,0:T(8,128)(2,1)S(1)}, bf16[16,1024]{1,0:T(8,128)(2,1)S(1)}, u32[]{:S(2)}, u32[]{:S(2)}) collective-permute-start(bf16[16,1024]{1,0:T(8,128)(2,1)S(1)} %get-tuple-element.8), channel_id=1, source_target_pairs={{0,1},{1,0},{2,3},{3,2},{4,5},{5,4},{6,7},{7,6},{8,9},{9,8},{10,11... | collective-permute-start | bytes 98312 | tf_op jit(solution)/shard_map/ppermute | solution.py:24
  109.3 9.7 %copy-start.4 = (s32[2]{0:T(128)S(1)}, s32[2]{0:T(128)}, u32[]{:S(2)}) copy-start(s32[2]{0:T(128)} %pad_add_fusion.here) | copy-start | bytes 28
  110.0 1.7 copy-start.2
  110.0 59.5 %collective-permute-start.2 = (bf16[2,1024,896]{2,1,0:T(8,128)(2,1)}, bf16[2,1024,896]{2,1,0:T(8,128)(2,1)}, u32[]{:S(2)}, u32[]{:S(2)}) collective-permute-start(bf16[2,1024,896]{2,1,0:T(8,128)(2,1)} %divide_convert_fusion.own), channel_id=1, source_target_pairs={{0,1},{1,0},{2,3},{3,2},{4,5},{5,4},{6,7},{7,6},{8,9},{9,8},{10,11... | collective-permute-start | bytes 11010056 | tf_op jit(solution)/shard_map/ppermute | solution.py:24
  110.8 23.5 %collective-permute-start.13 = (bf16[64,1792]{1,0:T(8,128)(2,1)}, bf16[64,1792]{1,0:T(8,128)(2,1)S(1)}, u32[]{:S(2)}, u32[]{:S(2)}) collective-permute-start(bf16[64,1792]{1,0:T(8,128)(2,1)} %slice.39), channel_id=1, source_target_pairs={{0,8},{8,16},{16,24},{24,32},{32,40},{40,48},{48,56},{56,0},{1,9},... | collective-permute-start | bytes 688136 | tf_op jit(solution)/shard_map/ppermute | solution.py:24
  111.6 22.6 %all-to-all-start.2 = ((bf16[8,16,2048]{2,1,0:T(8,128)(2,1)}), bf16[8,16,2048]{2,1,0:T(8,128)(2,1)}, u32[]{:S(2)}, u32[]{:S(2)}) async-start(bf16[8,16,2048]{2,1,0:T(8,128)(2,1)} %broadcast_in_dim.11), calls=%async_computation.2 | async-start | bytes 1048576 | tf_op jit(solution)/shard_map/all_to_all | solution.py:41
  116.2 18.1 %copy-start.1 = (bf16[64,3584]{1,0:T(8,128)(2,1)S(1)}, bf16[64,3584]{1,0:T(8,128)(2,1)}, u32[]{:S(2)}) copy-start(bf16[64,3584]{1,0:T(8,128)(2,1)} %join.1.refs_0_) | copy-start | bytes 1376260
  116.2 63.7 %all-gather.5.cloned.1.call-start = ((), (), s32[]{:S(2)}) async-start(), calls=%async_computation.7 | async-start | bytes 2621440 | tf_op jit(solution)/shard_map/all_gather | solution.py:206
  116.2 18.0 %collective-permute-start.14 = (bf16[64,1792]{1,0:T(8,128)(2,1)}, bf16[64,1792]{1,0:T(8,128)(2,1)}, u32[]{:S(2)}, u32[]{:S(2)}) collective-permute-start(bf16[64,1792]{1,0:T(8,128)(2,1)} %slice.40), channel_id=1, source_target_pairs={{0,56},{8,0},{16,8},{24,16},{32,24},{40,32},{48,40},{56,48},{1,57}... | collective-permute-start | bytes 688136 | tf_op jit(solution)/shard_map/ppermute | solution.py:24
  128.2 1.2 copy-start.8
  134.3 1.0 copy-start.3
  135.3 1.0 copy-start.7
  164.5 4.7 %copy-start.16 = (s32[1024]{0:T(1024)S(1)}, s32[1024]{0:T(1024)}, u32[]{:S(2)}) copy-start(s32[1024]{0:T(1024)} %param.13) | copy-start | bytes 12292
  165.6 14.2 %all-to-all-start.4 = ((bf16[4,128,896]{2,1,0:T(8,128)(2,1)}), bf16[4,128,896]{2,1,0:T(8,128)(2,1)S(1)}, u32[]{:S(2)}, u32[]{:S(2)}) async-start(bf16[4,128,896]{2,1,0:T(8,128)(2,1)} %broadcast_in_dim.12), calls=%async_computation.4 | async-start | bytes 1835008 | tf_op jit(solution)/shard_map/all_to_all | solution.py:41
  179.8 1.6 copy-start.5
Sparse Core Ops, SparseCore 0:
  9.9 37.3 all-gather.2
  134.4 29.3 all-gather.4

commit v4 on v3

v4 whole, which is shorter than its diff:
```python
import functools

import jax
import jax.numpy as jnp
from jax import lax
from jax.experimental import pallas as pl
from jax.experimental.pallas import tpu as pltpu
from jax.sharding import Mesh
from jax.sharding import PartitionSpec as P

WIDE = ("y", "z")
NARROW = ("x", "c")
ALL = ("y", "z", "x", "c")
SIZE = {"y": 4, "z": 8, "x": 4, "c": 2}
DOCS = 64
DAMPING = 0.1
F32 = jnp.float32
BF16 = jnp.bfloat16
STEP = 512
SPLIT = 4096


def shift(value, axis, hops):
    size = SIZE[axis]
    return lax.ppermute(value, axis, [(i, (i + hops) % size) for i in range(size)])


def ring(chunk, axis):
    size = SIZE[axis]
    half = size // 2
    got = [(0, 0, chunk)]
    ahead = back = chunk
    for step in range(1, half):
        ahead, back = shift(ahead, axis, 1), shift(back, axis, -1)
        got += [(step, 0, ahead), (size - step, 0, back)]
    cut = chunk.shape[1] // 2
    got += [(half, 0, shift(ahead[:, :cut], axis, 1)), (half, cut, shift(back[:, cut:], axis, -1))]
    return got


def spread(value, axes, size):
    return lax.all_to_all(jnp.broadcast_to(value[None], (size,) + value.shape), axes, 0, 0)


def join_kernel(places, rows, here, *refs):
    chunks, out = refs[: len(places)], refs[-1]
    for back, chunk in zip(places, chunks):
        row = pl.multiple_of(lax.rem(here[0] + len(places) - back, len(places)) * rows, rows)
        out[pl.ds(row, rows), :] = chunk[...]


PLACES = (0, 1, 3, 2)


def direct(value):
    return [value] + [shift(value, "y", back) for back in PLACES[1:]]


def join(value, here):
    rows, cols = value.shape
    return pl.pallas_call(
        functools.partial(join_kernel, PLACES, rows),
        out_shape=jax.ShapeDtypeStruct((4 * rows, cols), BF16),
        in_specs=[pl.BlockSpec(memory_space=pltpu.SMEM)] + [pl.BlockSpec(memory_space=pltpu.VMEM)] * 4,
        out_specs=pl.BlockSpec(memory_space=pltpu.VMEM),
        cost_estimate=pl.CostEstimate(flops=0, bytes_accessed=16 * rows * cols, transcendentals=0),
        name="join",
    )(here, *direct(value))


def project_kernel(here, own, other, first, second, third, fourth, precond, out):
    for half, rows in enumerate((own, other)):
        total = 0.0
        for back, basis in zip(PLACES, (first, second, third, fourth)):
            slot = pl.multiple_of(lax.rem(here[0] + 4 - back, 4) * 256, 256)
            total += jnp.dot(rows[:, pl.ds(slot, 256)], basis[...], preferred_element_type=F32)
        out[:, half] = total.astype(BF16).reshape(8, 16, 1024)


def project(own, other, bases, precond, here):
    vmem = pl.BlockSpec(memory_space=pltpu.VMEM)
    return pl.pallas_call(
        project_kernel,
        out_shape=jax.ShapeDtypeStruct((8, 2, 16, 1024), BF16),
        in_specs=[pl.BlockSpec(memory_space=pltpu.SMEM)] + [vmem] * 6 + [pl.BlockSpec(memory_space=pl.ANY)],
        out_specs=vmem,
        cost_estimate=pl.CostEstimate(flops=2**29, bytes_accessed=2**22, transcendentals=0),
        compiler_params=pltpu.CompilerParams(vmem_limit_bytes=16 << 20),
        name="project",
    )(here, own, other, *bases, precond)


def damp_kernel(queries, eigenvalues, _, out):
    damped = eigenvalues[...].astype(F32) + DAMPING
    for q in range(2):
        out[q] = (queries[q].astype(F32) / damped).astype(BF16)


def damp(queries, eigenvalues, ready):
    count, rows, cols = queries.shape
    return pl.pallas_call(
        damp_kernel,
        grid=(rows // 128,),
        out_shape=jax.ShapeDtypeStruct((count, rows, cols), BF16),
        in_specs=[
            pl.BlockSpec((count, 128, cols), lambda i: (0, i, 0)),
            pl.BlockSpec((128, cols), lambda i: (i, 0)),
            pl.BlockSpec(memory_space=pl.ANY),
        ],
        out_specs=pl.BlockSpec((count, 128, cols), lambda i: (0, i, 0)),
        cost_estimate=pl.CostEstimate(
            flops=2 * count * rows * cols, bytes_accessed=10 * rows * cols, transcendentals=0
        ),
        compiler_params=pltpu.CompilerParams(vmem_limit_bytes=8 << 20),
        name="damp",
    )(queries, eigenvalues, ready)


def rotate_kernel(places, axis, spans, summed, here, *refs):
    count = len(places)
    chunks, bases, refs = refs[:count], refs[count : count + len(spans)], refs[count + len(spans) :]
    before, (_, out, lhs, rhs, total, chunk_sems, basis_sems) = refs[:summed], refs[summed:]
    steps = rhs.shape[0]
    loads = []

    def load(chunk, row, rows, first, width):
        into = lhs.at[pl.ds(pl.multiple_of(row, rows), rows), pl.ds(first, width)]
        loads.append(pltpu.make_async_copy(chunk, into, chunk_sems.at[len(loads)]))

    for (back, first, width), chunk in zip(places, chunks):
        if axis == "y":
            load(chunk, lax.rem(here[0] + 4 - back, 4) * 128, 128, first, width)
        else:
            for y in range(4):
                row = y * 128 + lax.rem(here[1] + 8 - back, 8) * 16
                load(chunk.at[pl.ds(y * 16, 16)], row, 16, first, width)

    def basis_load(basis, row, k):
        return pltpu.make_async_copy(basis.at[pl.ds(row, STEP)], rhs.at[k], basis_sems.at[k])

    for n in loads:
        n.start()
    k = 0
    for basis, (first, last) in zip(bases, spans):
        for row in range(first, last, STEP):
            basis_load(basis, row, k).start()
            k += 1
    total[...] = before[0][...] if summed else jnp.zeros_like(total)
    for n in loads:
        n.wait()

    @pl.loop(0, steps)
    def _(k):
        basis_load(bases[0], 0, k).wait()
        part = lhs[:, pl.ds(pl.multiple_of(k * STEP, STEP), STEP)]
        total[...] += jnp.dot(part, rhs[k], preferred_element_type=F32)

    out[...] = total[...].astype(out.dtype)


def rotate(chunks, axis, bases, here, dtype, ready, before=()):
    spans = [span for _, span in bases]
    depth, cols = sum(last - first for first, last in spans), bases[0][0].shape[1]
    places = [(back, first, chunk.shape[1]) for back, first, chunk in chunks]
    count = 512
    steps = depth // STEP
    copies = len(places) * (1 if axis == "y" else 4)
    return pl.pallas_call(
        functools.partial(rotate_kernel, places, axis, spans, len(before)),
        out_shape=jax.ShapeDtypeStruct((count, cols), dtype),
        in_specs=[pl.BlockSpec(memory_space=pltpu.SMEM)]
        + [pl.BlockSpec(memory_space=pl.ANY)] * len(places)
        + [pl.BlockSpec(memory_space=pltpu.HBM)] * len(bases)
        + [pl.BlockSpec(memory_space=pltpu.VMEM)] * len(before)
        + [pl.BlockSpec(memory_space=pl.ANY)],
        out_specs=pl.BlockSpec(memory_space=pltpu.VMEM),
        scratch_shapes=[
            pltpu.VMEM((count, depth), BF16),
            pltpu.VMEM((steps, STEP, cols), BF16),
            pltpu.VMEM((count, cols), F32),
            pltpu.SemaphoreType.DMA((copies,)),
            pltpu.SemaphoreType.DMA((steps,)),
        ],
        cost_estimate=pl.CostEstimate(
            flops=(2 if axis == "y" else 2) * 2 * count * depth * cols,
            bytes_accessed=2 * (count * depth + depth * cols + count * cols),
            transcendentals=0,
        ),
        compiler_params=pltpu.CompilerParams(vmem_limit_bytes=48 << 20),
        name="rotate_" + axis,
    )(here, *[chunk for _, _, chunk in chunks], *[basis for basis, _ in bases], *before, ready)


def score_kernel(here, first, second, third, fourth, own, other, acts, ids, out, grads, sems):
    @pl.when(pl.program_id(0) == 0)
    def _():
        loads = []
        for n, (back, chunk) in enumerate(zip(PLACES, (first, second, third, fourth))):
            row = pl.multiple_of(lax.rem(here[0] + 4 - back, 4) * 128, 128)
            loads.append(pltpu.make_async_copy(chunk, grads.at[pl.ds(row, 128)], sems.at[n]))
        for load in loads:
            load.start()
        for load in loads:
            load.wait()

    half = own.shape[1]
    mixed = jnp.dot(grads[:, :half], own[0], preferred_element_type=F32)
    mixed += jnp.dot(grads[:, half:], other[0], preferred_element_type=F32)
    token = jnp.sum(mixed * acts[...].astype(F32), axis=1, keepdims=True)
    docs = lax.broadcasted_iota(jnp.int32, (token.shape[0], 128), 1)
    out[0] = jnp.sum(jnp.where(ids[...] == docs, token, 0.0), axis=0, keepdims=True)


def score(chunks, own, other, acts, ids, here):
    tokens, cols = acts.shape
    count, half, _ = own.shape
    return pl.pallas_call(
        score_kernel,
        grid=(count,),
        out_shape=jax.ShapeDtypeStruct((count, 1, 128), F32),
        in_specs=[pl.BlockSpec(memory_space=pltpu.SMEM)]
        + [pl.BlockSpec(memory_space=pl.ANY)] * 4
        + [
            pl.BlockSpec((1, half, cols), lambda q: (q, 0, 0)),
            pl.BlockSpec((1, half, cols), lambda q: (q, 0, 0)),
            pl.BlockSpec((tokens, cols), lambda q: (0, 0)),
            pl.BlockSpec((tokens, 1), lambda q: (0, 0)),
        ],
        out_specs=pl.BlockSpec((1, 1, 128), lambda q: (q, 0, 0)),
        scratch_shapes=[pltpu.VMEM((tokens, 2 * half), BF16), pltpu.SemaphoreType.DMA((4,))],
        cost_estimate=pl.CostEstimate(
            flops=4 * count * tokens * half * cols,
            bytes_accessed=2 * (2 * tokens * half + 2 * count * half * cols + tokens * cols),
            transcendentals=0,
        ),
        compiler_params=pltpu.CompilerParams(vmem_limit_bytes=48 << 20),
        name="score",
    )(here, *chunks, own, other, acts, ids.reshape(tokens, 1))


def after_kernel(value, ready, out):
    pass


def after(value, ready):
    anywhere = pl.BlockSpec(memory_space=pl.ANY)
    return pl.pallas_call(
        after_kernel,
        out_shape=jax.ShapeDtypeStruct(value.shape, value.dtype),
        in_specs=[anywhere, anywhere],
        out_specs=anywhere,
        input_output_aliases={0: 0},
        name="after",
    )(value, ready)


def over_x(partial):
    rows, cols = partial.shape
    parts = lax.all_to_all(partial.reshape(4, rows // 4, cols), "x", 0, 0)
    share = jnp.sum(parts.astype(F32), axis=0).astype(BF16)
    return spread(share, "x", 4).reshape(rows, cols)


def swap(value):
    return shift(value, "c", 1)


def shards(activations, out_grads, basis_in, basis_out, eigenvalues, queries, doc_ids):
    y, z, c = (lax.axis_index(axis) for axis in "yzc")
    here = jnp.stack([y, z])
    other_in = swap(basis_in)
    mine = lax.dynamic_slice_in_dim(activations, c * 16, 16)
    theirs = swap(lax.dynamic_slice_in_dim(activations, (1 - c) * 16, 16))
    bases = direct(basis_out)
    extra = SPLIT - mine.shape[1]
    low = join(theirs[:, extra:], here)
    precond = damp(queries, eigenvalues, low)
    rows = lax.dynamic_slice_in_dim(out_grads, c * 16, 16).reshape(16, 4, 8, 256)
    rows = rows.transpose(2, 0, 1, 3).reshape(8, 16, 1024)
    mine = jnp.concatenate([mine, theirs[:, :extra]], axis=1)
    copies = jnp.broadcast_to(mine[None], (8,) + mine.shape)
    sent = lax.all_to_all(jnp.concatenate([copies, rows], axis=2), "z", 0, 0)
    high = sent[:, :, :SPLIT].reshape(128, -1)
    rows = sent[:, :, SPLIT:].reshape(128, 1024)
    half = basis_in.shape[0]
    high_bases = ((basis_in, (0, half)), (other_in, (0, extra)))[: 1 + (extra > 0)]
    parts = lax.all_to_all(project(rows, swap(rows), bases, precond, here), "z", 0, 0)
    partial_acts = rotate(ring(high, "y"), "y", high_bases, here, F32, parts)
    grads = jnp.sum(parts.astype(F32), axis=0).astype(BF16)
    grads = jnp.concatenate([grads[0], swap(grads[1])], axis=1)
    copies = jnp.broadcast_to(grads[None], (8,) + grads.shape)
    grads = lax.all_to_all(copies, "z", 0, 0).reshape(128, 2048)
    low_bases = ((other_in, (extra, half)),)
    partial_acts = rotate(ring(low, "z"), "z", low_bases, here, BF16, copies, (partial_acts,))
    rot_acts = over_x(after(partial_acts, grads))
    grads = direct(grads)
    ids = lax.dynamic_index_in_dim(doc_ids.reshape(32, 2, 16), c, 1, keepdims=False)
    docs = score(grads, precond, swap(precond), rot_acts, ids, here)
    total = jnp.sum(spread(docs[:, 0, :DOCS].reshape(1, 2 * DOCS), ALL, 256), axis=0)
    return total.reshape(2, DOCS).T


def solution(mesh):
    finer = Mesh(mesh.devices.reshape(4, 8, 4, 2), ALL)
    in_specs = (
        P(WIDE, NARROW),
        P(WIDE, None),
        P(NARROW, WIDE),
        P(WIDE, NARROW),
        P(NARROW, WIDE),
        P(None, NARROW, WIDE),
        P(),
    )
    return jax.shard_map(
        shards, mesh=finer, in_specs=in_specs, out_specs=P(), check_vma=False
    )
```

time: 221 us -> 239 us (1.081)
  waiting for transfers between devices: 56.5 us -> 77.4 us
  starting transfers between devices: 48.4 us -> 62.9 us
  between operations: 13.7 us -> 0.27 us
  other arithmetic: 13.5 us -> 2.21 us
  Pallas kernels: 30.5 us -> 36.3 us
  local copies, waits for them, and re-layouts: 15.1 us -> 19.2 us
  matrix products: 2.63 us -> 0 us
    ppermute x20 -> x26, waiting for transfers between devices: 27.1 us -> 77.4 us  [shift(): lax.ppermute(value, axis, [(i, (i + hops) % size) for i in range(size)])]
    all_to_all x2 -> x1, waiting for transfers between devices: 15.1 us -> 0.01 us  [spread(): lax.all_to_all(jnp.broadcast_to(value[None], (size,) + value.shape), axes...]
    all_to_all x1, waiting for transfers between devices: 14.2 us -> 0.01 us  [shards(): sent = lax.all_to_all(jnp.concatenate([copies, rows], axis=2), 'z', 0, 0)]
    ppermute x20 -> x26, starting transfers between devices: 29.5 us -> 40.4 us  [shift(): lax.ppermute(value, axis, [(i, (i + hops) % size) for i in range(size)])]
    all_to_all x1 -> x2, starting transfers between devices: 4.14 us -> 12.4 us  [the longest x1 6.68 us: shards(): lax.all_to_all(project(rows, swap(rows), bases, precond, here), 'z', 0, 0)]
    convert_element_type x1 -> x0, other arithmetic: 5.98 us -> none  [shards(): (queries.astype(F32) / (eigenvalues.astype(F32)[None] + DAMPING)).astype(...]
    all_to_all x2 -> x1, starting transfers between devices: 8.01 us -> 3.5 us  [spread(): lax.all_to_all(jnp.broadcast_to(value[None], (size,) + value.shape), axes...]
    pallas_call x3 -> x6, Pallas kernels: 23.6 us -> 27.9 us  [the longest x2 21.5 us: rotate(): pl.pallas_call(functools.partial(rotate_kernel, places, axis, spans, len(...]
  transfers between devices with their start and end apart: 26 -> 30, of which waited for: 7 -> 9; matrix products, arithmetic and copies ran while one was open for 11% -> 6% of each run, Pallas kernels for 11% -> 12%
where the time goes in v4:
time: 239 us; the launch traced here: 238 us
  waiting for transfers between devices  77.4 us (32%)
  starting transfers between devices  62.9 us (26%)
  blocking collectives  39.6 us (17%)
  Pallas kernels  36.3 us (15%)
  local copies, waits for them, and re-layouts  19.2 us (8%)
    ppermute x26, waiting for transfers between devices, shift(): lax.ppermute(value, axis, [(i, (i + hops) % size) for i in range(size)])  77.4 us
    ppermute x26, starting transfers between devices, shift(): lax.ppermute(value, axis, [(i, (i + hops) % size) for i in range(size)])  40.4 us
    all_to_all x1, blocking collectives, spread(): lax.all_to_all(jnp.broadcast_to(value[None], (size,) + value.shape), axes...  23.4 us
    pallas_call x2, Pallas kernels, rotate(): pl.pallas_call(functools.partial(rotate_kernel, places, axis, spans, len(...  21.5 us
    all_to_all x1, blocking collectives, over_x(): parts = lax.all_to_all(partial.reshape(4, rows // 4, cols), 'x', 0, 0)  16.2 us
    pallas_call x1, Pallas kernels, score(): pl.pallas_call(score_kernel, grid=(count,), out_shape=jax.ShapeDtypeStruc...  8.34 us
    all_to_all x1, starting transfers between devices, shards(): lax.all_to_all(project(rows, swap(rows), bases, precond, here), 'z', 0, 0)  6.68 us
    all_to_all x1, starting transfers between devices, shards(): sent = lax.all_to_all(jnp.concatenate([copies, rows], axis=2), 'z', 0, 0)  6.58 us
  transfers between devices with their start and end apart: 30, of which 9 were waited for; matrix products, arithmetic and copies ran while one was open for 6% of the time, Pallas kernels for 12%

profile of v4, /device:TPU:1, one launch (start us, length us, event | category | flops | bytes accessed | tf_op | source)
XLA Modules:
  0.0 237.8 jit_solution(15272440948213647601)
XLA Ops:
  0.0 3.2 %collective-permute-start.21 = (bf16[3584,896]{1,0:T(8,128)(2,1)}, bf16[3584,896]{1,0:T(8,128)(2,1)}, u32[]{:S(2)}, u32[]{:S(2)}) collective-permute-start(bf16[3584,896]{1,0:T(8,128)(2,1)} %refs_5_.1), channel_id=1, source_target_pairs={{0,1},{1,0},{2,3},{3,2},{4,5},{5,4},{6,7},{7,6},{8,9},{9,8},{10,11... | collective-permute-start | bytes 19267592 | tf_op jit(solution)/shard_map/ppermute | solution.py:25
  3.2 1.0 constant_dynamic-slice_fusion.2
  4.7 8.6 %collective-permute-done = bf16[16,3584]{1,0:T(8,128)(2,1)S(1)} collective-permute-done((bf16[16,3584]{1,0:T(8,128)(2,1)S(1)}, bf16[16,3584]{1,0:T(8,128)(2,1)S(1)}, u32[]{:S(2)}, u32[]{:S(2)}) %collective-permute-start) | collective-permute-done | bytes 114720 | tf_op jit(solution)/shard_map/ppermute | solution.py:25
  13.5 1.3 pad_maximum_fusion
  14.8 6.6 %all-to-all-start = ((bf16[8,16,5120]{2,1,0:T(8,128)(2,1)}), bf16[8,16,5120]{2,1,0:T(8,128)(2,1)}, u32[]{:S(2)}, u32[]{:S(2)}) async-start(bf16[8,16,5120]{2,1,0:T(8,128)(2,1)} %pad_maximum_fusion), calls=%async_computation | async-start | bytes 2621440 | tf_op jit(solution)/shard_map/all_to_all | solution.py:282
  21.4 1.4 collective-permute-start.5
  22.8 1.3 collective-permute-start.2
  24.1 1.4 collective-permute-start.3
  25.4 1.4 collective-permute-start.4
  26.8 1.1 collective-permute-start.6
  27.9 21.8 %collective-permute-done.6.refs_2_ = bf16[16,3072]{1,0:T(8,128)(2,1)S(1)} collective-permute-done((bf16[16,3072]{1,0:T(8,128)(2,1)S(1)}, bf16[16,3072]{1,0:T(8,128)(2,1)S(1)}, u32[]{:S(2)}, u32[]{:S(2)}) %collective-permute-start.6) | collective-permute-done | bytes 98336 | tf_op jit(solution)/shard_map/ppermute | solution.py:25
  49.7 1.6 collective-permute-start.7
  52.0 3.1 %collective-permute-done.7.refs_3_ = bf16[16,3072]{1,0:T(8,128)(2,1)S(1)} collective-permute-done((bf16[16,3072]{1,0:T(8,128)(2,1)S(1)}, bf16[16,3072]{1,0:T(8,128)(2,1)S(1)}, u32[]{:S(2)}, u32[]{:S(2)}) %collective-permute-start.7) | collective-permute-done | bytes 98336 | tf_op jit(solution)/shard_map/ppermute | solution.py:25
  55.8 1.8 join.1._.refs_0_
  57.6 1.2 collective-permute-start.13
  59.8 3.4 %collective-permute-start.1 = (bf16[128,1024]{1,0:T(8,128)(2,1)S(1)}, bf16[128,1024]{1,0:T(8,128)(2,1)S(1)}, u32[]{:S(2)}, u32[]{:S(2)}) collective-permute-start(bf16[128,1024]{1,0:T(8,128)(2,1)S(1)} %bitcast.24), channel_id=1, source_target_pairs={{0,1},{1,0},{2,3},{3,2},{4,5},{5,4},{6,7},{7,6},{8,9},{9,8},{10,11... | collective-permute-start | bytes 786440 | tf_op jit(solution)/shard_map/ppermute | solution.py:25
  63.2 1.2 collective-permute-start.14
  64.4 2.3 slice.51
  67.7 1.7 collective-permute-start.23
  69.7 2.0 copy-done.3
  71.7 1.7 damp.1.precond.own
  73.4 2.9 %project.1 = bf16[8,2,16,1024]{3,2,1,0:T(8,128)(2,1)} custom-call(s32[2]{0:T(128)S(1)} %copy-done.9, bf16[128,1024]{1,0:T(8,128)(2,1)S(1)} %bitcast.25, bf16[128,1024]{1,0:T(8,128)(2,1)S(1)} %collective-permute-done.1.other, bf16[256,1024]{1,0:T(8,128)(2,1)S(1)} %copy-done.8, bf16[256,1024]{1,0:T(8,128)(2,1)} %collective-permute-done.2.second, ...), custom_call_target="tpu_custom_call" | custom-call | flops 536870912 | bytes 4194304 | tf_op jit(solution)/shard_map/project/pallas_call | solution.py:82
  76.3 1.9 copy-done.1
  78.2 6.7 %all-to-all-start.1 = ((bf16[8,2,16,1024]{3,2,1,0:T(8,128)(2,1)}), bf16[8,2,16,1024]{3,2,1,0:T(8,128)(2,1)S(1)}, u32[]{:S(2)}, u32[]{:S(2)}) async-start(bf16[8,2,16,1024]{3,2,1,0:T(8,128)(2,1)} %project.1), calls=%async_computation.1 | async-start | bytes 1048576 | tf_op jit(solution)/shard_map/all_to_all | solution.py:287
  84.9 2.7 %collective-permute-start.16 = (bf16[64,3072]{1,0:T(8,128)(2,1)}, bf16[64,3072]{1,0:T(8,128)(2,1)S(1)}, u32[]{:S(2)}, u32[]{:S(2)}) collective-permute-start(bf16[64,3072]{1,0:T(8,128)(2,1)} %collective-permute-done.14.refs_2_), channel_id=1, source_target_pairs={{0,56},{8,0},{16,8},{24,16},{32,24},{40,32},{48,40},{56,48},{1,57}... | collective-permute-start | bytes 1179656 | tf_op jit(solution)/shard_map/ppermute | solution.py:25
  87.6 4.2 %collective-permute-start.12 = (bf16[2,1024,896]{2,1,0:T(8,128)(2,1)}, bf16[2,1024,896]{2,1,0:T(8,128)(2,1)}, u32[]{:S(2)}, u32[]{:S(2)}) collective-permute-start(bf16[2,1024,896]{2,1,0:T(8,128)(2,1)} %copy-done.1), channel_id=1, source_target_pairs={{0,1},{1,0},{2,3},{3,2},{4,5},{5,4},{6,7},{7,6},{8,9},{9,8},{10,11... | collective-permute-start | bytes 11010056 | tf_op jit(solution)/shard_map/ppermute | solution.py:25
  91.8 13.2 %collective-permute-done.16.refs_4_ = bf16[64,3072]{1,0:T(8,128)(2,1)S(1)} collective-permute-done((bf16[64,3072]{1,0:T(8,128)(2,1)}, bf16[64,3072]{1,0:T(8,128)(2,1)S(1)}, u32[]{:S(2)}, u32[]{:S(2)}) %collective-permute-start.16) | collective-permute-done | bytes 393248 | tf_op jit(solution)/shard_map/ppermute | solution.py:25
  105.0 1.7 collective-permute-start.17
  106.7 1.0 collective-permute-start.18
  107.7 1.9 slice.52
  109.6 1.9 slice.53
  111.5 2.7 %collective-permute-done.17.refs_5_ = bf16[64,3072]{1,0:T(8,128)(2,1)S(1)} collective-permute-done((bf16[64,3072]{1,0:T(8,128)(2,1)}, bf16[64,3072]{1,0:T(8,128)(2,1)S(1)}, u32[]{:S(2)}, u32[]{:S(2)}) %collective-permute-start.17) | collective-permute-done | bytes 393248 | tf_op jit(solution)/shard_map/ppermute | solution.py:25
  114.2 2.7 %collective-permute-start.25 = (bf16[128,2048]{1,0:T(8,128)(2,1)}, bf16[128,2048]{1,0:T(8,128)(2,1)}, u32[]{:S(2)}, u32[]{:S(2)}) collective-permute-start(bf16[128,2048]{1,0:T(8,128)(2,1)} %slice.53), channel_id=1, source_target_pairs={{0,192},{64,0},{128,64},{192,128},{1,193},{65,1},{129,65},{193,129... | collective-permute-start | bytes 1572872 | tf_op jit(solution)/shard_map/ppermute | solution.py:25
  117.0 3.5 %collective-permute-start.8 = (bf16[16,1024]{1,0:T(8,128)(2,1)S(1)}, bf16[16,1024]{1,0:T(8,128)(2,1)S(1)}, u32[]{:S(2)}, u32[]{:S(2)}) collective-permute-start(bf16[16,1024]{1,0:T(8,128)(2,1)S(1)} %get-tuple-element.8), channel_id=1, source_target_pairs={{0,1},{1,0},{2,3},{3,2},{4,5},{5,4},{6,7},{7,6},{8,9},{9,8},{10,11... | collective-permute-start | bytes 98312 | tf_op jit(solution)/shard_map/ppermute | solution.py:25
  122.8 5.7 %all-to-all-start.2 = ((bf16[8,16,2048]{2,1,0:T(8,128)(2,1)}), bf16[8,16,2048]{2,1,0:T(8,128)(2,1)S(1)}, u32[]{:S(2)}, u32[]{:S(2)}) async-start(bf16[8,16,2048]{2,1,0:T(8,128)(2,1)} %broadcast_in_dim.11.refs_11_), calls=%async_computation.2 | async-start | bytes 1048576 | tf_op jit(solution)/shard_map/all_to_all | solution.py:292
  128.5 2.7 %collective-permute-start.20 = (bf16[64,1536]{1,0:T(8,128)(2,1)}, bf16[64,1536]{1,0:T(8,128)(2,1)S(1)}, u32[]{:S(2)}, u32[]{:S(2)}) collective-permute-start(bf16[64,1536]{1,0:T(8,128)(2,1)} %slice.50), channel_id=1, source_target_pairs={{0,56},{8,0},{16,8},{24,16},{32,24},{40,32},{48,40},{56,48},{1,57}... | collective-permute-start | bytes 589832 | tf_op jit(solution)/shard_map/ppermute | solution.py:25
  131.3 11.6 %rotate_y.1.refs_10_ = f32[512,896]{1,0:T(8,128)} custom-call(s32[2]{0:T(128)S(1)} %copy-done.9, bf16[128,4096]{1,0:T(8,128)(2,1)} %bitcast.7.refs_0_, bf16[128,4096]{1,0:T(8,128)(2,1)} %collective-permute-done.22.refs_1_, bf16[128,4096]{1,0:T(8,128)(2,1)} %collective-permute-done.23.refs_2_, bf16[128,2048]{1,0:T(8,128)(2,1)S(1)} %collective-permute-done.24.refs_3_, ...), custom_call_target="tpu_custom_call" | custom-call | flops 7516192768 | bytes 12451840 | tf_op jit(solution)/shard_map/rotate_y/pallas_call | solution.py:168
  142.9 2.9 %collective-permute-done.20.refs_8_ = bf16[64,1536]{1,0:T(8,128)(2,1)S(1)} collective-permute-done((bf16[64,1536]{1,0:T(8,128)(2,1)}, bf16[64,1536]{1,0:T(8,128)(2,1)S(1)}, u32[]{:S(2)}, u32[]{:S(2)}) %collective-permute-start.20) | collective-permute-done | bytes 196640 | tf_op jit(solution)/shard_map/ppermute | solution.py:25
  145.8 9.9 %rotate_z.1.value = bf16[512,896]{1,0:T(8,128)(2,1)S(1)} custom-call(s32[2]{0:T(128)S(1)} %copy-done.9, bf16[64,3072]{1,0:T(8,128)(2,1)S(1)} %copy-done.7, bf16[64,3072]{1,0:T(8,128)(2,1)} %collective-permute-done.13.refs_1_, bf16[64,3072]{1,0:T(8,128)(2,1)} %collective-permute-done.14.refs_2_, bf16[64,3072]{1,0:T(8,128)(2,1)} %collective-permute-done.15.refs_3_, ...), custom_call_target="tpu_custom_call" | custom-call | flops 5637144576 | bytes 9568256 | tf_op jit(solution)/shard_map/rotate_z/pallas_call | solution.py:168
  157.5 16.2 %all_to_all.30 = bf16[4,128,896]{2,1,0:T(8,128)(2,1)S(1)} all-to-all(bf16[4,128,896]{2,1,0:T(8,128)(2,1)} %bitcast.18), channel_id=1, replica_groups=mesh['y'=4,'z'=8,'x'=4,'c'=2] {'x'}, dimensions={0} | all-to-all | bytes 1835008 | tf_op jit(solution)/shard_map/all_to_all | solution.py:259
  173.8 1.0 broadcast_in_dim.12
  174.8 3.5 %all-to-all-start.4 = ((bf16[4,128,896]{2,1,0:T(8,128)(2,1)}), bf16[4,128,896]{2,1,0:T(8,128)(2,1)S(1)}, u32[]{:S(2)}, u32[]{:S(2)}) async-start(bf16[4,128,896]{2,1,0:T(8,128)(2,1)} %broadcast_in_dim.12), calls=%async_computation.4 | async-start | bytes 1835008 | tf_op jit(solution)/shard_map/all_to_all | solution.py:42
  178.4 1.5 collective-permute-start.11
  180.2 8.9 %collective-permute-done.10.third = bf16[128,2048]{1,0:T(8,128)(2,1)S(1)} collective-permute-done((bf16[128,2048]{1,0:T(8,128)(2,1)S(1)}, bf16[128,2048]{1,0:T(8,128)(2,1)S(1)}, u32[]{:S(2)}, u32[]{:S(2)}) %collective-permute-start.10) | collective-permute-done | bytes 524320 | tf_op jit(solution)/shard_map/ppermute | solution.py:25
  189.2 1.5 collective-permute-done.11.fourth
  190.6 14.5 %collective-permute-done.9.second = bf16[128,2048]{1,0:T(8,128)(2,1)} collective-permute-done((bf16[128,2048]{1,0:T(8,128)(2,1)S(1)}, bf16[128,2048]{1,0:T(8,128)(2,1)}, u32[]{:S(2)}, u32[]{:S(2)}) %collective-permute-start.9) | collective-permute-done | bytes 524320 | tf_op jit(solution)/shard_map/ppermute | solution.py:25
  205.2 8.3 %score.1 = f32[2,1,128]{2,1,0:T(1,128)S(1)} custom-call(s32[2]{0:T(128)S(1)} %copy-done.9, bf16[128,2048]{1,0:T(8,128)(2,1)S(1)} %bitcast.23, bf16[128,2048]{1,0:T(8,128)(2,1)} %collective-permute-done.9.second, bf16[128,2048]{1,0:T(8,128)(2,1)S(1)} %collective-permute-done.10.third, bf16[128,2048]{1,0:T(8,128)(2,1)S(1)} %collective-permute-done.11.fourth, ...), custom_call_target="tpu_custom_call" | custom-call | flops 3758096384 | bytes 10354688 | tf_op jit(solution)/shard_map/score/pallas_call | solution.py:217
  213.7 23.4 %all_to_all.31 = f32[256,1,128]{2,1,0:T(1,128)S(1)} all-to-all(f32[256,1,128]{2,1,0:T(1,128)S(1)} %broadcast_in_dim.14), channel_id=1, replica_groups=mesh['y'=4,'z'=8,'x'=4,'c'=2] {'y','z','x','c'}, dimensions={0} | all-to-all | bytes 262144 | tf_op jit(solution)/shard_map/all_to_all | solution.py:42
  (86 shorter events, 9.7 us)
Async XLA Ops:
  0.0 4.4 %copy-start = (bf16[32,8192]{1,0:T(8,128)(2,1)S(1)}, bf16[32,8192]{1,0:T(8,128)(2,1)}, u32[]{:S(2)}) copy-start(bf16[32,8192]{1,0:T(8,128)(2,1)} %param.8) | copy-start | bytes 1572868
  0.0 131.3 %collective-permute-start.21 = (bf16[3584,896]{1,0:T(8,128)(2,1)}, bf16[3584,896]{1,0:T(8,128)(2,1)}, u32[]{:S(2)}, u32[]{:S(2)}) collective-permute-start(bf16[3584,896]{1,0:T(8,128)(2,1)} %refs_5_.1), channel_id=1, source_target_pairs={{0,1},{1,0},{2,3},{3,2},{4,5},{5,4},{6,7},{7,6},{8,9},{9,8},{10,11... | collective-permute-start | bytes 19267592 | tf_op jit(solution)/shard_map/ppermute | solution.py:25
  4.2 9.2 %collective-permute-start = (bf16[16,3584]{1,0:T(8,128)(2,1)S(1)}, bf16[16,3584]{1,0:T(8,128)(2,1)S(1)}, u32[]{:S(2)}, u32[]{:S(2)}) collective-permute-start(bf16[16,3584]{1,0:T(8,128)(2,1)S(1)} %get-tuple-element.6), channel_id=1, source_target_pairs={{0,1},{1,0},{2,3},{3,2},{4,5},{5,4},{6,7},{7,6},{8,9},{9,8},{10,11... | collective-permute-start | bytes 344072 | tf_op jit(solution)/shard_map/ppermute | solution.py:25
  13.5 9.3 %copy-start.8 = (bf16[256,1024]{1,0:T(8,128)(2,1)S(1)}, bf16[256,1024]{1,0:T(8,128)(2,1)}, u32[]{:S(2)}) copy-start(bf16[256,1024]{1,0:T(8,128)(2,1)} %first.1) | copy-start | bytes 1572868
  14.8 54.9 %copy-start.6 = (bf16[1024,896]{1,0:T(8,128)(2,1)S(1)}, bf16[1024,896]{1,0:T(8,128)(2,1)}, u32[]{:S(2)}) copy-start(bf16[1024,896]{1,0:T(8,128)(2,1)} %eigenvalues.1) | copy-start | bytes 5505028
  14.8 44.0 %all-to-all-start = ((bf16[8,16,5120]{2,1,0:T(8,128)(2,1)}), bf16[8,16,5120]{2,1,0:T(8,128)(2,1)}, u32[]{:S(2)}, u32[]{:S(2)}) async-start(bf16[8,16,5120]{2,1,0:T(8,128)(2,1)} %pad_maximum_fusion), calls=%async_computation | async-start | bytes 2621440 | tf_op jit(solution)/shard_map/all_to_all | solution.py:282
  21.4 33.8 %copy-start.12 = (bf16[16,3072]{1,0:T(8,128)(2,1)}, bf16[16,3072]{1,0:T(8,128)(2,1)S(1)}, u32[]{:S(2)}) copy-start(bf16[16,3072]{1,0:T(8,128)(2,1)S(1)} %slice.46.refs_0_) | copy-start | bytes 294916
  21.4 5.5 %collective-permute-start.5 = (bf16[16,3072]{1,0:T(8,128)(2,1)S(1)}, bf16[16,3072]{1,0:T(8,128)(2,1)S(1)}, u32[]{:S(2)}, u32[]{:S(2)}) collective-permute-start(bf16[16,3072]{1,0:T(8,128)(2,1)S(1)} %slice.46.refs_0_), channel_id=1, source_target_pairs={{0,64},{64,128},{128,192},{192,0},{1,65},{65,129},{129,193},{193,1... | collective-permute-start | bytes 294920 | tf_op jit(solution)/shard_map/ppermute | solution.py:25
  22.8 37.0 %collective-permute-start.2 = (bf16[256,1024]{1,0:T(8,128)(2,1)S(1)}, bf16[256,1024]{1,0:T(8,128)(2,1)}, u32[]{:S(2)}, u32[]{:S(2)}) collective-permute-start(bf16[256,1024]{1,0:T(8,128)(2,1)S(1)} %copy-done.8), channel_id=1, source_target_pairs={{0,64},{64,128},{128,192},{192,0},{1,65},{65,129},{129,193},{193,1... | collective-permute-start | bytes 1572872 | tf_op jit(solution)/shard_map/ppermute | solution.py:25
  24.1 39.1 %collective-permute-start.3 = (bf16[256,1024]{1,0:T(8,128)(2,1)S(1)}, bf16[256,1024]{1,0:T(8,128)(2,1)}, u32[]{:S(2)}, u32[]{:S(2)}) collective-permute-start(bf16[256,1024]{1,0:T(8,128)(2,1)S(1)} %copy-done.8), channel_id=1, source_target_pairs={{0,192},{64,0},{128,64},{192,128},{1,193},{65,1},{129,65},{193,129... | collective-permute-start | bytes 1572872 | tf_op jit(solution)/shard_map/ppermute | solution.py:25
  25.4 41.3 %collective-permute-start.4 = (bf16[256,1024]{1,0:T(8,128)(2,1)S(1)}, bf16[256,1024]{1,0:T(8,128)(2,1)}, u32[]{:S(2)}, u32[]{:S(2)}) collective-permute-start(bf16[256,1024]{1,0:T(8,128)(2,1)S(1)} %copy-done.8), channel_id=1, source_target_pairs={{0,128},{64,192},{128,0},{192,64},{1,129},{65,193},{129,1},{193,65... | collective-permute-start | bytes 1572872 | tf_op jit(solution)/shard_map/ppermute | solution.py:25
  26.8 28.3 %copy-start.13 = (bf16[16,3072]{1,0:T(8,128)(2,1)}, bf16[16,3072]{1,0:T(8,128)(2,1)S(1)}, u32[]{:S(2)}) copy-start(bf16[16,3072]{1,0:T(8,128)(2,1)S(1)} %collective-permute-done.5.refs_1_) | copy-start | bytes 294916
  26.8 22.9 %collective-permute-start.6 = (bf16[16,3072]{1,0:T(8,128)(2,1)S(1)}, bf16[16,3072]{1,0:T(8,128)(2,1)S(1)}, u32[]{:S(2)}, u32[]{:S(2)}) collective-permute-start(bf16[16,3072]{1,0:T(8,128)(2,1)S(1)} %slice.46.refs_0_), channel_id=1, source_target_pairs={{0,192},{64,0},{128,64},{192,128},{1,193},{65,1},{129,65},{193,129... | collective-permute-start | bytes 294920 | tf_op jit(solution)/shard_map/ppermute | solution.py:25
  49.7 5.4 %copy-start.14 = (bf16[16,3072]{1,0:T(8,128)(2,1)}, bf16[16,3072]{1,0:T(8,128)(2,1)S(1)}, u32[]{:S(2)}) copy-start(bf16[16,3072]{1,0:T(8,128)(2,1)S(1)} %collective-permute-done.6.refs_2_) | copy-start | bytes 294916
  49.7 5.4 %collective-permute-start.7 = (bf16[16,3072]{1,0:T(8,128)(2,1)S(1)}, bf16[16,3072]{1,0:T(8,128)(2,1)S(1)}, u32[]{:S(2)}, u32[]{:S(2)}) collective-permute-start(bf16[16,3072]{1,0:T(8,128)(2,1)S(1)} %slice.46.refs_0_), channel_id=1, source_target_pairs={{0,128},{64,192},{128,0},{192,64},{1,129},{65,193},{129,1},{193,65... | collective-permute-start | bytes 294920 | tf_op jit(solution)/shard_map/ppermute | solution.py:25
  55.1 0.6 copy-start.15
  57.6 12.1 %copy-start.7 = (bf16[64,3072]{1,0:T(8,128)(2,1)S(1)}, bf16[64,3072]{1,0:T(8,128)(2,1)}, u32[]{:S(2)}) copy-start(bf16[64,3072]{1,0:T(8,128)(2,1)} %join.1._.refs_0_) | copy-start | bytes 1179652
  57.6 10.1 %collective-permute-start.13 = (bf16[64,3072]{1,0:T(8,128)(2,1)}, bf16[64,3072]{1,0:T(8,128)(2,1)}, u32[]{:S(2)}, u32[]{:S(2)}) collective-permute-start(bf16[64,3072]{1,0:T(8,128)(2,1)} %join.1._.refs_0_), channel_id=1, source_target_pairs={{0,8},{8,16},{16,24},{24,32},{32,40},{40,48},{48,56},{56,0},{1,9},... | collective-permute-start | bytes 1179656 | tf_op jit(solution)/shard_map/ppermute | solution.py:25
  59.8 9.7 %collective-permute-start.1 = (bf16[128,1024]{1,0:T(8,128)(2,1)S(1)}, bf16[128,1024]{1,0:T(8,128)(2,1)S(1)}, u32[]{:S(2)}, u32[]{:S(2)}) collective-permute-start(bf16[128,1024]{1,0:T(8,128)(2,1)S(1)} %bitcast.24), channel_id=1, source_target_pairs={{0,1},{1,0},{2,3},{3,2},{4,5},{5,4},{6,7},{7,6},{8,9},{9,8},{10,11... | collective-permute-start | bytes 786440 | tf_op jit(solution)/shard_map/ppermute | solution.py:25
  63.2 21.7 %collective-permute-start.14 = (bf16[64,3072]{1,0:T(8,128)(2,1)}, bf16[64,3072]{1,0:T(8,128)(2,1)}, u32[]{:S(2)}, u32[]{:S(2)}) collective-permute-start(bf16[64,3072]{1,0:T(8,128)(2,1)} %join.1._.refs_0_), channel_id=1, source_target_pairs={{0,56},{8,0},{16,8},{24,16},{32,24},{40,32},{48,40},{56,48},{1,57}... | collective-permute-start | bytes 1179656 | tf_op jit(solution)/shard_map/ppermute | solution.py:25
  66.7 6.7 %copy-start.9 = (s32[2]{0:T(128)S(1)}, s32[2]{0:T(128)}, u32[]{:S(2)}) copy-start(s32[2]{0:T(128)} %pad_add_fusion.here) | copy-start | bytes 28
  66.8 39.9 %collective-permute-start.22 = (bf16[128,4096]{1,0:T(8,128)(2,1)}, bf16[128,4096]{1,0:T(8,128)(2,1)}, u32[]{:S(2)}, u32[]{:S(2)}) collective-permute-start(bf16[128,4096]{1,0:T(8,128)(2,1)} %bitcast.7.refs_0_), channel_id=1, source_target_pairs={{0,64},{64,128},{128,192},{192,0},{1,65},{65,129},{129,193},{193,1... | collective-permute-start | bytes 3145736 | tf_op jit(solution)/shard_map/ppermute | solution.py:25
  67.7 41.9 %collective-permute-start.23 = (bf16[128,4096]{1,0:T(8,128)(2,1)}, bf16[128,4096]{1,0:T(8,128)(2,1)}, u32[]{:S(2)}, u32[]{:S(2)}) collective-permute-start(bf16[128,4096]{1,0:T(8,128)(2,1)} %bitcast.7.refs_0_), channel_id=1, source_target_pairs={{0,192},{64,0},{128,64},{192,128},{1,193},{65,1},{129,65},{193,129... | collective-permute-start | bytes 3145736 | tf_op jit(solution)/shard_map/ppermute | solution.py:25
  69.4 18.1 %collective-permute-start.15 = (bf16[64,3072]{1,0:T(8,128)(2,1)}, bf16[64,3072]{1,0:T(8,128)(2,1)}, u32[]{:S(2)}, u32[]{:S(2)}) collective-permute-start(bf16[64,3072]{1,0:T(8,128)(2,1)} %collective-permute-done.13.refs_1_), channel_id=1, source_target_pairs={{0,8},{8,16},{16,24},{24,32},{32,40},{40,48},{48,56},{56,0},{1,9},... | collective-permute-start | bytes 1179656 | tf_op jit(solution)/shard_map/ppermute | solution.py:25
  69.7 2.0 copy-start.3
  76.3 1.9 copy-start.1
  78.2 38.7 %all-to-all-start.1 = ((bf16[8,2,16,1024]{3,2,1,0:T(8,128)(2,1)}), bf16[8,2,16,1024]{3,2,1,0:T(8,128)(2,1)S(1)}, u32[]{:S(2)}, u32[]{:S(2)}) async-start(bf16[8,2,16,1024]{3,2,1,0:T(8,128)(2,1)} %project.1), calls=%async_computation.1 | async-start | bytes 1048576 | tf_op jit(solution)/shard_map/all_to_all | solution.py:287
  84.9 20.1 %collective-permute-start.16 = (bf16[64,3072]{1,0:T(8,128)(2,1)}, bf16[64,3072]{1,0:T(8,128)(2,1)S(1)}, u32[]{:S(2)}, u32[]{:S(2)}) collective-permute-start(bf16[64,3072]{1,0:T(8,128)(2,1)} %collective-permute-done.14.refs_2_), channel_id=1, source_target_pairs={{0,56},{8,0},{16,8},{24,16},{32,24},{40,32},{48,40},{56,48},{1,57}... | collective-permute-start | bytes 1179656 | tf_op jit(solution)/shard_map/ppermute | solution.py:25
  87.6 92.6 %collective-permute-start.12 = (bf16[2,1024,896]{2,1,0:T(8,128)(2,1)}, bf16[2,1024,896]{2,1,0:T(8,128)(2,1)}, u32[]{:S(2)}, u32[]{:S(2)}) collective-permute-start(bf16[2,1024,896]{2,1,0:T(8,128)(2,1)} %copy-done.1), channel_id=1, source_target_pairs={{0,1},{1,0},{2,3},{3,2},{4,5},{5,4},{6,7},{7,6},{8,9},{9,8},{10,11... | collective-permute-start | bytes 11010056 | tf_op jit(solution)/shard_map/ppermute | solution.py:25
  105.0 17.8 %copy-start.10 = (bf16[64,3072]{1,0:T(8,128)(2,1)}, bf16[64,3072]{1,0:T(8,128)(2,1)S(1)}, u32[]{:S(2)}) copy-start(bf16[64,3072]{1,0:T(8,128)(2,1)S(1)} %collective-permute-done.16.refs_4_) | copy-start | bytes 1179652
  105.0 9.2 %collective-permute-start.17 = (bf16[64,3072]{1,0:T(8,128)(2,1)}, bf16[64,3072]{1,0:T(8,128)(2,1)S(1)}, u32[]{:S(2)}, u32[]{:S(2)}) collective-permute-start(bf16[64,3072]{1,0:T(8,128)(2,1)} %collective-permute-done.15.refs_3_), channel_id=1, source_target_pairs={{0,8},{8,16},{16,24},{24,32},{32,40},{40,48},{48,56},{56,0},{1,9},... | collective-permute-start | bytes 1179656 | tf_op jit(solution)/shard_map/ppermute | solution.py:25
  106.7 10.3 %collective-permute-start.18 = (bf16[64,3072]{1,0:T(8,128)(2,1)S(1)}, bf16[64,3072]{1,0:T(8,128)(2,1)S(1)}, u32[]{:S(2)}, u32[]{:S(2)}) collective-permute-start(bf16[64,3072]{1,0:T(8,128)(2,1)S(1)} %collective-permute-done.16.refs_4_), channel_id=1, source_target_pairs={{0,56},{8,0},{16,8},{24,16},{32,24},{40,32},{48,40},{56,48},{1,57}... | collective-permute-start | bytes 1179656 | tf_op jit(solution)/shard_map/ppermute | solution.py:25
  109.6 18.9 %collective-permute-start.24 = (bf16[128,2048]{1,0:T(8,128)(2,1)}, bf16[128,2048]{1,0:T(8,128)(2,1)S(1)}, u32[]{:S(2)}, u32[]{:S(2)}) collective-permute-start(bf16[128,2048]{1,0:T(8,128)(2,1)} %slice.52), channel_id=1, source_target_pairs={{0,64},{64,128},{128,192},{192,0},{1,65},{65,129},{129,193},{193,1... | collective-permute-start | bytes 1572872 | tf_op jit(solution)/shard_map/ppermute | solution.py:25
  114.2 17.1 %collective-permute-start.25 = (bf16[128,2048]{1,0:T(8,128)(2,1)}, bf16[128,2048]{1,0:T(8,128)(2,1)}, u32[]{:S(2)}, u32[]{:S(2)}) collective-permute-start(bf16[128,2048]{1,0:T(8,128)(2,1)} %slice.53), channel_id=1, source_target_pairs={{0,192},{64,0},{128,64},{192,128},{1,193},{65,1},{129,65},{193,129... | collective-permute-start | bytes 1572872 | tf_op jit(solution)/shard_map/ppermute | solution.py:25
  117.0 4.8 %collective-permute-start.8 = (bf16[16,1024]{1,0:T(8,128)(2,1)S(1)}, bf16[16,1024]{1,0:T(8,128)(2,1)S(1)}, u32[]{:S(2)}, u32[]{:S(2)}) collective-permute-start(bf16[16,1024]{1,0:T(8,128)(2,1)S(1)} %get-tuple-element.8), channel_id=1, source_target_pairs={{0,1},{1,0},{2,3},{3,2},{4,5},{5,4},{6,7},{7,6},{8,9},{9,8},{10,11... | collective-permute-start | bytes 98312 | tf_op jit(solution)/shard_map/ppermute | solution.py:25
  121.9 21.1 %collective-permute-start.19 = (bf16[64,1536]{1,0:T(8,128)(2,1)}, bf16[64,1536]{1,0:T(8,128)(2,1)S(1)}, u32[]{:S(2)}, u32[]{:S(2)}) collective-permute-start(bf16[64,1536]{1,0:T(8,128)(2,1)} %slice.49), channel_id=1, source_target_pairs={{0,8},{8,16},{16,24},{24,32},{32,40},{40,48},{48,56},{56,0},{1,9},... | collective-permute-start | bytes 589832 | tf_op jit(solution)/shard_map/ppermute | solution.py:25
  122.8 33.9 %all-to-all-start.2 = ((bf16[8,16,2048]{2,1,0:T(8,128)(2,1)}), bf16[8,16,2048]{2,1,0:T(8,128)(2,1)S(1)}, u32[]{:S(2)}, u32[]{:S(2)}) async-start(bf16[8,16,2048]{2,1,0:T(8,128)(2,1)} %broadcast_in_dim.11.refs_11_), calls=%async_computation.2 | async-start | bytes 1048576 | tf_op jit(solution)/shard_map/all_to_all | solution.py:292
  128.5 17.3 %copy-start.11 = (bf16[64,3072]{1,0:T(8,128)(2,1)S(1)}, bf16[64,3072]{1,0:T(8,128)(2,1)}, u32[]{:S(2)}) copy-start(bf16[64,3072]{1,0:T(8,128)(2,1)} %copy-done.10) | copy-start | bytes 1179652
  128.5 17.3 %collective-permute-start.20 = (bf16[64,1536]{1,0:T(8,128)(2,1)}, bf16[64,1536]{1,0:T(8,128)(2,1)S(1)}, u32[]{:S(2)}, u32[]{:S(2)}) collective-permute-start(bf16[64,1536]{1,0:T(8,128)(2,1)} %slice.50), channel_id=1, source_target_pairs={{0,56},{8,0},{16,8},{24,16},{32,24},{40,32},{48,40},{56,48},{1,57}... | collective-permute-start | bytes 589832 | tf_op jit(solution)/shard_map/ppermute | solution.py:25
  155.7 0.9 copy-start.2
  156.6 0.8 copy-start.4
  157.5 20.8 %copy-start.5 = (bf16[8,16,2048]{2,1,0:T(8,128)(2,1)S(1)}, bf16[8,16,2048]{2,1,0:T(8,128)(2,1)}, u32[]{:S(2)}) copy-start(bf16[8,16,2048]{2,1,0:T(8,128)(2,1)} %copy-done.4) | copy-start | bytes 1572868
  157.5 22.4 %copy-start.16 = (s32[1024]{0:T(1024)S(1)}, s32[1024]{0:T(1024)}, u32[]{:S(2)}) copy-start(s32[1024]{0:T(1024)} %param.13) | copy-start | bytes 12292
  174.8 30.4 %all-to-all-start.4 = ((bf16[4,128,896]{2,1,0:T(8,128)(2,1)}), bf16[4,128,896]{2,1,0:T(8,128)(2,1)S(1)}, u32[]{:S(2)}, u32[]{:S(2)}) async-start(bf16[4,128,896]{2,1,0:T(8,128)(2,1)} %broadcast_in_dim.12), calls=%async_computation.4 | async-start | bytes 1835008 | tf_op jit(solution)/shard_map/all_to_all | solution.py:42
  178.3 10.9 %collective-permute-start.10 = (bf16[128,2048]{1,0:T(8,128)(2,1)S(1)}, bf16[128,2048]{1,0:T(8,128)(2,1)S(1)}, u32[]{:S(2)}, u32[]{:S(2)}) collective-permute-start(bf16[128,2048]{1,0:T(8,128)(2,1)S(1)} %bitcast.20), channel_id=1, source_target_pairs={{0,192},{64,0},{128,64},{192,128},{1,193},{65,1},{129,65},{193,129... | collective-permute-start | bytes 1572872 | tf_op jit(solution)/shard_map/ppermute | solution.py:25
  178.4 12.2 %collective-permute-start.11 = (bf16[128,2048]{1,0:T(8,128)(2,1)S(1)}, bf16[128,2048]{1,0:T(8,128)(2,1)S(1)}, u32[]{:S(2)}, u32[]{:S(2)}) collective-permute-start(bf16[128,2048]{1,0:T(8,128)(2,1)S(1)} %bitcast.21), channel_id=1, source_target_pairs={{0,128},{64,192},{128,0},{192,64},{1,129},{65,193},{129,1},{193,65... | collective-permute-start | bytes 1572872 | tf_op jit(solution)/shard_map/ppermute | solution.py:25
  179.9 25.3 %collective-permute-start.9 = (bf16[128,2048]{1,0:T(8,128)(2,1)S(1)}, bf16[128,2048]{1,0:T(8,128)(2,1)}, u32[]{:S(2)}, u32[]{:S(2)}) collective-permute-start(bf16[128,2048]{1,0:T(8,128)(2,1)S(1)} %bitcast.22), channel_id=1, source_target_pairs={{0,64},{64,128},{128,192},{192,0},{1,65},{65,129},{129,193},{193,1... | collective-permute-start | bytes 1572872 | tf_op jit(solution)/shard_map/ppermute | solution.py:25

commit v5 on v4

--- a/solution.py
+++ b/solution.py
@@ -17,7 +17,7 @@
 F32 = jnp.float32
 BF16 = jnp.bfloat16
 STEP = 512
-SPLIT = 4096
+SPLIT = 3584
 
 
 def shift(value, axis, hops):
@@ -119,21 +119,16 @@
 def rotate_kernel(places, axis, spans, summed, here, *refs):
     count = len(places)
     chunks, bases, refs = refs[:count], refs[count : count + len(spans)], refs[count + len(spans) :]
-    before, (_, out, lhs, rhs, total, chunk_sems, basis_sems) = refs[:summed], refs[summed:]
+    before, (out, lhs, rhs, total, chunk_sems, basis_sems) = refs[:summed], refs[-6:]
     steps = rhs.shape[0]
     loads = []
 
-    def load(chunk, row, rows, first, width):
-        into = lhs.at[pl.ds(pl.multiple_of(row, rows), rows), pl.ds(first, width)]
-        loads.append(pltpu.make_async_copy(chunk, into, chunk_sems.at[len(loads)]))
-
-    for (back, first, width), chunk in zip(places, chunks):
+    for n, ((back, first, width), chunk) in enumerate(zip(places, chunks)):
         if axis == "y":
-            load(chunk, lax.rem(here[0] + 4 - back, 4) * 128, 128, first, width)
+            into = lhs.at[lax.rem(here[0] + 4 - back, 4), :, :, pl.ds(first, width)]
+            loads.append(pltpu.make_async_copy(chunk, into, chunk_sems.at[n]))
         else:
-            for y in range(4):
-                row = y * 128 + lax.rem(here[1] + 8 - back, 8) * 16
-                load(chunk.at[pl.ds(y * 16, 16)], row, 16, first, width)
+            loads.append(pltpu.make_async_copy(chunk.at[:, back], lhs.at[back], chunk_sems.at[n]))
 
     def basis_load(basis, row, k):
         return pltpu.make_async_copy(basis.at[pl.ds(row, STEP)], rhs.at[k], basis_sems.at[k])
@@ -152,7 +147,7 @@
     @pl.loop(0, steps)
     def _(k):
         basis_load(bases[0], 0, k).wait()
-        part = lhs[:, pl.ds(pl.multiple_of(k * STEP, STEP), STEP)]
+        part = lhs[:, :, :, pl.ds(pl.multiple_of(k * STEP, STEP), STEP)].reshape(512, STEP)
         total[...] += jnp.dot(part, rhs[k], preferred_element_type=F32)
 
     out[...] = total[...].astype(out.dtype)
@@ -161,10 +156,10 @@
 def rotate(chunks, axis, bases, here, dtype, ready, before=()):
     spans = [span for _, span in bases]
     depth, cols = sum(last - first for first, last in spans), bases[0][0].shape[1]
-    places = [(back, first, chunk.shape[1]) for back, first, chunk in chunks]
+    places = [(back, first, chunk.shape[-1]) for back, first, chunk in chunks]
     count = 512
     steps = depth // STEP
-    copies = len(places) * (1 if axis == "y" else 4)
+    copies = len(places)
     return pl.pallas_call(
         functools.partial(rotate_kernel, places, axis, spans, len(before)),
         out_shape=jax.ShapeDtypeStruct((count, cols), dtype),
@@ -172,37 +167,26 @@
         + [pl.BlockSpec(memory_space=pl.ANY)] * len(places)
         + [pl.BlockSpec(memory_space=pltpu.HBM)] * len(bases)
         + [pl.BlockSpec(memory_space=pltpu.VMEM)] * len(before)
-        + [pl.BlockSpec(memory_space=pl.ANY)],
+        + [pl.BlockSpec(memory_space=pl.ANY)] * len(ready),
         out_specs=pl.BlockSpec(memory_space=pltpu.VMEM),
         scratch_shapes=[
-            pltpu.VMEM((count, depth), BF16),
+            pltpu.VMEM((4, 8, 16, depth), BF16),
             pltpu.VMEM((steps, STEP, cols), BF16),
             pltpu.VMEM((count, cols), F32),
             pltpu.SemaphoreType.DMA((copies,)),
             pltpu.SemaphoreType.DMA((steps,)),
         ],
         cost_estimate=pl.CostEstimate(
-            flops=(2 if axis == "y" else 2) * 2 * count * depth * cols,
+            flops=(8 if axis == "y" else 4) * 2 * count * depth * cols,
             bytes_accessed=2 * (count * depth + depth * cols + count * cols),
             transcendentals=0,
         ),
         compiler_params=pltpu.CompilerParams(vmem_limit_bytes=48 << 20),
         name="rotate_" + axis,
-    )(here, *[chunk for _, _, chunk in chunks], *[basis for basis, _ in bases], *before, ready)
-
-
-def score_kernel(here, first, second, third, fourth, own, other, acts, ids, out, grads, sems):
-    @pl.when(pl.program_id(0) == 0)
-    def _():
-        loads = []
-        for n, (back, chunk) in enumerate(zip(PLACES, (first, second, third, fourth))):
-            row = pl.multiple_of(lax.rem(here[0] + 4 - back, 4) * 128, 128)
-            loads.append(pltpu.make_async_copy(chunk, grads.at[pl.ds(row, 128)], sems.at[n]))
-        for load in loads:
-            load.start()
-        for load in loads:
-            load.wait()
-
+    )(here, *[chunk for _, _, chunk in chunks], *[basis for basis, _ in bases], *before, *ready)
+
+
+def score_kernel(grads, own, other, acts, ids, out):
     half = own.shape[1]
     mixed = jnp.dot(grads[:, :half], own[0], preferred_element_type=F32)
     mixed += jnp.dot(grads[:, half:], other[0], preferred_element_type=F32)
@@ -211,31 +195,29 @@
     out[0] = jnp.sum(jnp.where(ids[...] == docs, token, 0.0), axis=0, keepdims=True)
 
 
-def score(chunks, own, other, acts, ids, here):
+def score(grads, own, other, acts, ids):
     tokens, cols = acts.shape
     count, half, _ = own.shape
     return pl.pallas_call(
         score_kernel,
         grid=(count,),
         out_shape=jax.ShapeDtypeStruct((count, 1, 128), F32),
-        in_specs=[pl.BlockSpec(memory_space=pltpu.SMEM)]
-        + [pl.BlockSpec(memory_space=pl.ANY)] * 4
-        + [
+        in_specs=[
+            pl.BlockSpec((tokens, 2 * half), lambda q: (0, 0)),
             pl.BlockSpec((1, half, cols), lambda q: (q, 0, 0)),
             pl.BlockSpec((1, half, cols), lambda q: (q, 0, 0)),
             pl.BlockSpec((tokens, cols), lambda q: (0, 0)),
             pl.BlockSpec((tokens, 1), lambda q: (0, 0)),
         ],
         out_specs=pl.BlockSpec((1, 1, 128), lambda q: (q, 0, 0)),
-        scratch_shapes=[pltpu.VMEM((tokens, 2 * half), BF16), pltpu.SemaphoreType.DMA((4,))],
         cost_estimate=pl.CostEstimate(
             flops=4 * count * tokens * half * cols,
             bytes_accessed=2 * (2 * tokens * half + 2 * count * half * cols + tokens * cols),
             transcendentals=0,
         ),
-        compiler_params=pltpu.CompilerParams(vmem_limit_bytes=48 << 20),
+        compiler_params=pltpu.CompilerParams(vmem_limit_bytes=24 << 20),
         name="score",
-    )(here, *chunks, own, other, acts, ids.reshape(tokens, 1))
+    )(grads, own, other, acts, ids.reshape(tokens, 1))
 
 
 def after_kernel(value, ready, out):
@@ -271,31 +253,32 @@
     other_in = swap(basis_in)
     mine = lax.dynamic_slice_in_dim(activations, c * 16, 16)
     theirs = swap(lax.dynamic_slice_in_dim(activations, (1 - c) * 16, 16))
-    bases = direct(basis_out)
     extra = SPLIT - mine.shape[1]
-    low = join(theirs[:, extra:], here)
-    precond = damp(queries, eigenvalues, low)
+    low = first_low = join(theirs[:, extra:], here)
+    low = lax.all_gather(low, "z", axis=0, tiled=True).reshape(8, 4, 16, -1)
+    bases = direct(after(basis_out, first_low))
+    precond = damp(queries, eigenvalues, first_low)
     rows = lax.dynamic_slice_in_dim(out_grads, c * 16, 16).reshape(16, 4, 8, 256)
     rows = rows.transpose(2, 0, 1, 3).reshape(8, 16, 1024)
     mine = jnp.concatenate([mine, theirs[:, :extra]], axis=1)
     copies = jnp.broadcast_to(mine[None], (8,) + mine.shape)
     sent = lax.all_to_all(jnp.concatenate([copies, rows], axis=2), "z", 0, 0)
     high = sent[:, :, :SPLIT].reshape(128, -1)
-    rows = sent[:, :, SPLIT:].reshape(128, 1024)
+    rows = sent[:, :, SPLIT:].reshape(128, -1)
     half = basis_in.shape[0]
     high_bases = ((basis_in, (0, half)), (other_in, (0, extra)))[: 1 + (extra > 0)]
     parts = lax.all_to_all(project(rows, swap(rows), bases, precond, here), "z", 0, 0)
-    partial_acts = rotate(ring(high, "y"), "y", high_bases, here, F32, parts)
+    partial_acts = rotate([(back, first, chunk.reshape(8, 16, -1)) for back, first, chunk in ring(high, "y")], "y", high_bases, here, F32, (parts, low))
     grads = jnp.sum(parts.astype(F32), axis=0).astype(BF16)
     grads = jnp.concatenate([grads[0], swap(grads[1])], axis=1)
     copies = jnp.broadcast_to(grads[None], (8,) + grads.shape)
     grads = lax.all_to_all(copies, "z", 0, 0).reshape(128, 2048)
     low_bases = ((other_in, (extra, half)),)
-    partial_acts = rotate(ring(low, "z"), "z", low_bases, here, BF16, copies, (partial_acts,))
+    partial_acts = rotate([(y, 0, low) for y in range(4)], "z", low_bases, here, BF16, (copies,), (partial_acts,))
     rot_acts = over_x(after(partial_acts, grads))
-    grads = direct(grads)
+    rot_grads = lax.all_gather(grads, "y", axis=0, tiled=True)
     ids = lax.dynamic_index_in_dim(doc_ids.reshape(32, 2, 16), c, 1, keepdims=False)
-    docs = score(grads, precond, swap(precond), rot_acts, ids, here)
+    docs = score(rot_grads, precond, swap(precond), rot_acts, ids)
     total = jnp.sum(spread(docs[:, 0, :DOCS].reshape(1, 2 * DOCS), ALL, 256), axis=0)
     return total.reshape(2, DOCS).T
 

time: 239 us -> 229 us (0.958)
  starting transfers between devices: 62.9 us -> 38.4 us
  between operations: 0.27 us -> 13.7 us
  waiting for transfers between devices: 77.4 us -> 84 us
  Pallas kernels: 36.3 us -> 31.2 us
    ppermute x26 -> x15, waiting for transfers between devices: 77.4 us -> 6.34 us  [shift(): lax.ppermute(value, axis, [(i, (i + hops) % size) for i in range(size)])]
    all_to_all x1, waiting for transfers between devices: 0.01 us -> 39.6 us  [shards(): sent = lax.all_to_all(jnp.concatenate([copies, rows], axis=2), 'z', 0, 0)]
    ppermute x26 -> x15, starting transfers between devices: 40.4 us -> 19.1 us  [shift(): lax.ppermute(value, axis, [(i, (i + hops) % size) for i in range(size)])]
    all_to_all x1, waiting for transfers between devices: 0.01 us -> 14.8 us  [shards(): lax.all_to_all(project(rows, swap(rows), bases, precond, here), 'z', 0, 0)]
    all_to_all x1, waiting for transfers between devices: 0.01 us -> 11.7 us  [shards(): grads = lax.all_to_all(copies, 'z', 0, 0).reshape(128, 2048)]
    all_to_all x1, waiting for transfers between devices: 0.01 us -> 11.4 us  [spread(): lax.all_to_all(jnp.broadcast_to(value[None], (size,) + value.shape), axes...]
    unnamed x35 -> x32, local copies, waits for them, and re-layouts: 6.38 us -> 11.3 us
    all_to_all x1, starting transfers between devices: 6.68 us -> 3.49 us  [shards(): lax.all_to_all(project(rows, swap(rows), bases, precond, here), 'z', 0, 0)]
  transfers between devices with their start and end apart: 30 -> 21, of which waited for: 9 -> 9; matrix products, arithmetic and copies ran while one was open for 6% -> 4% of each run, Pallas kernels for 12% -> 10%
where the time goes in v5:
time: 229 us
  waiting for transfers between devices  84 us (37%)
  blocking collectives  38.8 us (17%)
  starting transfers between devices  38.4 us (17%)
  Pallas kernels  31.2 us (14%)
  local copies, waits for them, and re-layouts  20.5 us (9%)
  between operations  13.7 us (6%)
    all_to_all x1, waiting for transfers between devices, shards(): sent = lax.all_to_all(jnp.concatenate([copies, rows], axis=2), 'z', 0, 0)  39.6 us
    all_to_all x1, blocking collectives, spread(): lax.all_to_all(jnp.broadcast_to(value[None], (size,) + value.shape), axes...  22 us
    ppermute x15, starting transfers between devices, shift(): lax.ppermute(value, axis, [(i, (i + hops) % size) for i in range(size)])  19.1 us
    pallas_call x2, Pallas kernels, rotate(): pl.pallas_call(functools.partial(rotate_kernel, places, axis, spans, len(...  18.5 us
    all_to_all x1, blocking collectives, over_x(): parts = lax.all_to_all(partial.reshape(4, rows // 4, cols), 'x', 0, 0)  16.7 us
    all_to_all x1, waiting for transfers between devices, shards(): lax.all_to_all(project(rows, swap(rows), bases, precond, here), 'z', 0, 0)  14.8 us
    all_to_all x1, waiting for transfers between devices, shards(): grads = lax.all_to_all(copies, 'z', 0, 0).reshape(128, 2048)  11.7 us
    all_to_all x1, waiting for transfers between devices, spread(): lax.all_to_all(jnp.broadcast_to(value[None], (size,) + value.shape), axes...  11.4 us
  transfers between devices with their start and end apart: 21, of which 9 were waited for; matrix products, arithmetic and copies ran while one was open for 4% of the time, Pallas kernels for 10%

profile of v5, /device:TPU:1, one launch (start us, length us, event | category | flops | bytes accessed | tf_op | source)
XLA Modules:
  0.0 228.6 jit_solution(5245653361386764302)
XLA Ops:
  6.5 1.9 copy.21.value
  8.5 1.0 constant_dynamic-slice_fusion
  9.4 3.3 %collective-permute-start.1 = (bf16[16,3584]{1,0:T(8,128)(2,1)S(1)}, bf16[16,3584]{1,0:T(8,128)(2,1)S(1)}, u32[]{:S(2)}, u32[]{:S(2)}) collective-permute-start(bf16[16,3584]{1,0:T(8,128)(2,1)S(1)} %get-tuple-element.5), channel_id=1, source_target_pairs={{0,1},{1,0},{2,3},{3,2},{4,5},{5,4},{6,7},{7,6},{8,9},{9,8},{10,11... | collective-permute-start | bytes 344072 | tf_op jit(solution)/shard_map/ppermute | solution.py:25
  12.8 1.0 collective-permute-done.1.refs_0_
  13.7 2.7 %collective-permute-start.3 = (bf16[16,3584]{1,0:T(8,128)(2,1)S(1)}, bf16[16,3584]{1,0:T(8,128)(2,1)S(1)}, u32[]{:S(2)}, u32[]{:S(2)}) collective-permute-start(bf16[16,3584]{1,0:T(8,128)(2,1)S(1)} %collective-permute-done.1.refs_0_), channel_id=1, source_target_pairs={{0,192},{64,0},{128,64},{192,128},{1,193},{65,1},{129,65},{193,129... | collective-permute-start | bytes 344072 | tf_op jit(solution)/shard_map/ppermute | solution.py:25
  16.4 0.6 pad_add_fusion.here
  17.1 2.3 collective-permute-done.2.refs_1_
  19.3 1.7 collective-permute-done.3.refs_2_
  21.6 0.6 copy-done.13
  22.3 1.9 join.1.ready._
  24.7 1.1 pad_maximum_fusion
  25.8 8.1 %all-to-all-start = ((bf16[8,16,4608]{2,1,0:T(8,128)(2,1)}), bf16[8,16,4608]{2,1,0:T(8,128)(2,1)}, u32[]{:S(2)}, u32[]{:S(2)}) async-start(bf16[8,16,4608]{2,1,0:T(8,128)(2,1)} %pad_maximum_fusion), calls=%async_computation | async-start | bytes 2359296 | tf_op jit(solution)/shard_map/all_to_all | solution.py:265
  33.9 1.3 collective-permute-start.10
  35.2 0.9 collective-permute-start.5
  36.1 1.8 collective-permute-start.6
  37.9 0.6 collective-permute-start.7
  38.6 39.6 %all-to-all-done = bf16[8,16,4608]{2,1,0:T(8,128)(2,1)} async-done(((bf16[8,16,4608]{2,1,0:T(8,128)(2,1)}), bf16[8,16,4608]{2,1,0:T(8,128)(2,1)}, u32[]{:S(2)}, u32[]{:S(2)}) %all-to-all-start) | async-done | bytes 1179680 | tf_op jit(solution)/shard_map/all_to_all | solution.py:265
  78.2 1.0 slice.28
  79.2 0.8 collective-permute-start
  80.0 2.1 copy-done.6
  82.0 1.7 damp.1.precond.own
  83.8 2.8 %project.1 = bf16[8,2,16,1024]{3,2,1,0:T(8,128)(2,1)} custom-call(s32[2]{0:T(128)S(1)} %copy-done.8, bf16[128,1024]{1,0:T(8,128)(2,1)S(1)} %bitcast.25, bf16[128,1024]{1,0:T(8,128)(2,1)S(1)} %collective-permute-done.other, bf16[256,1024]{1,0:T(8,128)(2,1)S(1)} %copy-done.4, bf16[256,1024]{1,0:T(8,128)(2,1)S(1)} %collective-permute-done.5.second, ...), custom_call_target="tpu_custom_call" | custom-call | flops 536870912 | bytes 4194304 | tf_op jit(solution)/shard_map/project/pallas_call | solution.py:82
  86.6 1.9 copy-done.1
  88.5 3.5 %all-to-all-start.1 = ((bf16[8,2,16,1024]{3,2,1,0:T(8,128)(2,1)}), bf16[8,2,16,1024]{3,2,1,0:T(8,128)(2,1)S(1)}, u32[]{:S(2)}, u32[]{:S(2)}) async-start(bf16[8,2,16,1024]{3,2,1,0:T(8,128)(2,1)} %project.1), calls=%async_computation.1 | async-start | bytes 1048576 | tf_op jit(solution)/shard_map/all_to_all | solution.py:270
  92.0 1.3 slice.31.refs_0_
  93.3 2.7 %collective-permute-start.12 = (bf16[128,3584]{1,0:T(8,128)(2,1)S(1)}, bf16[128,3584]{1,0:T(8,128)(2,1)}, u32[]{:S(2)}, u32[]{:S(2)}) collective-permute-start(bf16[128,3584]{1,0:T(8,128)(2,1)S(1)} %bitcast.27), channel_id=1, source_target_pairs={{0,192},{64,0},{128,64},{192,128},{1,193},{65,1},{129,65},{193,129... | collective-permute-start | bytes 2752520 | tf_op jit(solution)/shard_map/ppermute | solution.py:25
  96.0 14.8 %all-to-all-done.1.refs_6_ = bf16[8,2,16,1024]{3,2,1,0:T(8,128)(2,1)S(1)} async-done(((bf16[8,2,16,1024]{3,2,1,0:T(8,128)(2,1)}), bf16[8,2,16,1024]{3,2,1,0:T(8,128)(2,1)S(1)}, u32[]{:S(2)}, u32[]{:S(2)}) %all-to-all-start.1) | async-done | bytes 524320 | tf_op jit(solution)/shard_map/all_to_all | solution.py:270
  110.9 1.3 collective-permute-start.8
  112.2 0.9 collective-permute-done.8
  113.1 0.9 broadcast_in_dim.11.refs_6_
  113.9 4.2 %all-to-all-start.2 = ((bf16[8,16,2048]{2,1,0:T(8,128)(2,1)}), bf16[8,16,2048]{2,1,0:T(8,128)(2,1)}, u32[]{:S(2)}, u32[]{:S(2)}) async-start(bf16[8,16,2048]{2,1,0:T(8,128)(2,1)} %broadcast_in_dim.11.refs_6_), calls=%async_computation.2 | async-start | bytes 1048576 | tf_op jit(solution)/shard_map/all_to_all | solution.py:275
  118.2 0.8 slice.32
  119.4 1.8 slice.33
  121.2 2.3 collective-permute-start.14
  123.5 0.9 collective-permute-start.9
  124.4 11.7 %all-to-all-done.2 = bf16[8,16,2048]{2,1,0:T(8,128)(2,1)} async-done(((bf16[8,16,2048]{2,1,0:T(8,128)(2,1)}), bf16[8,16,2048]{2,1,0:T(8,128)(2,1)}, u32[]{:S(2)}, u32[]{:S(2)}) %all-to-all-start.2) | async-done | bytes 524320 | tf_op jit(solution)/shard_map/all_to_all | solution.py:275
  136.2 9.1 %rotate_y.1.refs_5_ = f32[512,896]{1,0:T(8,128)S(1)} custom-call(s32[2]{0:T(128)S(1)} %copy-done.8, bf16[8,16,3584]{2,1,0:T(8,128)(2,1)S(1)} %slice.31.refs_0_, bf16[8,16,3584]{2,1,0:T(8,128)(2,1)S(1)} %bitcast.29, bf16[8,16,3584]{2,1,0:T(8,128)(2,1)} %bitcast.10.refs_2_, bf16[8,16,1792]{2,1,0:T(8,128)(2,1)S(1)} %bitcast.30, ...), custom_call_target="tpu_custom_call" | custom-call | flops 26306674688 | bytes 11010048 | tf_op jit(solution)/shard_map/rotate_y/pallas_call | solution.py:163
  145.4 9.4 %rotate_z.1.value = bf16[512,896]{1,0:T(8,128)(2,1)S(1)} custom-call(s32[2]{0:T(128)S(1)} %copy-done.8, bf16[8,4,16,3584]{3,2,1,0:T(8,128)(2,1)} %bitcast.35, bf16[8,4,16,3584]{3,2,1,0:T(8,128)(2,1)} %bitcast.36, bf16[8,4,16,3584]{3,2,1,0:T(8,128)(2,1)} %bitcast.37, bf16[8,4,16,3584]{3,2,1,0:T(8,128)(2,1)} %bitcast.38, ...), custom_call_target="tpu_custom_call" | custom-call | flops 13153337344 | bytes 11010048 | tf_op jit(solution)/shard_map/rotate_z/pallas_call | solution.py:163
  154.7 0.9 copy-done.5
  155.7 16.7 %all_to_all.30 = bf16[4,128,896]{2,1,0:T(8,128)(2,1)S(1)} all-to-all(bf16[4,128,896]{2,1,0:T(8,128)(2,1)} %bitcast.23), channel_id=1, replica_groups=mesh['y'=4,'z'=8,'x'=4,'c'=2] {'x'}, dimensions={0} | all-to-all | bytes 1835008 | tf_op jit(solution)/shard_map/all_to_all | solution.py:241
  172.5 1.0 broadcast_in_dim.12
  173.6 3.5 %all-to-all-start.4 = ((bf16[4,128,896]{2,1,0:T(8,128)(2,1)}), bf16[4,128,896]{2,1,0:T(8,128)(2,1)S(1)}, u32[]{:S(2)}, u32[]{:S(2)}) async-start(bf16[4,128,896]{2,1,0:T(8,128)(2,1)} %broadcast_in_dim.12), calls=%async_computation.4 | async-start | bytes 1835008 | tf_op jit(solution)/shard_map/all_to_all | solution.py:42
  177.5 11.4 %all-to-all-done.4 = bf16[4,128,896]{2,1,0:T(8,128)(2,1)S(1)} async-done(((bf16[4,128,896]{2,1,0:T(8,128)(2,1)}), bf16[4,128,896]{2,1,0:T(8,128)(2,1)S(1)}, u32[]{:S(2)}, u32[]{:S(2)}) %all-to-all-start.4) | async-done | bytes 917536 | tf_op jit(solution)/shard_map/all_to_all | solution.py:42
  188.9 2.0 copy-done.2
  190.9 1.6 copy-done.9
  192.5 6.4 %score.1 = f32[2,1,128]{2,1,0:T(1,128)S(1)} custom-call(bf16[512,2048]{1,0:T(8,128)(2,1)S(1)} %copy-done.9, bf16[2,1024,896]{2,1,0:T(8,128)(2,1)S(1)} %copy-done.2, bf16[2,1024,896]{2,1,0:T(8,128)(2,1)} %collective-permute-done.9.other, bf16[512,896]{1,0:T(8,128)(2,1)S(1)} %bitcast.28, s32[512,1]{1,0:T(8,128)S(1)} %reshape.69.ids), custom_call_target="tpu_custom_call" | custom-call | flops 3758096384 | bytes 10354688 | tf_op jit(solution)/shard_map/score/pallas_call | solution.py:201
  199.0 22.0 %all_to_all.31 = f32[256,1,128]{2,1,0:T(1,128)S(1)} all-to-all(f32[256,1,128]{2,1,0:T(1,128)S(1)} %broadcast_in_dim.14), channel_id=1, replica_groups=mesh['y'=4,'z'=8,'x'=4,'c'=2] {'y','z','x','c'}, dimensions={0} | all-to-all | bytes 262144 | tf_op jit(solution)/shard_map/all_to_all | solution.py:42
  221.1 0.6 reshape.68
  (63 shorter events, 2.5 us)
Async XLA Ops:
  6.5 17.7 %copy-start = (bf16[32,8192]{1,0:T(8,128)(2,1)S(1)}, bf16[32,8192]{1,0:T(8,128)(2,1)}, u32[]{:S(2)}) copy-start(bf16[32,8192]{1,0:T(8,128)(2,1)} %param.8) | copy-start | bytes 1572868
  6.5 129.6 %all-gather.5.cloned.1.call-start = ((), (), s32[]{:S(2)}) async-start(), calls=%async_computation.7 | async-start | bytes 4128768 | tf_op jit(solution)/shard_map/all_gather | solution.py:258
  9.4 4.3 %collective-permute-start.1 = (bf16[16,3584]{1,0:T(8,128)(2,1)S(1)}, bf16[16,3584]{1,0:T(8,128)(2,1)S(1)}, u32[]{:S(2)}, u32[]{:S(2)}) collective-permute-start(bf16[16,3584]{1,0:T(8,128)(2,1)S(1)} %get-tuple-element.5), channel_id=1, source_target_pairs={{0,1},{1,0},{2,3},{3,2},{4,5},{5,4},{6,7},{7,6},{8,9},{9,8},{10,11... | collective-permute-start | bytes 344072 | tf_op jit(solution)/shard_map/ppermute | solution.py:25
  13.7 7.8 %copy-start.10 = (bf16[16,3584]{1,0:T(8,128)(2,1)}, bf16[16,3584]{1,0:T(8,128)(2,1)S(1)}, u32[]{:S(2)}) copy-start(bf16[16,3584]{1,0:T(8,128)(2,1)S(1)} %collective-permute-done.1.refs_0_) | copy-start | bytes 344068
  13.7 5.6 %collective-permute-start.2 = (bf16[16,3584]{1,0:T(8,128)(2,1)S(1)}, bf16[16,3584]{1,0:T(8,128)(2,1)S(1)}, u32[]{:S(2)}, u32[]{:S(2)}) collective-permute-start(bf16[16,3584]{1,0:T(8,128)(2,1)S(1)} %collective-permute-done.1.refs_0_), channel_id=1, source_target_pairs={{0,64},{64,128},{128,192},{192,0},{1,65},{65,129},{129,193},{193,1... | collective-permute-start | bytes 344072 | tf_op jit(solution)/shard_map/ppermute | solution.py:25
  13.7 7.2 %collective-permute-start.3 = (bf16[16,3584]{1,0:T(8,128)(2,1)S(1)}, bf16[16,3584]{1,0:T(8,128)(2,1)S(1)}, u32[]{:S(2)}, u32[]{:S(2)}) collective-permute-start(bf16[16,3584]{1,0:T(8,128)(2,1)S(1)} %collective-permute-done.1.refs_0_), channel_id=1, source_target_pairs={{0,192},{64,0},{128,64},{192,128},{1,193},{65,1},{129,65},{193,129... | collective-permute-start | bytes 344072 | tf_op jit(solution)/shard_map/ppermute | solution.py:25
  16.4 5.1 %collective-permute-start.4 = (bf16[16,3584]{1,0:T(8,128)(2,1)S(1)}, bf16[16,3584]{1,0:T(8,128)(2,1)S(1)}, u32[]{:S(2)}, u32[]{:S(2)}) collective-permute-start(bf16[16,3584]{1,0:T(8,128)(2,1)S(1)} %collective-permute-done.1.refs_0_), channel_id=1, source_target_pairs={{0,128},{64,192},{128,0},{192,64},{1,129},{65,193},{129,1},{193,65... | collective-permute-start | bytes 344072 | tf_op jit(solution)/shard_map/ppermute | solution.py:25
  19.3 2.2 copy-start.11
  21.0 0.6 copy-start.12
  21.6 0.6 copy-start.13
  25.8 54.2 %copy-start.3 = (bf16[64,3584]{1,0:T(8,128)(2,1)S(1)}, bf16[64,3584]{1,0:T(8,128)(2,1)}, u32[]{:S(2)}) copy-start(bf16[64,3584]{1,0:T(8,128)(2,1)} %join.1.ready._) | copy-start | bytes 1376260
  25.8 54.2 %copy-start.7 = (bf16[1024,896]{1,0:T(8,128)(2,1)S(1)}, bf16[1024,896]{1,0:T(8,128)(2,1)}, u32[]{:S(2)}) copy-start(bf16[1024,896]{1,0:T(8,128)(2,1)} %eigenvalues.1) | copy-start | bytes 5505028
  25.8 52.4 %all-to-all-start = ((bf16[8,16,4608]{2,1,0:T(8,128)(2,1)}), bf16[8,16,4608]{2,1,0:T(8,128)(2,1)}, u32[]{:S(2)}, u32[]{:S(2)}) async-start(bf16[8,16,4608]{2,1,0:T(8,128)(2,1)} %pad_maximum_fusion), calls=%async_computation | async-start | bytes 2359296 | tf_op jit(solution)/shard_map/all_to_all | solution.py:265
  33.9 111.5 %collective-permute-start.10 = (bf16[3584,896]{1,0:T(8,128)(2,1)}, bf16[3584,896]{1,0:T(8,128)(2,1)}, u32[]{:S(2)}, u32[]{:S(2)}) collective-permute-start(bf16[3584,896]{1,0:T(8,128)(2,1)} %refs_5_.1), channel_id=1, source_target_pairs={{0,1},{1,0},{2,3},{3,2},{4,5},{5,4},{6,7},{7,6},{8,9},{9,8},{10,11... | collective-permute-start | bytes 19267592 | tf_op jit(solution)/shard_map/ppermute | solution.py:25
  35.2 48.5 %collective-permute-start.5 = (bf16[256,1024]{1,0:T(8,128)(2,1)}, bf16[256,1024]{1,0:T(8,128)(2,1)S(1)}, u32[]{:S(2)}, u32[]{:S(2)}) collective-permute-start(bf16[256,1024]{1,0:T(8,128)(2,1)} %after.2.first), channel_id=1, source_target_pairs={{0,64},{64,128},{128,192},{192,0},{1,65},{65,129},{129,193},{193,1... | collective-permute-start | bytes 1572872 | tf_op jit(solution)/shard_map/ppermute | solution.py:25
  36.1 47.6 %collective-permute-start.6 = (bf16[256,1024]{1,0:T(8,128)(2,1)}, bf16[256,1024]{1,0:T(8,128)(2,1)}, u32[]{:S(2)}, u32[]{:S(2)}) collective-permute-start(bf16[256,1024]{1,0:T(8,128)(2,1)} %after.2.first), channel_id=1, source_target_pairs={{0,192},{64,0},{128,64},{192,128},{1,193},{65,1},{129,65},{193,129... | collective-permute-start | bytes 1572872 | tf_op jit(solution)/shard_map/ppermute | solution.py:25
  37.9 45.8 %collective-permute-start.7 = (bf16[256,1024]{1,0:T(8,128)(2,1)}, bf16[256,1024]{1,0:T(8,128)(2,1)}, u32[]{:S(2)}, u32[]{:S(2)}) collective-permute-start(bf16[256,1024]{1,0:T(8,128)(2,1)} %after.2.first), channel_id=1, source_target_pairs={{0,128},{64,192},{128,0},{192,64},{1,129},{65,193},{129,1},{193,65... | collective-permute-start | bytes 1572872 | tf_op jit(solution)/shard_map/ppermute | solution.py:25
  79.2 4.6 %copy-start.4 = (bf16[256,1024]{1,0:T(8,128)(2,1)S(1)}, bf16[256,1024]{1,0:T(8,128)(2,1)}, u32[]{:S(2)}) copy-start(bf16[256,1024]{1,0:T(8,128)(2,1)} %after.2.first) | copy-start | bytes 1572868
  79.2 4.6 %collective-permute-start = (bf16[128,1024]{1,0:T(8,128)(2,1)S(1)}, bf16[128,1024]{1,0:T(8,128)(2,1)S(1)}, u32[]{:S(2)}, u32[]{:S(2)}) collective-permute-start(bf16[128,1024]{1,0:T(8,128)(2,1)S(1)} %bitcast.24), channel_id=1, source_target_pairs={{0,1},{1,0},{2,3},{3,2},{4,5},{5,4},{6,7},{7,6},{8,9},{9,8},{10,11... | collective-permute-start | bytes 786440 | tf_op jit(solution)/shard_map/ppermute | solution.py:25
  80.0 2.1 copy-start.6
  82.0 1.7 copy-start.8
  86.6 1.9 copy-start.1
  88.5 22.3 %all-to-all-start.1 = ((bf16[8,2,16,1024]{3,2,1,0:T(8,128)(2,1)}), bf16[8,2,16,1024]{3,2,1,0:T(8,128)(2,1)S(1)}, u32[]{:S(2)}, u32[]{:S(2)}) async-start(bf16[8,2,16,1024]{3,2,1,0:T(8,128)(2,1)} %project.1), calls=%async_computation.1 | async-start | bytes 1048576 | tf_op jit(solution)/shard_map/all_to_all | solution.py:270
  93.2 24.9 %collective-permute-start.11 = (bf16[128,3584]{1,0:T(8,128)(2,1)S(1)}, bf16[128,3584]{1,0:T(8,128)(2,1)S(1)}, u32[]{:S(2)}, u32[]{:S(2)}) collective-permute-start(bf16[128,3584]{1,0:T(8,128)(2,1)S(1)} %bitcast.26), channel_id=1, source_target_pairs={{0,64},{64,128},{128,192},{192,0},{1,65},{65,129},{129,193},{193,1... | collective-permute-start | bytes 2752520 | tf_op jit(solution)/shard_map/ppermute | solution.py:25
  93.3 26.1 %collective-permute-start.12 = (bf16[128,3584]{1,0:T(8,128)(2,1)S(1)}, bf16[128,3584]{1,0:T(8,128)(2,1)}, u32[]{:S(2)}, u32[]{:S(2)}) collective-permute-start(bf16[128,3584]{1,0:T(8,128)(2,1)S(1)} %bitcast.27), channel_id=1, source_target_pairs={{0,192},{64,0},{128,64},{192,128},{1,193},{65,1},{129,65},{193,129... | collective-permute-start | bytes 2752520 | tf_op jit(solution)/shard_map/ppermute | solution.py:25
  110.9 2.1 collective-permute-start.8
  113.9 22.2 %all-to-all-start.2 = ((bf16[8,16,2048]{2,1,0:T(8,128)(2,1)}), bf16[8,16,2048]{2,1,0:T(8,128)(2,1)}, u32[]{:S(2)}, u32[]{:S(2)}) async-start(bf16[8,16,2048]{2,1,0:T(8,128)(2,1)} %broadcast_in_dim.11.refs_6_), calls=%async_computation.2 | async-start | bytes 1048576 | tf_op jit(solution)/shard_map/all_to_all | solution.py:275
  118.1 59.3 %all-gather.3.cloned.1.call-start = ((), (), s32[]{:S(2)}) async-start(), calls=%async_computation.6 | async-start | bytes 2621440 | tf_op jit(solution)/shard_map/all_gather | solution.py:279
  119.0 17.2 %collective-permute-start.13 = (bf16[128,1792]{1,0:T(8,128)(2,1)}, bf16[128,1792]{1,0:T(8,128)(2,1)S(1)}, u32[]{:S(2)}, u32[]{:S(2)}) collective-permute-start(bf16[128,1792]{1,0:T(8,128)(2,1)} %slice.32), channel_id=1, source_target_pairs={{0,64},{64,128},{128,192},{192,0},{1,65},{65,129},{129,193},{193,1... | collective-permute-start | bytes 1376264 | tf_op jit(solution)/shard_map/ppermute | solution.py:25
  121.2 14.9 %collective-permute-start.14 = (bf16[128,1792]{1,0:T(8,128)(2,1)}, bf16[128,1792]{1,0:T(8,128)(2,1)}, u32[]{:S(2)}, u32[]{:S(2)}) collective-permute-start(bf16[128,1792]{1,0:T(8,128)(2,1)} %slice.33), channel_id=1, source_target_pairs={{0,192},{64,0},{128,64},{192,128},{1,193},{65,1},{129,65},{193,129... | collective-permute-start | bytes 1376264 | tf_op jit(solution)/shard_map/ppermute | solution.py:25
  123.5 53.9 %collective-permute-start.9 = (bf16[2,1024,896]{2,1,0:T(8,128)(2,1)}, bf16[2,1024,896]{2,1,0:T(8,128)(2,1)}, u32[]{:S(2)}, u32[]{:S(2)}) collective-permute-start(bf16[2,1024,896]{2,1,0:T(8,128)(2,1)} %copy-done.1), channel_id=1, source_target_pairs={{0,1},{1,0},{2,3},{3,2},{4,5},{5,4},{6,7},{7,6},{8,9},{9,8},{10,11... | collective-permute-start | bytes 11010056 | tf_op jit(solution)/shard_map/ppermute | solution.py:25
  154.7 0.9 copy-start.5
  172.4 4.7 %copy-start.14 = (s32[1024]{0:T(1024)S(1)}, s32[1024]{0:T(1024)}, u32[]{:S(2)}) copy-start(s32[1024]{0:T(1024)} %param.13) | copy-start | bytes 12292
  173.6 15.3 %all-to-all-start.4 = ((bf16[4,128,896]{2,1,0:T(8,128)(2,1)}), bf16[4,128,896]{2,1,0:T(8,128)(2,1)S(1)}, u32[]{:S(2)}, u32[]{:S(2)}) async-start(bf16[4,128,896]{2,1,0:T(8,128)(2,1)} %broadcast_in_dim.12), calls=%async_computation.4 | async-start | bytes 1835008 | tf_op jit(solution)/shard_map/all_to_all | solution.py:42
  188.8 2.0 copy-start.2
  190.9 1.6 copy-start.9
Sparse Core Ops, SparseCore 0:
  24.3 77.7 all-gather.4
  136.3 27.5 all-gather.2

commit v6 on v5

--- a/solution.py
+++ b/solution.py
@@ -56,16 +56,18 @@
     return [value] + [shift(value, "y", back) for back in PLACES[1:]]
 
 
-def join(value, here):
+def join(value, ready, here):
     rows, cols = value.shape
     return pl.pallas_call(
         functools.partial(join_kernel, PLACES, rows),
         out_shape=jax.ShapeDtypeStruct((4 * rows, cols), BF16),
-        in_specs=[pl.BlockSpec(memory_space=pltpu.SMEM)] + [pl.BlockSpec(memory_space=pltpu.VMEM)] * 4,
+        in_specs=[pl.BlockSpec(memory_space=pltpu.SMEM)]
+        + [pl.BlockSpec(memory_space=pltpu.VMEM)] * 4
+        + [pl.BlockSpec(memory_space=pl.ANY)],
         out_specs=pl.BlockSpec(memory_space=pltpu.VMEM),
         cost_estimate=pl.CostEstimate(flops=0, bytes_accessed=16 * rows * cols, transcendentals=0),
         name="join",
-    )(here, *direct(value))
+    )(here, *direct(value), ready)
 
 
 def project_kernel(here, own, other, first, second, third, fourth, precond, out):
@@ -90,30 +92,38 @@
     )(here, own, other, *bases, precond)
 
 
-def damp_kernel(queries, eigenvalues, _, out):
+def damp_kernel(queries, eigenvalues, basis, _, out, same):
+    same[...] = basis[...]
     damped = eigenvalues[...].astype(F32) + DAMPING
     for q in range(2):
         out[q] = (queries[q].astype(F32) / damped).astype(BF16)
 
 
-def damp(queries, eigenvalues, ready):
+def damp(queries, eigenvalues, basis, ready):
     count, rows, cols = queries.shape
     return pl.pallas_call(
         damp_kernel,
         grid=(rows // 128,),
-        out_shape=jax.ShapeDtypeStruct((count, rows, cols), BF16),
+        out_shape=(
+            jax.ShapeDtypeStruct((count, rows, cols), BF16),
+            jax.ShapeDtypeStruct(basis.shape, BF16),
+        ),
         in_specs=[
             pl.BlockSpec((count, 128, cols), lambda i: (0, i, 0)),
             pl.BlockSpec((128, cols), lambda i: (i, 0)),
+            pl.BlockSpec((32, basis.shape[1]), lambda i: (i, 0)),
             pl.BlockSpec(memory_space=pl.ANY),
         ],
-        out_specs=pl.BlockSpec((count, 128, cols), lambda i: (0, i, 0)),
+        out_specs=(
+            pl.BlockSpec((count, 128, cols), lambda i: (0, i, 0)),
+            pl.BlockSpec((32, basis.shape[1]), lambda i: (i, 0)),
+        ),
         cost_estimate=pl.CostEstimate(
             flops=2 * count * rows * cols, bytes_accessed=10 * rows * cols, transcendentals=0
         ),
-        compiler_params=pltpu.CompilerParams(vmem_limit_bytes=8 << 20),
+        compiler_params=pltpu.CompilerParams(vmem_limit_bytes=56 << 20),
         name="damp",
-    )(queries, eigenvalues, ready)
+    )(queries, eigenvalues, basis, ready)
 
 
 def rotate_kernel(places, axis, spans, summed, here, *refs):
@@ -177,7 +187,7 @@
             pltpu.SemaphoreType.DMA((steps,)),
         ],
         cost_estimate=pl.CostEstimate(
-            flops=(8 if axis == "y" else 4) * 2 * count * depth * cols,
+            flops=(4 if axis == "y" else 4) * 2 * count * depth * cols,
             bytes_accessed=2 * (count * depth + depth * cols + count * cols),
             transcendentals=0,
         ),
@@ -215,7 +225,7 @@
             bytes_accessed=2 * (2 * tokens * half + 2 * count * half * cols + tokens * cols),
             transcendentals=0,
         ),
-        compiler_params=pltpu.CompilerParams(vmem_limit_bytes=24 << 20),
+        compiler_params=pltpu.CompilerParams(vmem_limit_bytes=56 << 20),
         name="score",
     )(grads, own, other, acts, ids.reshape(tokens, 1))
 
@@ -254,17 +264,15 @@
     mine = lax.dynamic_slice_in_dim(activations, c * 16, 16)
     theirs = swap(lax.dynamic_slice_in_dim(activations, (1 - c) * 16, 16))
     extra = SPLIT - mine.shape[1]
-    low = first_low = join(theirs[:, extra:], here)
-    low = lax.all_gather(low, "z", axis=0, tiled=True).reshape(8, 4, 16, -1)
-    bases = direct(after(basis_out, first_low))
-    precond = damp(queries, eigenvalues, first_low)
     rows = lax.dynamic_slice_in_dim(out_grads, c * 16, 16).reshape(16, 4, 8, 256)
     rows = rows.transpose(2, 0, 1, 3).reshape(8, 16, 1024)
+    rows = lax.all_to_all(rows, "z", 0, 0).reshape(128, -1)
+    low = first_low = join(theirs[:, extra:], rows, here)
+    low = lax.all_gather(low, "z", axis=0, tiled=True).reshape(8, 4, 16, -1)
+    precond, basis_out = damp(queries, eigenvalues, basis_out, first_low)
+    bases = direct(basis_out)
     mine = jnp.concatenate([mine, theirs[:, :extra]], axis=1)
-    copies = jnp.broadcast_to(mine[None], (8,) + mine.shape)
-    sent = lax.all_to_all(jnp.concatenate([copies, rows], axis=2), "z", 0, 0)
-    high = sent[:, :, :SPLIT].reshape(128, -1)
-    rows = sent[:, :, SPLIT:].reshape(128, -1)
+    high = spread(mine, "z", 8).reshape(128, -1)
     half = basis_in.shape[0]
     high_bases = ((basis_in, (0, half)), (other_in, (0, extra)))[: 1 + (extra > 0)]
     parts = lax.all_to_all(project(rows, swap(rows), bases, precond, here), "z", 0, 0)

time: 229 us -> 230 us (level)
  waiting for transfers between devices: 84 us -> 71.1 us
  starting transfers between devices: 38.4 us -> 48.8 us
  Pallas kernels: 31.2 us -> 38 us
  local copies, waits for them, and re-layouts: 20.5 us -> 16.8 us
    all_to_all x1, waiting for transfers between devices: 39.6 us -> 0.01 us  [shards(): rows = lax.all_to_all(rows, 'z', 0, 0).reshape(128, -1)]
    ppermute x15, waiting for transfers between devices: 6.34 us -> 28.6 us  [shift(): lax.ppermute(value, axis, [(i, (i + hops) % size) for i in range(size)])]
    all_to_all x1 -> x2, starting transfers between devices: 3.5 us -> 10.4 us  [spread(): lax.all_to_all(jnp.broadcast_to(value[None], (size,) + value.shape), axes...]
    pallas_call x1, Pallas kernels: 1.68 us -> 7.23 us  [damp(): pl.pallas_call(damp_kernel, grid=(rows // 128,), out_shape=(jax.ShapeDtyp...]
    all_to_all x1, waiting for transfers between devices: 14.8 us -> 20.1 us  [shards(): lax.all_to_all(project(rows, swap(rows), bases, precond, here), 'z', 0, 0)]
    unnamed x32 -> x27, local copies, waits for them, and re-layouts: 11.3 us -> 6.8 us
    all_to_all x1, starting transfers between devices: 3.49 us -> 6.32 us  [shards(): lax.all_to_all(project(rows, swap(rows), bases, precond, here), 'z', 0, 0)]
    all_to_all x1 -> x2, waiting for transfers between devices: 11.4 us -> 10.7 us  [spread(): lax.all_to_all(jnp.broadcast_to(value[None], (size,) + value.shape), axes...]
  transfers between devices with their start and end apart: 21 -> 22, of which waited for: 9 -> 10; matrix products, arithmetic and copies ran while one was open for 4% -> 4% of each run, Pallas kernels for 10% -> 12%
where the time goes in v6:
time: 230 us; the launch traced here: 229 us
  waiting for transfers between devices  71.1 us (31%)
  starting transfers between devices  48.8 us (21%)
  blocking collectives  39.4 us (17%)
  Pallas kernels  38 us (17%)
  local copies, waits for them, and re-layouts  16.8 us (7%)
  between operations  13.6 us (6%)
    ppermute x15, waiting for transfers between devices, shift(): lax.ppermute(value, axis, [(i, (i + hops) % size) for i in range(size)])  28.6 us
    all_to_all x1, blocking collectives, spread(): lax.all_to_all(jnp.broadcast_to(value[None], (size,) + value.shape), axes...  22.6 us
    all_to_all x1, waiting for transfers between devices, shards(): lax.all_to_all(project(rows, swap(rows), bases, precond, here), 'z', 0, 0)  20.1 us
    ppermute x15, starting transfers between devices, shift(): lax.ppermute(value, axis, [(i, (i + hops) % size) for i in range(size)])  18.9 us
    pallas_call x2, Pallas kernels, rotate(): pl.pallas_call(functools.partial(rotate_kernel, places, axis, spans, len(...  18.5 us
    all_to_all x1, blocking collectives, over_x(): parts = lax.all_to_all(partial.reshape(4, rows // 4, cols), 'x', 0, 0)  16.9 us
    all_to_all x1, waiting for transfers between devices, shards(): grads = lax.all_to_all(copies, 'z', 0, 0).reshape(128, 2048)  11.7 us
    all_to_all x2, waiting for transfers between devices, spread(): lax.all_to_all(jnp.broadcast_to(value[None], (size,) + value.shape), axes...  10.7 us
  transfers between devices with their start and end apart: 22, of which 10 were waited for; matrix products, arithmetic and copies ran while one was open for 4% of the time, Pallas kernels for 12%

profile of v6, /device:TPU:1, one launch (start us, length us, event | category | flops | bytes accessed | tf_op | source)
XLA Modules:
  0.0 228.7 jit_solution(3554047202059496961)
XLA Ops:
  6.5 1.0 copy-done
  7.8 0.9 reshape.55
  8.6 9.0 %all-to-all-start = ((bf16[8,16,1024]{2,1,0:T(8,128)(2,1)}), bf16[8,16,1024]{2,1,0:T(8,128)(2,1)S(1)}, u32[]{:S(2)}, u32[]{:S(2)}) async-start(bf16[8,16,1024]{2,1,0:T(8,128)(2,1)} %reshape.55), calls=%async_computation | async-start | bytes 524288 | tf_op jit(solution)/shard_map/all_to_all | solution.py:269
  17.7 1.0 constant_dynamic-slice_fusion
  18.7 1.0 collective-permute-start.1
  19.7 1.0 collective-permute-done.1.refs_0_
  20.7 1.3 collective-permute-start.2
  22.0 1.4 collective-permute-start.3
  23.4 1.6 collective-permute-start.4
  25.6 0.8 collective-permute-done.2.refs_1_
  26.4 3.7 %collective-permute-done.4.refs_3_ = bf16[16,3584]{1,0:T(8,128)(2,1)S(1)} collective-permute-done((bf16[16,3584]{1,0:T(8,128)(2,1)S(1)}, bf16[16,3584]{1,0:T(8,128)(2,1)S(1)}, u32[]{:S(2)}, u32[]{:S(2)}) %collective-permute-start.4) | collective-permute-done | bytes 114720 | tf_op jit(solution)/shard_map/ppermute | solution.py:25
  30.8 1.9 join.1._
  32.8 1.2 collective-permute-start.10
  33.9 1.0 broadcast_in_dim.11
  34.9 6.9 %all-to-all-start.3 = ((bf16[8,16,3584]{2,1,0:T(8,128)(2,1)}), bf16[8,16,3584]{2,1,0:T(8,128)(2,1)S(1)}, u32[]{:S(2)}, u32[]{:S(2)}) async-start(bf16[8,16,3584]{2,1,0:T(8,128)(2,1)} %broadcast_in_dim.11), calls=%async_computation.3 | async-start | bytes 1835008 | tf_op jit(solution)/shard_map/all_to_all | solution.py:42
  41.8 7.2 %damp.1 = (bf16[2,1024,896]{2,1,0:T(8,128)(2,1)}, bf16[256,1024]{1,0:T(8,128)(2,1)}) custom-call(bf16[2,1024,896]{2,1,0:T(8,128)(2,1)} %queries.1, bf16[1024,896]{1,0:T(8,128)(2,1)} %eigenvalues.1, bf16[256,1024]{1,0:T(8,128)(2,1)} %basis.1, bf16[64,3584]{1,0:T(8,128)(2,1)} %join.1._), custom_call_target="tpu_custom_call" | custom-call | flops 3670016 | bytes 9175040 | tf_op jit(solution)/shard_map/damp/pallas_call | solution.py:104
  49.1 0.9 collective-permute-start.5
  50.0 1.8 collective-permute-start.6
  51.8 0.9 collective-permute-start
  52.8 1.2 collective-permute-done.other
  53.9 9.8 %collective-permute-done.5.second = bf16[256,1024]{1,0:T(8,128)(2,1)S(1)} collective-permute-done((bf16[256,1024]{1,0:T(8,128)(2,1)}, bf16[256,1024]{1,0:T(8,128)(2,1)S(1)}, u32[]{:S(2)}, u32[]{:S(2)}) %collective-permute-start.5) | collective-permute-done | bytes 524320 | tf_op jit(solution)/shard_map/ppermute | solution.py:25
  63.7 11.3 %collective-permute-done.7.fourth = bf16[256,1024]{1,0:T(8,128)(2,1)S(1)} collective-permute-done((bf16[256,1024]{1,0:T(8,128)(2,1)}, bf16[256,1024]{1,0:T(8,128)(2,1)S(1)}, u32[]{:S(2)}, u32[]{:S(2)}) %collective-permute-start.7) | collective-permute-done | bytes 524320 | tf_op jit(solution)/shard_map/ppermute | solution.py:25
  75.0 2.1 copy-done.2
  77.1 1.0 copy-done.5
  78.1 2.1 project.1
  80.3 6.3 %all-to-all-start.1 = ((bf16[8,2,16,1024]{3,2,1,0:T(8,128)(2,1)}), bf16[8,2,16,1024]{3,2,1,0:T(8,128)(2,1)S(1)}, u32[]{:S(2)}, u32[]{:S(2)}) async-start(bf16[8,2,16,1024]{3,2,1,0:T(8,128)(2,1)} %project.1), calls=%async_computation.1 | async-start | bytes 1048576 | tf_op jit(solution)/shard_map/all_to_all | solution.py:278
  87.2 2.0 collective-permute-start.12
  89.3 20.1 %all-to-all-done.1.refs_6_ = bf16[8,2,16,1024]{3,2,1,0:T(8,128)(2,1)S(1)} async-done(((bf16[8,2,16,1024]{3,2,1,0:T(8,128)(2,1)}), bf16[8,2,16,1024]{3,2,1,0:T(8,128)(2,1)S(1)}, u32[]{:S(2)}, u32[]{:S(2)}) %all-to-all-start.1) | async-done | bytes 524320 | tf_op jit(solution)/shard_map/all_to_all | solution.py:278
  109.4 2.3 %collective-permute-start.8 = (bf16[16,1024]{1,0:T(8,128)(2,1)S(1)}, bf16[16,1024]{1,0:T(8,128)(2,1)S(1)}, u32[]{:S(2)}, u32[]{:S(2)}) collective-permute-start(bf16[16,1024]{1,0:T(8,128)(2,1)S(1)} %get-tuple-element.12), channel_id=1, source_target_pairs={{0,1},{1,0},{2,3},{3,2},{4,5},{5,4},{6,7},{7,6},{8,9},{9,8},{10,11... | collective-permute-start | bytes 98312 | tf_op jit(solution)/shard_map/ppermute | solution.py:25
  111.7 0.9 collective-permute-done.8
  112.6 0.9 broadcast_in_dim.10.refs_6_
  113.4 4.2 %all-to-all-start.2 = ((bf16[8,16,2048]{2,1,0:T(8,128)(2,1)}), bf16[8,16,2048]{2,1,0:T(8,128)(2,1)}, u32[]{:S(2)}, u32[]{:S(2)}) async-start(bf16[8,16,2048]{2,1,0:T(8,128)(2,1)} %broadcast_in_dim.10.refs_6_), calls=%async_computation.2 | async-start | bytes 1048576 | tf_op jit(solution)/shard_map/all_to_all | solution.py:283
  117.7 0.8 slice.22
  119.2 1.8 slice.23
  121.0 2.0 collective-permute-start.14
  123.0 0.9 collective-permute-start.9
  123.9 11.7 %all-to-all-done.2 = bf16[8,16,2048]{2,1,0:T(8,128)(2,1)} async-done(((bf16[8,16,2048]{2,1,0:T(8,128)(2,1)}), bf16[8,16,2048]{2,1,0:T(8,128)(2,1)}, u32[]{:S(2)}, u32[]{:S(2)}) %all-to-all-start.2) | async-done | bytes 524320 | tf_op jit(solution)/shard_map/all_to_all | solution.py:283
  135.7 9.1 %rotate_y.1.refs_5_ = f32[512,896]{1,0:T(8,128)S(1)} custom-call(s32[2]{0:T(128)S(1)} %copy-done.6, bf16[8,16,3584]{2,1,0:T(8,128)(2,1)S(1)} %all-to-all-done.3.refs_0_, bf16[8,16,3584]{2,1,0:T(8,128)(2,1)S(1)} %bitcast.29, bf16[8,16,3584]{2,1,0:T(8,128)(2,1)} %bitcast.10.refs_2_, bf16[8,16,1792]{2,1,0:T(8,128)(2,1)S(1)} %bitcast.30, ...), custom_call_target="tpu_custom_call" | custom-call | flops 13153337344 | bytes 11010048 | tf_op jit(solution)/shard_map/rotate_y/pallas_call | solution.py:173
  144.9 9.3 %rotate_z.1.value = bf16[512,896]{1,0:T(8,128)(2,1)S(1)} custom-call(s32[2]{0:T(128)S(1)} %copy-done.6, bf16[8,4,16,3584]{3,2,1,0:T(8,128)(2,1)} %bitcast.36, bf16[8,4,16,3584]{3,2,1,0:T(8,128)(2,1)} %bitcast.37, bf16[8,4,16,3584]{3,2,1,0:T(8,128)(2,1)} %bitcast.38, bf16[8,4,16,3584]{3,2,1,0:T(8,128)(2,1)} %bitcast.39, ...), custom_call_target="tpu_custom_call" | custom-call | flops 13153337344 | bytes 11010048 | tf_op jit(solution)/shard_map/rotate_z/pallas_call | solution.py:173
  154.2 0.9 copy-done.1
  155.2 16.9 %all_to_all.35 = bf16[4,128,896]{2,1,0:T(8,128)(2,1)S(1)} all-to-all(bf16[4,128,896]{2,1,0:T(8,128)(2,1)} %bitcast.23), channel_id=1, replica_groups=mesh['y'=4,'z'=8,'x'=4,'c'=2] {'x'}, dimensions={0} | all-to-all | bytes 1835008 | tf_op jit(solution)/shard_map/all_to_all | solution.py:251
  172.2 1.0 broadcast_in_dim.12
  173.2 3.5 %all-to-all-start.5 = ((bf16[4,128,896]{2,1,0:T(8,128)(2,1)}), bf16[4,128,896]{2,1,0:T(8,128)(2,1)S(1)}, u32[]{:S(2)}, u32[]{:S(2)}) async-start(bf16[4,128,896]{2,1,0:T(8,128)(2,1)} %broadcast_in_dim.12), calls=%async_computation.5 | async-start | bytes 1835008 | tf_op jit(solution)/shard_map/all_to_all | solution.py:42
  176.9 0.9 reshape.69.ids
  177.8 10.7 %all-to-all-done.5 = bf16[4,128,896]{2,1,0:T(8,128)(2,1)S(1)} async-done(((bf16[4,128,896]{2,1,0:T(8,128)(2,1)}), bf16[4,128,896]{2,1,0:T(8,128)(2,1)S(1)}, u32[]{:S(2)}, u32[]{:S(2)}) %all-to-all-start.5) | async-done | bytes 917536 | tf_op jit(solution)/shard_map/all_to_all | solution.py:42
  188.5 0.9 copy-done.7
  189.4 8.3 %score.1 = f32[2,1,128]{2,1,0:T(1,128)} custom-call(bf16[512,2048]{1,0:T(8,128)(2,1)} %all-gather.3.cloned.1.call-done.grads, bf16[2,1024,896]{2,1,0:T(8,128)(2,1)} %get-tuple-element.8.precond.own, bf16[2,1024,896]{2,1,0:T(8,128)(2,1)} %collective-permute-done.9.other, bf16[512,896]{1,0:T(8,128)(2,1)} %bitcast.33, s32[512,1]{1,0:T(8,128)} %reshape.69.ids), custom_call_target="tpu_custom_call" | custom-call | flops 3758096384 | bytes 10354688 | tf_op jit(solution)/shard_map/score/pallas_call | solution.py:211
  198.6 22.6 %all_to_all.36 = f32[256,1,128]{2,1,0:T(1,128)S(1)} all-to-all(f32[256,1,128]{2,1,0:T(1,128)S(1)} %broadcast_in_dim.14), channel_id=1, replica_groups=mesh['y'=4,'z'=8,'x'=4,'c'=2] {'y','z','x','c'}, dimensions={0} | all-to-all | bytes 262144 | tf_op jit(solution)/shard_map/all_to_all | solution.py:42
  (56 shorter events, 5.0 us)
Async XLA Ops:
  6.5 1.0 copy-start
  8.6 21.5 %all-to-all-start = ((bf16[8,16,1024]{2,1,0:T(8,128)(2,1)}), bf16[8,16,1024]{2,1,0:T(8,128)(2,1)S(1)}, u32[]{:S(2)}, u32[]{:S(2)}) async-start(bf16[8,16,1024]{2,1,0:T(8,128)(2,1)} %reshape.55), calls=%async_computation | async-start | bytes 524288 | tf_op jit(solution)/shard_map/all_to_all | solution.py:269
  17.6 118.1 %all-gather.5.cloned.1.call-start = ((), (), s32[]{:S(2)}) async-start(), calls=%async_computation.8 | async-start | bytes 4128768 | tf_op jit(solution)/shard_map/all_gather | solution.py:271
  18.7 2.0 collective-permute-start.1
  20.7 9.4 %copy-start.8 = (bf16[16,3584]{1,0:T(8,128)(2,1)}, bf16[16,3584]{1,0:T(8,128)(2,1)S(1)}, u32[]{:S(2)}) copy-start(bf16[16,3584]{1,0:T(8,128)(2,1)S(1)} %collective-permute-done.1.refs_0_) | copy-start | bytes 344068
  20.7 5.7 %collective-permute-start.2 = (bf16[16,3584]{1,0:T(8,128)(2,1)S(1)}, bf16[16,3584]{1,0:T(8,128)(2,1)S(1)}, u32[]{:S(2)}, u32[]{:S(2)}) collective-permute-start(bf16[16,3584]{1,0:T(8,128)(2,1)S(1)} %collective-permute-done.1.refs_0_), channel_id=1, source_target_pairs={{0,64},{64,128},{128,192},{192,0},{1,65},{65,129},{129,193},{193,1... | collective-permute-start | bytes 344072 | tf_op jit(solution)/shard_map/ppermute | solution.py:25
  22.0 4.4 %collective-permute-start.3 = (bf16[16,3584]{1,0:T(8,128)(2,1)S(1)}, bf16[16,3584]{1,0:T(8,128)(2,1)S(1)}, u32[]{:S(2)}, u32[]{:S(2)}) collective-permute-start(bf16[16,3584]{1,0:T(8,128)(2,1)S(1)} %collective-permute-done.1.refs_0_), channel_id=1, source_target_pairs={{0,192},{64,0},{128,64},{192,128},{1,193},{65,1},{129,65},{193,129... | collective-permute-start | bytes 344072 | tf_op jit(solution)/shard_map/ppermute | solution.py:25
  23.4 6.7 %collective-permute-start.4 = (bf16[16,3584]{1,0:T(8,128)(2,1)S(1)}, bf16[16,3584]{1,0:T(8,128)(2,1)S(1)}, u32[]{:S(2)}, u32[]{:S(2)}) collective-permute-start(bf16[16,3584]{1,0:T(8,128)(2,1)S(1)} %collective-permute-done.1.refs_0_), channel_id=1, source_target_pairs={{0,128},{64,192},{128,0},{192,64},{1,129},{65,193},{129,1},{193,65... | collective-permute-start | bytes 344072 | tf_op jit(solution)/shard_map/ppermute | solution.py:25
  26.4 3.7 %copy-start.9 = (bf16[16,3584]{1,0:T(8,128)(2,1)}, bf16[16,3584]{1,0:T(8,128)(2,1)S(1)}, u32[]{:S(2)}) copy-start(bf16[16,3584]{1,0:T(8,128)(2,1)S(1)} %collective-permute-done.2.refs_1_) | copy-start | bytes 344068
  26.4 3.7 %copy-start.10 = (bf16[16,3584]{1,0:T(8,128)(2,1)}, bf16[16,3584]{1,0:T(8,128)(2,1)S(1)}, u32[]{:S(2)}) copy-start(bf16[16,3584]{1,0:T(8,128)(2,1)S(1)} %collective-permute-done.3.refs_2_) | copy-start | bytes 344068
  30.1 0.7 copy-start.11
  30.1 0.8 copy-start.3
  32.8 112.1 %collective-permute-start.10 = (bf16[3584,896]{1,0:T(8,128)(2,1)}, bf16[3584,896]{1,0:T(8,128)(2,1)}, u32[]{:S(2)}, u32[]{:S(2)}) collective-permute-start(bf16[3584,896]{1,0:T(8,128)(2,1)} %refs_5_.1), channel_id=1, source_target_pairs={{0,1},{1,0},{2,3},{3,2},{4,5},{5,4},{6,7},{7,6},{8,9},{9,8},{10,11... | collective-permute-start | bytes 19267592 | tf_op jit(solution)/shard_map/ppermute | solution.py:25
  34.9 45.3 %all-to-all-start.3 = ((bf16[8,16,3584]{2,1,0:T(8,128)(2,1)}), bf16[8,16,3584]{2,1,0:T(8,128)(2,1)S(1)}, u32[]{:S(2)}, u32[]{:S(2)}) async-start(bf16[8,16,3584]{2,1,0:T(8,128)(2,1)} %broadcast_in_dim.11), calls=%async_computation.3 | async-start | bytes 1835008 | tf_op jit(solution)/shard_map/all_to_all | solution.py:42
  41.8 10.0 %copy-start.4 = (bf16[8,16,1024]{2,1,0:T(8,128)(2,1)S(1)}, bf16[8,16,1024]{2,1,0:T(8,128)(2,1)}, u32[]{:S(2)}) copy-start(bf16[8,16,1024]{2,1,0:T(8,128)(2,1)} %copy-done.3) | copy-start | bytes 786436
  41.8 33.2 %copy-start.6 = (s32[2]{0:T(128)S(1)}, s32[2]{0:T(128)}, u32[]{:S(2)}) copy-start(s32[2]{0:T(128)} %pad_add_fusion.here) | copy-start | bytes 28
  49.1 14.7 %collective-permute-start.5 = (bf16[256,1024]{1,0:T(8,128)(2,1)}, bf16[256,1024]{1,0:T(8,128)(2,1)S(1)}, u32[]{:S(2)}, u32[]{:S(2)}) collective-permute-start(bf16[256,1024]{1,0:T(8,128)(2,1)} %get-tuple-element.7.first), channel_id=1, source_target_pairs={{0,64},{64,128},{128,192},{192,0},{1,65},{65,129},{129,193},{193,1... | collective-permute-start | bytes 1572872 | tf_op jit(solution)/shard_map/ppermute | solution.py:25
  50.0 13.8 %collective-permute-start.6 = (bf16[256,1024]{1,0:T(8,128)(2,1)}, bf16[256,1024]{1,0:T(8,128)(2,1)S(1)}, u32[]{:S(2)}, u32[]{:S(2)}) collective-permute-start(bf16[256,1024]{1,0:T(8,128)(2,1)} %get-tuple-element.7.first), channel_id=1, source_target_pairs={{0,192},{64,0},{128,64},{192,128},{1,193},{65,1},{129,65},{193,129... | collective-permute-start | bytes 1572872 | tf_op jit(solution)/shard_map/ppermute | solution.py:25
  51.7 23.3 %collective-permute-start.7 = (bf16[256,1024]{1,0:T(8,128)(2,1)}, bf16[256,1024]{1,0:T(8,128)(2,1)S(1)}, u32[]{:S(2)}, u32[]{:S(2)}) collective-permute-start(bf16[256,1024]{1,0:T(8,128)(2,1)} %get-tuple-element.7.first), channel_id=1, source_target_pairs={{0,128},{64,192},{128,0},{192,64},{1,129},{65,193},{129,1},{193,65... | collective-permute-start | bytes 1572872 | tf_op jit(solution)/shard_map/ppermute | solution.py:25
  51.8 2.1 collective-permute-start
  75.0 2.1 copy-start.2
  77.1 1.0 copy-start.5
  80.3 29.1 %all-to-all-start.1 = ((bf16[8,2,16,1024]{3,2,1,0:T(8,128)(2,1)}), bf16[8,2,16,1024]{3,2,1,0:T(8,128)(2,1)S(1)}, u32[]{:S(2)}, u32[]{:S(2)}) async-start(bf16[8,2,16,1024]{3,2,1,0:T(8,128)(2,1)} %project.1), calls=%async_computation.1 | async-start | bytes 1048576 | tf_op jit(solution)/shard_map/all_to_all | solution.py:278
  86.6 31.1 %collective-permute-start.11 = (bf16[128,3584]{1,0:T(8,128)(2,1)S(1)}, bf16[128,3584]{1,0:T(8,128)(2,1)S(1)}, u32[]{:S(2)}, u32[]{:S(2)}) collective-permute-start(bf16[128,3584]{1,0:T(8,128)(2,1)S(1)} %bitcast.27), channel_id=1, source_target_pairs={{0,64},{64,128},{128,192},{192,0},{1,65},{65,129},{129,193},{193,1... | collective-permute-start | bytes 2752520 | tf_op jit(solution)/shard_map/ppermute | solution.py:25
  87.2 32.0 %collective-permute-start.12 = (bf16[128,3584]{1,0:T(8,128)(2,1)S(1)}, bf16[128,3584]{1,0:T(8,128)(2,1)}, u32[]{:S(2)}, u32[]{:S(2)}) collective-permute-start(bf16[128,3584]{1,0:T(8,128)(2,1)S(1)} %bitcast.28), channel_id=1, source_target_pairs={{0,192},{64,0},{128,64},{192,128},{1,193},{65,1},{129,65},{193,129... | collective-permute-start | bytes 2752520 | tf_op jit(solution)/shard_map/ppermute | solution.py:25
  109.4 3.2 %collective-permute-start.8 = (bf16[16,1024]{1,0:T(8,128)(2,1)S(1)}, bf16[16,1024]{1,0:T(8,128)(2,1)S(1)}, u32[]{:S(2)}, u32[]{:S(2)}) collective-permute-start(bf16[16,1024]{1,0:T(8,128)(2,1)S(1)} %get-tuple-element.12), channel_id=1, source_target_pairs={{0,1},{1,0},{2,3},{3,2},{4,5},{5,4},{6,7},{7,6},{8,9},{9,8},{10,11... | collective-permute-start | bytes 98312 | tf_op jit(solution)/shard_map/ppermute | solution.py:25
  113.4 22.2 %all-to-all-start.2 = ((bf16[8,16,2048]{2,1,0:T(8,128)(2,1)}), bf16[8,16,2048]{2,1,0:T(8,128)(2,1)}, u32[]{:S(2)}, u32[]{:S(2)}) async-start(bf16[8,16,2048]{2,1,0:T(8,128)(2,1)} %broadcast_in_dim.10.refs_6_), calls=%async_computation.2 | async-start | bytes 1048576 | tf_op jit(solution)/shard_map/all_to_all | solution.py:283
  117.6 60.1 %all-gather.3.cloned.1.call-start = ((), (), s32[]{:S(2)}) async-start(), calls=%async_computation.7 | async-start | bytes 2621440 | tf_op jit(solution)/shard_map/all_gather | solution.py:287
  118.5 17.2 %collective-permute-start.13 = (bf16[128,1792]{1,0:T(8,128)(2,1)}, bf16[128,1792]{1,0:T(8,128)(2,1)S(1)}, u32[]{:S(2)}, u32[]{:S(2)}) collective-permute-start(bf16[128,1792]{1,0:T(8,128)(2,1)} %slice.22), channel_id=1, source_target_pairs={{0,64},{64,128},{128,192},{192,0},{1,65},{65,129},{129,193},{193,1... | collective-permute-start | bytes 1376264 | tf_op jit(solution)/shard_map/ppermute | solution.py:25
  121.0 14.6 %collective-permute-start.14 = (bf16[128,1792]{1,0:T(8,128)(2,1)}, bf16[128,1792]{1,0:T(8,128)(2,1)}, u32[]{:S(2)}, u32[]{:S(2)}) collective-permute-start(bf16[128,1792]{1,0:T(8,128)(2,1)} %slice.23), channel_id=1, source_target_pairs={{0,192},{64,0},{128,64},{192,128},{1,193},{65,1},{129,65},{193,129... | collective-permute-start | bytes 1376264 | tf_op jit(solution)/shard_map/ppermute | solution.py:25
  123.0 54.7 %collective-permute-start.9 = (bf16[2,1024,896]{2,1,0:T(8,128)(2,1)}, bf16[2,1024,896]{2,1,0:T(8,128)(2,1)}, u32[]{:S(2)}, u32[]{:S(2)}) collective-permute-start(bf16[2,1024,896]{2,1,0:T(8,128)(2,1)} %get-tuple-element.8.precond.own), channel_id=1, source_target_pairs={{0,1},{1,0},{2,3},{3,2},{4,5},{5,4},{6,7},{7,6},{8,9},{9,8},{10,11... | collective-permute-start | bytes 11010056 | tf_op jit(solution)/shard_map/ppermute | solution.py:25
  154.2 0.9 copy-start.1
  155.2 21.5 %copy-start.12 = (s32[1024]{0:T(1024)S(1)}, s32[1024]{0:T(1024)}, u32[]{:S(2)}) copy-start(s32[1024]{0:T(1024)} %param.13) | copy-start | bytes 12292
  173.2 15.3 %all-to-all-start.5 = ((bf16[4,128,896]{2,1,0:T(8,128)(2,1)}), bf16[4,128,896]{2,1,0:T(8,128)(2,1)S(1)}, u32[]{:S(2)}, u32[]{:S(2)}) async-start(bf16[4,128,896]{2,1,0:T(8,128)(2,1)} %broadcast_in_dim.12), calls=%async_computation.5 | async-start | bytes 1835008 | tf_op jit(solution)/shard_map/all_to_all | solution.py:42
  188.5 0.9 copy-start.7
Sparse Core Ops, SparseCore 0:
  32.9 78.8 all-gather.4
  135.8 28.6 all-gather.2

commit v7 on v5

--- a/solution.py
+++ b/solution.py
@@ -43,7 +43,8 @@
 
 
 def join_kernel(places, rows, here, *refs):
-    chunks, out = refs[: len(places)], refs[-1]
+    chunks, (basis, out, same) = refs[: len(places)], refs[len(places) :]
+    same[...] = basis[...]
     for back, chunk in zip(places, chunks):
         row = pl.multiple_of(lax.rem(here[0] + len(places) - back, len(places)) * rows, rows)
         out[pl.ds(row, rows), :] = chunk[...]
@@ -56,38 +57,40 @@
     return [value] + [shift(value, "y", back) for back in PLACES[1:]]
 
 
-def join(value, here):
+def join(value, basis, here):
     rows, cols = value.shape
     return pl.pallas_call(
         functools.partial(join_kernel, PLACES, rows),
-        out_shape=jax.ShapeDtypeStruct((4 * rows, cols), BF16),
-        in_specs=[pl.BlockSpec(memory_space=pltpu.SMEM)] + [pl.BlockSpec(memory_space=pltpu.VMEM)] * 4,
-        out_specs=pl.BlockSpec(memory_space=pltpu.VMEM),
+        out_shape=(jax.ShapeDtypeStruct((4 * rows, cols), BF16), jax.ShapeDtypeStruct(basis.shape, BF16)),
+        in_specs=[pl.BlockSpec(memory_space=pltpu.SMEM)] + [pl.BlockSpec(memory_space=pltpu.VMEM)] * 5,
+        out_specs=(pl.BlockSpec(memory_space=pltpu.VMEM), pl.BlockSpec(memory_space=pltpu.VMEM)),
         cost_estimate=pl.CostEstimate(flops=0, bytes_accessed=16 * rows * cols, transcendentals=0),
         name="join",
-    )(here, *direct(value))
-
-
-def project_kernel(here, own, other, first, second, third, fourth, precond, out):
+    )(here, *direct(value), basis)
+
+
+def project_kernel(here, own, other, first, second, third, left, right, out):
     for half, rows in enumerate((own, other)):
         total = 0.0
-        for back, basis in zip(PLACES, (first, second, third, fourth)):
+        for back, parts in ((0, (first,)), (1, (second,)), (3, (third,)), (2, (left, right))):
             slot = pl.multiple_of(lax.rem(here[0] + 4 - back, 4) * 256, 256)
-            total += jnp.dot(rows[:, pl.ds(slot, 256)], basis[...], preferred_element_type=F32)
+            part = rows[:, pl.ds(slot, 256)]
+            sums = [jnp.dot(part, basis[...], preferred_element_type=F32) for basis in parts]
+            total += sums[0] if len(sums) == 1 else jnp.concatenate(sums, axis=1)
         out[:, half] = total.astype(BF16).reshape(8, 16, 1024)
 
 
-def project(own, other, bases, precond, here):
+def project(own, other, bases, here):
     vmem = pl.BlockSpec(memory_space=pltpu.VMEM)
     return pl.pallas_call(
         project_kernel,
         out_shape=jax.ShapeDtypeStruct((8, 2, 16, 1024), BF16),
-        in_specs=[pl.BlockSpec(memory_space=pltpu.SMEM)] + [vmem] * 6 + [pl.BlockSpec(memory_space=pl.ANY)],
+        in_specs=[pl.BlockSpec(memory_space=pltpu.SMEM)] + [vmem] * 7,
         out_specs=vmem,
-        cost_estimate=pl.CostEstimate(flops=2**29, bytes_accessed=2**22, transcendentals=0),
+        cost_estimate=pl.CostEstimate(flops=50 * 2**29, bytes_accessed=2**22, transcendentals=0),
         compiler_params=pltpu.CompilerParams(vmem_limit_bytes=16 << 20),
         name="project",
-    )(here, own, other, *bases, precond)
+    )(here, own, other, *bases)
 
 
 def damp_kernel(queries, eigenvalues, _, out):
@@ -111,7 +114,7 @@
         cost_estimate=pl.CostEstimate(
             flops=2 * count * rows * cols, bytes_accessed=10 * rows * cols, transcendentals=0
         ),
-        compiler_params=pltpu.CompilerParams(vmem_limit_bytes=8 << 20),
+        compiler_params=pltpu.CompilerParams(vmem_limit_bytes=56 << 20),
         name="damp",
     )(queries, eigenvalues, ready)
 
@@ -177,7 +180,7 @@
             pltpu.SemaphoreType.DMA((steps,)),
         ],
         cost_estimate=pl.CostEstimate(
-            flops=(8 if axis == "y" else 4) * 2 * count * depth * cols,
+            flops=(4 if axis == "y" else 4) * 2 * count * depth * cols,
             bytes_accessed=2 * (count * depth + depth * cols + count * cols),
             transcendentals=0,
         ),
@@ -215,7 +218,7 @@
             bytes_accessed=2 * (2 * tokens * half + 2 * count * half * cols + tokens * cols),
             transcendentals=0,
         ),
-        compiler_params=pltpu.CompilerParams(vmem_limit_bytes=24 << 20),
+        compiler_params=pltpu.CompilerParams(vmem_limit_bytes=56 << 20),
         name="score",
     )(grads, own, other, acts, ids.reshape(tokens, 1))
 
@@ -254,9 +257,12 @@
     mine = lax.dynamic_slice_in_dim(activations, c * 16, 16)
     theirs = swap(lax.dynamic_slice_in_dim(activations, (1 - c) * 16, 16))
     extra = SPLIT - mine.shape[1]
-    low = first_low = join(theirs[:, extra:], here)
+    first_low, basis_out = join(theirs[:, extra:], basis_out, here)
+    low = first_low
     low = lax.all_gather(low, "z", axis=0, tiled=True).reshape(8, 4, 16, -1)
-    bases = direct(after(basis_out, first_low))
+    cut = basis_out.shape[1] // 2
+    bases = [basis_out, shift(basis_out, "y", 1), shift(basis_out, "y", -1)]
+    bases += [shift(basis_out[:, :cut], "y", 2), shift(basis_out[:, cut:], "y", -2)]
     precond = damp(queries, eigenvalues, first_low)
     rows = lax.dynamic_slice_in_dim(out_grads, c * 16, 16).reshape(16, 4, 8, 256)
     rows = rows.transpose(2, 0, 1, 3).reshape(8, 16, 1024)
@@ -267,7 +273,7 @@
     rows = sent[:, :, SPLIT:].reshape(128, -1)
     half = basis_in.shape[0]
     high_bases = ((basis_in, (0, half)), (other_in, (0, extra)))[: 1 + (extra > 0)]
-    parts = lax.all_to_all(project(rows, swap(rows), bases, precond, here), "z", 0, 0)
+    parts = lax.all_to_all(project(rows, swap(rows), bases, here), "z", 0, 0)
     partial_acts = rotate([(back, first, chunk.reshape(8, 16, -1)) for back, first, chunk in ring(high, "y")], "y", high_bases, here, F32, (parts, low))
     grads = jnp.sum(parts.astype(F32), axis=0).astype(BF16)
     grads = jnp.concatenate([grads[0], swap(grads[1])], axis=1)

time: 229 us -> 214 us (0.934)
  waiting for transfers between devices: 84 us -> 48.4 us
  starting transfers between devices: 38.4 us -> 52.8 us
  Pallas kernels: 31.2 us -> 38.4 us
  local copies, waits for them, and re-layouts: 20.5 us -> 16.3 us
  blocking collectives: 38.8 us -> 41.1 us
    all_to_all x1, waiting for transfers between devices: 39.6 us -> 9.5 us  [shards(): sent = lax.all_to_all(jnp.concatenate([copies, rows], axis=2), 'z', 0, 0)]
    ppermute x15 -> x16, starting transfers between devices: 19.1 us -> 29.3 us  [shift(): lax.ppermute(value, axis, [(i, (i + hops) % size) for i in range(size)])]
    all_to_all x1, waiting for transfers between devices: 11.7 us -> 3.62 us  [shards(): grads = lax.all_to_all(copies, 'z', 0, 0).reshape(128, 2048)]
    unnamed x32 -> x21, local copies, waits for them, and re-layouts: 11.3 us -> 4.66 us
    pallas_call x1, Pallas kernels: 1.68 us -> 7.03 us  [damp(): pl.pallas_call(damp_kernel, grid=(rows // 128,), out_shape=jax.ShapeDtype...]
    all_to_all x1, starting transfers between devices: 3.49 us -> 6.81 us  [shards(): parts = lax.all_to_all(project(rows, swap(rows), bases, here), 'z', 0, 0)]
    ppermute x15 -> x16, waiting for transfers between devices: 6.34 us -> 7.48 us  [shift(): lax.ppermute(value, axis, [(i, (i + hops) % size) for i in range(size)])]
  transfers between devices with their start and end apart: 21 -> 22, of which waited for: 9 -> 9; matrix products, arithmetic and copies ran while one was open for 4% -> 5% of each run, Pallas kernels for 10% -> 14%
where the time goes in v7:
time: 214 us; the launch traced here: 213 us
  starting transfers between devices  52.8 us (25%)
  waiting for transfers between devices  48.4 us (23%)
  blocking collectives  41.1 us (19%)
  Pallas kernels  38.4 us (18%)
  local copies, waits for them, and re-layouts  16.3 us (8%)
  between operations  13.6 us (6%)
    ppermute x16, starting transfers between devices, shift(): lax.ppermute(value, axis, [(i, (i + hops) % size) for i in range(size)])  29.3 us
    all_to_all x1, blocking collectives, spread(): lax.all_to_all(jnp.broadcast_to(value[None], (size,) + value.shape), axes...  24.3 us
    pallas_call x2, Pallas kernels, rotate(): pl.pallas_call(functools.partial(rotate_kernel, places, axis, spans, len(...  18.7 us
    all_to_all x1, waiting for transfers between devices, shards(): parts = lax.all_to_all(project(rows, swap(rows), bases, here), 'z', 0, 0)  17 us
    all_to_all x1, blocking collectives, over_x(): parts = lax.all_to_all(partial.reshape(4, rows // 4, cols), 'x', 0, 0)  16.8 us
    all_to_all x1, waiting for transfers between devices, spread(): lax.all_to_all(jnp.broadcast_to(value[None], (size,) + value.shape), axes...  10.7 us
    all_to_all x1, waiting for transfers between devices, shards(): sent = lax.all_to_all(jnp.concatenate([copies, rows], axis=2), 'z', 0, 0)  9.5 us
    all_to_all x1, starting transfers between devices, shards(): sent = lax.all_to_all(jnp.concatenate([copies, rows], axis=2), 'z', 0, 0)  9.01 us
  transfers between devices with their start and end apart: 22, of which 9 were waited for; matrix products, arithmetic and copies ran while one was open for 5% of the time, Pallas kernels for 14%

profile of v7, /device:TPU:1, one launch (start us, length us, event | category | flops | bytes accessed | tf_op | source)
XLA Modules:
  0.0 212.7 jit_solution(17341719848527326768)
XLA Ops:
  6.5 1.0 copy-done
  7.9 1.0 constant_dynamic-slice_fusion
  9.0 1.1 pad_maximum_fusion
  10.1 9.0 %all-to-all-start = ((bf16[8,16,4608]{2,1,0:T(8,128)(2,1)}), bf16[8,16,4608]{2,1,0:T(8,128)(2,1)}, u32[]{:S(2)}, u32[]{:S(2)}) async-start(bf16[8,16,4608]{2,1,0:T(8,128)(2,1)} %pad_maximum_fusion), calls=%async_computation | async-start | bytes 2359296 | tf_op jit(solution)/shard_map/all_to_all | solution.py:271
  19.2 1.0 collective-permute-start.1
  20.2 1.0 collective-permute-done.1.refs_0_
  21.2 1.3 collective-permute-start.2
  22.5 1.4 collective-permute-start.3
  23.9 1.6 collective-permute-start.4
  26.9 3.8 %collective-permute-done.4.refs_3_ = bf16[16,3584]{1,0:T(8,128)(2,1)S(1)} collective-permute-done((bf16[16,3584]{1,0:T(8,128)(2,1)S(1)}, bf16[16,3584]{1,0:T(8,128)(2,1)S(1)}, u32[]{:S(2)}, u32[]{:S(2)}) %collective-permute-start.4) | collective-permute-done | bytes 114720 | tf_op jit(solution)/shard_map/ppermute | solution.py:25
  31.4 2.3 %join.1 = (bf16[64,3584]{1,0:T(8,128)(2,1)}, bf16[256,1024]{1,0:T(8,128)(2,1)}) custom-call(s32[2]{0:T(128)} %pad_add_fusion.here, bf16[16,3584]{1,0:T(8,128)(2,1)} %copy-done.5, bf16[16,3584]{1,0:T(8,128)(2,1)} %copy-done.6, bf16[16,3584]{1,0:T(8,128)(2,1)} %copy-done.7, bf16[16,3584]{1,0:T(8,128)(2,1)} %copy-done.8, bf16[256,1024]{1,0:T(8,128)(2,1)} %refs_4_.1), custom_call_target="tpu_custom_call" | custom-call | bytes 917504 | tf_op jit(solution)/shard_map/join/pallas_call | solution.py:62
  34.2 1.1 fusion
  35.3 1.8 collective-permute-start.7
  37.0 0.7 collective-permute-start.6
  37.8 2.2 %collective-permute-start.11 = (bf16[3584,896]{1,0:T(8,128)(2,1)}, bf16[3584,896]{1,0:T(8,128)(2,1)}, u32[]{:S(2)}, u32[]{:S(2)}) collective-permute-start(bf16[3584,896]{1,0:T(8,128)(2,1)} %refs_5_.1), channel_id=1, source_target_pairs={{0,1},{1,0},{2,3},{3,2},{4,5},{5,4},{6,7},{7,6},{8,9},{9,8},{10,11... | collective-permute-start | bytes 19267592 | tf_op jit(solution)/shard_map/ppermute | solution.py:25
  39.9 1.8 collective-permute-start.8
  41.8 9.5 %all-to-all-done = bf16[8,16,4608]{2,1,0:T(8,128)(2,1)} async-done(((bf16[8,16,4608]{2,1,0:T(8,128)(2,1)}), bf16[8,16,4608]{2,1,0:T(8,128)(2,1)}, u32[]{:S(2)}, u32[]{:S(2)}) %all-to-all-start) | async-done | bytes 1179680 | tf_op jit(solution)/shard_map/all_to_all | solution.py:271
  51.3 1.0 slice.36
  52.3 5.1 %collective-permute-start = (bf16[128,1024]{1,0:T(8,128)(2,1)S(1)}, bf16[128,1024]{1,0:T(8,128)(2,1)S(1)}, u32[]{:S(2)}, u32[]{:S(2)}) collective-permute-start(bf16[128,1024]{1,0:T(8,128)(2,1)S(1)} %bitcast.26), channel_id=1, source_target_pairs={{0,1},{1,0},{2,3},{3,2},{4,5},{5,4},{6,7},{7,6},{8,9},{9,8},{10,11... | collective-permute-start | bytes 786440 | tf_op jit(solution)/shard_map/ppermute | solution.py:25
  57.4 1.1 collective-permute-done.other
  58.6 1.0 copy-done.2
  59.6 2.1 project.1
  61.7 6.8 %all-to-all-start.1 = ((bf16[8,2,16,1024]{3,2,1,0:T(8,128)(2,1)}), bf16[8,2,16,1024]{3,2,1,0:T(8,128)(2,1)S(1)}, u32[]{:S(2)}, u32[]{:S(2)}) async-start(bf16[8,2,16,1024]{3,2,1,0:T(8,128)(2,1)} %project.1), calls=%async_computation.1 | async-start | bytes 1048576 | tf_op jit(solution)/shard_map/all_to_all | solution.py:276
  68.5 1.2 slice.39.refs_0_
  69.7 1.6 collective-permute-start.12
  71.3 2.6 %collective-permute-start.13 = (bf16[128,3584]{1,0:T(8,128)(2,1)S(1)}, bf16[128,3584]{1,0:T(8,128)(2,1)}, u32[]{:S(2)}, u32[]{:S(2)}) collective-permute-start(bf16[128,3584]{1,0:T(8,128)(2,1)S(1)} %bitcast.25), channel_id=1, source_target_pairs={{0,192},{64,0},{128,64},{192,128},{1,193},{65,1},{129,65},{193,129... | collective-permute-start | bytes 2752520 | tf_op jit(solution)/shard_map/ppermute | solution.py:25
  74.0 17.0 %all-to-all-done.1.refs_6_ = bf16[8,2,16,1024]{3,2,1,0:T(8,128)(2,1)S(1)} async-done(((bf16[8,2,16,1024]{3,2,1,0:T(8,128)(2,1)}), bf16[8,2,16,1024]{3,2,1,0:T(8,128)(2,1)S(1)}, u32[]{:S(2)}, u32[]{:S(2)}) %all-to-all-start.1) | async-done | bytes 524320 | tf_op jit(solution)/shard_map/all_to_all | solution.py:276
  91.0 2.9 %collective-permute-start.9 = (bf16[16,1024]{1,0:T(8,128)(2,1)S(1)}, bf16[16,1024]{1,0:T(8,128)(2,1)S(1)}, u32[]{:S(2)}, u32[]{:S(2)}) collective-permute-start(bf16[16,1024]{1,0:T(8,128)(2,1)S(1)} %get-tuple-element.14), channel_id=1, source_target_pairs={{0,1},{1,0},{2,3},{3,2},{4,5},{5,4},{6,7},{7,6},{8,9},{9,8},{10,11... | collective-permute-start | bytes 98312 | tf_op jit(solution)/shard_map/ppermute | solution.py:25
  93.9 0.9 collective-permute-done.9
  94.8 0.9 broadcast_in_dim.11.refs_6_
  95.6 4.1 %all-to-all-start.2 = ((bf16[8,16,2048]{2,1,0:T(8,128)(2,1)}), bf16[8,16,2048]{2,1,0:T(8,128)(2,1)}, u32[]{:S(2)}, u32[]{:S(2)}) async-start(bf16[8,16,2048]{2,1,0:T(8,128)(2,1)} %broadcast_in_dim.11.refs_6_), calls=%async_computation.2 | async-start | bytes 1048576 | tf_op jit(solution)/shard_map/all_to_all | solution.py:281
  99.8 0.8 slice.40
  100.6 1.6 collective-permute-start.14
  102.2 1.8 slice.41
  104.1 2.4 %collective-permute-start.15 = (bf16[128,1792]{1,0:T(8,128)(2,1)}, bf16[128,1792]{1,0:T(8,128)(2,1)}, u32[]{:S(2)}, u32[]{:S(2)}) collective-permute-start(bf16[128,1792]{1,0:T(8,128)(2,1)} %slice.41), channel_id=1, source_target_pairs={{0,192},{64,0},{128,64},{192,128},{1,193},{65,1},{129,65},{193,129... | collective-permute-start | bytes 1376264 | tf_op jit(solution)/shard_map/ppermute | solution.py:25
  106.5 7.0 %damp.1.own = bf16[2,1024,896]{2,1,0:T(8,128)(2,1)} custom-call(bf16[2,1024,896]{2,1,0:T(8,128)(2,1)} %queries.1, bf16[1024,896]{1,0:T(8,128)(2,1)} %eigenvalues.1, bf16[64,3584]{1,0:T(8,128)(2,1)} %get-tuple-element.8._), custom_call_target="tpu_custom_call" | custom-call | flops 3670016 | bytes 9175040 | tf_op jit(solution)/shard_map/damp/pallas_call | solution.py:104
  114.2 3.6 %all-to-all-done.2 = bf16[8,16,2048]{2,1,0:T(8,128)(2,1)} async-done(((bf16[8,16,2048]{2,1,0:T(8,128)(2,1)}), bf16[8,16,2048]{2,1,0:T(8,128)(2,1)}, u32[]{:S(2)}, u32[]{:S(2)}) %all-to-all-start.2) | async-done | bytes 524320 | tf_op jit(solution)/shard_map/all_to_all | solution.py:281
  117.9 9.1 %rotate_y.1.refs_5_ = f32[512,896]{1,0:T(8,128)S(1)} custom-call(s32[2]{0:T(128)S(1)} %copy-done.3, bf16[8,16,3584]{2,1,0:T(8,128)(2,1)S(1)} %slice.39.refs_0_, bf16[8,16,3584]{2,1,0:T(8,128)(2,1)S(1)} %bitcast.28, bf16[8,16,3584]{2,1,0:T(8,128)(2,1)} %bitcast.10.refs_2_, bf16[8,16,1792]{2,1,0:T(8,128)(2,1)S(1)} %bitcast.29, ...), custom_call_target="tpu_custom_call" | custom-call | flops 13153337344 | bytes 11010048 | tf_op jit(solution)/shard_map/rotate_y/pallas_call | solution.py:166
  127.0 9.5 %rotate_z.1.value = bf16[512,896]{1,0:T(8,128)(2,1)S(1)} custom-call(s32[2]{0:T(128)S(1)} %copy-done.3, bf16[8,4,16,3584]{3,2,1,0:T(8,128)(2,1)} %bitcast.35, bf16[8,4,16,3584]{3,2,1,0:T(8,128)(2,1)} %bitcast.36, bf16[8,4,16,3584]{3,2,1,0:T(8,128)(2,1)} %bitcast.37, bf16[8,4,16,3584]{3,2,1,0:T(8,128)(2,1)} %bitcast.38, ...), custom_call_target="tpu_custom_call" | custom-call | flops 13153337344 | bytes 11010048 | tf_op jit(solution)/shard_map/rotate_z/pallas_call | solution.py:166
  136.6 0.9 copy-done.1
  137.5 16.8 %all_to_all.30 = bf16[4,128,896]{2,1,0:T(8,128)(2,1)S(1)} all-to-all(bf16[4,128,896]{2,1,0:T(8,128)(2,1)} %bitcast.23), channel_id=1, replica_groups=mesh['y'=4,'z'=8,'x'=4,'c'=2] {'x'}, dimensions={0} | all-to-all | bytes 1835008 | tf_op jit(solution)/shard_map/all_to_all | solution.py:244
  154.4 1.0 broadcast_in_dim.12
  155.4 3.5 %all-to-all-start.4 = ((bf16[4,128,896]{2,1,0:T(8,128)(2,1)}), bf16[4,128,896]{2,1,0:T(8,128)(2,1)S(1)}, u32[]{:S(2)}, u32[]{:S(2)}) async-start(bf16[4,128,896]{2,1,0:T(8,128)(2,1)} %broadcast_in_dim.12), calls=%async_computation.4 | async-start | bytes 1835008 | tf_op jit(solution)/shard_map/all_to_all | solution.py:42
  159.1 0.9 reshape.69.ids
  160.0 10.7 %all-to-all-done.4 = bf16[4,128,896]{2,1,0:T(8,128)(2,1)S(1)} async-done(((bf16[4,128,896]{2,1,0:T(8,128)(2,1)}), bf16[4,128,896]{2,1,0:T(8,128)(2,1)S(1)}, u32[]{:S(2)}, u32[]{:S(2)}) %all-to-all-start.4) | async-done | bytes 917536 | tf_op jit(solution)/shard_map/all_to_all | solution.py:42
  170.7 0.9 copy-done.4
  171.7 8.3 %score.1 = f32[2,1,128]{2,1,0:T(1,128)} custom-call(bf16[512,2048]{1,0:T(8,128)(2,1)} %all-gather.3.cloned.1.call-done.grads, bf16[2,1024,896]{2,1,0:T(8,128)(2,1)} %damp.1.own, bf16[2,1024,896]{2,1,0:T(8,128)(2,1)} %collective-permute-done.10.other, bf16[512,896]{1,0:T(8,128)(2,1)} %bitcast.32, s32[512,1]{1,0:T(8,128)} %reshape.69.ids), custom_call_target="tpu_custom_call" | custom-call | flops 3758096384 | bytes 10354688 | tf_op jit(solution)/shard_map/score/pallas_call | solution.py:204
  180.8 24.3 %all_to_all.31 = f32[256,1,128]{2,1,0:T(1,128)S(1)} all-to-all(f32[256,1,128]{2,1,0:T(1,128)S(1)} %broadcast_in_dim.14), channel_id=1, replica_groups=mesh['y'=4,'z'=8,'x'=4,'c'=2] {'y','z','x','c'}, dimensions={0} | all-to-all | bytes 262144 | tf_op jit(solution)/shard_map/all_to_all | solution.py:42
  (54 shorter events, 5.6 us)
Async XLA Ops:
  6.5 1.0 copy-start
  10.1 41.2 %all-to-all-start = ((bf16[8,16,4608]{2,1,0:T(8,128)(2,1)}), bf16[8,16,4608]{2,1,0:T(8,128)(2,1)}, u32[]{:S(2)}, u32[]{:S(2)}) async-start(bf16[8,16,4608]{2,1,0:T(8,128)(2,1)} %pad_maximum_fusion), calls=%async_computation | async-start | bytes 2359296 | tf_op jit(solution)/shard_map/all_to_all | solution.py:271
  19.1 98.7 %all-gather.5.cloned.1.call-start = ((), (), s32[]{:S(2)}) async-start(), calls=%async_computation.7 | async-start | bytes 4128768 | tf_op jit(solution)/shard_map/all_gather | solution.py:262
  19.2 2.0 collective-permute-start.1
  21.2 9.5 %copy-start.5 = (bf16[16,3584]{1,0:T(8,128)(2,1)}, bf16[16,3584]{1,0:T(8,128)(2,1)S(1)}, u32[]{:S(2)}) copy-start(bf16[16,3584]{1,0:T(8,128)(2,1)S(1)} %collective-permute-done.1.refs_0_) | copy-start | bytes 344068
  21.2 5.7 %collective-permute-start.2 = (bf16[16,3584]{1,0:T(8,128)(2,1)S(1)}, bf16[16,3584]{1,0:T(8,128)(2,1)S(1)}, u32[]{:S(2)}, u32[]{:S(2)}) collective-permute-start(bf16[16,3584]{1,0:T(8,128)(2,1)S(1)} %collective-permute-done.1.refs_0_), channel_id=1, source_target_pairs={{0,64},{64,128},{128,192},{192,0},{1,65},{65,129},{129,193},{193,1... | collective-permute-start | bytes 344072 | tf_op jit(solution)/shard_map/ppermute | solution.py:25
  22.5 4.4 %collective-permute-start.3 = (bf16[16,3584]{1,0:T(8,128)(2,1)S(1)}, bf16[16,3584]{1,0:T(8,128)(2,1)S(1)}, u32[]{:S(2)}, u32[]{:S(2)}) collective-permute-start(bf16[16,3584]{1,0:T(8,128)(2,1)S(1)} %collective-permute-done.1.refs_0_), channel_id=1, source_target_pairs={{0,192},{64,0},{128,64},{192,128},{1,193},{65,1},{129,65},{193,129... | collective-permute-start | bytes 344072 | tf_op jit(solution)/shard_map/ppermute | solution.py:25
  23.9 6.8 %collective-permute-start.4 = (bf16[16,3584]{1,0:T(8,128)(2,1)S(1)}, bf16[16,3584]{1,0:T(8,128)(2,1)S(1)}, u32[]{:S(2)}, u32[]{:S(2)}) collective-permute-start(bf16[16,3584]{1,0:T(8,128)(2,1)S(1)} %collective-permute-done.1.refs_0_), channel_id=1, source_target_pairs={{0,128},{64,192},{128,0},{192,64},{1,129},{65,193},{129,1},{193,65... | collective-permute-start | bytes 344072 | tf_op jit(solution)/shard_map/ppermute | solution.py:25
  26.2 32.3 %copy-start.3 = (s32[2]{0:T(128)S(1)}, s32[2]{0:T(128)}, u32[]{:S(2)}) copy-start(s32[2]{0:T(128)} %pad_add_fusion.here) | copy-start | bytes 28
  26.9 3.8 %copy-start.6 = (bf16[16,3584]{1,0:T(8,128)(2,1)}, bf16[16,3584]{1,0:T(8,128)(2,1)S(1)}, u32[]{:S(2)}) copy-start(bf16[16,3584]{1,0:T(8,128)(2,1)S(1)} %collective-permute-done.2.refs_1_) | copy-start | bytes 344068
  26.9 3.8 %copy-start.7 = (bf16[16,3584]{1,0:T(8,128)(2,1)}, bf16[16,3584]{1,0:T(8,128)(2,1)S(1)}, u32[]{:S(2)}) copy-start(bf16[16,3584]{1,0:T(8,128)(2,1)S(1)} %collective-permute-done.3.refs_2_) | copy-start | bytes 344068
  30.7 0.7 copy-start.8
  33.7 23.7 %collective-permute-start.5 = (bf16[256,1024]{1,0:T(8,128)(2,1)}, bf16[256,1024]{1,0:T(8,128)(2,1)S(1)}, u32[]{:S(2)}, u32[]{:S(2)}) collective-permute-start(bf16[256,1024]{1,0:T(8,128)(2,1)} %get-tuple-element.7.first), channel_id=1, source_target_pairs={{0,64},{64,128},{128,192},{192,0},{1,65},{65,129},{129,193},{193,1... | collective-permute-start | bytes 1572872 | tf_op jit(solution)/shard_map/ppermute | solution.py:25
  35.3 17.0 %collective-permute-start.7 = (bf16[256,512]{1,0:T(8,128)(2,1)S(1)}, bf16[256,512]{1,0:T(8,128)(2,1)S(1)}, u32[]{:S(2)}, u32[]{:S(2)}) collective-permute-start(bf16[256,512]{1,0:T(8,128)(2,1)S(1)} %get-tuple-element.10), channel_id=1, source_target_pairs={{0,128},{64,192},{128,0},{192,64},{1,129},{65,193},{129,1},{193,65... | collective-permute-start | bytes 786440 | tf_op jit(solution)/shard_map/ppermute | solution.py:25
  37.0 20.3 %collective-permute-start.6 = (bf16[256,1024]{1,0:T(8,128)(2,1)}, bf16[256,1024]{1,0:T(8,128)(2,1)S(1)}, u32[]{:S(2)}, u32[]{:S(2)}) collective-permute-start(bf16[256,1024]{1,0:T(8,128)(2,1)} %get-tuple-element.7.first), channel_id=1, source_target_pairs={{0,192},{64,0},{128,64},{192,128},{1,193},{65,1},{129,65},{193,129... | collective-permute-start | bytes 1572872 | tf_op jit(solution)/shard_map/ppermute | solution.py:25
  37.8 89.3 %collective-permute-start.11 = (bf16[3584,896]{1,0:T(8,128)(2,1)}, bf16[3584,896]{1,0:T(8,128)(2,1)}, u32[]{:S(2)}, u32[]{:S(2)}) collective-permute-start(bf16[3584,896]{1,0:T(8,128)(2,1)} %refs_5_.1), channel_id=1, source_target_pairs={{0,1},{1,0},{2,3},{3,2},{4,5},{5,4},{6,7},{7,6},{8,9},{9,8},{10,11... | collective-permute-start | bytes 19267592 | tf_op jit(solution)/shard_map/ppermute | solution.py:25
  39.9 17.4 %collective-permute-start.8 = (bf16[256,512]{1,0:T(8,128)(2,1)S(1)}, bf16[256,512]{1,0:T(8,128)(2,1)S(1)}, u32[]{:S(2)}, u32[]{:S(2)}) collective-permute-start(bf16[256,512]{1,0:T(8,128)(2,1)S(1)} %get-tuple-element.9), channel_id=1, source_target_pairs={{0,128},{64,192},{128,0},{192,64},{1,129},{65,193},{129,1},{193,65... | collective-permute-start | bytes 786440 | tf_op jit(solution)/shard_map/ppermute | solution.py:25
  52.3 6.3 %collective-permute-start = (bf16[128,1024]{1,0:T(8,128)(2,1)S(1)}, bf16[128,1024]{1,0:T(8,128)(2,1)S(1)}, u32[]{:S(2)}, u32[]{:S(2)}) collective-permute-start(bf16[128,1024]{1,0:T(8,128)(2,1)S(1)} %bitcast.26), channel_id=1, source_target_pairs={{0,1},{1,0},{2,3},{3,2},{4,5},{5,4},{6,7},{7,6},{8,9},{9,8},{10,11... | collective-permute-start | bytes 786440 | tf_op jit(solution)/shard_map/ppermute | solution.py:25
  58.5 1.0 copy-start.2
  61.7 29.3 %all-to-all-start.1 = ((bf16[8,2,16,1024]{3,2,1,0:T(8,128)(2,1)}), bf16[8,2,16,1024]{3,2,1,0:T(8,128)(2,1)S(1)}, u32[]{:S(2)}, u32[]{:S(2)}) async-start(bf16[8,2,16,1024]{3,2,1,0:T(8,128)(2,1)} %project.1), calls=%async_computation.1 | async-start | bytes 1048576 | tf_op jit(solution)/shard_map/all_to_all | solution.py:276
  69.7 30.1 %collective-permute-start.12 = (bf16[128,3584]{1,0:T(8,128)(2,1)S(1)}, bf16[128,3584]{1,0:T(8,128)(2,1)S(1)}, u32[]{:S(2)}, u32[]{:S(2)}) collective-permute-start(bf16[128,3584]{1,0:T(8,128)(2,1)S(1)} %bitcast.24), channel_id=1, source_target_pairs={{0,64},{64,128},{128,192},{192,0},{1,65},{65,129},{129,193},{193,1... | collective-permute-start | bytes 2752520 | tf_op jit(solution)/shard_map/ppermute | solution.py:25
  71.3 30.9 %collective-permute-start.13 = (bf16[128,3584]{1,0:T(8,128)(2,1)S(1)}, bf16[128,3584]{1,0:T(8,128)(2,1)}, u32[]{:S(2)}, u32[]{:S(2)}) collective-permute-start(bf16[128,3584]{1,0:T(8,128)(2,1)S(1)} %bitcast.25), channel_id=1, source_target_pairs={{0,192},{64,0},{128,64},{192,128},{1,193},{65,1},{129,65},{193,129... | collective-permute-start | bytes 2752520 | tf_op jit(solution)/shard_map/ppermute | solution.py:25
  91.0 3.7 %collective-permute-start.9 = (bf16[16,1024]{1,0:T(8,128)(2,1)S(1)}, bf16[16,1024]{1,0:T(8,128)(2,1)S(1)}, u32[]{:S(2)}, u32[]{:S(2)}) collective-permute-start(bf16[16,1024]{1,0:T(8,128)(2,1)S(1)} %get-tuple-element.14), channel_id=1, source_target_pairs={{0,1},{1,0},{2,3},{3,2},{4,5},{5,4},{6,7},{7,6},{8,9},{9,8},{10,11... | collective-permute-start | bytes 98312 | tf_op jit(solution)/shard_map/ppermute | solution.py:25
  95.6 22.2 %all-to-all-start.2 = ((bf16[8,16,2048]{2,1,0:T(8,128)(2,1)}), bf16[8,16,2048]{2,1,0:T(8,128)(2,1)}, u32[]{:S(2)}, u32[]{:S(2)}) async-start(bf16[8,16,2048]{2,1,0:T(8,128)(2,1)} %broadcast_in_dim.11.refs_6_), calls=%async_computation.2 | async-start | bytes 1048576 | tf_op jit(solution)/shard_map/all_to_all | solution.py:281
  99.8 60.2 %all-gather.3.cloned.1.call-start = ((), (), s32[]{:S(2)}) async-start(), calls=%async_computation.6 | async-start | bytes 2621440 | tf_op jit(solution)/shard_map/all_gather | solution.py:285
  100.6 17.2 %collective-permute-start.14 = (bf16[128,1792]{1,0:T(8,128)(2,1)}, bf16[128,1792]{1,0:T(8,128)(2,1)S(1)}, u32[]{:S(2)}, u32[]{:S(2)}) collective-permute-start(bf16[128,1792]{1,0:T(8,128)(2,1)} %slice.40), channel_id=1, source_target_pairs={{0,64},{64,128},{128,192},{192,0},{1,65},{65,129},{129,193},{193,1... | collective-permute-start | bytes 1376264 | tf_op jit(solution)/shard_map/ppermute | solution.py:25
  104.1 13.7 %collective-permute-start.15 = (bf16[128,1792]{1,0:T(8,128)(2,1)}, bf16[128,1792]{1,0:T(8,128)(2,1)}, u32[]{:S(2)}, u32[]{:S(2)}) collective-permute-start(bf16[128,1792]{1,0:T(8,128)(2,1)} %slice.41), channel_id=1, source_target_pairs={{0,192},{64,0},{128,64},{192,128},{1,193},{65,1},{129,65},{193,129... | collective-permute-start | bytes 1376264 | tf_op jit(solution)/shard_map/ppermute | solution.py:25
  113.5 46.5 %collective-permute-start.10 = (bf16[2,1024,896]{2,1,0:T(8,128)(2,1)}, bf16[2,1024,896]{2,1,0:T(8,128)(2,1)}, u32[]{:S(2)}, u32[]{:S(2)}) collective-permute-start(bf16[2,1024,896]{2,1,0:T(8,128)(2,1)} %damp.1.own), channel_id=1, source_target_pairs={{0,1},{1,0},{2,3},{3,2},{4,5},{5,4},{6,7},{7,6},{8,9},{9,8},{10,11... | collective-permute-start | bytes 11010056 | tf_op jit(solution)/shard_map/ppermute | solution.py:25
  136.6 0.9 copy-start.1
  154.3 4.7 %copy-start.9 = (s32[1024]{0:T(1024)S(1)}, s32[1024]{0:T(1024)}, u32[]{:S(2)}) copy-start(s32[1024]{0:T(1024)} %param.13) | copy-start | bytes 12292
  155.4 15.3 %all-to-all-start.4 = ((bf16[4,128,896]{2,1,0:T(8,128)(2,1)}), bf16[4,128,896]{2,1,0:T(8,128)(2,1)S(1)}, u32[]{:S(2)}, u32[]{:S(2)}) async-start(bf16[4,128,896]{2,1,0:T(8,128)(2,1)} %broadcast_in_dim.12), calls=%async_computation.4 | async-start | bytes 1835008 | tf_op jit(solution)/shard_map/all_to_all | solution.py:42
  170.7 0.9 copy-start.4
Sparse Core Ops, SparseCore 0:
  33.8 62.4 all-gather.4
  117.9 30.6 all-gather.2

commit v8 on v7

--- a/solution.py
+++ b/solution.py
@@ -87,7 +87,7 @@
         out_shape=jax.ShapeDtypeStruct((8, 2, 16, 1024), BF16),
         in_specs=[pl.BlockSpec(memory_space=pltpu.SMEM)] + [vmem] * 7,
         out_specs=vmem,
-        cost_estimate=pl.CostEstimate(flops=50 * 2**29, bytes_accessed=2**22, transcendentals=0),
+        cost_estimate=pl.CostEstimate(flops=75 * 2**29, bytes_accessed=2**22, transcendentals=0),
         compiler_params=pltpu.CompilerParams(vmem_limit_bytes=16 << 20),
         name="project",
     )(here, own, other, *bases)
@@ -281,7 +281,8 @@
     grads = lax.all_to_all(copies, "z", 0, 0).reshape(128, 2048)
     low_bases = ((other_in, (extra, half)),)
     partial_acts = rotate([(y, 0, low) for y in range(4)], "z", low_bases, here, BF16, (copies,), (partial_acts,))
-    rot_acts = over_x(after(partial_acts, grads))
+    grads = after(grads, partial_acts)
+    rot_acts = over_x(partial_acts)
     rot_grads = lax.all_gather(grads, "y", axis=0, tiled=True)
     ids = lax.dynamic_index_in_dim(doc_ids.reshape(32, 2, 16), c, 1, keepdims=False)
     docs = score(rot_grads, precond, swap(precond), rot_acts, ids)

time: 214 us -> 208 us (0.972)
  starting transfers between devices: 52.8 us -> 47.3 us
  waiting for transfers between devices: 48.4 us -> 44.4 us
  local copies, waits for them, and re-layouts: 16.3 us -> 19.8 us
    all_to_all x1, waiting for transfers between devices: 17 us -> 9.15 us  [shards(): parts = lax.all_to_all(project(rows, swap(rows), bases, here), 'z', 0, 0)]
    ppermute x16, waiting for transfers between devices: 7.48 us -> 13.8 us  [shift(): lax.ppermute(value, axis, [(i, (i + hops) % size) for i in range(size)])]
    ppermute x16, starting transfers between devices: 29.3 us -> 23.7 us  [shift(): lax.ppermute(value, axis, [(i, (i + hops) % size) for i in range(size)])]
    all_to_all x1, waiting for transfers between devices: 3.62 us -> 0.01 us  [shards(): grads = lax.all_to_all(copies, 'z', 0, 0).reshape(128, 2048)]
    unnamed x21 -> x31, local copies, waits for them, and re-layouts: 4.66 us -> 8.09 us
  transfers between devices with their start and end apart: 22 -> 22, of which waited for: 9 -> 7; matrix products, arithmetic and copies ran while one was open for 5% -> 5% of each run, Pallas kernels for 14% -> 15%
where the time goes in v8:
time: 208 us; the launch traced here: 207 us
  starting transfers between devices  47.3 us (23%)
  waiting for transfers between devices  44.4 us (21%)
  blocking collectives  40.8 us (20%)
  Pallas kernels  38.7 us (19%)
  local copies, waits for them, and re-layouts  19.8 us (10%)
  between operations  13.7 us (7%)
    all_to_all x1, blocking collectives, spread(): lax.all_to_all(jnp.broadcast_to(value[None], (size,) + value.shape), axes...  24.3 us
    ppermute x16, starting transfers between devices, shift(): lax.ppermute(value, axis, [(i, (i + hops) % size) for i in range(size)])  23.7 us
    pallas_call x2, Pallas kernels, rotate(): pl.pallas_call(functools.partial(rotate_kernel, places, axis, spans, len(...  18.5 us
    all_to_all x1, blocking collectives, over_x(): parts = lax.all_to_all(partial.reshape(4, rows // 4, cols), 'x', 0, 0)  16.5 us
    ppermute x16, waiting for transfers between devices, shift(): lax.ppermute(value, axis, [(i, (i + hops) % size) for i in range(size)])  13.8 us
    all_to_all x1, waiting for transfers between devices, shards(): sent = lax.all_to_all(jnp.concatenate([copies, rows], axis=2), 'z', 0, 0)  10.8 us
    all_to_all x1, waiting for transfers between devices, spread(): lax.all_to_all(jnp.broadcast_to(value[None], (size,) + value.shape), axes...  10.7 us
    all_to_all x1, waiting for transfers between devices, shards(): parts = lax.all_to_all(project(rows, swap(rows), bases, here), 'z', 0, 0)  9.15 us
  transfers between devices with their start and end apart: 22, of which 7 were waited for; matrix products, arithmetic and copies ran while one was open for 5% of the time, Pallas kernels for 15%

profile of v8, /device:TPU:1, one launch (start us, length us, event | category | flops | bytes accessed | tf_op | source)
XLA Modules:
  0.0 206.6 jit_solution(14651140881041336833)
XLA Ops:
  6.5 1.0 copy-done
  7.9 1.0 constant_dynamic-slice_fusion
  9.0 1.1 pad_maximum_fusion
  10.1 9.0 %all-to-all-start = ((bf16[8,16,4608]{2,1,0:T(8,128)(2,1)}), bf16[8,16,4608]{2,1,0:T(8,128)(2,1)}, u32[]{:S(2)}, u32[]{:S(2)}) async-start(bf16[8,16,4608]{2,1,0:T(8,128)(2,1)} %pad_maximum_fusion), calls=%async_computation | async-start | bytes 2359296 | tf_op jit(solution)/shard_map/all_to_all | solution.py:271
  19.2 1.0 collective-permute-start.1
  20.2 1.0 collective-permute-done.1.refs_0_
  21.2 1.3 collective-permute-start.2
  22.5 1.4 collective-permute-start.3
  23.9 1.6 collective-permute-start.4
  26.1 0.8 collective-permute-done.2.refs_1_
  26.9 3.8 %collective-permute-done.4.refs_3_ = bf16[16,3584]{1,0:T(8,128)(2,1)S(1)} collective-permute-done((bf16[16,3584]{1,0:T(8,128)(2,1)S(1)}, bf16[16,3584]{1,0:T(8,128)(2,1)S(1)}, u32[]{:S(2)}, u32[]{:S(2)}) %collective-permute-start.4) | collective-permute-done | bytes 114720 | tf_op jit(solution)/shard_map/ppermute | solution.py:25
  31.3 2.3 %join.1 = (bf16[64,3584]{1,0:T(8,128)(2,1)}, bf16[256,1024]{1,0:T(8,128)(2,1)}) custom-call(s32[2]{0:T(128)} %pad_add_fusion.here, bf16[16,3584]{1,0:T(8,128)(2,1)} %copy-done.10, bf16[16,3584]{1,0:T(8,128)(2,1)} %copy-done.11, bf16[16,3584]{1,0:T(8,128)(2,1)} %copy-done.12, bf16[16,3584]{1,0:T(8,128)(2,1)} %copy-done.13, bf16[256,1024]{1,0:T(8,128)(2,1)} %refs_4_.1), custom_call_target="tpu_custom_call" | custom-call | bytes 917504 | tf_op jit(solution)/shard_map/join/pallas_call | solution.py:62
  34.1 2.3 %collective-permute-start.6 = (bf16[256,1024]{1,0:T(8,128)(2,1)}, bf16[256,1024]{1,0:T(8,128)(2,1)}, u32[]{:S(2)}, u32[]{:S(2)}) collective-permute-start(bf16[256,1024]{1,0:T(8,128)(2,1)} %get-tuple-element.7.first), channel_id=1, source_target_pairs={{0,192},{64,0},{128,64},{192,128},{1,193},{65,1},{129,65},{193,129... | collective-permute-start | bytes 1572872 | tf_op jit(solution)/shard_map/ppermute | solution.py:25
  36.4 1.1 fusion
  37.6 3.0 %collective-permute-start.8 = (bf16[256,512]{1,0:T(8,128)(2,1)S(1)}, bf16[256,512]{1,0:T(8,128)(2,1)S(1)}, u32[]{:S(2)}, u32[]{:S(2)}) collective-permute-start(bf16[256,512]{1,0:T(8,128)(2,1)S(1)} %get-tuple-element.9), channel_id=1, source_target_pairs={{0,128},{64,192},{128,0},{192,64},{1,129},{65,193},{129,1},{193,65... | collective-permute-start | bytes 786440 | tf_op jit(solution)/shard_map/ppermute | solution.py:25
  40.5 10.8 %all-to-all-done = bf16[8,16,4608]{2,1,0:T(8,128)(2,1)} async-done(((bf16[8,16,4608]{2,1,0:T(8,128)(2,1)}), bf16[8,16,4608]{2,1,0:T(8,128)(2,1)}, u32[]{:S(2)}, u32[]{:S(2)}) %all-to-all-start) | async-done | bytes 1179680 | tf_op jit(solution)/shard_map/all_to_all | solution.py:271
  51.3 1.0 slice.36
  52.2 0.7 collective-permute-start
  53.0 0.7 copy-done.5
  53.7 4.4 %collective-permute-start.10 = (bf16[3584,896]{1,0:T(8,128)(2,1)}, bf16[3584,896]{1,0:T(8,128)(2,1)}, u32[]{:S(2)}, u32[]{:S(2)}) collective-permute-start(bf16[3584,896]{1,0:T(8,128)(2,1)} %refs_5_.1), channel_id=1, source_target_pairs={{0,1},{1,0},{2,3},{3,2},{4,5},{5,4},{6,7},{7,6},{8,9},{9,8},{10,11... | collective-permute-start | bytes 19267592 | tf_op jit(solution)/shard_map/ppermute | solution.py:25
  58.1 1.3 slice.39.refs_0_
  60.0 1.0 collective-permute-start.11
  61.1 1.6 collective-permute-start.12
  62.7 0.9 copy-done.6
  63.7 0.9 copy-done.8
  64.6 2.6 %project.1 = bf16[8,2,16,1024]{3,2,1,0:T(8,128)(2,1)} custom-call(s32[2]{0:T(128)S(1)} %copy-done.4, bf16[128,1024]{1,0:T(8,128)(2,1)S(1)} %bitcast.27, bf16[128,1024]{1,0:T(8,128)(2,1)S(1)} %collective-permute-done.other, bf16[256,1024]{1,0:T(8,128)(2,1)S(1)} %copy-done.3, bf16[256,1024]{1,0:T(8,128)(2,1)S(1)} %collective-permute-done.5.second, ...), custom_call_target="tpu_custom_call" | custom-call | flops 40265318400 | bytes 4194304 | tf_op jit(solution)/shard_map/project/pallas_call | solution.py:85
  67.2 6.8 %all-to-all-start.1 = ((bf16[8,2,16,1024]{3,2,1,0:T(8,128)(2,1)}), bf16[8,2,16,1024]{3,2,1,0:T(8,128)(2,1)S(1)}, u32[]{:S(2)}, u32[]{:S(2)}) async-start(bf16[8,2,16,1024]{3,2,1,0:T(8,128)(2,1)} %project.1), calls=%async_computation.1 | async-start | bytes 1048576 | tf_op jit(solution)/shard_map/all_to_all | solution.py:276
  74.0 8.2 %collective-permute-done.11 = bf16[128,3584]{1,0:T(8,128)(2,1)S(1)} collective-permute-done((bf16[128,3584]{1,0:T(8,128)(2,1)S(1)}, bf16[128,3584]{1,0:T(8,128)(2,1)S(1)}, u32[]{:S(2)}, u32[]{:S(2)}) %collective-permute-start.11) | collective-permute-done | bytes 917536 | tf_op jit(solution)/shard_map/ppermute | solution.py:25
  82.3 0.8 slice.40
  83.1 1.8 slice.41
  84.9 2.7 %collective-permute-start.14 = (bf16[128,1792]{1,0:T(8,128)(2,1)}, bf16[128,1792]{1,0:T(8,128)(2,1)}, u32[]{:S(2)}, u32[]{:S(2)}) collective-permute-start(bf16[128,1792]{1,0:T(8,128)(2,1)} %slice.41), channel_id=1, source_target_pairs={{0,192},{64,0},{128,64},{192,128},{1,193},{65,1},{129,65},{193,129... | collective-permute-start | bytes 1376264 | tf_op jit(solution)/shard_map/ppermute | solution.py:25
  87.6 9.2 %all-to-all-done.1.refs_6_ = bf16[8,2,16,1024]{3,2,1,0:T(8,128)(2,1)S(1)} async-done(((bf16[8,2,16,1024]{3,2,1,0:T(8,128)(2,1)}), bf16[8,2,16,1024]{3,2,1,0:T(8,128)(2,1)S(1)}, u32[]{:S(2)}, u32[]{:S(2)}) %all-to-all-start.1) | async-done | bytes 524320 | tf_op jit(solution)/shard_map/all_to_all | solution.py:276
  96.8 2.0 collective-permute-start.9
  98.9 7.0 %damp.1.own = bf16[2,1024,896]{2,1,0:T(8,128)(2,1)} custom-call(bf16[2,1024,896]{2,1,0:T(8,128)(2,1)} %queries.1, bf16[1024,896]{1,0:T(8,128)(2,1)} %eigenvalues.1, bf16[64,3584]{1,0:T(8,128)(2,1)} %get-tuple-element.8._), custom_call_target="tpu_custom_call" | custom-call | flops 3670016 | bytes 9175040 | tf_op jit(solution)/shard_map/damp/pallas_call | solution.py:104
  105.9 0.9 broadcast_in_dim.11.refs_6_
  106.8 4.2 %all-to-all-start.2 = ((bf16[8,16,2048]{2,1,0:T(8,128)(2,1)}), bf16[8,16,2048]{2,1,0:T(8,128)(2,1)}, u32[]{:S(2)}, u32[]{:S(2)}) async-start(bf16[8,16,2048]{2,1,0:T(8,128)(2,1)} %broadcast_in_dim.11.refs_6_), calls=%async_computation.2 | async-start | bytes 1048576 | tf_op jit(solution)/shard_map/all_to_all | solution.py:281
  111.0 9.1 %rotate_y.1.refs_5_ = f32[512,896]{1,0:T(8,128)S(1)} custom-call(s32[2]{0:T(128)S(1)} %copy-done.4, bf16[8,16,3584]{2,1,0:T(8,128)(2,1)S(1)} %slice.39.refs_0_, bf16[8,16,3584]{2,1,0:T(8,128)(2,1)S(1)} %bitcast.28, bf16[8,16,3584]{2,1,0:T(8,128)(2,1)} %bitcast.10.refs_2_, bf16[8,16,1792]{2,1,0:T(8,128)(2,1)S(1)} %bitcast.29, ...), custom_call_target="tpu_custom_call" | custom-call | flops 13153337344 | bytes 11010048 | tf_op jit(solution)/shard_map/rotate_y/pallas_call | solution.py:166
  120.2 9.3 %rotate_z.1.ready = bf16[512,896]{1,0:T(8,128)(2,1)S(1)} custom-call(s32[2]{0:T(128)S(1)} %copy-done.4, bf16[8,4,16,3584]{3,2,1,0:T(8,128)(2,1)} %bitcast.35, bf16[8,4,16,3584]{3,2,1,0:T(8,128)(2,1)} %bitcast.36, bf16[8,4,16,3584]{3,2,1,0:T(8,128)(2,1)} %bitcast.37, bf16[8,4,16,3584]{3,2,1,0:T(8,128)(2,1)} %bitcast.38, ...), custom_call_target="tpu_custom_call" | custom-call | flops 13153337344 | bytes 11010048 | tf_op jit(solution)/shard_map/rotate_z/pallas_call | solution.py:166
  129.6 0.9 copy-done.1
  130.5 1.2 copy-done.2
  131.7 16.5 %all_to_all.30 = bf16[4,128,896]{2,1,0:T(8,128)(2,1)S(1)} all-to-all(bf16[4,128,896]{2,1,0:T(8,128)(2,1)S(1)} %bitcast.23), channel_id=1, replica_groups=mesh['y'=4,'z'=8,'x'=4,'c'=2] {'x'}, dimensions={0} | all-to-all | bytes 1835008 | tf_op jit(solution)/shard_map/all_to_all | solution.py:244
  148.3 1.0 broadcast_in_dim.12
  149.3 3.5 %all-to-all-start.4 = ((bf16[4,128,896]{2,1,0:T(8,128)(2,1)}), bf16[4,128,896]{2,1,0:T(8,128)(2,1)S(1)}, u32[]{:S(2)}, u32[]{:S(2)}) async-start(bf16[4,128,896]{2,1,0:T(8,128)(2,1)} %broadcast_in_dim.12), calls=%async_computation.4 | async-start | bytes 1835008 | tf_op jit(solution)/shard_map/all_to_all | solution.py:42
  153.0 0.9 reshape.69.ids
  153.9 10.7 %all-to-all-done.4 = bf16[4,128,896]{2,1,0:T(8,128)(2,1)S(1)} async-done(((bf16[4,128,896]{2,1,0:T(8,128)(2,1)}), bf16[4,128,896]{2,1,0:T(8,128)(2,1)S(1)}, u32[]{:S(2)}, u32[]{:S(2)}) %all-to-all-start.4) | async-done | bytes 917536 | tf_op jit(solution)/shard_map/all_to_all | solution.py:42
  164.6 0.9 copy-done.9
  165.6 8.3 %score.1 = f32[2,1,128]{2,1,0:T(1,128)} custom-call(bf16[512,2048]{1,0:T(8,128)(2,1)} %all-gather.5.cloned.1.call-done.grads, bf16[2,1024,896]{2,1,0:T(8,128)(2,1)} %damp.1.own, bf16[2,1024,896]{2,1,0:T(8,128)(2,1)} %collective-permute-done.15.other, bf16[512,896]{1,0:T(8,128)(2,1)} %bitcast.32, s32[512,1]{1,0:T(8,128)} %reshape.69.ids), custom_call_target="tpu_custom_call" | custom-call | flops 3758096384 | bytes 10354688 | tf_op jit(solution)/shard_map/score/pallas_call | solution.py:204
  174.7 24.3 %all_to_all.31 = f32[256,1,128]{2,1,0:T(1,128)S(1)} all-to-all(f32[256,1,128]{2,1,0:T(1,128)S(1)} %broadcast_in_dim.14), channel_id=1, replica_groups=mesh['y'=4,'z'=8,'x'=4,'c'=2] {'y','z','x','c'}, dimensions={0} | all-to-all | bytes 262144 | tf_op jit(solution)/shard_map/all_to_all | solution.py:42
  (64 shorter events, 5.1 us)
Async XLA Ops:
  6.5 1.0 copy-start
  10.1 41.2 %all-to-all-start = ((bf16[8,16,4608]{2,1,0:T(8,128)(2,1)}), bf16[8,16,4608]{2,1,0:T(8,128)(2,1)}, u32[]{:S(2)}, u32[]{:S(2)}) async-start(bf16[8,16,4608]{2,1,0:T(8,128)(2,1)} %pad_maximum_fusion), calls=%async_computation | async-start | bytes 2359296 | tf_op jit(solution)/shard_map/all_to_all | solution.py:271
  19.1 91.9 %all-gather.3.cloned.1.call-start = ((), (), s32[]{:S(2)}) async-start(), calls=%async_computation.6 | async-start | bytes 4128768 | tf_op jit(solution)/shard_map/all_gather | solution.py:262
  19.2 2.0 collective-permute-start.1
  21.2 9.5 %copy-start.10 = (bf16[16,3584]{1,0:T(8,128)(2,1)}, bf16[16,3584]{1,0:T(8,128)(2,1)S(1)}, u32[]{:S(2)}) copy-start(bf16[16,3584]{1,0:T(8,128)(2,1)S(1)} %collective-permute-done.1.refs_0_) | copy-start | bytes 344068
  21.2 5.7 %collective-permute-start.2 = (bf16[16,3584]{1,0:T(8,128)(2,1)S(1)}, bf16[16,3584]{1,0:T(8,128)(2,1)S(1)}, u32[]{:S(2)}, u32[]{:S(2)}) collective-permute-start(bf16[16,3584]{1,0:T(8,128)(2,1)S(1)} %collective-permute-done.1.refs_0_), channel_id=1, source_target_pairs={{0,64},{64,128},{128,192},{192,0},{1,65},{65,129},{129,193},{193,1... | collective-permute-start | bytes 344072 | tf_op jit(solution)/shard_map/ppermute | solution.py:25
  22.5 4.4 %collective-permute-start.3 = (bf16[16,3584]{1,0:T(8,128)(2,1)S(1)}, bf16[16,3584]{1,0:T(8,128)(2,1)S(1)}, u32[]{:S(2)}, u32[]{:S(2)}) collective-permute-start(bf16[16,3584]{1,0:T(8,128)(2,1)S(1)} %collective-permute-done.1.refs_0_), channel_id=1, source_target_pairs={{0,192},{64,0},{128,64},{192,128},{1,193},{65,1},{129,65},{193,129... | collective-permute-start | bytes 344072 | tf_op jit(solution)/shard_map/ppermute | solution.py:25
  23.9 6.8 %collective-permute-start.4 = (bf16[16,3584]{1,0:T(8,128)(2,1)S(1)}, bf16[16,3584]{1,0:T(8,128)(2,1)S(1)}, u32[]{:S(2)}, u32[]{:S(2)}) collective-permute-start(bf16[16,3584]{1,0:T(8,128)(2,1)S(1)} %collective-permute-done.1.refs_0_), channel_id=1, source_target_pairs={{0,128},{64,192},{128,0},{192,64},{1,129},{65,193},{129,1},{193,65... | collective-permute-start | bytes 344072 | tf_op jit(solution)/shard_map/ppermute | solution.py:25
  26.1 36.6 %copy-start.4 = (s32[2]{0:T(128)S(1)}, s32[2]{0:T(128)}, u32[]{:S(2)}) copy-start(s32[2]{0:T(128)} %pad_add_fusion.here) | copy-start | bytes 28
  26.9 3.8 %copy-start.11 = (bf16[16,3584]{1,0:T(8,128)(2,1)}, bf16[16,3584]{1,0:T(8,128)(2,1)S(1)}, u32[]{:S(2)}) copy-start(bf16[16,3584]{1,0:T(8,128)(2,1)S(1)} %collective-permute-done.2.refs_1_) | copy-start | bytes 344068
  26.9 3.8 %copy-start.12 = (bf16[16,3584]{1,0:T(8,128)(2,1)}, bf16[16,3584]{1,0:T(8,128)(2,1)S(1)}, u32[]{:S(2)}) copy-start(bf16[16,3584]{1,0:T(8,128)(2,1)S(1)} %collective-permute-done.3.refs_2_) | copy-start | bytes 344068
  30.7 0.6 copy-start.13
  33.6 29.1 %copy-start.3 = (bf16[256,1024]{1,0:T(8,128)(2,1)S(1)}, bf16[256,1024]{1,0:T(8,128)(2,1)}, u32[]{:S(2)}) copy-start(bf16[256,1024]{1,0:T(8,128)(2,1)} %get-tuple-element.7.first) | copy-start | bytes 1572868
  33.6 27.4 %collective-permute-start.5 = (bf16[256,1024]{1,0:T(8,128)(2,1)}, bf16[256,1024]{1,0:T(8,128)(2,1)S(1)}, u32[]{:S(2)}, u32[]{:S(2)}) collective-permute-start(bf16[256,1024]{1,0:T(8,128)(2,1)} %get-tuple-element.7.first), channel_id=1, source_target_pairs={{0,64},{64,128},{128,192},{192,0},{1,65},{65,129},{129,193},{193,1... | collective-permute-start | bytes 1572872 | tf_op jit(solution)/shard_map/ppermute | solution.py:25
  34.1 28.6 %collective-permute-start.6 = (bf16[256,1024]{1,0:T(8,128)(2,1)}, bf16[256,1024]{1,0:T(8,128)(2,1)}, u32[]{:S(2)}, u32[]{:S(2)}) collective-permute-start(bf16[256,1024]{1,0:T(8,128)(2,1)} %get-tuple-element.7.first), channel_id=1, source_target_pairs={{0,192},{64,0},{128,64},{192,128},{1,193},{65,1},{129,65},{193,129... | collective-permute-start | bytes 1572872 | tf_op jit(solution)/shard_map/ppermute | solution.py:25
  37.5 15.5 %collective-permute-start.7 = (bf16[256,512]{1,0:T(8,128)(2,1)S(1)}, bf16[256,512]{1,0:T(8,128)(2,1)S(1)}, u32[]{:S(2)}, u32[]{:S(2)}) collective-permute-start(bf16[256,512]{1,0:T(8,128)(2,1)S(1)} %get-tuple-element.10), channel_id=1, source_target_pairs={{0,128},{64,192},{128,0},{192,64},{1,129},{65,193},{129,1},{193,65... | collective-permute-start | bytes 786440 | tf_op jit(solution)/shard_map/ppermute | solution.py:25
  37.6 21.7 %collective-permute-start.8 = (bf16[256,512]{1,0:T(8,128)(2,1)S(1)}, bf16[256,512]{1,0:T(8,128)(2,1)S(1)}, u32[]{:S(2)}, u32[]{:S(2)}) collective-permute-start(bf16[256,512]{1,0:T(8,128)(2,1)S(1)} %get-tuple-element.9), channel_id=1, source_target_pairs={{0,128},{64,192},{128,0},{192,64},{1,129},{65,193},{129,1},{193,65... | collective-permute-start | bytes 786440 | tf_op jit(solution)/shard_map/ppermute | solution.py:25
  52.2 10.5 %collective-permute-start = (bf16[128,1024]{1,0:T(8,128)(2,1)S(1)}, bf16[128,1024]{1,0:T(8,128)(2,1)S(1)}, u32[]{:S(2)}, u32[]{:S(2)}) collective-permute-start(bf16[128,1024]{1,0:T(8,128)(2,1)S(1)} %bitcast.26), channel_id=1, source_target_pairs={{0,1},{1,0},{2,3},{3,2},{4,5},{5,4},{6,7},{7,6},{8,9},{9,8},{10,11... | collective-permute-start | bytes 786440 | tf_op jit(solution)/shard_map/ppermute | solution.py:25
  53.0 0.7 copy-start.5
  53.7 66.5 %collective-permute-start.10 = (bf16[3584,896]{1,0:T(8,128)(2,1)}, bf16[3584,896]{1,0:T(8,128)(2,1)}, u32[]{:S(2)}, u32[]{:S(2)}) collective-permute-start(bf16[3584,896]{1,0:T(8,128)(2,1)} %refs_5_.1), channel_id=1, source_target_pairs={{0,1},{1,0},{2,3},{3,2},{4,5},{5,4},{6,7},{7,6},{8,9},{9,8},{10,11... | collective-permute-start | bytes 19267592 | tf_op jit(solution)/shard_map/ppermute | solution.py:25
  59.3 0.7 copy-start.7
  60.0 22.2 %collective-permute-start.11 = (bf16[128,3584]{1,0:T(8,128)(2,1)S(1)}, bf16[128,3584]{1,0:T(8,128)(2,1)S(1)}, u32[]{:S(2)}, u32[]{:S(2)}) collective-permute-start(bf16[128,3584]{1,0:T(8,128)(2,1)S(1)} %bitcast.24), channel_id=1, source_target_pairs={{0,64},{64,128},{128,192},{192,0},{1,65},{65,129},{129,193},{193,1... | collective-permute-start | bytes 2752520 | tf_op jit(solution)/shard_map/ppermute | solution.py:25
  61.1 22.0 %collective-permute-start.12 = (bf16[128,3584]{1,0:T(8,128)(2,1)S(1)}, bf16[128,3584]{1,0:T(8,128)(2,1)}, u32[]{:S(2)}, u32[]{:S(2)}) collective-permute-start(bf16[128,3584]{1,0:T(8,128)(2,1)S(1)} %bitcast.25), channel_id=1, source_target_pairs={{0,192},{64,0},{128,64},{192,128},{1,193},{65,1},{129,65},{193,129... | collective-permute-start | bytes 2752520 | tf_op jit(solution)/shard_map/ppermute | solution.py:25
  62.7 1.0 copy-start.6
  63.7 0.9 copy-start.8
  67.2 29.5 %all-to-all-start.1 = ((bf16[8,2,16,1024]{3,2,1,0:T(8,128)(2,1)}), bf16[8,2,16,1024]{3,2,1,0:T(8,128)(2,1)S(1)}, u32[]{:S(2)}, u32[]{:S(2)}) async-start(bf16[8,2,16,1024]{3,2,1,0:T(8,128)(2,1)} %project.1), calls=%async_computation.1 | async-start | bytes 1048576 | tf_op jit(solution)/shard_map/all_to_all | solution.py:276
  83.1 27.9 %collective-permute-start.13 = (bf16[128,1792]{1,0:T(8,128)(2,1)}, bf16[128,1792]{1,0:T(8,128)(2,1)S(1)}, u32[]{:S(2)}, u32[]{:S(2)}) collective-permute-start(bf16[128,1792]{1,0:T(8,128)(2,1)} %slice.40), channel_id=1, source_target_pairs={{0,64},{64,128},{128,192},{192,0},{1,65},{65,129},{129,193},{193,1... | collective-permute-start | bytes 1376264 | tf_op jit(solution)/shard_map/ppermute | solution.py:25
  84.9 26.1 %collective-permute-start.14 = (bf16[128,1792]{1,0:T(8,128)(2,1)}, bf16[128,1792]{1,0:T(8,128)(2,1)}, u32[]{:S(2)}, u32[]{:S(2)}) collective-permute-start(bf16[128,1792]{1,0:T(8,128)(2,1)} %slice.41), channel_id=1, source_target_pairs={{0,192},{64,0},{128,64},{192,128},{1,193},{65,1},{129,65},{193,129... | collective-permute-start | bytes 1376264 | tf_op jit(solution)/shard_map/ppermute | solution.py:25
  96.8 9.1 %collective-permute-start.9 = (bf16[16,1024]{1,0:T(8,128)(2,1)S(1)}, bf16[16,1024]{1,0:T(8,128)(2,1)S(1)}, u32[]{:S(2)}, u32[]{:S(2)}) collective-permute-start(bf16[16,1024]{1,0:T(8,128)(2,1)S(1)} %get-tuple-element.14), channel_id=1, source_target_pairs={{0,1},{1,0},{2,3},{3,2},{4,5},{5,4},{6,7},{7,6},{8,9},{9,8},{10,11... | collective-permute-start | bytes 98312 | tf_op jit(solution)/shard_map/ppermute | solution.py:25
  105.9 48.0 %collective-permute-start.15 = (bf16[2,1024,896]{2,1,0:T(8,128)(2,1)}, bf16[2,1024,896]{2,1,0:T(8,128)(2,1)}, u32[]{:S(2)}, u32[]{:S(2)}) collective-permute-start(bf16[2,1024,896]{2,1,0:T(8,128)(2,1)} %damp.1.own), channel_id=1, source_target_pairs={{0,1},{1,0},{2,3},{3,2},{4,5},{5,4},{6,7},{7,6},{8,9},{9,8},{10,11... | collective-permute-start | bytes 11010056 | tf_op jit(solution)/shard_map/ppermute | solution.py:25
  106.8 23.7 %all-to-all-start.2 = ((bf16[8,16,2048]{2,1,0:T(8,128)(2,1)}), bf16[8,16,2048]{2,1,0:T(8,128)(2,1)}, u32[]{:S(2)}, u32[]{:S(2)}) async-start(bf16[8,16,2048]{2,1,0:T(8,128)(2,1)} %broadcast_in_dim.11.refs_6_), calls=%async_computation.2 | async-start | bytes 1048576 | tf_op jit(solution)/shard_map/all_to_all | solution.py:281
  110.9 53.7 %all-gather.5.cloned.1.call-start = ((), (), s32[]{:S(2)}) async-start(), calls=%async_computation.7 | async-start | bytes 2621440 | tf_op jit(solution)/shard_map/all_gather | solution.py:286
  129.6 0.9 copy-start.1
  130.5 1.2 copy-start.2
  148.2 4.7 %copy-start.14 = (s32[1024]{0:T(1024)S(1)}, s32[1024]{0:T(1024)}, u32[]{:S(2)}) copy-start(s32[1024]{0:T(1024)} %param.13) | copy-start | bytes 12292
  149.3 15.3 %all-to-all-start.4 = ((bf16[4,128,896]{2,1,0:T(8,128)(2,1)}), bf16[4,128,896]{2,1,0:T(8,128)(2,1)S(1)}, u32[]{:S(2)}, u32[]{:S(2)}) async-start(bf16[4,128,896]{2,1,0:T(8,128)(2,1)} %broadcast_in_dim.12), calls=%async_computation.4 | async-start | bytes 1835008 | tf_op jit(solution)/shard_map/all_to_all | solution.py:42
  164.6 0.9 copy-start.9
Sparse Core Ops, SparseCore 0:
  33.8 60.4 all-gather.2
  130.7 32.9 all-gather.4

commit v9 on v8

--- a/solution.py
+++ b/solution.py
@@ -262,8 +262,8 @@
     low = lax.all_gather(low, "z", axis=0, tiled=True).reshape(8, 4, 16, -1)
     cut = basis_out.shape[1] // 2
     bases = [basis_out, shift(basis_out, "y", 1), shift(basis_out, "y", -1)]
-    bases += [shift(basis_out[:, :cut], "y", 2), shift(basis_out[:, cut:], "y", -2)]
     precond = damp(queries, eigenvalues, first_low)
+    bases += [shift(after(basis_out[:, :cut], precond), "y", 2), shift(basis_out[:, cut:], "y", -2)]
     rows = lax.dynamic_slice_in_dim(out_grads, c * 16, 16).reshape(16, 4, 8, 256)
     rows = rows.transpose(2, 0, 1, 3).reshape(8, 16, 1024)
     mine = jnp.concatenate([mine, theirs[:, :extra]], axis=1)

time: 208 us -> 202 us (0.971)
  waiting for transfers between devices: 44.4 us -> 38.4 us
    all_to_all x1, waiting for transfers between devices: 10.8 us -> 4.03 us  [shards(): sent = lax.all_to_all(jnp.concatenate([copies, rows], axis=2), 'z', 0, 0)]
  transfers between devices with their start and end apart: 22 -> 22, of which waited for: 7 -> 8; matrix products, arithmetic and copies ran while one was open for 5% -> 5% of each run, Pallas kernels for 15% -> 15%
where the time goes in v9:
time: 202 us; the launch traced here: 201 us
  starting transfers between devices  47.5 us (24%)
  blocking collectives  40.6 us (20%)
  Pallas kernels  38.8 us (19%)
  waiting for transfers between devices  38.4 us (19%)
  local copies, waits for them, and re-layouts  19.6 us (10%)
  between operations  13.6 us (7%)
    all_to_all x1, blocking collectives, spread(): lax.all_to_all(jnp.broadcast_to(value[None], (size,) + value.shape), axes...  24 us
    ppermute x16, starting transfers between devices, shift(): lax.ppermute(value, axis, [(i, (i + hops) % size) for i in range(size)])  24 us
    pallas_call x2, Pallas kernels, rotate(): pl.pallas_call(functools.partial(rotate_kernel, places, axis, spans, len(...  18.5 us
    all_to_all x1, blocking collectives, over_x(): parts = lax.all_to_all(partial.reshape(4, rows // 4, cols), 'x', 0, 0)  16.7 us
    ppermute x16, waiting for transfers between devices, shift(): lax.ppermute(value, axis, [(i, (i + hops) % size) for i in range(size)])  13.8 us
    all_to_all x1, waiting for transfers between devices, spread(): lax.all_to_all(jnp.broadcast_to(value[None], (size,) + value.shape), axes...  10.9 us
    all_to_all x1, waiting for transfers between devices, shards(): parts = lax.all_to_all(project(rows, swap(rows), bases, here), 'z', 0, 0)  9.67 us
    all_to_all x1, starting transfers between devices, shards(): sent = lax.all_to_all(jnp.concatenate([copies, rows], axis=2), 'z', 0, 0)  9.01 us
  transfers between devices with their start and end apart: 22, of which 8 were waited for; matrix products, arithmetic and copies ran while one was open for 5% of the time, Pallas kernels for 15%

profile of v9, /device:TPU:1, one launch (start us, length us, event | category | flops | bytes accessed | tf_op | source)
XLA Modules:
  0.0 200.5 jit_solution(13302784022777720528)
XLA Ops:
  6.5 1.0 copy-done
  7.9 1.0 constant_dynamic-slice_fusion
  9.0 1.1 pad_maximum_fusion
  10.1 9.0 %all-to-all-start = ((bf16[8,16,4608]{2,1,0:T(8,128)(2,1)}), bf16[8,16,4608]{2,1,0:T(8,128)(2,1)}, u32[]{:S(2)}, u32[]{:S(2)}) async-start(bf16[8,16,4608]{2,1,0:T(8,128)(2,1)} %pad_maximum_fusion), calls=%async_computation | async-start | bytes 2359296 | tf_op jit(solution)/shard_map/all_to_all | solution.py:271
  19.2 1.0 collective-permute-start.1
  20.2 1.0 collective-permute-done.1.refs_0_
  21.2 1.3 collective-permute-start.2
  22.5 1.4 collective-permute-start.3
  23.9 1.6 collective-permute-start.4
  26.1 0.8 collective-permute-done.2.refs_1_
  26.9 3.8 %collective-permute-done.4.refs_3_ = bf16[16,3584]{1,0:T(8,128)(2,1)S(1)} collective-permute-done((bf16[16,3584]{1,0:T(8,128)(2,1)S(1)}, bf16[16,3584]{1,0:T(8,128)(2,1)S(1)}, u32[]{:S(2)}, u32[]{:S(2)}) %collective-permute-start.4) | collective-permute-done | bytes 114720 | tf_op jit(solution)/shard_map/ppermute | solution.py:25
  31.3 2.3 %join.1 = (bf16[64,3584]{1,0:T(8,128)(2,1)}, bf16[256,1024]{1,0:T(8,128)(2,1)}) custom-call(s32[2]{0:T(128)} %pad_add_fusion.here, bf16[16,3584]{1,0:T(8,128)(2,1)} %copy-done.10, bf16[16,3584]{1,0:T(8,128)(2,1)} %copy-done.11, bf16[16,3584]{1,0:T(8,128)(2,1)} %copy-done.12, bf16[16,3584]{1,0:T(8,128)(2,1)} %copy-done.13, bf16[256,1024]{1,0:T(8,128)(2,1)} %refs_4_.1), custom_call_target="tpu_custom_call" | custom-call | bytes 917504 | tf_op jit(solution)/shard_map/join/pallas_call | solution.py:62
  34.2 2.3 %collective-permute-start.6 = (bf16[256,1024]{1,0:T(8,128)(2,1)}, bf16[256,1024]{1,0:T(8,128)(2,1)}, u32[]{:S(2)}, u32[]{:S(2)}) collective-permute-start(bf16[256,1024]{1,0:T(8,128)(2,1)} %get-tuple-element.7.first), channel_id=1, source_target_pairs={{0,192},{64,0},{128,64},{192,128},{1,193},{65,1},{129,65},{193,129... | collective-permute-start | bytes 1572872 | tf_op jit(solution)/shard_map/ppermute | solution.py:25
  36.5 7.0 %damp.1.ready.own = bf16[2,1024,896]{2,1,0:T(8,128)(2,1)} custom-call(bf16[2,1024,896]{2,1,0:T(8,128)(2,1)} %queries.1, bf16[1024,896]{1,0:T(8,128)(2,1)} %eigenvalues.1, bf16[64,3584]{1,0:T(8,128)(2,1)} %get-tuple-element.8._), custom_call_target="tpu_custom_call" | custom-call | flops 3670016 | bytes 9175040 | tf_op jit(solution)/shard_map/damp/pallas_call | solution.py:104
  43.5 0.8 fusion
  44.3 3.0 %collective-permute-start.8 = (bf16[256,512]{1,0:T(8,128)(2,1)S(1)}, bf16[256,512]{1,0:T(8,128)(2,1)S(1)}, u32[]{:S(2)}, u32[]{:S(2)}) collective-permute-start(bf16[256,512]{1,0:T(8,128)(2,1)S(1)} %get-tuple-element.9), channel_id=1, source_target_pairs={{0,128},{64,192},{128,0},{192,64},{1,129},{65,193},{129,1},{193,65... | collective-permute-start | bytes 786440 | tf_op jit(solution)/shard_map/ppermute | solution.py:25
  47.2 4.0 %all-to-all-done = bf16[8,16,4608]{2,1,0:T(8,128)(2,1)} async-done(((bf16[8,16,4608]{2,1,0:T(8,128)(2,1)}), bf16[8,16,4608]{2,1,0:T(8,128)(2,1)}, u32[]{:S(2)}, u32[]{:S(2)}) %all-to-all-start) | async-done | bytes 1179680 | tf_op jit(solution)/shard_map/all_to_all | solution.py:271
  51.3 1.0 slice.36
  53.0 0.7 copy-done.5
  53.7 3.9 %collective-permute-start.10 = (bf16[3584,896]{1,0:T(8,128)(2,1)}, bf16[3584,896]{1,0:T(8,128)(2,1)}, u32[]{:S(2)}, u32[]{:S(2)}) collective-permute-start(bf16[3584,896]{1,0:T(8,128)(2,1)} %refs_5_.1), channel_id=1, source_target_pairs={{0,1},{1,0},{2,3},{3,2},{4,5},{5,4},{6,7},{7,6},{8,9},{9,8},{10,11... | collective-permute-start | bytes 19267592 | tf_op jit(solution)/shard_map/ppermute | solution.py:25
  57.5 1.2 slice.39.refs_0_
  59.5 0.8 collective-permute-start.11
  60.2 1.9 collective-permute-start.12
  62.2 0.9 copy-done.6
  63.1 1.0 copy-done.8
  64.1 2.6 %project.1 = bf16[8,2,16,1024]{3,2,1,0:T(8,128)(2,1)} custom-call(s32[2]{0:T(128)S(1)} %copy-done.4, bf16[128,1024]{1,0:T(8,128)(2,1)S(1)} %bitcast.27, bf16[128,1024]{1,0:T(8,128)(2,1)S(1)} %collective-permute-done.other, bf16[256,1024]{1,0:T(8,128)(2,1)S(1)} %copy-done.3, bf16[256,1024]{1,0:T(8,128)(2,1)S(1)} %collective-permute-done.5.second, ...), custom_call_target="tpu_custom_call" | custom-call | flops 40265318400 | bytes 4194304 | tf_op jit(solution)/shard_map/project/pallas_call | solution.py:85
  66.7 6.8 %all-to-all-start.1 = ((bf16[8,2,16,1024]{3,2,1,0:T(8,128)(2,1)}), bf16[8,2,16,1024]{3,2,1,0:T(8,128)(2,1)S(1)}, u32[]{:S(2)}, u32[]{:S(2)}) async-start(bf16[8,2,16,1024]{3,2,1,0:T(8,128)(2,1)} %project.1), calls=%async_computation.1 | async-start | bytes 1048576 | tf_op jit(solution)/shard_map/all_to_all | solution.py:276
  73.5 7.5 %collective-permute-done.11 = bf16[128,3584]{1,0:T(8,128)(2,1)S(1)} collective-permute-done((bf16[128,3584]{1,0:T(8,128)(2,1)S(1)}, bf16[128,3584]{1,0:T(8,128)(2,1)S(1)}, u32[]{:S(2)}, u32[]{:S(2)}) %collective-permute-start.11) | collective-permute-done | bytes 917536 | tf_op jit(solution)/shard_map/ppermute | solution.py:25
  81.0 0.8 slice.40
  81.8 1.8 slice.41
  83.6 2.7 %collective-permute-start.14 = (bf16[128,1792]{1,0:T(8,128)(2,1)}, bf16[128,1792]{1,0:T(8,128)(2,1)}, u32[]{:S(2)}, u32[]{:S(2)}) collective-permute-start(bf16[128,1792]{1,0:T(8,128)(2,1)} %slice.41), channel_id=1, source_target_pairs={{0,192},{64,0},{128,64},{192,128},{1,193},{65,1},{129,65},{193,129... | collective-permute-start | bytes 1376264 | tf_op jit(solution)/shard_map/ppermute | solution.py:25
  86.3 9.7 %all-to-all-done.1.refs_6_ = bf16[8,2,16,1024]{3,2,1,0:T(8,128)(2,1)S(1)} async-done(((bf16[8,2,16,1024]{3,2,1,0:T(8,128)(2,1)}), bf16[8,2,16,1024]{3,2,1,0:T(8,128)(2,1)S(1)}, u32[]{:S(2)}, u32[]{:S(2)}) %all-to-all-start.1) | async-done | bytes 524320 | tf_op jit(solution)/shard_map/all_to_all | solution.py:276
  96.1 2.8 %collective-permute-start.9 = (bf16[16,1024]{1,0:T(8,128)(2,1)S(1)}, bf16[16,1024]{1,0:T(8,128)(2,1)S(1)}, u32[]{:S(2)}, u32[]{:S(2)}) collective-permute-start(bf16[16,1024]{1,0:T(8,128)(2,1)S(1)} %get-tuple-element.14), channel_id=1, source_target_pairs={{0,1},{1,0},{2,3},{3,2},{4,5},{5,4},{6,7},{7,6},{8,9},{9,8},{10,11... | collective-permute-start | bytes 98312 | tf_op jit(solution)/shard_map/ppermute | solution.py:25
  99.0 0.8 collective-permute-done.9
  99.7 0.9 broadcast_in_dim.11.refs_6_
  100.6 4.2 %all-to-all-start.2 = ((bf16[8,16,2048]{2,1,0:T(8,128)(2,1)}), bf16[8,16,2048]{2,1,0:T(8,128)(2,1)}, u32[]{:S(2)}, u32[]{:S(2)}) async-start(bf16[8,16,2048]{2,1,0:T(8,128)(2,1)} %broadcast_in_dim.11.refs_6_), calls=%async_computation.2 | async-start | bytes 1048576 | tf_op jit(solution)/shard_map/all_to_all | solution.py:281
  104.9 9.1 %rotate_y.1.refs_5_ = f32[512,896]{1,0:T(8,128)S(1)} custom-call(s32[2]{0:T(128)S(1)} %copy-done.4, bf16[8,16,3584]{2,1,0:T(8,128)(2,1)S(1)} %slice.39.refs_0_, bf16[8,16,3584]{2,1,0:T(8,128)(2,1)S(1)} %bitcast.28, bf16[8,16,3584]{2,1,0:T(8,128)(2,1)} %bitcast.10.refs_2_, bf16[8,16,1792]{2,1,0:T(8,128)(2,1)S(1)} %bitcast.29, ...), custom_call_target="tpu_custom_call" | custom-call | flops 13153337344 | bytes 11010048 | tf_op jit(solution)/shard_map/rotate_y/pallas_call | solution.py:166
  114.0 9.3 %rotate_z.1.ready = bf16[512,896]{1,0:T(8,128)(2,1)S(1)} custom-call(s32[2]{0:T(128)S(1)} %copy-done.4, bf16[8,4,16,3584]{3,2,1,0:T(8,128)(2,1)} %bitcast.35, bf16[8,4,16,3584]{3,2,1,0:T(8,128)(2,1)} %bitcast.36, bf16[8,4,16,3584]{3,2,1,0:T(8,128)(2,1)} %bitcast.37, bf16[8,4,16,3584]{3,2,1,0:T(8,128)(2,1)} %bitcast.38, ...), custom_call_target="tpu_custom_call" | custom-call | flops 13153337344 | bytes 11010048 | tf_op jit(solution)/shard_map/rotate_z/pallas_call | solution.py:166
  123.4 1.0 copy-done.1
  124.4 1.2 copy-done.2
  125.5 16.7 %all_to_all.30 = bf16[4,128,896]{2,1,0:T(8,128)(2,1)S(1)} all-to-all(bf16[4,128,896]{2,1,0:T(8,128)(2,1)S(1)} %bitcast.23), channel_id=1, replica_groups=mesh['y'=4,'z'=8,'x'=4,'c'=2] {'x'}, dimensions={0} | all-to-all | bytes 1835008 | tf_op jit(solution)/shard_map/all_to_all | solution.py:244
  142.4 1.1 broadcast_in_dim.12
  143.4 3.5 %all-to-all-start.4 = ((bf16[4,128,896]{2,1,0:T(8,128)(2,1)}), bf16[4,128,896]{2,1,0:T(8,128)(2,1)S(1)}, u32[]{:S(2)}, u32[]{:S(2)}) async-start(bf16[4,128,896]{2,1,0:T(8,128)(2,1)} %broadcast_in_dim.12), calls=%async_computation.4 | async-start | bytes 1835008 | tf_op jit(solution)/shard_map/all_to_all | solution.py:42
  147.1 0.9 reshape.69.ids
  148.0 10.9 %all-to-all-done.4 = bf16[4,128,896]{2,1,0:T(8,128)(2,1)S(1)} async-done(((bf16[4,128,896]{2,1,0:T(8,128)(2,1)}), bf16[4,128,896]{2,1,0:T(8,128)(2,1)S(1)}, u32[]{:S(2)}, u32[]{:S(2)}) %all-to-all-start.4) | async-done | bytes 917536 | tf_op jit(solution)/shard_map/all_to_all | solution.py:42
  158.9 1.0 copy-done.9
  159.9 8.3 %score.1 = f32[2,1,128]{2,1,0:T(1,128)} custom-call(bf16[512,2048]{1,0:T(8,128)(2,1)} %all-gather.5.cloned.1.call-done.grads, bf16[2,1024,896]{2,1,0:T(8,128)(2,1)} %damp.1.ready.own, bf16[2,1024,896]{2,1,0:T(8,128)(2,1)} %collective-permute-done.15.other, bf16[512,896]{1,0:T(8,128)(2,1)} %bitcast.32, s32[512,1]{1,0:T(8,128)} %reshape.69.ids), custom_call_target="tpu_custom_call" | custom-call | flops 3758096384 | bytes 10354688 | tf_op jit(solution)/shard_map/score/pallas_call | solution.py:204
  169.1 24.0 %all_to_all.31 = f32[256,1,128]{2,1,0:T(1,128)S(1)} all-to-all(f32[256,1,128]{2,1,0:T(1,128)S(1)} %broadcast_in_dim.14), channel_id=1, replica_groups=mesh['y'=4,'z'=8,'x'=4,'c'=2] {'y','z','x','c'}, dimensions={0} | all-to-all | bytes 262144 | tf_op jit(solution)/shard_map/all_to_all | solution.py:42
  (65 shorter events, 5.8 us)
Async XLA Ops:
  6.5 1.0 copy-start
  10.1 41.2 %all-to-all-start = ((bf16[8,16,4608]{2,1,0:T(8,128)(2,1)}), bf16[8,16,4608]{2,1,0:T(8,128)(2,1)}, u32[]{:S(2)}, u32[]{:S(2)}) async-start(bf16[8,16,4608]{2,1,0:T(8,128)(2,1)} %pad_maximum_fusion), calls=%async_computation | async-start | bytes 2359296 | tf_op jit(solution)/shard_map/all_to_all | solution.py:271
  19.1 85.7 %all-gather.3.cloned.1.call-start = ((), (), s32[]{:S(2)}) async-start(), calls=%async_computation.6 | async-start | bytes 4128768 | tf_op jit(solution)/shard_map/all_gather | solution.py:262
  19.2 2.0 %collective-permute-start.1 = (bf16[16,3584]{1,0:T(8,128)(2,1)S(1)}, bf16[16,3584]{1,0:T(8,128)(2,1)S(1)}, u32[]{:S(2)}, u32[]{:S(2)}) collective-permute-start(bf16[16,3584]{1,0:T(8,128)(2,1)S(1)} %get-tuple-element.11), channel_id=1, source_target_pairs={{0,1},{1,0},{2,3},{3,2},{4,5},{5,4},{6,7},{7,6},{8,9},{9,8},{10,11... | collective-permute-start | bytes 344072 | tf_op jit(solution)/shard_map/ppermute | solution.py:25
  21.2 9.5 %copy-start.10 = (bf16[16,3584]{1,0:T(8,128)(2,1)}, bf16[16,3584]{1,0:T(8,128)(2,1)S(1)}, u32[]{:S(2)}) copy-start(bf16[16,3584]{1,0:T(8,128)(2,1)S(1)} %collective-permute-done.1.refs_0_) | copy-start | bytes 344068
  21.2 5.7 %collective-permute-start.2 = (bf16[16,3584]{1,0:T(8,128)(2,1)S(1)}, bf16[16,3584]{1,0:T(8,128)(2,1)S(1)}, u32[]{:S(2)}, u32[]{:S(2)}) collective-permute-start(bf16[16,3584]{1,0:T(8,128)(2,1)S(1)} %collective-permute-done.1.refs_0_), channel_id=1, source_target_pairs={{0,64},{64,128},{128,192},{192,0},{1,65},{65,129},{129,193},{193,1... | collective-permute-start | bytes 344072 | tf_op jit(solution)/shard_map/ppermute | solution.py:25
  22.5 4.4 %collective-permute-start.3 = (bf16[16,3584]{1,0:T(8,128)(2,1)S(1)}, bf16[16,3584]{1,0:T(8,128)(2,1)S(1)}, u32[]{:S(2)}, u32[]{:S(2)}) collective-permute-start(bf16[16,3584]{1,0:T(8,128)(2,1)S(1)} %collective-permute-done.1.refs_0_), channel_id=1, source_target_pairs={{0,192},{64,0},{128,64},{192,128},{1,193},{65,1},{129,65},{193,129... | collective-permute-start | bytes 344072 | tf_op jit(solution)/shard_map/ppermute | solution.py:25
  23.9 6.8 %collective-permute-start.4 = (bf16[16,3584]{1,0:T(8,128)(2,1)S(1)}, bf16[16,3584]{1,0:T(8,128)(2,1)S(1)}, u32[]{:S(2)}, u32[]{:S(2)}) collective-permute-start(bf16[16,3584]{1,0:T(8,128)(2,1)S(1)} %collective-permute-done.1.refs_0_), channel_id=1, source_target_pairs={{0,128},{64,192},{128,0},{192,64},{1,129},{65,193},{129,1},{193,65... | collective-permute-start | bytes 344072 | tf_op jit(solution)/shard_map/ppermute | solution.py:25
  26.9 3.8 %copy-start.11 = (bf16[16,3584]{1,0:T(8,128)(2,1)}, bf16[16,3584]{1,0:T(8,128)(2,1)S(1)}, u32[]{:S(2)}) copy-start(bf16[16,3584]{1,0:T(8,128)(2,1)S(1)} %collective-permute-done.2.refs_1_) | copy-start | bytes 344068
  26.9 3.8 %copy-start.12 = (bf16[16,3584]{1,0:T(8,128)(2,1)}, bf16[16,3584]{1,0:T(8,128)(2,1)S(1)}, u32[]{:S(2)}) copy-start(bf16[16,3584]{1,0:T(8,128)(2,1)S(1)} %collective-permute-done.3.refs_2_) | copy-start | bytes 344068
  30.7 0.7 copy-start.13
  33.7 9.8 %copy-start.3 = (bf16[256,1024]{1,0:T(8,128)(2,1)S(1)}, bf16[256,1024]{1,0:T(8,128)(2,1)}, u32[]{:S(2)}) copy-start(bf16[256,1024]{1,0:T(8,128)(2,1)} %get-tuple-element.7.first) | copy-start | bytes 1572868
  33.7 26.5 %collective-permute-start.5 = (bf16[256,1024]{1,0:T(8,128)(2,1)}, bf16[256,1024]{1,0:T(8,128)(2,1)S(1)}, u32[]{:S(2)}, u32[]{:S(2)}) collective-permute-start(bf16[256,1024]{1,0:T(8,128)(2,1)} %get-tuple-element.7.first), channel_id=1, source_target_pairs={{0,64},{64,128},{128,192},{192,0},{1,65},{65,129},{129,193},{193,1... | collective-permute-start | bytes 1572872 | tf_op jit(solution)/shard_map/ppermute | solution.py:25
  34.2 28.0 %collective-permute-start.6 = (bf16[256,1024]{1,0:T(8,128)(2,1)}, bf16[256,1024]{1,0:T(8,128)(2,1)}, u32[]{:S(2)}, u32[]{:S(2)}) collective-permute-start(bf16[256,1024]{1,0:T(8,128)(2,1)} %get-tuple-element.7.first), channel_id=1, source_target_pairs={{0,192},{64,0},{128,64},{192,128},{1,193},{65,1},{129,65},{193,129... | collective-permute-start | bytes 1572872 | tf_op jit(solution)/shard_map/ppermute | solution.py:25
  44.3 17.9 %copy-start.4 = (s32[2]{0:T(128)S(1)}, s32[2]{0:T(128)}, u32[]{:S(2)}) copy-start(s32[2]{0:T(128)} %pad_add_fusion.here) | copy-start | bytes 28
  44.3 8.7 %collective-permute-start.7 = (bf16[256,512]{1,0:T(8,128)(2,1)}, bf16[256,512]{1,0:T(8,128)(2,1)S(1)}, u32[]{:S(2)}, u32[]{:S(2)}) collective-permute-start(bf16[256,512]{1,0:T(8,128)(2,1)} %after.2), channel_id=1, source_target_pairs={{0,128},{64,192},{128,0},{192,64},{1,129},{65,193},{129,1},{193,65... | collective-permute-start | bytes 786440 | tf_op jit(solution)/shard_map/ppermute | solution.py:25
  44.3 14.5 %collective-permute-start.8 = (bf16[256,512]{1,0:T(8,128)(2,1)S(1)}, bf16[256,512]{1,0:T(8,128)(2,1)S(1)}, u32[]{:S(2)}, u32[]{:S(2)}) collective-permute-start(bf16[256,512]{1,0:T(8,128)(2,1)S(1)} %get-tuple-element.9), channel_id=1, source_target_pairs={{0,128},{64,192},{128,0},{192,64},{1,129},{65,193},{129,1},{193,65... | collective-permute-start | bytes 786440 | tf_op jit(solution)/shard_map/ppermute | solution.py:25
  52.2 9.9 %collective-permute-start = (bf16[128,1024]{1,0:T(8,128)(2,1)S(1)}, bf16[128,1024]{1,0:T(8,128)(2,1)S(1)}, u32[]{:S(2)}, u32[]{:S(2)}) collective-permute-start(bf16[128,1024]{1,0:T(8,128)(2,1)S(1)} %bitcast.26), channel_id=1, source_target_pairs={{0,1},{1,0},{2,3},{3,2},{4,5},{5,4},{6,7},{7,6},{8,9},{9,8},{10,11... | collective-permute-start | bytes 786440 | tf_op jit(solution)/shard_map/ppermute | solution.py:25
  53.0 0.7 copy-start.5
  53.7 60.3 %collective-permute-start.10 = (bf16[3584,896]{1,0:T(8,128)(2,1)}, bf16[3584,896]{1,0:T(8,128)(2,1)}, u32[]{:S(2)}, u32[]{:S(2)}) collective-permute-start(bf16[3584,896]{1,0:T(8,128)(2,1)} %refs_5_.1), channel_id=1, source_target_pairs={{0,1},{1,0},{2,3},{3,2},{4,5},{5,4},{6,7},{7,6},{8,9},{9,8},{10,11... | collective-permute-start | bytes 19267592 | tf_op jit(solution)/shard_map/ppermute | solution.py:25
  58.8 0.7 copy-start.7
  59.5 21.5 %collective-permute-start.11 = (bf16[128,3584]{1,0:T(8,128)(2,1)S(1)}, bf16[128,3584]{1,0:T(8,128)(2,1)S(1)}, u32[]{:S(2)}, u32[]{:S(2)}) collective-permute-start(bf16[128,3584]{1,0:T(8,128)(2,1)S(1)} %bitcast.24), channel_id=1, source_target_pairs={{0,64},{64,128},{128,192},{192,0},{1,65},{65,129},{129,193},{193,1... | collective-permute-start | bytes 2752520 | tf_op jit(solution)/shard_map/ppermute | solution.py:25
  60.2 21.6 %collective-permute-start.12 = (bf16[128,3584]{1,0:T(8,128)(2,1)S(1)}, bf16[128,3584]{1,0:T(8,128)(2,1)}, u32[]{:S(2)}, u32[]{:S(2)}) collective-permute-start(bf16[128,3584]{1,0:T(8,128)(2,1)S(1)} %bitcast.25), channel_id=1, source_target_pairs={{0,192},{64,0},{128,64},{192,128},{1,193},{65,1},{129,65},{193,129... | collective-permute-start | bytes 2752520 | tf_op jit(solution)/shard_map/ppermute | solution.py:25
  62.2 1.0 copy-start.6
  63.1 1.0 copy-start.8
  66.7 29.3 %all-to-all-start.1 = ((bf16[8,2,16,1024]{3,2,1,0:T(8,128)(2,1)}), bf16[8,2,16,1024]{3,2,1,0:T(8,128)(2,1)S(1)}, u32[]{:S(2)}, u32[]{:S(2)}) async-start(bf16[8,2,16,1024]{3,2,1,0:T(8,128)(2,1)} %project.1), calls=%async_computation.1 | async-start | bytes 1048576 | tf_op jit(solution)/shard_map/all_to_all | solution.py:276
  81.8 23.0 %collective-permute-start.13 = (bf16[128,1792]{1,0:T(8,128)(2,1)}, bf16[128,1792]{1,0:T(8,128)(2,1)S(1)}, u32[]{:S(2)}, u32[]{:S(2)}) collective-permute-start(bf16[128,1792]{1,0:T(8,128)(2,1)} %slice.40), channel_id=1, source_target_pairs={{0,64},{64,128},{128,192},{192,0},{1,65},{65,129},{129,193},{193,1... | collective-permute-start | bytes 1376264 | tf_op jit(solution)/shard_map/ppermute | solution.py:25
  83.6 21.2 %collective-permute-start.14 = (bf16[128,1792]{1,0:T(8,128)(2,1)}, bf16[128,1792]{1,0:T(8,128)(2,1)}, u32[]{:S(2)}, u32[]{:S(2)}) collective-permute-start(bf16[128,1792]{1,0:T(8,128)(2,1)} %slice.41), channel_id=1, source_target_pairs={{0,192},{64,0},{128,64},{192,128},{1,193},{65,1},{129,65},{193,129... | collective-permute-start | bytes 1376264 | tf_op jit(solution)/shard_map/ppermute | solution.py:25
  96.1 3.7 %collective-permute-start.9 = (bf16[16,1024]{1,0:T(8,128)(2,1)S(1)}, bf16[16,1024]{1,0:T(8,128)(2,1)S(1)}, u32[]{:S(2)}, u32[]{:S(2)}) collective-permute-start(bf16[16,1024]{1,0:T(8,128)(2,1)S(1)} %get-tuple-element.14), channel_id=1, source_target_pairs={{0,1},{1,0},{2,3},{3,2},{4,5},{5,4},{6,7},{7,6},{8,9},{9,8},{10,11... | collective-permute-start | bytes 98312 | tf_op jit(solution)/shard_map/ppermute | solution.py:25
  98.9 49.1 %collective-permute-start.15 = (bf16[2,1024,896]{2,1,0:T(8,128)(2,1)}, bf16[2,1024,896]{2,1,0:T(8,128)(2,1)}, u32[]{:S(2)}, u32[]{:S(2)}) collective-permute-start(bf16[2,1024,896]{2,1,0:T(8,128)(2,1)} %damp.1.ready.own), channel_id=1, source_target_pairs={{0,1},{1,0},{2,3},{3,2},{4,5},{5,4},{6,7},{7,6},{8,9},{9,8},{10,11... | collective-permute-start | bytes 11010056 | tf_op jit(solution)/shard_map/ppermute | solution.py:25
  100.6 23.8 %all-to-all-start.2 = ((bf16[8,16,2048]{2,1,0:T(8,128)(2,1)}), bf16[8,16,2048]{2,1,0:T(8,128)(2,1)}, u32[]{:S(2)}, u32[]{:S(2)}) async-start(bf16[8,16,2048]{2,1,0:T(8,128)(2,1)} %broadcast_in_dim.11.refs_6_), calls=%async_computation.2 | async-start | bytes 1048576 | tf_op jit(solution)/shard_map/all_to_all | solution.py:281
  104.8 54.1 %all-gather.5.cloned.1.call-start = ((), (), s32[]{:S(2)}) async-start(), calls=%async_computation.7 | async-start | bytes 2621440 | tf_op jit(solution)/shard_map/all_gather | solution.py:286
  123.4 1.0 copy-start.1
  124.4 1.2 copy-start.2
  142.2 4.7 %copy-start.14 = (s32[1024]{0:T(1024)S(1)}, s32[1024]{0:T(1024)}, u32[]{:S(2)}) copy-start(s32[1024]{0:T(1024)} %param.13) | copy-start | bytes 12292
  143.4 15.5 %all-to-all-start.4 = ((bf16[4,128,896]{2,1,0:T(8,128)(2,1)}), bf16[4,128,896]{2,1,0:T(8,128)(2,1)S(1)}, u32[]{:S(2)}, u32[]{:S(2)}) async-start(bf16[4,128,896]{2,1,0:T(8,128)(2,1)} %broadcast_in_dim.12), calls=%async_computation.4 | async-start | bytes 1835008 | tf_op jit(solution)/shard_map/all_to_all | solution.py:42
  158.9 1.0 copy-start.9
Sparse Core Ops, SparseCore 0:
  33.8 60.8 all-gather.2
  124.5 32.7 all-gather.4

commit v10 on v9

--- a/solution.py
+++ b/solution.py
@@ -16,7 +16,7 @@
 DAMPING = 0.1
 F32 = jnp.float32
 BF16 = jnp.bfloat16
-STEP = 512
+STEP = 896
 SPLIT = 3584
 
 

time: 202 us -> 201 us (level)
  no operation moved by 1% of the time
where the time goes in v10:
time: 201 us; the launch traced here: 200 us
  starting transfers between devices  47.5 us (24%)
  blocking collectives  40.6 us (20%)
  waiting for transfers between devices  38.4 us (19%)
  Pallas kernels  38.1 us (19%)
  local copies, waits for them, and re-layouts  19.6 us (10%)
  between operations  13.6 us (7%)
    ppermute x16, starting transfers between devices, shift(): lax.ppermute(value, axis, [(i, (i + hops) % size) for i in range(size)])  24 us
    all_to_all x1, blocking collectives, spread(): lax.all_to_all(jnp.broadcast_to(value[None], (size,) + value.shape), axes...  23.9 us
    pallas_call x2, Pallas kernels, rotate(): pl.pallas_call(functools.partial(rotate_kernel, places, axis, spans, len(...  17.8 us
    all_to_all x1, blocking collectives, over_x(): parts = lax.all_to_all(partial.reshape(4, rows // 4, cols), 'x', 0, 0)  16.7 us
    ppermute x16, waiting for transfers between devices, shift(): lax.ppermute(value, axis, [(i, (i + hops) % size) for i in range(size)])  13.8 us
    all_to_all x1, waiting for transfers between devices, spread(): lax.all_to_all(jnp.broadcast_to(value[None], (size,) + value.shape), axes...  10.9 us
    all_to_all x1, waiting for transfers between devices, shards(): parts = lax.all_to_all(project(rows, swap(rows), bases, here), 'z', 0, 0)  9.67 us
    all_to_all x1, starting transfers between devices, shards(): sent = lax.all_to_all(jnp.concatenate([copies, rows], axis=2), 'z', 0, 0)  9.01 us
  transfers between devices with their start and end apart: 22, of which 8 were waited for; matrix products, arithmetic and copies ran while one was open for 5% of the time, Pallas kernels for 15%

profile of v10, /device:TPU:1, one launch (start us, length us, event | category | flops | bytes accessed | tf_op | source)
XLA Modules:
  0.0 199.9 jit_solution(11999532493198227105)
XLA Ops:
  6.5 1.0 copy-done
  7.9 1.0 constant_dynamic-slice_fusion
  9.0 1.1 pad_maximum_fusion
  10.1 9.0 %all-to-all-start = ((bf16[8,16,4608]{2,1,0:T(8,128)(2,1)}), bf16[8,16,4608]{2,1,0:T(8,128)(2,1)}, u32[]{:S(2)}, u32[]{:S(2)}) async-start(bf16[8,16,4608]{2,1,0:T(8,128)(2,1)} %pad_maximum_fusion), calls=%async_computation | async-start | bytes 2359296 | tf_op jit(solution)/shard_map/all_to_all | solution.py:271
  19.2 1.0 collective-permute-start.1
  20.2 1.0 collective-permute-done.1.refs_0_
  21.2 1.3 collective-permute-start.2
  22.5 1.4 collective-permute-start.3
  23.9 1.6 collective-permute-start.4
  26.1 0.8 collective-permute-done.2.refs_1_
  26.9 3.8 %collective-permute-done.4.refs_3_ = bf16[16,3584]{1,0:T(8,128)(2,1)S(1)} collective-permute-done((bf16[16,3584]{1,0:T(8,128)(2,1)S(1)}, bf16[16,3584]{1,0:T(8,128)(2,1)S(1)}, u32[]{:S(2)}, u32[]{:S(2)}) %collective-permute-start.4) | collective-permute-done | bytes 114720 | tf_op jit(solution)/shard_map/ppermute | solution.py:25
  31.3 2.3 %join.1 = (bf16[64,3584]{1,0:T(8,128)(2,1)}, bf16[256,1024]{1,0:T(8,128)(2,1)}) custom-call(s32[2]{0:T(128)} %pad_add_fusion.here, bf16[16,3584]{1,0:T(8,128)(2,1)} %copy-done.10, bf16[16,3584]{1,0:T(8,128)(2,1)} %copy-done.11, bf16[16,3584]{1,0:T(8,128)(2,1)} %copy-done.12, bf16[16,3584]{1,0:T(8,128)(2,1)} %copy-done.13, bf16[256,1024]{1,0:T(8,128)(2,1)} %refs_4_.1), custom_call_target="tpu_custom_call" | custom-call | bytes 917504 | tf_op jit(solution)/shard_map/join/pallas_call | solution.py:62
  34.2 2.3 %collective-permute-start.6 = (bf16[256,1024]{1,0:T(8,128)(2,1)}, bf16[256,1024]{1,0:T(8,128)(2,1)}, u32[]{:S(2)}, u32[]{:S(2)}) collective-permute-start(bf16[256,1024]{1,0:T(8,128)(2,1)} %get-tuple-element.7.first), channel_id=1, source_target_pairs={{0,192},{64,0},{128,64},{192,128},{1,193},{65,1},{129,65},{193,129... | collective-permute-start | bytes 1572872 | tf_op jit(solution)/shard_map/ppermute | solution.py:25
  36.5 7.0 %damp.1.ready.own = bf16[2,1024,896]{2,1,0:T(8,128)(2,1)} custom-call(bf16[2,1024,896]{2,1,0:T(8,128)(2,1)} %queries.1, bf16[1024,896]{1,0:T(8,128)(2,1)} %eigenvalues.1, bf16[64,3584]{1,0:T(8,128)(2,1)} %get-tuple-element.8._), custom_call_target="tpu_custom_call" | custom-call | flops 3670016 | bytes 9175040 | tf_op jit(solution)/shard_map/damp/pallas_call | solution.py:104
  43.5 0.8 fusion
  44.3 3.0 %collective-permute-start.8 = (bf16[256,512]{1,0:T(8,128)(2,1)S(1)}, bf16[256,512]{1,0:T(8,128)(2,1)S(1)}, u32[]{:S(2)}, u32[]{:S(2)}) collective-permute-start(bf16[256,512]{1,0:T(8,128)(2,1)S(1)} %get-tuple-element.9), channel_id=1, source_target_pairs={{0,128},{64,192},{128,0},{192,64},{1,129},{65,193},{129,1},{193,65... | collective-permute-start | bytes 786440 | tf_op jit(solution)/shard_map/ppermute | solution.py:25
  47.2 4.0 %all-to-all-done = bf16[8,16,4608]{2,1,0:T(8,128)(2,1)} async-done(((bf16[8,16,4608]{2,1,0:T(8,128)(2,1)}), bf16[8,16,4608]{2,1,0:T(8,128)(2,1)}, u32[]{:S(2)}, u32[]{:S(2)}) %all-to-all-start) | async-done | bytes 1179680 | tf_op jit(solution)/shard_map/all_to_all | solution.py:271
  51.3 1.0 slice.36
  53.0 0.7 copy-done.5
  53.7 3.9 %collective-permute-start.10 = (bf16[3584,896]{1,0:T(8,128)(2,1)}, bf16[3584,896]{1,0:T(8,128)(2,1)}, u32[]{:S(2)}, u32[]{:S(2)}) collective-permute-start(bf16[3584,896]{1,0:T(8,128)(2,1)} %refs_5_.1), channel_id=1, source_target_pairs={{0,1},{1,0},{2,3},{3,2},{4,5},{5,4},{6,7},{7,6},{8,9},{9,8},{10,11... | collective-permute-start | bytes 19267592 | tf_op jit(solution)/shard_map/ppermute | solution.py:25
  57.5 1.2 slice.39.refs_0_
  59.5 0.8 collective-permute-start.11
  60.2 1.9 collective-permute-start.12
  62.2 0.9 copy-done.6
  63.1 1.0 copy-done.8
  64.1 2.6 %project.1 = bf16[8,2,16,1024]{3,2,1,0:T(8,128)(2,1)} custom-call(s32[2]{0:T(128)S(1)} %copy-done.4, bf16[128,1024]{1,0:T(8,128)(2,1)S(1)} %bitcast.27, bf16[128,1024]{1,0:T(8,128)(2,1)S(1)} %collective-permute-done.other, bf16[256,1024]{1,0:T(8,128)(2,1)S(1)} %copy-done.3, bf16[256,1024]{1,0:T(8,128)(2,1)S(1)} %collective-permute-done.5.second, ...), custom_call_target="tpu_custom_call" | custom-call | flops 40265318400 | bytes 4194304 | tf_op jit(solution)/shard_map/project/pallas_call | solution.py:85
  66.7 6.8 %all-to-all-start.1 = ((bf16[8,2,16,1024]{3,2,1,0:T(8,128)(2,1)}), bf16[8,2,16,1024]{3,2,1,0:T(8,128)(2,1)S(1)}, u32[]{:S(2)}, u32[]{:S(2)}) async-start(bf16[8,2,16,1024]{3,2,1,0:T(8,128)(2,1)} %project.1), calls=%async_computation.1 | async-start | bytes 1048576 | tf_op jit(solution)/shard_map/all_to_all | solution.py:276
  73.5 7.5 %collective-permute-done.11 = bf16[128,3584]{1,0:T(8,128)(2,1)S(1)} collective-permute-done((bf16[128,3584]{1,0:T(8,128)(2,1)S(1)}, bf16[128,3584]{1,0:T(8,128)(2,1)S(1)}, u32[]{:S(2)}, u32[]{:S(2)}) %collective-permute-start.11) | collective-permute-done | bytes 917536 | tf_op jit(solution)/shard_map/ppermute | solution.py:25
  81.0 0.8 slice.40
  81.8 1.8 slice.41
  83.6 2.7 %collective-permute-start.14 = (bf16[128,1792]{1,0:T(8,128)(2,1)}, bf16[128,1792]{1,0:T(8,128)(2,1)}, u32[]{:S(2)}, u32[]{:S(2)}) collective-permute-start(bf16[128,1792]{1,0:T(8,128)(2,1)} %slice.41), channel_id=1, source_target_pairs={{0,192},{64,0},{128,64},{192,128},{1,193},{65,1},{129,65},{193,129... | collective-permute-start | bytes 1376264 | tf_op jit(solution)/shard_map/ppermute | solution.py:25
  86.3 9.7 %all-to-all-done.1.refs_6_ = bf16[8,2,16,1024]{3,2,1,0:T(8,128)(2,1)S(1)} async-done(((bf16[8,2,16,1024]{3,2,1,0:T(8,128)(2,1)}), bf16[8,2,16,1024]{3,2,1,0:T(8,128)(2,1)S(1)}, u32[]{:S(2)}, u32[]{:S(2)}) %all-to-all-start.1) | async-done | bytes 524320 | tf_op jit(solution)/shard_map/all_to_all | solution.py:276
  96.1 2.8 %collective-permute-start.9 = (bf16[16,1024]{1,0:T(8,128)(2,1)S(1)}, bf16[16,1024]{1,0:T(8,128)(2,1)S(1)}, u32[]{:S(2)}, u32[]{:S(2)}) collective-permute-start(bf16[16,1024]{1,0:T(8,128)(2,1)S(1)} %get-tuple-element.14), channel_id=1, source_target_pairs={{0,1},{1,0},{2,3},{3,2},{4,5},{5,4},{6,7},{7,6},{8,9},{9,8},{10,11... | collective-permute-start | bytes 98312 | tf_op jit(solution)/shard_map/ppermute | solution.py:25
  99.0 0.8 collective-permute-done.9
  99.7 0.9 broadcast_in_dim.11.refs_6_
  100.6 4.2 %all-to-all-start.2 = ((bf16[8,16,2048]{2,1,0:T(8,128)(2,1)}), bf16[8,16,2048]{2,1,0:T(8,128)(2,1)}, u32[]{:S(2)}, u32[]{:S(2)}) async-start(bf16[8,16,2048]{2,1,0:T(8,128)(2,1)} %broadcast_in_dim.11.refs_6_), calls=%async_computation.2 | async-start | bytes 1048576 | tf_op jit(solution)/shard_map/all_to_all | solution.py:281
  104.9 8.8 %rotate_y.1.refs_5_ = f32[512,896]{1,0:T(8,128)S(1)} custom-call(s32[2]{0:T(128)S(1)} %copy-done.4, bf16[8,16,3584]{2,1,0:T(8,128)(2,1)S(1)} %slice.39.refs_0_, bf16[8,16,3584]{2,1,0:T(8,128)(2,1)S(1)} %bitcast.28, bf16[8,16,3584]{2,1,0:T(8,128)(2,1)} %bitcast.10.refs_2_, bf16[8,16,1792]{2,1,0:T(8,128)(2,1)S(1)} %bitcast.29, ...), custom_call_target="tpu_custom_call" | custom-call | flops 13153337344 | bytes 11010048 | tf_op jit(solution)/shard_map/rotate_y/pallas_call | solution.py:166
  113.7 9.0 %rotate_z.1.ready = bf16[512,896]{1,0:T(8,128)(2,1)S(1)} custom-call(s32[2]{0:T(128)S(1)} %copy-done.4, bf16[8,4,16,3584]{3,2,1,0:T(8,128)(2,1)} %bitcast.35, bf16[8,4,16,3584]{3,2,1,0:T(8,128)(2,1)} %bitcast.36, bf16[8,4,16,3584]{3,2,1,0:T(8,128)(2,1)} %bitcast.37, bf16[8,4,16,3584]{3,2,1,0:T(8,128)(2,1)} %bitcast.38, ...), custom_call_target="tpu_custom_call" | custom-call | flops 13153337344 | bytes 11010048 | tf_op jit(solution)/shard_map/rotate_z/pallas_call | solution.py:166
  122.7 1.0 copy-done.1
  123.7 1.2 copy-done.2
  124.9 16.7 %all_to_all.30 = bf16[4,128,896]{2,1,0:T(8,128)(2,1)S(1)} all-to-all(bf16[4,128,896]{2,1,0:T(8,128)(2,1)S(1)} %bitcast.23), channel_id=1, replica_groups=mesh['y'=4,'z'=8,'x'=4,'c'=2] {'x'}, dimensions={0} | all-to-all | bytes 1835008 | tf_op jit(solution)/shard_map/all_to_all | solution.py:244
  141.7 1.1 broadcast_in_dim.12
  142.8 3.5 %all-to-all-start.4 = ((bf16[4,128,896]{2,1,0:T(8,128)(2,1)}), bf16[4,128,896]{2,1,0:T(8,128)(2,1)S(1)}, u32[]{:S(2)}, u32[]{:S(2)}) async-start(bf16[4,128,896]{2,1,0:T(8,128)(2,1)} %broadcast_in_dim.12), calls=%async_computation.4 | async-start | bytes 1835008 | tf_op jit(solution)/shard_map/all_to_all | solution.py:42
  146.5 0.9 reshape.69.ids
  147.3 10.9 %all-to-all-done.4 = bf16[4,128,896]{2,1,0:T(8,128)(2,1)S(1)} async-done(((bf16[4,128,896]{2,1,0:T(8,128)(2,1)}), bf16[4,128,896]{2,1,0:T(8,128)(2,1)S(1)}, u32[]{:S(2)}, u32[]{:S(2)}) %all-to-all-start.4) | async-done | bytes 917536 | tf_op jit(solution)/shard_map/all_to_all | solution.py:42
  158.2 1.0 copy-done.9
  159.2 8.3 %score.1 = f32[2,1,128]{2,1,0:T(1,128)} custom-call(bf16[512,2048]{1,0:T(8,128)(2,1)} %all-gather.5.cloned.1.call-done.grads, bf16[2,1024,896]{2,1,0:T(8,128)(2,1)} %damp.1.ready.own, bf16[2,1024,896]{2,1,0:T(8,128)(2,1)} %collective-permute-done.15.other, bf16[512,896]{1,0:T(8,128)(2,1)} %bitcast.32, s32[512,1]{1,0:T(8,128)} %reshape.69.ids), custom_call_target="tpu_custom_call" | custom-call | flops 3758096384 | bytes 10354688 | tf_op jit(solution)/shard_map/score/pallas_call | solution.py:204
  168.4 23.9 %all_to_all.31 = f32[256,1,128]{2,1,0:T(1,128)S(1)} all-to-all(f32[256,1,128]{2,1,0:T(1,128)S(1)} %broadcast_in_dim.14), channel_id=1, replica_groups=mesh['y'=4,'z'=8,'x'=4,'c'=2] {'y','z','x','c'}, dimensions={0} | all-to-all | bytes 262144 | tf_op jit(solution)/shard_map/all_to_all | solution.py:42
  (65 shorter events, 5.8 us)
Async XLA Ops:
  6.5 1.0 copy-start
  10.1 41.2 %all-to-all-start = ((bf16[8,16,4608]{2,1,0:T(8,128)(2,1)}), bf16[8,16,4608]{2,1,0:T(8,128)(2,1)}, u32[]{:S(2)}, u32[]{:S(2)}) async-start(bf16[8,16,4608]{2,1,0:T(8,128)(2,1)} %pad_maximum_fusion), calls=%async_computation | async-start | bytes 2359296 | tf_op jit(solution)/shard_map/all_to_all | solution.py:271
  19.1 85.7 %all-gather.3.cloned.1.call-start = ((), (), s32[]{:S(2)}) async-start(), calls=%async_computation.6 | async-start | bytes 4128768 | tf_op jit(solution)/shard_map/all_gather | solution.py:262
  19.2 2.0 %collective-permute-start.1 = (bf16[16,3584]{1,0:T(8,128)(2,1)S(1)}, bf16[16,3584]{1,0:T(8,128)(2,1)S(1)}, u32[]{:S(2)}, u32[]{:S(2)}) collective-permute-start(bf16[16,3584]{1,0:T(8,128)(2,1)S(1)} %get-tuple-element.11), channel_id=1, source_target_pairs={{0,1},{1,0},{2,3},{3,2},{4,5},{5,4},{6,7},{7,6},{8,9},{9,8},{10,11... | collective-permute-start | bytes 344072 | tf_op jit(solution)/shard_map/ppermute | solution.py:25
  21.2 9.5 %copy-start.10 = (bf16[16,3584]{1,0:T(8,128)(2,1)}, bf16[16,3584]{1,0:T(8,128)(2,1)S(1)}, u32[]{:S(2)}) copy-start(bf16[16,3584]{1,0:T(8,128)(2,1)S(1)} %collective-permute-done.1.refs_0_) | copy-start | bytes 344068
  21.2 5.7 %collective-permute-start.2 = (bf16[16,3584]{1,0:T(8,128)(2,1)S(1)}, bf16[16,3584]{1,0:T(8,128)(2,1)S(1)}, u32[]{:S(2)}, u32[]{:S(2)}) collective-permute-start(bf16[16,3584]{1,0:T(8,128)(2,1)S(1)} %collective-permute-done.1.refs_0_), channel_id=1, source_target_pairs={{0,64},{64,128},{128,192},{192,0},{1,65},{65,129},{129,193},{193,1... | collective-permute-start | bytes 344072 | tf_op jit(solution)/shard_map/ppermute | solution.py:25
  22.5 4.4 %collective-permute-start.3 = (bf16[16,3584]{1,0:T(8,128)(2,1)S(1)}, bf16[16,3584]{1,0:T(8,128)(2,1)S(1)}, u32[]{:S(2)}, u32[]{:S(2)}) collective-permute-start(bf16[16,3584]{1,0:T(8,128)(2,1)S(1)} %collective-permute-done.1.refs_0_), channel_id=1, source_target_pairs={{0,192},{64,0},{128,64},{192,128},{1,193},{65,1},{129,65},{193,129... | collective-permute-start | bytes 344072 | tf_op jit(solution)/shard_map/ppermute | solution.py:25
  23.9 6.8 %collective-permute-start.4 = (bf16[16,3584]{1,0:T(8,128)(2,1)S(1)}, bf16[16,3584]{1,0:T(8,128)(2,1)S(1)}, u32[]{:S(2)}, u32[]{:S(2)}) collective-permute-start(bf16[16,3584]{1,0:T(8,128)(2,1)S(1)} %collective-permute-done.1.refs_0_), channel_id=1, source_target_pairs={{0,128},{64,192},{128,0},{192,64},{1,129},{65,193},{129,1},{193,65... | collective-permute-start | bytes 344072 | tf_op jit(solution)/shard_map/ppermute | solution.py:25
  26.9 3.8 %copy-start.11 = (bf16[16,3584]{1,0:T(8,128)(2,1)}, bf16[16,3584]{1,0:T(8,128)(2,1)S(1)}, u32[]{:S(2)}) copy-start(bf16[16,3584]{1,0:T(8,128)(2,1)S(1)} %collective-permute-done.2.refs_1_) | copy-start | bytes 344068
  26.9 3.8 %copy-start.12 = (bf16[16,3584]{1,0:T(8,128)(2,1)}, bf16[16,3584]{1,0:T(8,128)(2,1)S(1)}, u32[]{:S(2)}) copy-start(bf16[16,3584]{1,0:T(8,128)(2,1)S(1)} %collective-permute-done.3.refs_2_) | copy-start | bytes 344068
  30.7 0.7 copy-start.13
  33.7 9.8 %copy-start.3 = (bf16[256,1024]{1,0:T(8,128)(2,1)S(1)}, bf16[256,1024]{1,0:T(8,128)(2,1)}, u32[]{:S(2)}) copy-start(bf16[256,1024]{1,0:T(8,128)(2,1)} %get-tuple-element.7.first) | copy-start | bytes 1572868
  33.7 26.5 %collective-permute-start.5 = (bf16[256,1024]{1,0:T(8,128)(2,1)}, bf16[256,1024]{1,0:T(8,128)(2,1)S(1)}, u32[]{:S(2)}, u32[]{:S(2)}) collective-permute-start(bf16[256,1024]{1,0:T(8,128)(2,1)} %get-tuple-element.7.first), channel_id=1, source_target_pairs={{0,64},{64,128},{128,192},{192,0},{1,65},{65,129},{129,193},{193,1... | collective-permute-start | bytes 1572872 | tf_op jit(solution)/shard_map/ppermute | solution.py:25
  34.2 28.0 %collective-permute-start.6 = (bf16[256,1024]{1,0:T(8,128)(2,1)}, bf16[256,1024]{1,0:T(8,128)(2,1)}, u32[]{:S(2)}, u32[]{:S(2)}) collective-permute-start(bf16[256,1024]{1,0:T(8,128)(2,1)} %get-tuple-element.7.first), channel_id=1, source_target_pairs={{0,192},{64,0},{128,64},{192,128},{1,193},{65,1},{129,65},{193,129... | collective-permute-start | bytes 1572872 | tf_op jit(solution)/shard_map/ppermute | solution.py:25
  44.3 17.9 %copy-start.4 = (s32[2]{0:T(128)S(1)}, s32[2]{0:T(128)}, u32[]{:S(2)}) copy-start(s32[2]{0:T(128)} %pad_add_fusion.here) | copy-start | bytes 28
  44.3 8.7 %collective-permute-start.7 = (bf16[256,512]{1,0:T(8,128)(2,1)}, bf16[256,512]{1,0:T(8,128)(2,1)S(1)}, u32[]{:S(2)}, u32[]{:S(2)}) collective-permute-start(bf16[256,512]{1,0:T(8,128)(2,1)} %after.2), channel_id=1, source_target_pairs={{0,128},{64,192},{128,0},{192,64},{1,129},{65,193},{129,1},{193,65... | collective-permute-start | bytes 786440 | tf_op jit(solution)/shard_map/ppermute | solution.py:25
  44.3 14.5 %collective-permute-start.8 = (bf16[256,512]{1,0:T(8,128)(2,1)S(1)}, bf16[256,512]{1,0:T(8,128)(2,1)S(1)}, u32[]{:S(2)}, u32[]{:S(2)}) collective-permute-start(bf16[256,512]{1,0:T(8,128)(2,1)S(1)} %get-tuple-element.9), channel_id=1, source_target_pairs={{0,128},{64,192},{128,0},{192,64},{1,129},{65,193},{129,1},{193,65... | collective-permute-start | bytes 786440 | tf_op jit(solution)/shard_map/ppermute | solution.py:25
  52.2 9.9 %collective-permute-start = (bf16[128,1024]{1,0:T(8,128)(2,1)S(1)}, bf16[128,1024]{1,0:T(8,128)(2,1)S(1)}, u32[]{:S(2)}, u32[]{:S(2)}) collective-permute-start(bf16[128,1024]{1,0:T(8,128)(2,1)S(1)} %bitcast.26), channel_id=1, source_target_pairs={{0,1},{1,0},{2,3},{3,2},{4,5},{5,4},{6,7},{7,6},{8,9},{9,8},{10,11... | collective-permute-start | bytes 786440 | tf_op jit(solution)/shard_map/ppermute | solution.py:25
  53.0 0.7 copy-start.5
  53.7 60.0 %collective-permute-start.10 = (bf16[3584,896]{1,0:T(8,128)(2,1)}, bf16[3584,896]{1,0:T(8,128)(2,1)}, u32[]{:S(2)}, u32[]{:S(2)}) collective-permute-start(bf16[3584,896]{1,0:T(8,128)(2,1)} %refs_5_.1), channel_id=1, source_target_pairs={{0,1},{1,0},{2,3},{3,2},{4,5},{5,4},{6,7},{7,6},{8,9},{9,8},{10,11... | collective-permute-start | bytes 19267592 | tf_op jit(solution)/shard_map/ppermute | solution.py:25
  58.8 0.7 copy-start.7
  59.5 21.5 %collective-permute-start.11 = (bf16[128,3584]{1,0:T(8,128)(2,1)S(1)}, bf16[128,3584]{1,0:T(8,128)(2,1)S(1)}, u32[]{:S(2)}, u32[]{:S(2)}) collective-permute-start(bf16[128,3584]{1,0:T(8,128)(2,1)S(1)} %bitcast.24), channel_id=1, source_target_pairs={{0,64},{64,128},{128,192},{192,0},{1,65},{65,129},{129,193},{193,1... | collective-permute-start | bytes 2752520 | tf_op jit(solution)/shard_map/ppermute | solution.py:25
  60.2 21.6 %collective-permute-start.12 = (bf16[128,3584]{1,0:T(8,128)(2,1)S(1)}, bf16[128,3584]{1,0:T(8,128)(2,1)}, u32[]{:S(2)}, u32[]{:S(2)}) collective-permute-start(bf16[128,3584]{1,0:T(8,128)(2,1)S(1)} %bitcast.25), channel_id=1, source_target_pairs={{0,192},{64,0},{128,64},{192,128},{1,193},{65,1},{129,65},{193,129... | collective-permute-start | bytes 2752520 | tf_op jit(solution)/shard_map/ppermute | solution.py:25
  62.2 1.0 copy-start.6
  63.1 1.0 copy-start.8
  66.7 29.3 %all-to-all-start.1 = ((bf16[8,2,16,1024]{3,2,1,0:T(8,128)(2,1)}), bf16[8,2,16,1024]{3,2,1,0:T(8,128)(2,1)S(1)}, u32[]{:S(2)}, u32[]{:S(2)}) async-start(bf16[8,2,16,1024]{3,2,1,0:T(8,128)(2,1)} %project.1), calls=%async_computation.1 | async-start | bytes 1048576 | tf_op jit(solution)/shard_map/all_to_all | solution.py:276
  81.8 23.0 %collective-permute-start.13 = (bf16[128,1792]{1,0:T(8,128)(2,1)}, bf16[128,1792]{1,0:T(8,128)(2,1)S(1)}, u32[]{:S(2)}, u32[]{:S(2)}) collective-permute-start(bf16[128,1792]{1,0:T(8,128)(2,1)} %slice.40), channel_id=1, source_target_pairs={{0,64},{64,128},{128,192},{192,0},{1,65},{65,129},{129,193},{193,1... | collective-permute-start | bytes 1376264 | tf_op jit(solution)/shard_map/ppermute | solution.py:25
  83.6 21.2 %collective-permute-start.14 = (bf16[128,1792]{1,0:T(8,128)(2,1)}, bf16[128,1792]{1,0:T(8,128)(2,1)}, u32[]{:S(2)}, u32[]{:S(2)}) collective-permute-start(bf16[128,1792]{1,0:T(8,128)(2,1)} %slice.41), channel_id=1, source_target_pairs={{0,192},{64,0},{128,64},{192,128},{1,193},{65,1},{129,65},{193,129... | collective-permute-start | bytes 1376264 | tf_op jit(solution)/shard_map/ppermute | solution.py:25
  96.1 3.7 %collective-permute-start.9 = (bf16[16,1024]{1,0:T(8,128)(2,1)S(1)}, bf16[16,1024]{1,0:T(8,128)(2,1)S(1)}, u32[]{:S(2)}, u32[]{:S(2)}) collective-permute-start(bf16[16,1024]{1,0:T(8,128)(2,1)S(1)} %get-tuple-element.14), channel_id=1, source_target_pairs={{0,1},{1,0},{2,3},{3,2},{4,5},{5,4},{6,7},{7,6},{8,9},{9,8},{10,11... | collective-permute-start | bytes 98312 | tf_op jit(solution)/shard_map/ppermute | solution.py:25
  98.9 48.5 %collective-permute-start.15 = (bf16[2,1024,896]{2,1,0:T(8,128)(2,1)}, bf16[2,1024,896]{2,1,0:T(8,128)(2,1)}, u32[]{:S(2)}, u32[]{:S(2)}) collective-permute-start(bf16[2,1024,896]{2,1,0:T(8,128)(2,1)} %damp.1.ready.own), channel_id=1, source_target_pairs={{0,1},{1,0},{2,3},{3,2},{4,5},{5,4},{6,7},{7,6},{8,9},{9,8},{10,11... | collective-permute-start | bytes 11010056 | tf_op jit(solution)/shard_map/ppermute | solution.py:25
  100.6 23.1 %all-to-all-start.2 = ((bf16[8,16,2048]{2,1,0:T(8,128)(2,1)}), bf16[8,16,2048]{2,1,0:T(8,128)(2,1)}, u32[]{:S(2)}, u32[]{:S(2)}) async-start(bf16[8,16,2048]{2,1,0:T(8,128)(2,1)} %broadcast_in_dim.11.refs_6_), calls=%async_computation.2 | async-start | bytes 1048576 | tf_op jit(solution)/shard_map/all_to_all | solution.py:281
  104.8 53.5 %all-gather.5.cloned.1.call-start = ((), (), s32[]{:S(2)}) async-start(), calls=%async_computation.7 | async-start | bytes 2621440 | tf_op jit(solution)/shard_map/all_gather | solution.py:286
  122.7 1.0 copy-start.1
  123.7 1.2 copy-start.2
  141.6 4.7 %copy-start.14 = (s32[1024]{0:T(1024)S(1)}, s32[1024]{0:T(1024)}, u32[]{:S(2)}) copy-start(s32[1024]{0:T(1024)} %param.13) | copy-start | bytes 12292
  142.8 15.5 %all-to-all-start.4 = ((bf16[4,128,896]{2,1,0:T(8,128)(2,1)}), bf16[4,128,896]{2,1,0:T(8,128)(2,1)S(1)}, u32[]{:S(2)}, u32[]{:S(2)}) async-start(bf16[4,128,896]{2,1,0:T(8,128)(2,1)} %broadcast_in_dim.12), calls=%async_computation.4 | async-start | bytes 1835008 | tf_op jit(solution)/shard_map/all_to_all | solution.py:42
  158.2 1.0 copy-start.9
Sparse Core Ops, SparseCore 0:
  33.8 60.8 all-gather.2
  123.9 32.7 all-gather.4
